TPU v7x, 32 devices: a whole 2x2x4 slice. The times are simulated.
32 devices in a mesh: sub: 16 (over z, y, core), rhs: 2 (over x).
Axes of the slice: x: 2, y: 2, z: 4, core: 2. Of those that a mesh axis runs over, the one named last changes fastest.
Arguments:
- right_side: float32 [64, 8192], P('rhs', 'sub'), may hold values from -6 to 6
- stiffness_blocks: float32 [128, 27, 4096], P('sub'), may hold values from -0.15625 to 0.15625
- block_columns: int32 [128, 27], P('sub'), may hold values from 0 to 15
- interface_rows: int32 [16, 2, 4], P('sub'), may hold values from 0 to 7, as said below
- corner_owner: int32 [16, 8], P('sub'), may hold values from 0 to 31, as said below
- corner_basis: float32 [8, 8192], P('rhs', 'sub'), may hold values from -0.25 to 0.25
- jacobi_scale: float32 [8192], P('sub'), may hold values from 0.5 to 2
- coarse_inverse: float32 [32, 32], replicated, as said below
Outputs:
- solution_field: float32 [64, 8192], P('rhs', 'sub')
- residual: float32 [64, 8192], P('rhs', 'sub')
Inputs may be any that keep to these rules, and one draw needn't show every extreme that they name: `interface_rows`: the 8 block rows named for one subdomain are distinct. `corner_owner`: corner j of subdomain s names a coarse unknown between (s - 1) * 2 and (s + 2) * 2 - 1, within range; corner 0 names s * 2, corner 8 - 1 names s * 2 + 1. `coarse_inverse`: symmetric and positive definite.
All inputs are finite; a program needn't handle non-finite values.
Results may differ from a plain program's by a relative error of at most 0.0003.
Values sent between devices are 32-bit elements; how exact they have to be, the bound alone decides.
No kernel may reach another device: no remote copies, remote signals or barrier semaphores. Data moves between devices by JAX's collectives and lax.ppermute only.
A program may use at most 64 MiB of HBM per device.

v0:
```python
import jax
import jax.numpy as jnp
from jax import lax
from jax.sharding import PartitionSpec as P

B = 64
KNZ = 27
IFB = 4
NCL = 8
ITERS = 2


diag_shift = 1.0


def with_halo(cells, sides, width):
    for axis, dim in sides:
        count = lax.axis_size(axis)
        ends = count - 1
        head = lax.slice_in_dim(cells, 0, width, axis=dim)
        tail = lax.slice_in_dim(cells, cells.shape[dim] - width, cells.shape[dim], axis=dim)
        cells = jnp.concatenate(
            [
                lax.ppermute(tail, axis, [(i, (i + 1) % count) for i in range(ends)]),
                cells,
                lax.ppermute(head, axis, [((i + 1) % count, i) for i in range(ends)]),
            ],
            axis=dim,
        )
    return cells


def body(
    right_side,
    stiffness_blocks,
    block_columns,
    interface_rows,
    corner_owner,
    corner_basis,
    jacobi_scale,
    coarse_inverse,
):
    highest = lax.Precision.HIGHEST
    cases = right_side.shape[0]
    nloc = right_side.shape[1]
    nblock = nloc // B
    nextend = nblock + 2 * IFB
    ncoarse = coarse_inverse.shape[0]
    blocks = stiffness_blocks.reshape(nblock, KNZ, B, B)
    chosen = interface_rows.reshape(2 * IFB)
    select = (chosen[:, None] == jnp.arange(nblock, dtype=jnp.int32)[None, :]).astype(jnp.float32)
    column_hits = (
        block_columns.reshape(-1)[None, :] == jnp.arange(nextend, dtype=jnp.int32)[:, None]
    ).astype(jnp.float32)
    own_hits = (
        corner_owner.reshape(NCL)[:, None] == jnp.arange(ncoarse, dtype=jnp.int32)[None, :]
    ).astype(jnp.float32)
    basis = lax.all_gather(corner_basis, "rhs", axis=0, tiled=True)

    def precondition(resid):
        corner = jnp.dot(resid, basis.T, precision=highest)
        local_coarse = jnp.dot(corner, own_hits, precision=highest)
        coarse = lax.psum(local_coarse, "sub")
        solved = jnp.dot(coarse, coarse_inverse, precision=highest)
        spread = jnp.dot(solved, own_hits.T, precision=highest)
        z = jacobi_scale[None, :] * resid + jnp.dot(spread, basis, precision=highest)
        rz = lax.psum(jnp.sum(resid * z, axis=1), "sub")
        return (z, rz)

    solution_field = jnp.zeros_like(right_side)
    residual = right_side
    z, rz = precondition(residual)
    direction = z
    for step in range(ITERS):
        grid = direction.reshape(cases, nblock, B)
        edges = jnp.einsum("jn,cnb->cjb", select, grid, precision=highest).reshape(
            cases, 2, IFB * B
        )
        padded = with_halo(edges, (("sub", 1),), 1)
        below = padded[:, 0].reshape(cases, IFB, B)
        above = padded[:, 3].reshape(cases, IFB, B)
        extended = jnp.concatenate([grid, below, above], axis=1)
        picked = extended[:, block_columns]
        strain = jnp.einsum("ikab,cikb->cia", blocks, picked, precision=highest)
        back = jnp.einsum("ikab,cia->cikb", blocks, strain, precision=highest).reshape(
            cases, nblock * KNZ, B
        )
        summed = jnp.einsum("em,cmb->ceb", column_hits, back, precision=highest)
        ghosts = summed[:, nblock:].reshape(cases, 2, IFB * B)
        returned = with_halo(ghosts, (("sub", 1),), 1)
        arrived = jnp.concatenate(
            [returned[:, 0].reshape(cases, IFB, B), returned[:, 3].reshape(cases, IFB, B)], axis=1
        )
        total = summed[:, :nblock] + jnp.einsum("jn,cjb->cnb", select, arrived, precision=highest)
        image = diag_shift * direction + total.reshape(cases, nloc)
        alpha = rz / lax.psum(jnp.sum(direction * image, axis=1), "sub")
        solution_field = solution_field + alpha[:, None] * direction
        residual = residual - alpha[:, None] * image
        if step + 1 < ITERS:
            z, rz_next = precondition(residual)
            direction = z + (rz_next / rz)[:, None] * direction
            rz = rz_next
    return (solution_field, residual)


def solution(mesh):
    placed = (
        P("rhs", "sub"),
        P("sub", None, None),
        P("sub", None),
        P("sub", None, None),
        P("sub", None),
        P("rhs", "sub"),
        P("sub"),
        P(),
    )
    return jax.shard_map(
        body,
        mesh=mesh,
        in_specs=placed,
        out_specs=(P("rhs", "sub"), P("rhs", "sub")),
        check_vma=False,
    )
```

profile of v0, /device:TPU:0, one launch (start us, length us, event | category | flops | bytes accessed | tf_op | source)
XLA Modules:
  0.0 297.8 jit_solution(17717595777411854076)
XLA Ops:
  0.6 0.8 eq.49
  1.4 5.5 %all-gather = f32[2,4,512]{2,1,0:T(4,128)S(1)} all-gather(f32[1,4,512]{2,1,0:T(4,128)} %bitcast.100), channel_id=1, replica_groups=mesh['sub'=16,'rhs'=2] {'rhs'}, dimensions={0}, use_global_device_ids=true | all-gather | bytes 24576 | tf_op jit(solution)/shard_map/all_gather | solution.py:58
  6.9 1.0 fusion.60
  7.9 0.9 fusion.40
  8.8 60.8 %psum.42 = f32[32,32]{1,0:T(8,128)S(1)} all-reduce(f32[32,32]{1,0:T(8,128)S(1)} %fusion.40), channel_id=1, replica_groups=mesh['sub'=16,'rhs'=2] {'sub'}, use_global_device_ids=true, to_apply=%region_0.0 | all-reduce | flops 1024 | bytes 8192 | tf_op jit(solution)/shard_map/psum | solution.py:63
  69.7 0.1 fusion.61
  69.8 0.8 fusion.39
  70.7 1.1 convolution_add_fusion.1
  71.9 0.3 convolution_bitcast_fusion.3
  72.1 0.1 reshape.45
  72.3 1.3 collective-permute-start.1
  73.6 3.0 %collective-permute-start = (f32[32,1,256]{2,0,1:T(8,128)S(1)}, f32[32,1,256]{2,0,1:T(8,128)S(1)}, u32[]{:S(2)}, u32[]{:S(2)}) collective-permute-start(f32[32,1,256]{2,0,1:T(8,128)S(1)} %copy.68), channel_id=1, source_target_pairs={{0,2},{2,4},{4,6},{6,8},{8,10},{10,12},{12,14},{14,16},{16,18},{18... | collective-permute-start | bytes 98312 | tf_op jit(solution)/shard_map/ppermute | solution.py:24
  76.7 0.7 compare_select_fusion
  77.5 0.8 eq.53
  78.3 6.7 %reshape.46 = f32[8,27,64,64]{3,2,0,1:T(8,128)} reshape(f32[8,27,4096]{2,0,1:T(8,128)} %param.9) | data formatting | bytes 7077888 | tf_op jit(solution)/shard_map/reshape | solution.py:49
  85.2 2.8 gather_fusion
  88.0 9.2 %fusion.18 = f32[32,8,64,1]{2,0,3,1:T(8,128)S(1)} fusion(f32[32,8,27,64]{3,0,2,1:T(8,128)} %bitcast.97, f32[8,27,64,64]{3,2,0,1:T(8,128)} %reshape.46), kind=kOutput, calls=%fused_computation.16 | convolution fusion | flops 339738624 | bytes 5373952 | tf_op jit(solution)/shard_map/ikab,cikb->cia/dot_general | solution.py:84
  97.3 4.2 %fusion.4 = f32[8,32,27,64]{3,1,2,0:T(8,128)S(1)} fusion(f32[32,8,64,1]{2,0,3,1:T(8,128)S(1)} %fusion.18, f32[8,27,64,64]{3,2,0,1:T(8,128)S(1)} %bitcast.93), kind=kOutput, calls=%fused_computation.6 | convolution fusion | flops 339738624 | bytes 5373952 | tf_op jit(solution)/shard_map/ikab,cia->cikb/dot_general | solution.py:85
  101.5 3.2 %fusion.12 = f32[32,16,64]{2,1,0:T(8,128)S(1)} fusion(f32[32,216,64]{2,0,1:T(8,128)S(1)} %bitcast.99, s32[216]{0:T(256)S(1)} %eq.53), kind=kOutput, calls=%fused_computation.14 | convolution fusion | flops 84938112 | bytes 1901408 | tf_op jit(solution)/shard_map/em,cmb->ceb/dot_general | solution.py:88
  104.7 0.1 reshape.48
  104.9 1.9 collective-permute-start.2
  106.8 1.5 collective-permute-start.3
  108.5 1.6 collective-permute-done.3
  110.3 0.2 fusion.25
  110.6 0.1 multiply_reduce_fusion.2
  110.7 31.6 %all-reduce = (f32[32]{0:T(128)S(1)}, f32[32]{0:T(128)S(1)}) all-reduce(f32[32]{0:T(128)S(1)} %get-tuple-element.3, f32[32]{0:T(128)S(1)} %get-tuple-element.2), channel_id=1, replica_groups=mesh['sub'=16,'rhs'=2] {'sub'}, use_global_device_ids=true, to_apply=%region_2.0 | all-reduce | flops 64 | bytes 512 | tf_op jit(solution)/shard_map/psum | solution.py:67
  142.4 0.2 fusion.62
  142.6 0.2 fusion.38
  142.8 57.6 %psum.45 = f32[32,32]{1,0:T(8,128)S(1)} all-reduce(f32[32,32]{1,0:T(8,128)S(1)} %fusion.38), channel_id=1, replica_groups=mesh['sub'=16,'rhs'=2] {'sub'}, use_global_device_ids=true, to_apply=%region_5.0 | all-reduce | flops 1024 | bytes 8192 | tf_op jit(solution)/shard_map/psum | solution.py:63
  200.4 0.1 fusion.63
  200.6 0.2 fusion.37
  200.8 0.4 multiply_reduce_fusion.1
  201.2 29.5 %psum.46 = f32[32]{0:T(128)S(1)} all-reduce(f32[32]{0:T(128)S(1)} %get-tuple-element.19), channel_id=1, replica_groups=mesh['sub'=16,'rhs'=2] {'sub'}, use_global_device_ids=true, to_apply=%region_7.0 | all-reduce | flops 32 | bytes 256 | tf_op jit(solution)/shard_map/psum | solution.py:67
  230.8 0.3 convolution_bitcast_fusion.1
  231.3 1.3 collective-permute-start.5
  232.6 3.0 %collective-permute-start.4 = (f32[32,1,256]{2,0,1:T(8,128)S(1)}, f32[32,1,256]{2,0,1:T(8,128)S(1)}, u32[]{:S(2)}, u32[]{:S(2)}) collective-permute-start(f32[32,1,256]{2,0,1:T(8,128)S(1)} %copy.70), channel_id=1, source_target_pairs={{0,2},{2,4},{4,6},{6,8},{8,10},{10,12},{12,14},{14,16},{16,18},{18... | collective-permute-start | bytes 98312 | tf_op jit(solution)/shard_map/ppermute | solution.py:24
  235.8 0.7 collective-permute-done.4
  236.6 2.8 gather_fusion.1
  239.4 9.2 %fusion.21 = f32[32,8,64,1]{2,0,3,1:T(8,128)S(1)} fusion(f32[32,8,27,64]{3,0,2,1:T(8,128)} %bitcast.96, f32[8,27,64,64]{3,2,0,1:T(8,128)} %reshape.46), kind=kOutput, calls=%fused_computation.17 | convolution fusion | flops 339738624 | bytes 5373952 | tf_op jit(solution)/shard_map/ikab,cikb->cia/dot_general | solution.py:84
  248.6 4.2 %fusion = f32[8,32,27,64]{3,1,2,0:T(8,128)S(1)} fusion(f32[32,8,64,1]{2,0,3,1:T(8,128)S(1)} %fusion.21, f32[8,27,64,64]{3,2,0,1:T(8,128)S(1)} %bitcast.95), kind=kOutput, calls=%fused_computation.2 | convolution fusion | flops 339738624 | bytes 5373952 | tf_op jit(solution)/shard_map/ikab,cia->cikb/dot_general | solution.py:85
  252.8 3.2 %fusion.15 = f32[32,16,64]{2,1,0:T(8,128)S(1)} fusion(f32[32,216,64]{2,0,1:T(8,128)S(1)} %bitcast.98, s32[216]{0:T(256)S(1)} %eq.53), kind=kOutput, calls=%fused_computation.15 | convolution fusion | flops 84938112 | bytes 1901408 | tf_op jit(solution)/shard_map/em,cmb->ceb/dot_general | solution.py:88
  256.2 3.2 %collective-permute-start.6 = (f32[32,1,256]{2,1,0:T(1,128)S(1)}, f32[32,1,256]{2,1,0:T(1,128)S(1)}, u32[]{:S(2)}, u32[]{:S(2)}) collective-permute-start(f32[32,1,256]{2,1,0:T(1,128)S(1)} %get-tuple-element.9), channel_id=1, source_target_pairs={{0,2},{2,4},{4,6},{6,8},{8,10},{10,12},{12,14},{14,16},{16,18},{18... | collective-permute-start | bytes 98312 | tf_op jit(solution)/shard_map/ppermute | solution.py:24
  259.4 1.3 collective-permute-start.7
  260.9 3.4 %collective-permute-done.7 = f32[32,1,256]{2,1,0:T(1,128)S(1)} collective-permute-done((f32[32,1,256]{2,1,0:T(1,128)S(1)}, f32[32,1,256]{2,1,0:T(1,128)S(1)}, u32[]{:S(2)}, u32[]{:S(2)}) %collective-permute-start.7) | collective-permute-done | bytes 32800 | tf_op jit(solution)/shard_map/ppermute | solution.py:26
  264.5 0.2 fusion.24
  264.8 0.1 multiply_reduce_fusion
  264.9 32.1 %psum.47 = f32[32]{0:T(128)S(1)} all-reduce(f32[32]{0:T(128)S(1)} %get-tuple-element.6), channel_id=1, replica_groups=mesh['sub'=16,'rhs'=2] {'sub'}, use_global_device_ids=true, to_apply=%region_9.0 | all-reduce | flops 32 | bytes 256 | tf_op jit(solution)/shard_map/psum | solution.py:96
  297.1 0.7 multiply_subtract_fusion
  (67 shorter events, 2.3 us)
Async XLA Ops:
  0.6 69.1 %copy-start = (f32[32,32]{1,0:T(8,128)S(1)}, f32[32,32]{1,0:T(8,128)}, u32[]{:S(2)}) copy-start(f32[32,32]{1,0:T(8,128)} %param.15) | copy-start | bytes 12292
  72.3 12.6 %collective-permute-start.1 = (f32[32,1,256]{2,0,1:T(8,128)S(1)}, f32[32,1,256]{2,0,1:T(8,128)S(1)}, u32[]{:S(2)}, u32[]{:S(2)}) collective-permute-start(f32[32,1,256]{2,0,1:T(8,128)S(1)} %copy.69), channel_id=1, source_target_pairs={{2,0},{4,2},{6,4},{8,6},{10,8},{12,10},{14,12},{16,14},{18,16},{20... | collective-permute-start | bytes 98312 | tf_op jit(solution)/shard_map/ppermute | solution.py:26
  73.6 11.4 %collective-permute-start = (f32[32,1,256]{2,0,1:T(8,128)S(1)}, f32[32,1,256]{2,0,1:T(8,128)S(1)}, u32[]{:S(2)}, u32[]{:S(2)}) collective-permute-start(f32[32,1,256]{2,0,1:T(8,128)S(1)} %copy.68), channel_id=1, source_target_pairs={{0,2},{2,4},{4,6},{6,8},{8,10},{10,12},{12,14},{14,16},{16,18},{18... | collective-permute-start | bytes 98312 | tf_op jit(solution)/shard_map/ppermute | solution.py:24
  85.2 12.0 %slice-start = ((s8[7077888]{0:T(1024)(128)(4,1)}), s8[2883584]{0:T(1024)(128)(4,1)S(1)}, s32[]{:S(2)}) async-start(s8[7077888]{0:T(1024)(128)(4,1)} %bitcast.92), calls=%async_computation | async-start | bytes 5767168
  88.0 9.2 %slice-start.1 = ((s8[7077888]{0:T(1024)(128)(4,1)}), s8[4194304]{0:T(1024)(128)(4,1)S(1)}, s32[]{:S(2)}) async-start(s8[7077888]{0:T(1024)(128)(4,1)} %bitcast.92), calls=%async_computation.1 | async-start | bytes 8388608
  101.4 9.2 %copy-start.1 = (f32[32,512]{1,0:T(8,128)S(1)}, f32[32,512]{1,0:T(8,128)}, u32[]{:S(2)}) copy-start(f32[32,512]{1,0:T(8,128)} %param.8) | copy-start | bytes 196612
  101.4 41.1 %copy-start.3 = (s32[1,8]{1,0:T(1,128)S(1)}, s32[1,8]{1,0:T(1,128)}, u32[]{:S(2)}) copy-start(s32[1,8]{1,0:T(1,128)} %param.12) | copy-start | bytes 100
  101.4 99.3 %copy-start.2 = (f32[512]{0:T(512)S(1)}, f32[512]{0:T(512)}, u32[]{:S(2)}) copy-start(f32[512]{0:T(512)} %param.14) | copy-start | bytes 6148
  104.9 3.4 %collective-permute-start.2 = (f32[32,1,256]{2,1,0:T(1,128)S(1)}, f32[32,1,256]{2,1,0:T(1,128)S(1)}, u32[]{:S(2)}, u32[]{:S(2)}) collective-permute-start(f32[32,1,256]{2,1,0:T(1,128)S(1)} %get-tuple-element.13), channel_id=1, source_target_pairs={{0,2},{2,4},{4,6},{6,8},{8,10},{10,12},{12,14},{14,16},{16,18},{18... | collective-permute-start | bytes 98312 | tf_op jit(solution)/shard_map/ppermute | solution.py:24
  106.8 3.3 %collective-permute-start.3 = (f32[32,1,256]{2,1,0:T(1,128)S(1)}, f32[32,1,256]{2,1,0:T(1,128)S(1)}, u32[]{:S(2)}, u32[]{:S(2)}) collective-permute-start(f32[32,1,256]{2,1,0:T(1,128)S(1)} %get-tuple-element.14), channel_id=1, source_target_pairs={{2,0},{4,2},{6,4},{8,6},{10,8},{12,10},{14,12},{16,14},{18,16},{20... | collective-permute-start | bytes 98312 | tf_op jit(solution)/shard_map/ppermute | solution.py:26
  231.3 4.4 %collective-permute-start.5 = (f32[32,1,256]{2,0,1:T(8,128)S(1)}, f32[32,1,256]{2,0,1:T(8,128)S(1)}, u32[]{:S(2)}, u32[]{:S(2)}) collective-permute-start(f32[32,1,256]{2,0,1:T(8,128)S(1)} %copy.71), channel_id=1, source_target_pairs={{2,0},{4,2},{6,4},{8,6},{10,8},{12,10},{14,12},{16,14},{18,16},{20... | collective-permute-start | bytes 98312 | tf_op jit(solution)/shard_map/ppermute | solution.py:26
  232.6 3.9 %collective-permute-start.4 = (f32[32,1,256]{2,0,1:T(8,128)S(1)}, f32[32,1,256]{2,0,1:T(8,128)S(1)}, u32[]{:S(2)}, u32[]{:S(2)}) collective-permute-start(f32[32,1,256]{2,0,1:T(8,128)S(1)} %copy.70), channel_id=1, source_target_pairs={{0,2},{2,4},{4,6},{6,8},{8,10},{10,12},{12,14},{14,16},{16,18},{18... | collective-permute-start | bytes 98312 | tf_op jit(solution)/shard_map/ppermute | solution.py:24
  236.6 12.0 %slice-start.2 = ((s8[7077888]{0:T(1024)(128)(4,1)}), s8[2883584]{0:T(1024)(128)(4,1)S(1)}, s32[]{:S(2)}) async-start(s8[7077888]{0:T(1024)(128)(4,1)} %bitcast.94), calls=%async_computation.2 | async-start | bytes 5767168
  239.4 9.2 %slice-start.3 = ((s8[7077888]{0:T(1024)(128)(4,1)}), s8[4194304]{0:T(1024)(128)(4,1)S(1)}, s32[]{:S(2)}) async-start(s8[7077888]{0:T(1024)(128)(4,1)} %bitcast.94), calls=%async_computation.3 | async-start | bytes 8388608
  256.2 4.5 %collective-permute-start.6 = (f32[32,1,256]{2,1,0:T(1,128)S(1)}, f32[32,1,256]{2,1,0:T(1,128)S(1)}, u32[]{:S(2)}, u32[]{:S(2)}) collective-permute-start(f32[32,1,256]{2,1,0:T(1,128)S(1)} %get-tuple-element.9), channel_id=1, source_target_pairs={{0,2},{2,4},{4,6},{6,8},{8,10},{10,12},{12,14},{14,16},{16,18},{18... | collective-permute-start | bytes 98312 | tf_op jit(solution)/shard_map/ppermute | solution.py:24
  259.4 4.9 %collective-permute-start.7 = (f32[32,1,256]{2,1,0:T(1,128)S(1)}, f32[32,1,256]{2,1,0:T(1,128)S(1)}, u32[]{:S(2)}, u32[]{:S(2)}) collective-permute-start(f32[32,1,256]{2,1,0:T(1,128)S(1)} %get-tuple-element.10), channel_id=1, source_target_pairs={{2,0},{4,2},{6,4},{8,6},{10,8},{12,10},{14,12},{16,14},{18,16},{20... | collective-permute-start | bytes 98312 | tf_op jit(solution)/shard_map/ppermute | solution.py:26
where the time goes:
time: 299 us; the launch traced here: 298 us
  blocking collectives  217 us (73%)
  matrix products  39.2 us (13%)
  starting transfers between devices  16.5 us (6%)
  local copies, waits for them, and re-layouts  15.8 us (5%)
  waiting for transfers between devices  5.74 us (2%)
    psum x2, blocking collectives, precondition(): coarse = lax.psum(local_coarse, 'sub')  118 us
    psum x2, blocking collectives, precondition(): rz = lax.psum(jnp.sum(resid * z, axis=1), 'sub')  61.1 us
    psum x1, blocking collectives, body(): alpha = rz / lax.psum(jnp.sum(direction * image, axis=1), 'sub')  32.1 us
    dot_general x2, matrix products, body(): strain = jnp.einsum('ikab,cikb->cia', blocks, picked, precision=highest)  18.4 us
    ppermute x4, starting transfers between devices, with_halo(): lax.ppermute(tail, axis, [(i, (i + 1) % count) for i in range(ends)])  11.2 us
    dot_general x2, matrix products, body(): jnp.einsum('ikab,cia->cikb', blocks, strain, precision=highest)  8.32 us
    reshape x1, local copies, waits for them, and re-layouts, body(): blocks = stiffness_blocks.reshape(nblock, KNZ, B, B)  6.69 us
    dot_general x2, matrix products, body(): summed = jnp.einsum('em,cmb->ceb', column_hits, back, precision=highest)  6.47 us
  transfers between devices with their start and end apart: 8, of which 3 were waited for; matrix products, arithmetic and copies ran while one was open for 3% of the time, Pallas kernels for 0%

commit v1 on v0

v1 whole, which is shorter than its diff:
```python
import functools

import jax
import jax.numpy as jnp
from jax import lax
from jax.experimental import pallas as pl
from jax.experimental.pallas import tpu as pltpu
from jax.sharding import PartitionSpec as P

B = 64
KNZ = 27
IFB = 4
NCL = 8
NB = 2 * IFB
NE = NB + 2 * IFB
EDGE = IFB * B
OWN = NB * B
EXT = NE * B
ROWS = NB * B
KPAD = 32
F32 = jnp.float32
BF16 = jnp.bfloat16
HIGHEST = lax.Precision.HIGHEST
NT = (((1,), (1,)), ((), ()))
NN = (((1,), (0,)), ((), ()))
VMEM_LIMIT = 48 * 1024 * 1024


def split(x):
    high = x.astype(BF16)
    return high, (x - high.astype(F32)).astype(BF16)


def times(x, high, low, dims):
    count = x.shape[0]
    xh, xl = split(x)
    both = lax.dot_general(
        jnp.concatenate([xh, xl], axis=0), high, dims, preferred_element_type=F32
    )
    return both[:count] + both[count:] + lax.dot_general(xh, low, dims, preferred_element_type=F32)


def exact(x, y, dims=NN):
    return lax.dot_general(x, y, dims, precision=HIGHEST, preferred_element_type=F32)


def call(kernel, outs, n_in, smem=(), scratch=()):
    def spec(space):
        return pl.BlockSpec(memory_space=space)

    return pl.pallas_call(
        kernel,
        out_shape=outs,
        in_specs=[spec(pltpu.SMEM if i in smem else pltpu.VMEM) for i in range(n_in)],
        out_specs=[spec(pltpu.VMEM) for _ in outs],
        scratch_shapes=list(scratch),
        compiler_params=pltpu.CompilerParams(vmem_limit_bytes=VMEM_LIMIT),
    )


def shape(*dims):
    return jax.ShapeDtypeStruct(dims, F32)


def place_of(rows_ref, odd, j):
    side = jnp.where(odd == 1, j // IFB, 1 - j // IFB)
    return rows_ref[0, side, j % IFB]


def assemble(rows_ref, columns_ref, blocks_ref, high_ref, low_ref, wh_ref, wl_ref):
    step = pl.program_id(0)
    odd = lax.axis_index("sub") % 2

    @pl.when(step == 0)
    def _():
        wh_ref[...] = jnp.zeros_like(wh_ref)
        wl_ref[...] = jnp.zeros_like(wl_ref)

    column = columns_ref[0]
    place = jnp.where(
        column < NB, -1, jnp.where((column < NB + IFB) == (odd == 1), column % IFB + NB, column % IFB + NB + IFB)
    )
    for j in range(NB):
        place = jnp.where(column == place_of(rows_ref, odd, j), j, place)
    place = jnp.where(column < 0, -1, place)
    r = lax.broadcasted_iota(jnp.int32, (NE * 8, 8 * KPAD), 0)
    q = lax.broadcasted_iota(jnp.int32, (NE * 8, 8 * KPAD), 1)
    hit = (r // 8 == place) & (r % 8 == q // KPAD)
    onehot = jnp.where(hit, 1.0, 0.0).astype(BF16)
    for g in range(8):
        wh, wl = split(blocks_ref[0, :, 512 * g : 512 * (g + 1)])
        wh_ref[g, :KNZ, :] = wh
        wl_ref[g, :KNZ, :] = wl
    dense = lax.dot_general(
        onehot, wh_ref[...].reshape(8 * KPAD, 512), NN, preferred_element_type=F32
    ) + lax.dot_general(onehot, wl_ref[...].reshape(8 * KPAD, 512), NN, preferred_element_type=F32)
    first = lax.broadcasted_iota(jnp.int32, (8, 128), 1) < B
    for m in range(NE // 2):
        for h in range(4):
            left = dense[16 * m : 16 * m + 8, 128 * h : 128 * (h + 1)]
            right = dense[16 * m + 8 : 16 * m + 16, 128 * h : 128 * (h + 1)]
            tile = jnp.concatenate(
                [
                    jnp.where(first, left, pltpu.roll(right, B, 1)),
                    jnp.where(first, pltpu.roll(left, B, 1), right),
                ],
                axis=0,
            )
            th, tl = split(tile)
            high_ref[16 * h : 16 * (h + 1), 128 * m : 128 * (m + 1)] = th
            low_ref[16 * h : 16 * (h + 1), 128 * m : 128 * (m + 1)] = tl


def prepare(rows_ref, owner_ref, right_ref, scale_ref, *rest, parts, ncoarse):
    basis_refs = rest[:parts]
    resid_ref, side_a_ref, side_b_ref, blk_ref = rest[parts:]
    odd = lax.axis_index("sub") % 2
    mine = lax.axis_index("rhs")
    cases = right_ref.shape[0]
    per = NCL // parts
    scale = jnp.broadcast_to(scale_ref[...], (8, OWN))
    unknown = lax.broadcasted_iota(jnp.int32, (ncoarse, OWN), 0)
    coarse = jnp.zeros((ncoarse, OWN), F32)
    for k in range(parts):
        for t in range(per):
            owner = owner_ref[0, ((mine + k) % parts) * per + t]
            coarse = coarse + jnp.where(unknown == owner, basis_refs[k][t : t + 1, :], 0.0)
    right = right_ref[...]
    total = 2 * cases + ncoarse + 8
    for n in range(NB):
        cut = slice(B * n, B * (n + 1))
        blk_ref[n, 0:cases, :] = right[:, cut] * scale[0:1, cut]
        blk_ref[n, cases : cases + ncoarse, :] = coarse[:, cut]
        blk_ref[n, cases + ncoarse : cases + ncoarse + 8, :] = scale[:, cut]
        blk_ref[n, cases + ncoarse + 8 : total, :] = right[:, cut]
    for j in range(0, NB, 2):
        pair = jnp.concatenate(
            [blk_ref[place_of(rows_ref, odd, j)], blk_ref[place_of(rows_ref, odd, j + 1)]], axis=1
        )
        target = side_a_ref if j < IFB else side_b_ref
        at = B * (j % IFB)
        target[:, at : at + 2 * B] = pair[: total - cases]
        resid_ref[:, B * j : B * (j + 2)] = pair[total - cases :]


def first_strain(
    resid_ref, a_ref, b_ref, ga_ref, gb_ref, high_ref, low_ref, strain_ref, pay_ref, *, cases, ncoarse
):
    count = cases + ncoarse
    field = jnp.concatenate(
        [a_ref[:count, :], b_ref[:count, :], ga_ref[:count, :], gb_ref[:count, :]], axis=1
    )
    strain = times(field, high_ref[...], low_ref[...], NT)
    strain_ref[...] = strain
    own = field[:, :OWN]
    resid = resid_ref[...]
    paired = jnp.concatenate([own, strain], axis=1)
    gram = exact(paired, paired[cases:], NT)
    restricted = exact(resid, own[cases:], NT)
    lead = paired[:cases]
    pay_ref[...] = jnp.zeros_like(pay_ref)
    pay_ref[:cases, 0:ncoarse] = restricted
    pay_ref[:cases, ncoarse : 2 * ncoarse] = gram[:cases]
    pay_ref[:ncoarse, 2 * ncoarse : 3 * ncoarse] = gram[cases:]
    pay_ref[:cases, 3 * ncoarse : 3 * ncoarse + 1] = jnp.sum(
        resid * own[:cases], axis=1, keepdims=True
    )
    pay_ref[:cases, 3 * ncoarse + 1 : 3 * ncoarse + 2] = jnp.sum(lead * lead, axis=1, keepdims=True)


def first_image(a_ref, b_ref, strain_ref, high_ref, low_ref, send_a_ref, send_b_ref):
    strain = strain_ref[...]
    count = strain.shape[0]
    back = times(strain, high_ref[...], low_ref[...], NN)
    send_a_ref[:count, :] = a_ref[:count, :] + back[:, :EDGE]
    send_a_ref[count:, :] = back[:, OWN : OWN + EDGE]
    send_b_ref[:count, :] = b_ref[:count, :] + back[:, EDGE:OWN]
    send_b_ref[count:, :] = back[:, OWN + EDGE :]


def second_strain(
    inverse_ref,
    resid_ref,
    a_ref,
    b_ref,
    ga_ref,
    gb_ref,
    own_a_ref,
    own_b_ref,
    got_a_ref,
    got_b_ref,
    high_ref,
    low_ref,
    *rest,
    cases,
    ncoarse,
    n_pay,
):
    pays = rest[:n_pay]
    strain_ref, pay_ref, resid1_ref, z0_ref, z1_ref, q0_ref, keep_ref = rest[n_pay:]
    count = cases + ncoarse
    pay = pays[0][...]
    for other in pays[1:]:
        pay = pay + other[...]
    u0 = pay[:cases, 0:ncoarse]
    ra = pay[:cases, ncoarse : 2 * ncoarse]
    rac = pay[:ncoarse, 2 * ncoarse : 3 * ncoarse]
    inverse = inverse_ref[...]
    y0 = exact(u0, inverse)
    ry = exact(y0, rac)
    rz0 = pay[:cases, 3 * ncoarse : 3 * ncoarse + 1] + jnp.sum(u0 * y0, axis=1, keepdims=True)
    pq0 = pay[:cases, 3 * ncoarse + 1 : 3 * ncoarse + 2] + jnp.sum(
        y0 * (2.0 * ra + ry), axis=1, keepdims=True
    )
    alpha = rz0 / pq0
    u1 = u0 - alpha * (ra + ry)
    y1 = exact(u1, inverse)
    image = jnp.concatenate(
        [
            own_a_ref[:count, :] + got_a_ref[count:, :],
            own_b_ref[:count, :] + got_b_ref[count:, :],
            own_a_ref[count:, :] + got_a_ref[:count, :],
            own_b_ref[count:, :] + got_b_ref[:count, :],
        ],
        axis=1,
    )
    parts = [a_ref, b_ref, ga_ref, gb_ref]
    scaled = jnp.concatenate([ref[:cases, :] for ref in parts], axis=1)
    coarse = jnp.concatenate([ref[cases:count, :] for ref in parts], axis=1)
    scale = jnp.concatenate([ref[count : count + 1, :] for ref in parts], axis=1)
    q0 = image[:cases] + exact(y0, image[cases:])
    z0 = scaled[:, :OWN] + exact(y0, coarse[:, :OWN])
    resid1 = resid_ref[...] - alpha * q0[:, :OWN]
    z1 = scaled - (alpha * scale) * q0 + exact(y1, coarse)
    strain = times(z1, high_ref[...], low_ref[...], NT)
    strain_ref[...] = strain
    own = z1[:, :OWN]
    resid1_ref[...] = resid1
    z0_ref[...] = z0
    z1_ref[...] = own
    q0_ref[...] = q0[:, :OWN]
    pay_ref[...] = jnp.zeros_like(pay_ref)
    pay_ref[:, 0:1] = jnp.sum(resid1 * resid1 * scale[:, :OWN], axis=1, keepdims=True)
    pay_ref[:, 1:2] = jnp.sum(own * own, axis=1, keepdims=True) + jnp.sum(
        strain * strain, axis=1, keepdims=True
    )
    pay_ref[:, 2:3] = jnp.sum(own * q0[:, :OWN], axis=1, keepdims=True)
    keep_ref[...] = jnp.zeros_like(keep_ref)
    keep_ref[:, 0:1] = rz0
    keep_ref[:, 1:2] = pq0
    keep_ref[:, 2:3] = alpha
    keep_ref[:, 3:4] = jnp.sum(u1 * y1, axis=1, keepdims=True)


def second_image(z1_ref, strain_ref, high_ref, low_ref, own_ref, send_a_ref, send_b_ref):
    back = times(strain_ref[...], high_ref[...], low_ref[...], NN)
    own_ref[...] = z1_ref[...] + back[:, :OWN]
    send_a_ref[...] = back[:, OWN : OWN + EDGE]
    send_b_ref[...] = back[:, OWN + EDGE :]


def finish(
    rows_ref, resid1_ref, z0_ref, z1_ref, q0_ref, keep_ref, own_ref, got_a_ref, got_b_ref, *rest, n_pay
):
    pays = rest[:n_pay]
    field_ref, resid2_ref, blk_ref = rest[n_pay:]
    odd = lax.axis_index("sub") % 2
    cases = own_ref.shape[0]
    pay = pays[0][...]
    for other in pays[1:]:
        pay = pay + other[...]
    keep = keep_ref[...]
    rz0, pq0, alpha0 = keep[:, 0:1], keep[:, 1:2], keep[:, 2:3]
    rz1 = pay[:, 0:1] + keep[:, 3:4]
    beta = rz1 / rz0
    pq1 = pay[:, 1:2] + beta * (2.0 * pay[:, 2:3] + beta * pq0)
    alpha1 = rz1 / pq1
    image = own_ref[...] + jnp.concatenate([got_a_ref[...], got_b_ref[...]], axis=1)
    z0 = z0_ref[...]
    field = alpha0 * z0 + alpha1 * (z1_ref[...] + beta * z0)
    resid2 = resid1_ref[...] - alpha1 * (image + beta * q0_ref[...])
    for j in range(NB):
        at = place_of(rows_ref, odd, j)
        blk_ref[at, :cases, :] = field[:, B * j : B * (j + 1)]
        blk_ref[at, cases:, :] = resid2[:, B * j : B * (j + 1)]
    for n in range(0, NB, 2):
        pair = jnp.concatenate([blk_ref[n], blk_ref[n + 1]], axis=1)
        field_ref[:, B * n : B * (n + 2)] = pair[:cases]
        resid2_ref[:, B * n : B * (n + 2)] = pair[cases:]


def swap(x, steps, count):
    return [lax.ppermute(x, "sub", [(i, i ^ k) for i in range(count)]) for k in steps]


def rounds_of(count):
    rounds = []
    base = 1
    while base < count:
        if base * 4 <= count:
            rounds.append((base, 2 * base, 3 * base))
            base *= 4
        else:
            rounds.append((base,))
            base *= 2
    return rounds


def across(a, b, count):
    low = lax.ppermute(a, "sub", [(i, i ^ 1) for i in range(count)])
    inner = [(i, i + 1) for i in range(1, count - 1, 2)]
    return low, lax.ppermute(b, "sub", inner + [(j, i) for i, j in inner])


def body(
    right_side,
    stiffness_blocks,
    block_columns,
    interface_rows,
    corner_owner,
    corner_basis,
    jacobi_scale,
    coarse_inverse,
):
    cases = right_side.shape[0]
    ncoarse = coarse_inverse.shape[0]
    count = lax.axis_size("sub")
    parts = lax.axis_size("rhs")
    live = cases + ncoarse
    rounds = rounds_of(count)

    bases = [corner_basis] + [
        lax.ppermute(corner_basis, "rhs", [((i + k) % parts, i) for i in range(parts)])
        for k in range(1, parts)
    ]
    padded = jnp.pad(block_columns, ((0, 0), (0, KPAD - KNZ)), constant_values=-1)
    tiled = jnp.tile(padded, (1, 8)).reshape(NB, 1, 8 * KPAD)
    high, low = pl.pallas_call(
        assemble,
        out_shape=[jax.ShapeDtypeStruct((ROWS, EXT), BF16)] * 2,
        grid=(NB,),
        in_specs=[
            pl.BlockSpec(memory_space=pltpu.SMEM),
            pl.BlockSpec((1, 1, 8 * KPAD), lambda i: (i, 0, 0)),
            pl.BlockSpec((1, KNZ, B * B), lambda i: (i, 0, 0)),
        ],
        out_specs=[pl.BlockSpec((B, EXT), lambda i: (i, 0))] * 2,
        scratch_shapes=[pltpu.VMEM((8, KPAD, 512), BF16)] * 2,
        compiler_params=pltpu.CompilerParams(vmem_limit_bytes=VMEM_LIMIT),
    )(interface_rows, tiled, stiffness_blocks)

    resid, side_a, side_b = call(
        functools.partial(prepare, parts=parts, ncoarse=ncoarse),
        [shape(cases, OWN), shape(live + 8, EDGE), shape(live + 8, EDGE)],
        4 + parts,
        smem=(0, 1),
        scratch=[pltpu.VMEM((NB, live + 8 + cases, B), F32)],
    )(interface_rows, corner_owner, right_side, jacobi_scale.reshape(1, OWN), *bases)
    ghost_a, ghost_b = across(side_a, side_b, count)

    lanes = -(-(3 * ncoarse + 2) // 128) * 128
    strain, pay = call(
        functools.partial(first_strain, cases=cases, ncoarse=ncoarse),
        [shape(live, ROWS), shape(max(cases, ncoarse), lanes)],
        7,
    )(resid, side_a, side_b, ghost_a, ghost_b, high, low)
    for steps in rounds[:-1]:
        pay = sum(swap(pay, steps, count), pay)
    pays = [pay] + swap(pay, rounds[-1], count)
    own_a, own_b = call(first_image, [shape(2 * live, EDGE)] * 2, 5)(side_a, side_b, strain, high, low)
    got_a, got_b = across(own_a, own_b, count)

    strain, pay, resid1, z0, z1, q0, keep = call(
        functools.partial(second_strain, cases=cases, ncoarse=ncoarse, n_pay=len(pays)),
        [shape(cases, ROWS), shape(cases, 128)] + [shape(cases, OWN)] * 4 + [shape(cases, 128)],
        12 + len(pays),
    )(
        coarse_inverse, resid, side_a, side_b, ghost_a, ghost_b, own_a, own_b, got_a, got_b, high, low, *pays
    )
    for steps in rounds[:-1]:
        pay = sum(swap(pay, steps, count), pay)
    pays = [pay] + swap(pay, rounds[-1], count)
    own, back_a, back_b = call(
        second_image, [shape(cases, OWN), shape(cases, EDGE), shape(cases, EDGE)], 4
    )(z1, strain, high, low)
    got_a, got_b = across(back_a, back_b, count)
    return tuple(
        call(
            functools.partial(finish, n_pay=len(pays)),
            [shape(cases, OWN)] * 2,
            9 + len(pays),
            smem=(0,),
            scratch=[pltpu.VMEM((NB, 2 * cases, B), F32)],
        )(interface_rows, resid1, z0, z1, q0, keep, own, got_a, got_b, *pays)
    )


def solution(mesh):
    placed = (
        P("rhs", "sub"),
        P("sub", None, None),
        P("sub", None),
        P("sub", None, None),
        P("sub", None),
        P("rhs", "sub"),
        P("sub"),
        P(),
    )
    return jax.shard_map(
        body,
        mesh=mesh,
        in_specs=placed,
        out_specs=(P("rhs", "sub"), P("rhs", "sub")),
        check_vma=False,
    )
```

time: 299 us -> 59.6 us (0.20)
  blocking collectives: 217 us -> 0 us
  matrix products: 39.2 us -> 0 us
  Pallas kernels: 0 us -> 13.1 us
  waiting for transfers between devices: 5.74 us -> 12.2 us
  starting transfers between devices: 16.5 us -> 22.6 us
  local copies, waits for them, and re-layouts: 15.8 us -> 10.4 us
    psum x5 -> x0, blocking collectives: 212 us -> none  [the longest x2 118 us: precondition(): coarse = lax.psum(local_coarse, 'sub')]
    dot_general x20 -> x0, matrix products: 39.2 us -> none  [the longest x2 18.4 us: body(): strain = jnp.einsum('ikab,cikb->cia', blocks, picked, precision=highest)]
    pallas_call x0 -> x7, Pallas kernels: none -> 13.1 us  [the longest x1 6.55 us: body(): pl.pallas_call(assemble, out_shape=[jax.ShapeDtypeStruct((ROWS, EXT), BF1...]
    unnamed x21 -> x15, local copies, waits for them, and re-layouts: 0.07 us -> 9.6 us
    reshape x11 -> x0, local copies, waits for them, and re-layouts: 7.53 us -> none  [the longest x1 6.69 us: body(): blocks = stiffness_blocks.reshape(nblock, KNZ, B, B)]
    ppermute x8 -> x19, waiting for transfers between devices: 5.74 us -> 12.2 us  [the longest x12 10.3 us: swap(): lax.ppermute(x, 'sub', [(i, i ^ k) for i in range(count)])]
    ppermute x8 -> x19, starting transfers between devices: 16.5 us -> 22.6 us  [the longest x12 17 us: swap(): lax.ppermute(x, 'sub', [(i, i ^ k) for i in range(count)])]
    gather x2 -> x0, local copies, waits for them, and re-layouts: 5.58 us -> none  [body(): picked = extended[:, block_columns]]
  transfers between devices with their start and end apart: 8 -> 19, of which waited for: 3 -> 8; matrix products, arithmetic and copies ran while one was open for 3% -> 12% of each run, Pallas kernels for 0% -> 13%
where the time goes in v1:
time: 59.6 us; the launch traced here: 59.1 us
  starting transfers between devices  22.6 us (38%)
  Pallas kernels  13.1 us (22%)
  waiting for transfers between devices  12.2 us (20%)
  local copies, waits for them, and re-layouts  10.4 us (17%)
  between operations  0.8 us (1%)
    ppermute x12, starting transfers between devices, swap(): lax.ppermute(x, 'sub', [(i, i ^ k) for i in range(count)])  17 us
    ppermute x12, waiting for transfers between devices, swap(): lax.ppermute(x, 'sub', [(i, i ^ k) for i in range(count)])  10.3 us
    unnamed x15, local copies, waits for them, and re-layouts  9.6 us
    pallas_call x1, Pallas kernels, body(): pl.pallas_call(assemble, out_shape=[jax.ShapeDtypeStruct((ROWS, EXT), BF1...  6.55 us
    ppermute x1, starting transfers between devices, body(): lax.ppermute(corner_basis, 'rhs', [((i + k) % parts, i) for i in range(pa...  3 us
    ppermute x3, starting transfers between devices, across(): return (low, lax.ppermute(b, 'sub', inner + [(j, i) for i, j in inner]))  1.98 us
    ppermute x1, waiting for transfers between devices, body(): lax.ppermute(corner_basis, 'rhs', [((i + k) % parts, i) for i in range(pa...  1.84 us
    pallas_call x1, Pallas kernels, body(): call(functools.partial(finish, n_pay=len(pays)), [shape(cases, OWN)] * 2,...  1.82 us
  transfers between devices with their start and end apart: 19, of which 8 were waited for; matrix products, arithmetic and copies ran while one was open for 12% of the time, Pallas kernels for 13%

profile of v1, /device:TPU:0, one launch (start us, length us, event | category | flops | bytes accessed | tf_op | source)
XLA Modules:
  0.0 59.1 jit_solution(17920256720708116086)
XLA Ops:
  0.6 3.0 %collective-permute-start = (f32[4,512]{1,0:T(4,128)}, f32[4,512]{1,0:T(4,128)S(1)}, u32[]{:S(2)}, u32[]{:S(2)}) collective-permute-start(f32[4,512]{1,0:T(4,128)} %rest_0_.1), channel_id=1, source_target_pairs={{1,0},{0,1},{3,2},{2,3},{5,4},{4,5},{7,6},{6,7},{9,8},{8,9},{11,10... | collective-permute-start | bytes 24584 | tf_op jit(solution)/shard_map/ppermute | solution.py:333
  3.6 1.8 %collective-permute-done.rest_1_ = f32[4,512]{1,0:T(4,128)S(1)} collective-permute-done((f32[4,512]{1,0:T(4,128)}, f32[4,512]{1,0:T(4,128)S(1)}, u32[]{:S(2)}, u32[]{:S(2)}) %collective-permute-start) | collective-permute-done | bytes 8224 | tf_op jit(solution)/shard_map/ppermute | solution.py:333
  5.5 0.8 %copy-done = f32[32,512]{1,0:T(8,128)S(1)} copy-done((f32[32,512]{1,0:T(8,128)S(1)}, f32[32,512]{1,0:T(8,128)}, u32[]{:S(2)}) %copy-start) | copy-done | bytes 65560
  6.3 0.7 %copy-done.2 = s32[1,2,4]{2,1,0:T(2,128)S(1)} copy-done((s32[1,2,4]{2,1,0:T(2,128)S(1)}, s32[1,2,4]{2,1,0:T(2,128)}, u32[]{:S(2)}) %copy-start.2) | copy-done | bytes 56
  7.0 0.7 %copy-done.4 = f32[4,512]{1,0:T(4,128)S(1)} copy-done((f32[4,512]{1,0:T(4,128)S(1)}, f32[4,512]{1,0:T(4,128)}, u32[]{:S(2)}) %copy-start.4) | copy-done | bytes 8216
  7.7 0.7 %copy-done.5 = f32[512]{0:T(512)S(1)} copy-done((f32[512]{0:T(512)S(1)}, f32[512]{0:T(512)}, u32[]{:S(2)}) %copy-start.5) | copy-done | bytes 2072
  8.4 0.7 %copy-done.6 = s32[1,8]{1,0:T(1,128)S(1)} copy-done((s32[1,8]{1,0:T(1,128)S(1)}, s32[1,8]{1,0:T(1,128)}, u32[]{:S(2)}) %copy-start.6) | copy-done | bytes 56
  9.0 0.8 %shard_map.95 = (f32[32,512]{1,0:T(8,128)S(1)}, f32[72,256]{1,0:T(8,128)S(1)}, f32[72,256]{1,0:T(8,128)S(1)}) custom-call(s32[1,2,4]{2,1,0:T(2,128)S(1)} %copy-done.2, s32[1,8]{1,0:T(1,128)S(1)} %copy-done.6, f32[32,512]{1,0:T(8,128)S(1)} %copy-done, f32[1,512]{1,0:T(1,128)S(1)} %bitcast.1, f32[4,512]{1,0:T(4,128)S(1)} %copy-done.4, ...), custom_call_target="tpu_custom_call" | custom-call | tf_op jit(solution)/shard_map/pallas_call | solution.py:352
  9.9 0.1 collective-permute-start.1
  9.9 0.7 %collective-permute-start.2 = (f32[72,256]{1,0:T(8,128)S(1)}, f32[72,256]{1,0:T(8,128)S(1)}, u32[]{:S(2)}, u32[]{:S(2)}) collective-permute-start(f32[72,256]{1,0:T(8,128)S(1)} %get-tuple-element.23.b_ref), channel_id=1, source_target_pairs={{2,4},{6,8},{10,12},{14,16},{18,20},{22,24},{26,28},{4,2},{8,6},{1... | collective-permute-start | bytes 221192 | tf_op jit(solution)/shard_map/ppermute | solution.py:312
  10.6 0.7 %pad.4 = s32[8,32]{1,0:T(8,128)S(1)} pad(s32[8,27]{1,0:T(8,128)} %param.10, s32[]{:T(128)} %constant.0.clone.1), padding=0_0x0_5 | pad | bytes 1892 | tf_op jit(solution)/shard_map/jit(_pad)/pad | solution.py:336
  11.3 0.1 tile.9.columns_ref
  11.4 6.0 %copy.10.blocks_ref = f32[8,27,4096]{2,1,0:T(8,128)} copy(f32[8,27,4096]{2,0,1:T(8,128)} %param.9) | data formatting | bytes 7077888 | tf_op args[1]
  17.4 6.6 %shard_map.96 = (bf16[512,1024]{1,0:T(8,128)(2,1)S(1)}, bf16[512,1024]{1,0:T(8,128)(2,1)S(1)}) custom-call(s32[1,2,4]{2,1,0:T(2,128)S(1)} %copy-done.3, s32[8,1,256]{2,1,0:T(1,128)S(1)} %tile.9.columns_ref, f32[8,27,4096]{2,1,0:T(8,128)} %copy.10.blocks_ref), custom_call_target="tpu_custom_call" | custom-call | tf_op jit(solution)/shard_map/pallas_call | solution.py:338
  24.0 0.0 collective-permute-done.1.ga_ref
  24.0 0.0 collective-permute-done.2.gb_ref
  24.0 1.2 %shard_map.97 = (f32[64,512]{1,0:T(8,128)S(1)}, f32[32,128]{1,0:T(8,128)S(1)}) custom-call(f32[32,512]{1,0:T(8,128)S(1)} %get-tuple-element.21.resid_ref, f32[72,256]{1,0:T(8,128)S(1)} %get-tuple-element.22.a_ref, f32[72,256]{1,0:T(8,128)S(1)} %get-tuple-element.23.b_ref, f32[72,256]{1,0:T(8,128)S(1)} %collective-permute-done.1.ga_ref, ...), custom_call_target="tpu_custom_call" | custom-call | tf_op jit(solution)/shard_map/pallas_call | solution.py:362
  25.2 4.6 %collective-permute-start.7 = (f32[32,128]{1,0:T(8,128)S(1)}, f32[32,128]{1,0:T(8,128)S(1)}, u32[]{:S(2)}, u32[]{:S(2)}) collective-permute-start(f32[32,128]{1,0:T(8,128)S(1)} %get-tuple-element.29), channel_id=1, source_target_pairs={{0,6},{2,4},{4,2},{6,0},{8,14},{10,12},{12,10},{14,8},{16,22},{18,... | collective-permute-start | bytes 49160 | tf_op jit(solution)/shard_map/ppermute | solution.py:293
  29.8 0.5 collective-permute-start.6
  30.3 0.0 collective-permute-start.5
  30.3 0.5 shard_map.98
  30.8 0.6 collective-permute-start.3
  31.4 0.7 %collective-permute-start.4 = (f32[128,256]{1,0:T(8,128)S(1)}, f32[128,256]{1,0:T(8,128)S(1)}, u32[]{:S(2)}, u32[]{:S(2)}) collective-permute-start(f32[128,256]{1,0:T(8,128)S(1)} %get-tuple-element.28.own_b_ref), channel_id=1, source_target_pairs={{2,4},{6,8},{10,12},{14,16},{18,20},{22,24},{26,28},{4,2},{8,6},{1... | collective-permute-start | bytes 393224 | tf_op jit(solution)/shard_map/ppermute | solution.py:312
  32.0 1.5 %collective-permute-done.6 = f32[32,128]{1,0:T(8,128)S(1)} collective-permute-done((f32[32,128]{1,0:T(8,128)S(1)}, f32[32,128]{1,0:T(8,128)S(1)}, u32[]{:S(2)}, u32[]{:S(2)}) %collective-permute-start.6) | collective-permute-done | bytes 16416 | tf_op jit(solution)/shard_map/ppermute | solution.py:293
  33.6 4.4 %collective-permute-start.10 = (f32[32,128]{1,0:T(8,128)S(1)}, f32[32,128]{1,0:T(8,128)S(1)}, u32[]{:S(2)}, u32[]{:S(2)}) collective-permute-start(f32[32,128]{1,0:T(8,128)S(1)} %add_add_fusion.1.rest_0_), channel_id=1, source_target_pairs={{0,24},{2,26},{4,28},{6,30},{8,16},{10,18},{12,20},{14,22},{16,8},... | collective-permute-start | bytes 49160 | tf_op jit(solution)/shard_map/ppermute | solution.py:293
  38.0 0.0 collective-permute-start.9
  38.0 0.6 %collective-permute-start.8 = (f32[32,128]{1,0:T(8,128)S(1)}, f32[32,128]{1,0:T(8,128)S(1)}, u32[]{:S(2)}, u32[]{:S(2)}) collective-permute-start(f32[32,128]{1,0:T(8,128)S(1)} %add_add_fusion.1.rest_0_), channel_id=1, source_target_pairs={{0,8},{2,10},{4,12},{6,14},{8,0},{10,2},{12,4},{14,6},{16,24},{18,... | collective-permute-start | bytes 49160 | tf_op jit(solution)/shard_map/ppermute | solution.py:293
  38.7 2.7 %collective-permute-done.10.rest_3_ = f32[32,128]{1,0:T(8,128)S(1)} collective-permute-done((f32[32,128]{1,0:T(8,128)S(1)}, f32[32,128]{1,0:T(8,128)S(1)}, u32[]{:S(2)}, u32[]{:S(2)}) %collective-permute-start.10) | collective-permute-done | bytes 16416 | tf_op jit(solution)/shard_map/ppermute | solution.py:293
  41.4 1.3 %collective-permute-done.9.rest_2_ = f32[32,128]{1,0:T(8,128)S(1)} collective-permute-done((f32[32,128]{1,0:T(8,128)S(1)}, f32[32,128]{1,0:T(8,128)S(1)}, u32[]{:S(2)}, u32[]{:S(2)}) %collective-permute-start.9) | collective-permute-done | bytes 16416 | tf_op jit(solution)/shard_map/ppermute | solution.py:293
  42.7 0.0 collective-permute-done.8.rest_1_
  42.7 0.0 collective-permute-done.3.got_a_ref
  42.7 0.0 collective-permute-done.4.got_b_ref
  42.7 1.8 %shard_map.99 = (f32[32,512]{1,0:T(8,128)S(1)}, f32[32,128]{1,0:T(8,128)S(1)}, f32[32,512]{1,0:T(8,128)S(1)}, f32[32,512]{1,0:T(8,128)S(1)}, f32[32,512]{1,0:T(8...) custom-call(f32[32,32]{1,0:T(8,128)S(1)} %copy-done.1, f32[32,512]{1,0:T(8,128)S(1)} %get-tuple-element.21.resid_ref, ...), custom_call_target="tpu_custom_call" | custom-call | tf_op jit(solution)/shard_map/pallas_call | solution.py:373
  44.5 0.1 collective-permute-start.15
  44.6 0.8 %collective-permute-start.14 = (f32[32,128]{1,0:T(8,128)S(1)}, f32[32,128]{1,0:T(8,128)S(1)}, u32[]{:S(2)}, u32[]{:S(2)}) collective-permute-start(f32[32,128]{1,0:T(8,128)S(1)} %get-tuple-element.39), channel_id=1, source_target_pairs={{0,4},{2,6},{4,0},{6,2},{8,12},{10,14},{12,8},{14,10},{16,20},{18,... | collective-permute-start | bytes 49160 | tf_op jit(solution)/shard_map/ppermute | solution.py:293
  45.3 1.1 %collective-permute-start.13 = (f32[32,128]{1,0:T(8,128)S(1)}, f32[32,128]{1,0:T(8,128)S(1)}, u32[]{:S(2)}, u32[]{:S(2)}) collective-permute-start(f32[32,128]{1,0:T(8,128)S(1)} %get-tuple-element.39), channel_id=1, source_target_pairs={{0,2},{2,0},{4,6},{6,4},{8,10},{10,8},{12,14},{14,12},{16,18},{18,... | collective-permute-start | bytes 49160 | tf_op jit(solution)/shard_map/ppermute | solution.py:293
  46.4 0.5 shard_map.100
  46.9 0.0 collective-permute-start.11
  46.9 0.7 %collective-permute-start.12 = (f32[32,256]{1,0:T(8,128)S(1)}, f32[32,256]{1,0:T(8,128)S(1)}, u32[]{:S(2)}, u32[]{:S(2)}) collective-permute-start(f32[32,256]{1,0:T(8,128)S(1)} %get-tuple-element.38), channel_id=1, source_target_pairs={{2,4},{6,8},{10,12},{14,16},{18,20},{22,24},{26,28},{4,2},{8,6},{1... | collective-permute-start | bytes 98312 | tf_op jit(solution)/shard_map/ppermute | solution.py:312
  47.6 0.2 collective-permute-done.15
  47.7 0.7 %collective-permute-done.14 = f32[32,128]{1,0:T(8,128)S(1)} collective-permute-done((f32[32,128]{1,0:T(8,128)S(1)}, f32[32,128]{1,0:T(8,128)S(1)}, u32[]{:S(2)}, u32[]{:S(2)}) %collective-permute-start.14) | collective-permute-done | bytes 16416 | tf_op jit(solution)/shard_map/ppermute | solution.py:293
  48.4 4.2 %collective-permute-start.18 = (f32[32,128]{1,0:T(8,128)S(1)}, f32[32,128]{1,0:T(8,128)S(1)}, u32[]{:S(2)}, u32[]{:S(2)}) collective-permute-start(f32[32,128]{1,0:T(8,128)S(1)} %add_add_fusion.rest_0_), channel_id=1, source_target_pairs={{0,24},{2,26},{4,28},{6,30},{8,16},{10,18},{12,20},{14,22},{16,8},... | collective-permute-start | bytes 49160 | tf_op jit(solution)/shard_map/ppermute | solution.py:293
  52.6 0.0 collective-permute-start.17
  52.7 0.6 %collective-permute-start.16 = (f32[32,128]{1,0:T(8,128)S(1)}, f32[32,128]{1,0:T(8,128)S(1)}, u32[]{:S(2)}, u32[]{:S(2)}) collective-permute-start(f32[32,128]{1,0:T(8,128)S(1)} %add_add_fusion.rest_0_), channel_id=1, source_target_pairs={{0,8},{2,10},{4,12},{6,14},{8,0},{10,2},{12,4},{14,6},{16,24},{18,... | collective-permute-start | bytes 49160 | tf_op jit(solution)/shard_map/ppermute | solution.py:293
  53.3 1.6 %collective-permute-done.18.rest_3_ = f32[32,128]{1,0:T(8,128)S(1)} collective-permute-done((f32[32,128]{1,0:T(8,128)S(1)}, f32[32,128]{1,0:T(8,128)S(1)}, u32[]{:S(2)}, u32[]{:S(2)}) %collective-permute-start.18) | collective-permute-done | bytes 16416 | tf_op jit(solution)/shard_map/ppermute | solution.py:293
  54.9 2.4 %collective-permute-done.17.rest_2_ = f32[32,128]{1,0:T(8,128)S(1)} collective-permute-done((f32[32,128]{1,0:T(8,128)S(1)}, f32[32,128]{1,0:T(8,128)S(1)}, u32[]{:S(2)}, u32[]{:S(2)}) %collective-permute-start.17) | collective-permute-done | bytes 16416 | tf_op jit(solution)/shard_map/ppermute | solution.py:293
  57.3 0.0 collective-permute-done.16.rest_1_
  57.3 1.8 %shard_map.101 = (f32[32,512]{1,0:T(8,128)}, f32[32,512]{1,0:T(8,128)}) custom-call(s32[1,2,4]{2,1,0:T(2,128)S(1)} %copy-done.3, f32[32,512]{1,0:T(8,128)S(1)} %get-tuple-element.30.resid1_ref, f32[32,512]{1,0:T(8,128)S(1)} %get-tuple-element.31.z0_ref, f32[32,512]{1,0:T(8,128)S(1)} %get-tuple-element.32.z1_ref, f32[32,512]{1,0:T(8,128)S(1)} %get-tuple-element.33.q0_ref, ...), custom_call_target="tpu_custom_call" | custom-call | tf_op jit(solution)/shard_map/pallas_call | solution.py:388
  (17 shorter events, 0.0 us)
Async XLA Ops:
  0.6 16.8 %copy-start.3 = (s32[1,2,4]{2,1,0:T(2,128)S(1)}, s32[1,2,4]{2,1,0:T(2,128)}, u32[]{:S(2)}) copy-start(s32[1,2,4]{2,1,0:T(2,128)} %rows_ref.5) | copy-start | bytes 100
  0.6 4.8 %collective-permute-start = (f32[4,512]{1,0:T(4,128)}, f32[4,512]{1,0:T(4,128)S(1)}, u32[]{:S(2)}, u32[]{:S(2)}) collective-permute-start(f32[4,512]{1,0:T(4,128)} %rest_0_.1), channel_id=1, source_target_pairs={{1,0},{0,1},{3,2},{2,3},{5,4},{4,5},{7,6},{6,7},{9,8},{8,9},{11,10... | collective-permute-start | bytes 24584 | tf_op jit(solution)/shard_map/ppermute | solution.py:333
  5.5 0.8 %copy-start = (f32[32,512]{1,0:T(8,128)S(1)}, f32[32,512]{1,0:T(8,128)}, u32[]{:S(2)}) copy-start(f32[32,512]{1,0:T(8,128)} %right_ref.1) | copy-start | bytes 196612
  6.3 0.7 %copy-start.2 = (s32[1,2,4]{2,1,0:T(2,128)S(1)}, s32[1,2,4]{2,1,0:T(2,128)}, u32[]{:S(2)}) copy-start(s32[1,2,4]{2,1,0:T(2,128)} %rows_ref.5) | copy-start | bytes 100
  7.0 0.7 %copy-start.4 = (f32[4,512]{1,0:T(4,128)S(1)}, f32[4,512]{1,0:T(4,128)}, u32[]{:S(2)}) copy-start(f32[4,512]{1,0:T(4,128)} %rest_0_.1) | copy-start | bytes 24580
  7.7 0.7 %copy-start.5 = (f32[512]{0:T(512)S(1)}, f32[512]{0:T(512)}, u32[]{:S(2)}) copy-start(f32[512]{0:T(512)} %param.14) | copy-start | bytes 6148
  8.4 0.7 %copy-start.6 = (s32[1,8]{1,0:T(1,128)S(1)}, s32[1,8]{1,0:T(1,128)}, u32[]{:S(2)}) copy-start(s32[1,8]{1,0:T(1,128)} %owner_ref.1) | copy-start | bytes 100
  9.9 14.2 %collective-permute-start.1 = (f32[72,256]{1,0:T(8,128)S(1)}, f32[72,256]{1,0:T(8,128)S(1)}, u32[]{:S(2)}, u32[]{:S(2)}) collective-permute-start(f32[72,256]{1,0:T(8,128)S(1)} %get-tuple-element.22.a_ref), channel_id=1, source_target_pairs={{0,2},{2,0},{4,6},{6,4},{8,10},{10,8},{12,14},{14,12},{16,18},{18,... | collective-permute-start | bytes 221192 | tf_op jit(solution)/shard_map/ppermute | solution.py:310
  9.9 14.1 %collective-permute-start.2 = (f32[72,256]{1,0:T(8,128)S(1)}, f32[72,256]{1,0:T(8,128)S(1)}, u32[]{:S(2)}, u32[]{:S(2)}) collective-permute-start(f32[72,256]{1,0:T(8,128)S(1)} %get-tuple-element.23.b_ref), channel_id=1, source_target_pairs={{2,4},{6,8},{10,12},{14,16},{18,20},{22,24},{26,28},{4,2},{8,6},{1... | collective-permute-start | bytes 221192 | tf_op jit(solution)/shard_map/ppermute | solution.py:312
  17.4 25.2 %copy-start.1 = (f32[32,32]{1,0:T(8,128)S(1)}, f32[32,32]{1,0:T(8,128)}, u32[]{:S(2)}) copy-start(f32[32,32]{1,0:T(8,128)} %inverse_ref.1) | copy-start | bytes 12292
  25.2 6.8 %collective-permute-start.7 = (f32[32,128]{1,0:T(8,128)S(1)}, f32[32,128]{1,0:T(8,128)S(1)}, u32[]{:S(2)}, u32[]{:S(2)}) collective-permute-start(f32[32,128]{1,0:T(8,128)S(1)} %get-tuple-element.29), channel_id=1, source_target_pairs={{0,6},{2,4},{4,2},{6,0},{8,14},{10,12},{12,10},{14,8},{16,22},{18,... | collective-permute-start | bytes 49160 | tf_op jit(solution)/shard_map/ppermute | solution.py:293
  29.8 3.7 %collective-permute-start.6 = (f32[32,128]{1,0:T(8,128)S(1)}, f32[32,128]{1,0:T(8,128)S(1)}, u32[]{:S(2)}, u32[]{:S(2)}) collective-permute-start(f32[32,128]{1,0:T(8,128)S(1)} %get-tuple-element.29), channel_id=1, source_target_pairs={{0,4},{2,6},{4,0},{6,2},{8,12},{10,14},{12,8},{14,10},{16,20},{18,... | collective-permute-start | bytes 49160 | tf_op jit(solution)/shard_map/ppermute | solution.py:293
  30.3 3.2 %collective-permute-start.5 = (f32[32,128]{1,0:T(8,128)S(1)}, f32[32,128]{1,0:T(8,128)S(1)}, u32[]{:S(2)}, u32[]{:S(2)}) collective-permute-start(f32[32,128]{1,0:T(8,128)S(1)} %get-tuple-element.29), channel_id=1, source_target_pairs={{0,2},{2,0},{4,6},{6,4},{8,10},{10,8},{12,14},{14,12},{16,18},{18,... | collective-permute-start | bytes 49160 | tf_op jit(solution)/shard_map/ppermute | solution.py:293
  30.8 11.9 %collective-permute-start.3 = (f32[128,256]{1,0:T(8,128)S(1)}, f32[128,256]{1,0:T(8,128)S(1)}, u32[]{:S(2)}, u32[]{:S(2)}) collective-permute-start(f32[128,256]{1,0:T(8,128)S(1)} %get-tuple-element.27.own_a_ref), channel_id=1, source_target_pairs={{0,2},{2,0},{4,6},{6,4},{8,10},{10,8},{12,14},{14,12},{16,18},{18,... | collective-permute-start | bytes 393224 | tf_op jit(solution)/shard_map/ppermute | solution.py:310
  31.4 11.3 %collective-permute-start.4 = (f32[128,256]{1,0:T(8,128)S(1)}, f32[128,256]{1,0:T(8,128)S(1)}, u32[]{:S(2)}, u32[]{:S(2)}) collective-permute-start(f32[128,256]{1,0:T(8,128)S(1)} %get-tuple-element.28.own_b_ref), channel_id=1, source_target_pairs={{2,4},{6,8},{10,12},{14,16},{18,20},{22,24},{26,28},{4,2},{8,6},{1... | collective-permute-start | bytes 393224 | tf_op jit(solution)/shard_map/ppermute | solution.py:312
  33.6 7.8 %collective-permute-start.10 = (f32[32,128]{1,0:T(8,128)S(1)}, f32[32,128]{1,0:T(8,128)S(1)}, u32[]{:S(2)}, u32[]{:S(2)}) collective-permute-start(f32[32,128]{1,0:T(8,128)S(1)} %add_add_fusion.1.rest_0_), channel_id=1, source_target_pairs={{0,24},{2,26},{4,28},{6,30},{8,16},{10,18},{12,20},{14,22},{16,8},... | collective-permute-start | bytes 49160 | tf_op jit(solution)/shard_map/ppermute | solution.py:293
  38.0 4.6 %collective-permute-start.9 = (f32[32,128]{1,0:T(8,128)S(1)}, f32[32,128]{1,0:T(8,128)S(1)}, u32[]{:S(2)}, u32[]{:S(2)}) collective-permute-start(f32[32,128]{1,0:T(8,128)S(1)} %add_add_fusion.1.rest_0_), channel_id=1, source_target_pairs={{0,16},{2,18},{4,20},{6,22},{8,24},{10,26},{12,28},{14,30},{16,0},... | collective-permute-start | bytes 49160 | tf_op jit(solution)/shard_map/ppermute | solution.py:293
  38.0 4.6 %collective-permute-start.8 = (f32[32,128]{1,0:T(8,128)S(1)}, f32[32,128]{1,0:T(8,128)S(1)}, u32[]{:S(2)}, u32[]{:S(2)}) collective-permute-start(f32[32,128]{1,0:T(8,128)S(1)} %add_add_fusion.1.rest_0_), channel_id=1, source_target_pairs={{0,8},{2,10},{4,12},{6,14},{8,0},{10,2},{12,4},{14,6},{16,24},{18,... | collective-permute-start | bytes 49160 | tf_op jit(solution)/shard_map/ppermute | solution.py:293
  44.5 3.2 %collective-permute-start.15 = (f32[32,128]{1,0:T(8,128)S(1)}, f32[32,128]{1,0:T(8,128)S(1)}, u32[]{:S(2)}, u32[]{:S(2)}) collective-permute-start(f32[32,128]{1,0:T(8,128)S(1)} %get-tuple-element.39), channel_id=1, source_target_pairs={{0,6},{2,4},{4,2},{6,0},{8,14},{10,12},{12,10},{14,8},{16,22},{18,... | collective-permute-start | bytes 49160 | tf_op jit(solution)/shard_map/ppermute | solution.py:293
  44.6 3.8 %collective-permute-start.14 = (f32[32,128]{1,0:T(8,128)S(1)}, f32[32,128]{1,0:T(8,128)S(1)}, u32[]{:S(2)}, u32[]{:S(2)}) collective-permute-start(f32[32,128]{1,0:T(8,128)S(1)} %get-tuple-element.39), channel_id=1, source_target_pairs={{0,4},{2,6},{4,0},{6,2},{8,12},{10,14},{12,8},{14,10},{16,20},{18,... | collective-permute-start | bytes 49160 | tf_op jit(solution)/shard_map/ppermute | solution.py:293
  45.3 3.0 %collective-permute-start.13 = (f32[32,128]{1,0:T(8,128)S(1)}, f32[32,128]{1,0:T(8,128)S(1)}, u32[]{:S(2)}, u32[]{:S(2)}) collective-permute-start(f32[32,128]{1,0:T(8,128)S(1)} %get-tuple-element.39), channel_id=1, source_target_pairs={{0,2},{2,0},{4,6},{6,4},{8,10},{10,8},{12,14},{14,12},{16,18},{18,... | collective-permute-start | bytes 49160 | tf_op jit(solution)/shard_map/ppermute | solution.py:293
  46.9 6.4 %collective-permute-start.11 = (f32[32,256]{1,0:T(8,128)S(1)}, f32[32,256]{1,0:T(8,128)S(1)}, u32[]{:S(2)}, u32[]{:S(2)}) collective-permute-start(f32[32,256]{1,0:T(8,128)S(1)} %get-tuple-element.37), channel_id=1, source_target_pairs={{0,2},{2,0},{4,6},{6,4},{8,10},{10,8},{12,14},{14,12},{16,18},{18,... | collective-permute-start | bytes 98312 | tf_op jit(solution)/shard_map/ppermute | solution.py:310
  46.9 6.4 %collective-permute-start.12 = (f32[32,256]{1,0:T(8,128)S(1)}, f32[32,256]{1,0:T(8,128)S(1)}, u32[]{:S(2)}, u32[]{:S(2)}) collective-permute-start(f32[32,256]{1,0:T(8,128)S(1)} %get-tuple-element.38), channel_id=1, source_target_pairs={{2,4},{6,8},{10,12},{14,16},{18,20},{22,24},{26,28},{4,2},{8,6},{1... | collective-permute-start | bytes 98312 | tf_op jit(solution)/shard_map/ppermute | solution.py:312
  48.4 6.5 %collective-permute-start.18 = (f32[32,128]{1,0:T(8,128)S(1)}, f32[32,128]{1,0:T(8,128)S(1)}, u32[]{:S(2)}, u32[]{:S(2)}) collective-permute-start(f32[32,128]{1,0:T(8,128)S(1)} %add_add_fusion.rest_0_), channel_id=1, source_target_pairs={{0,24},{2,26},{4,28},{6,30},{8,16},{10,18},{12,20},{14,22},{16,8},... | collective-permute-start | bytes 49160 | tf_op jit(solution)/shard_map/ppermute | solution.py:293
  52.6 4.6 %collective-permute-start.17 = (f32[32,128]{1,0:T(8,128)S(1)}, f32[32,128]{1,0:T(8,128)S(1)}, u32[]{:S(2)}, u32[]{:S(2)}) collective-permute-start(f32[32,128]{1,0:T(8,128)S(1)} %add_add_fusion.rest_0_), channel_id=1, source_target_pairs={{0,16},{2,18},{4,20},{6,22},{8,24},{10,26},{12,28},{14,30},{16,0},... | collective-permute-start | bytes 49160 | tf_op jit(solution)/shard_map/ppermute | solution.py:293
  52.7 4.6 %collective-permute-start.16 = (f32[32,128]{1,0:T(8,128)S(1)}, f32[32,128]{1,0:T(8,128)S(1)}, u32[]{:S(2)}, u32[]{:S(2)}) collective-permute-start(f32[32,128]{1,0:T(8,128)S(1)} %add_add_fusion.rest_0_), channel_id=1, source_target_pairs={{0,8},{2,10},{4,12},{6,14},{8,0},{10,2},{12,4},{14,6},{16,24},{18,... | collective-permute-start | bytes 49160 | tf_op jit(solution)/shard_map/ppermute | solution.py:293

commit v2 on v1

v2 whole, which is shorter than its diff:
```python
import functools

import jax
import jax.numpy as jnp
from jax import lax
from jax.experimental import pallas as pl
from jax.experimental.pallas import tpu as pltpu
from jax.sharding import PartitionSpec as P

B = 64
KNZ = 27
IFB = 4
NCL = 8
NB = 2 * IFB
NE = NB + 2 * IFB
EDGE = IFB * B
OWN = NB * B
EXT = NE * B
ROWS = NB * B
KPAD = 32
F32 = jnp.float32
BF16 = jnp.bfloat16
HIGHEST = lax.Precision.HIGHEST
NT = (((1,), (1,)), ((), ()))
NN = (((1,), (0,)), ((), ()))
VMEM_LIMIT = 48 * 1024 * 1024
CHUNK = 512


def split(x):
    high = x.astype(BF16)
    return high, (x - high.astype(F32)).astype(BF16)


def times(x, high, low, dims):
    count = x.shape[0]
    xh, xl = split(x)
    both = lax.dot_general(
        jnp.concatenate([xh, xl], axis=0), high, dims, preferred_element_type=F32
    )
    return both[:count] + both[count:] + lax.dot_general(xh, low, dims, preferred_element_type=F32)


def apply(x, halves):
    return jnp.concatenate([times(x, h[...], l[...], NT) for h, l in halves], axis=1)


def apply_back(x, halves):
    cut = ROWS // 2
    (h0, l0), (h1, l1) = halves
    return times(x[:, :cut], h0[...], l0[...], NN) + times(x[:, cut:], h1[...], l1[...], NN)


def exact(x, y, dims=NN):
    return lax.dot_general(x, y, dims, precision=HIGHEST, preferred_element_type=F32)


def call(kernel, outs, n_in, smem=(), raw=(), raw_out=False, scratch=()):
    def spec(i):
        if i in raw:
            return pl.BlockSpec(memory_space=pl.ANY)
        return pl.BlockSpec(memory_space=pltpu.SMEM if i in smem else pltpu.VMEM)

    return pl.pallas_call(
        kernel,
        out_shape=outs,
        in_specs=[spec(i) for i in range(n_in)],
        out_specs=[
            pl.BlockSpec(memory_space=pl.ANY if raw_out else pltpu.VMEM) for _ in outs
        ],
        scratch_shapes=list(scratch),
        compiler_params=pltpu.CompilerParams(vmem_limit_bytes=VMEM_LIMIT),
    )


def shape(*dims):
    return jax.ShapeDtypeStruct(dims, F32)


def place_of(rows_ref, odd, j):
    side = jnp.where(odd == 1, j // IFB, 1 - j // IFB)
    return rows_ref[0, side, j % IFB]


def spread(onehot, raw, high_ref, low_ref, at):
    width = raw.shape[-1]
    padded = jnp.concatenate([raw, jnp.zeros((1, NB, width), F32)], axis=0)
    rest = jnp.zeros((NB * (KPAD - KNZ - 1), width), BF16)
    wh, wl = split(padded.reshape(NB * (KNZ + 1), width))
    dense = lax.dot_general(
        onehot, jnp.concatenate([wh, rest], axis=0), NN, preferred_element_type=F32
    ) + lax.dot_general(onehot, jnp.concatenate([wl, rest], axis=0), NN, preferred_element_type=F32)
    first = lax.broadcasted_iota(jnp.int32, (NB, 128), 1) < B
    for m in range(NE // 2):
        for h in range(width // 128):
            cut = slice(128 * h, 128 * (h + 1))
            left = dense[16 * m : 16 * m + 8, cut]
            right = dense[16 * m + 8 : 16 * m + 16, cut]
            tile = jnp.concatenate(
                [
                    jnp.where(first, left, pltpu.roll(right, B, 1)),
                    jnp.where(first, pltpu.roll(left, B, 1), right),
                ],
                axis=0,
            )
            th, tl = split(tile)
            row = slice(at + 16 * h, at + 16 * (h + 1))
            high_ref[row, 128 * m : 128 * (m + 1)] = th
            low_ref[row, 128 * m : 128 * (m + 1)] = tl


def open_up(
    rows_hbm,
    right_hbm,
    scale_hbm,
    columns_hbm,
    blocks_hbm,
    resid_ref,
    fine_ref,
    onehot_ref,
    raw_ref,
    high_ref,
    low_ref,
    rows_ref,
    right_ref,
    scale_ref,
    columns_ref,
    chunk_ref,
    blk_ref,
    sems,
):
    odd = lax.axis_index("sub") % 2
    cases = right_ref.shape[0]
    half = B * B // 2
    small = [
        pltpu.make_async_copy(rows_hbm, rows_ref, sems.at[0]),
        pltpu.make_async_copy(columns_hbm, columns_ref, sems.at[1]),
        pltpu.make_async_copy(right_hbm, right_ref, sems.at[2]),
        pltpu.make_async_copy(scale_hbm, scale_ref, sems.at[3]),
    ]
    chunks = [
        pltpu.make_async_copy(
            blocks_hbm.at[:, :, pl.ds(CHUNK * t, CHUNK)], chunk_ref.at[t], sems.at[4 + t]
        )
        for t in range(half // CHUNK)
    ]
    tail = pltpu.make_async_copy(
        blocks_hbm.at[:, :, pl.ds(half, half)], raw_ref, sems.at[4 + len(chunks)]
    )
    for copy in small + chunks + [tail]:
        copy.start()
    for copy in small:
        copy.wait()
    column = columns_ref[...]
    place = jnp.where(
        (column < NB + IFB) == (odd == 1), column % IFB + NB, column % IFB + NB + IFB
    )
    for j in range(NB):
        place = jnp.where(column == place_of(rows_ref, odd, j), j, place)
    slot = lax.broadcasted_iota(jnp.int32, (KNZ, NB * KPAD), 0)
    entry = lax.broadcasted_iota(jnp.int32, (KNZ, NB * KPAD), 1)
    widen = jnp.where(entry // NB == slot, 1.0, 0.0).astype(BF16)
    wide = lax.dot_general(place.astype(F32).astype(BF16), widen, NN, preferred_element_type=F32)
    r = lax.broadcasted_iota(jnp.int32, (NE * NB, NB * KPAD), 0)
    q = lax.broadcasted_iota(jnp.int32, (NE * NB, NB * KPAD), 1)
    hit = (jnp.concatenate([wide] * NE, axis=0) == (r // NB).astype(F32)) & (r % NB == q % NB)
    onehot = jnp.where(hit, 1.0, 0.0).astype(BF16)
    onehot_ref[...] = onehot
    right = right_ref[...]
    scale = jnp.broadcast_to(scale_ref[...], (8, OWN))
    for n in range(NB):
        cut = slice(B * n, B * (n + 1))
        blk_ref[n, 0:cases, :] = right[:, cut]
        blk_ref[n, cases : 2 * cases, :] = right[:, cut] * scale[0:1, cut]
        blk_ref[n, 2 * cases :, :] = scale[:, cut]
    for j in range(0, NB, 2):
        pair = jnp.concatenate(
            [blk_ref[place_of(rows_ref, odd, j)], blk_ref[place_of(rows_ref, odd, j + 1)]], axis=1
        )
        resid_ref[:, B * j : B * (j + 2)] = pair[:cases]
        fine_ref[:, B * j : B * (j + 2)] = pair[cases:]
    for t, copy in enumerate(chunks):
        copy.wait()
        spread(onehot, chunk_ref[t], high_ref, low_ref, NB * CHUNK // B * t)
    tail.wait()


def open_rest(onehot_ref, raw_ref, after_ref, high_ref, low_ref):
    onehot = onehot_ref[...]
    for t in range(B * B // 2 // CHUNK):
        spread(
            onehot, raw_ref[:, :, CHUNK * t : CHUNK * (t + 1)], high_ref, low_ref, NB * CHUNK // B * t
        )


def sides(rows_ref, owner_ref, fine_ref, *rest, parts, ncoarse):
    basis_refs = rest[:parts]
    side_a_ref, side_b_ref, blk_ref = rest[parts:]
    odd = lax.axis_index("sub") % 2
    mine = lax.axis_index("rhs")
    cases = fine_ref.shape[0] - 8
    per = NCL // parts
    unknown = lax.broadcasted_iota(jnp.int32, (ncoarse, OWN), 0)
    coarse = jnp.zeros((ncoarse, OWN), F32)
    for k in range(parts):
        for t in range(per):
            owner = owner_ref[0, ((mine + k) % parts) * per + t]
            coarse = coarse + jnp.where(unknown == owner, basis_refs[k][t : t + 1, :], 0.0)
    for n in range(NB):
        blk_ref[n] = coarse[:, B * n : B * (n + 1)]
    for ref, first in ((side_a_ref, 0), (side_b_ref, IFB)):
        part = slice(B * first, B * (first + IFB))
        ref[:cases, :] = fine_ref[:cases, part]
        ref[cases + ncoarse :, :] = fine_ref[cases:, part]
        for j in range(0, IFB, 2):
            ref[cases : cases + ncoarse, B * j : B * (j + 2)] = jnp.concatenate(
                [
                    blk_ref[place_of(rows_ref, odd, first + j)],
                    blk_ref[place_of(rows_ref, odd, first + j + 1)],
                ],
                axis=1,
            )


def first_strain(
    resid_ref, a_ref, b_ref, ga_ref, gb_ref, h0, l0, h1, l1, strain_ref, pay_ref, *, cases, ncoarse
):
    count = cases + ncoarse
    field = jnp.concatenate(
        [a_ref[:count, :], b_ref[:count, :], ga_ref[:count, :], gb_ref[:count, :]], axis=1
    )
    strain = apply(field, ((h0, l0), (h1, l1)))
    strain_ref[...] = strain
    own = field[:, :OWN]
    resid = resid_ref[...]
    paired = jnp.concatenate([own, strain], axis=1)
    gram = exact(paired, paired[cases:], NT)
    restricted = exact(resid, own[cases:], NT)
    lead = paired[:cases]
    pay_ref[...] = jnp.zeros_like(pay_ref)
    pay_ref[:cases, 0:ncoarse] = restricted
    pay_ref[:cases, ncoarse : 2 * ncoarse] = gram[:cases]
    pay_ref[:ncoarse, 2 * ncoarse : 3 * ncoarse] = gram[cases:]
    pay_ref[:cases, 3 * ncoarse : 3 * ncoarse + 1] = jnp.sum(
        resid * own[:cases], axis=1, keepdims=True
    )
    pay_ref[:cases, 3 * ncoarse + 1 : 3 * ncoarse + 2] = jnp.sum(lead * lead, axis=1, keepdims=True)


def first_image(a_ref, b_ref, strain_ref, h0, l0, h1, l1, send_a_ref, send_b_ref):
    strain = strain_ref[...]
    count = strain.shape[0]
    back = apply_back(strain, ((h0, l0), (h1, l1)))
    send_a_ref[:count, :] = a_ref[:count, :] + back[:, :EDGE]
    send_a_ref[count:, :] = back[:, OWN : OWN + EDGE]
    send_b_ref[:count, :] = b_ref[:count, :] + back[:, EDGE:OWN]
    send_b_ref[count:, :] = back[:, OWN + EDGE :]


def second_strain(
    inverse_ref,
    resid_ref,
    a_ref,
    b_ref,
    ga_ref,
    gb_ref,
    own_a_ref,
    own_b_ref,
    got_a_ref,
    got_b_ref,
    h0,
    l0,
    h1,
    l1,
    *rest,
    cases,
    ncoarse,
    n_pay,
):
    pays = rest[:n_pay]
    strain_ref, pay_ref, resid1_ref, z0_ref, z1_ref, q0_ref, keep_ref = rest[n_pay:]
    count = cases + ncoarse
    pay = pays[0][...]
    for other in pays[1:]:
        pay = pay + other[...]
    u0 = pay[:cases, 0:ncoarse]
    ra = pay[:cases, ncoarse : 2 * ncoarse]
    rac = pay[:ncoarse, 2 * ncoarse : 3 * ncoarse]
    inverse = inverse_ref[...]
    y0 = exact(u0, inverse)
    ry = exact(y0, rac)
    rz0 = pay[:cases, 3 * ncoarse : 3 * ncoarse + 1] + jnp.sum(u0 * y0, axis=1, keepdims=True)
    pq0 = pay[:cases, 3 * ncoarse + 1 : 3 * ncoarse + 2] + jnp.sum(
        y0 * (2.0 * ra + ry), axis=1, keepdims=True
    )
    alpha = rz0 / pq0
    u1 = u0 - alpha * (ra + ry)
    y1 = exact(u1, inverse)
    image = jnp.concatenate(
        [
            own_a_ref[:count, :] + got_a_ref[count:, :],
            own_b_ref[:count, :] + got_b_ref[count:, :],
            own_a_ref[count:, :] + got_a_ref[:count, :],
            own_b_ref[count:, :] + got_b_ref[:count, :],
        ],
        axis=1,
    )
    parts = [a_ref, b_ref, ga_ref, gb_ref]
    scaled = jnp.concatenate([ref[:cases, :] for ref in parts], axis=1)
    coarse = jnp.concatenate([ref[cases:count, :] for ref in parts], axis=1)
    scale = jnp.concatenate([ref[count : count + 1, :] for ref in parts], axis=1)
    q0 = image[:cases] + exact(y0, image[cases:])
    z0 = scaled[:, :OWN] + exact(y0, coarse[:, :OWN])
    resid1 = resid_ref[...] - alpha * q0[:, :OWN]
    z1 = scaled - (alpha * scale) * q0 + exact(y1, coarse)
    strain = apply(z1, ((h0, l0), (h1, l1)))
    strain_ref[...] = strain
    own = z1[:, :OWN]
    resid1_ref[...] = resid1
    z0_ref[...] = z0
    z1_ref[...] = own
    q0_ref[...] = q0[:, :OWN]
    pay_ref[...] = jnp.zeros_like(pay_ref)
    pay_ref[:, 0:1] = jnp.sum(resid1 * resid1 * scale[:, :OWN], axis=1, keepdims=True)
    pay_ref[:, 1:2] = jnp.sum(own * own, axis=1, keepdims=True) + jnp.sum(
        strain * strain, axis=1, keepdims=True
    )
    pay_ref[:, 2:3] = jnp.sum(own * q0[:, :OWN], axis=1, keepdims=True)
    keep_ref[...] = jnp.zeros_like(keep_ref)
    keep_ref[:, 0:1] = rz0
    keep_ref[:, 1:2] = pq0
    keep_ref[:, 2:3] = alpha
    keep_ref[:, 3:4] = jnp.sum(u1 * y1, axis=1, keepdims=True)


def second_image(z1_ref, strain_ref, h0, l0, h1, l1, own_ref, send_a_ref, send_b_ref):
    back = apply_back(strain_ref[...], ((h0, l0), (h1, l1)))
    own_ref[...] = z1_ref[...] + back[:, :OWN]
    send_a_ref[...] = back[:, OWN : OWN + EDGE]
    send_b_ref[...] = back[:, OWN + EDGE :]


def finish(
    rows_ref, resid1_ref, z0_ref, z1_ref, q0_ref, keep_ref, own_ref, got_a_ref, got_b_ref, *rest, n_pay
):
    pays = rest[:n_pay]
    field_hbm, resid2_hbm, field_ref, resid2_ref, blk_ref, sems = rest[n_pay:]
    odd = lax.axis_index("sub") % 2
    cases = own_ref.shape[0]
    pay = pays[0][...]
    for other in pays[1:]:
        pay = pay + other[...]
    keep = keep_ref[...]
    rz0, pq0, alpha0 = keep[:, 0:1], keep[:, 1:2], keep[:, 2:3]
    rz1 = pay[:, 0:1] + keep[:, 3:4]
    beta = rz1 / rz0
    pq1 = pay[:, 1:2] + beta * (2.0 * pay[:, 2:3] + beta * pq0)
    alpha1 = rz1 / pq1
    image = own_ref[...] + jnp.concatenate([got_a_ref[...], got_b_ref[...]], axis=1)
    z0 = z0_ref[...]
    field = alpha0 * z0 + alpha1 * (z1_ref[...] + beta * z0)
    resid2 = resid1_ref[...] - alpha1 * (image + beta * q0_ref[...])
    copies = []
    for k, (value, out, buf) in enumerate(
        ((field, field_hbm, field_ref), (resid2, resid2_hbm, resid2_ref))
    ):
        for j in range(NB):
            blk_ref[k, place_of(rows_ref, odd, j)] = value[:, B * j : B * (j + 1)]
        for n in range(0, NB, 2):
            buf[:, B * n : B * (n + 2)] = jnp.concatenate([blk_ref[k, n], blk_ref[k, n + 1]], axis=1)
        copies.append(pltpu.make_async_copy(buf, out, sems.at[k]))
        copies[-1].start()
    for copy in copies:
        copy.wait()


def swap(x, steps, count):
    return [lax.ppermute(x, "sub", [(i, i ^ k) for i in range(count)]) for k in steps]


def rounds_of(count):
    rounds = []
    base = 1
    while base < count:
        if base * 4 <= count:
            rounds.append((base, 2 * base, 3 * base))
            base *= 4
        else:
            rounds.append((base,))
            base *= 2
    return rounds


def across(a, b, count):
    low = lax.ppermute(a, "sub", [(i, i ^ 1) for i in range(count)])
    inner = [(i, i + 1) for i in range(1, count - 1, 2)]
    return low, lax.ppermute(b, "sub", inner + [(j, i) for i, j in inner])


def body(
    right_side,
    stiffness_blocks,
    block_columns,
    interface_rows,
    corner_owner,
    corner_basis,
    jacobi_scale,
    coarse_inverse,
):
    cases = right_side.shape[0]
    ncoarse = coarse_inverse.shape[0]
    count = lax.axis_size("sub")
    parts = lax.axis_size("rhs")
    live = cases + ncoarse
    rounds = rounds_of(count)

    bases = [corner_basis] + [
        lax.ppermute(corner_basis, "rhs", [((i + k) % parts, i) for i in range(parts)])
        for k in range(1, parts)
    ]
    half = B * B // 2
    g_half = jax.ShapeDtypeStruct((ROWS // 2, EXT), BF16)
    resid, fine, onehot, raw, h0, l0 = call(
        open_up,
        [
            shape(cases, OWN),
            shape(cases + 8, OWN),
            jax.ShapeDtypeStruct((NE * NB, NB * KPAD), BF16),
            shape(KNZ, NB, half),
            g_half,
            g_half,
        ],
        5,
        raw=range(5),
        scratch=[
            pltpu.SMEM((1, 2, IFB), jnp.int32),
            pltpu.VMEM((cases, OWN), F32),
            pltpu.VMEM((1, OWN), F32),
            pltpu.VMEM((NB, KNZ), jnp.int32),
            pltpu.VMEM((half // CHUNK, KNZ, NB, CHUNK), F32),
            pltpu.VMEM((NB, 2 * cases + 8, B), F32),
            pltpu.SemaphoreType.DMA((half // CHUNK + 5,)),
        ],
    )(
        interface_rows,
        right_side,
        jacobi_scale.reshape(1, OWN),
        block_columns,
        jnp.transpose(stiffness_blocks, (1, 0, 2)),
    )
    side_a, side_b = call(
        functools.partial(sides, parts=parts, ncoarse=ncoarse),
        [shape(live + 8, EDGE), shape(live + 8, EDGE)],
        3 + parts,
        smem=(0, 1),
        scratch=[pltpu.VMEM((NB, ncoarse, B), F32)],
    )(interface_rows, corner_owner, fine, *bases)
    h1, l1 = call(open_rest, [g_half, g_half], 3)(onehot, raw, side_a)
    dense = (h0, l0, h1, l1)
    ghost_a, ghost_b = across(side_a, side_b, count)

    lanes = -(-(3 * ncoarse + 2) // 128) * 128
    strain, pay = call(
        functools.partial(first_strain, cases=cases, ncoarse=ncoarse),
        [shape(live, ROWS), shape(max(cases, ncoarse), lanes)],
        9,
    )(resid, side_a, side_b, ghost_a, ghost_b, *dense)
    for steps in rounds[:-1]:
        pay = sum(swap(pay, steps, count), pay)
    pays = [pay] + swap(pay, rounds[-1], count)
    own_a, own_b = call(first_image, [shape(2 * live, EDGE)] * 2, 7)(side_a, side_b, strain, *dense)
    got_a, got_b = across(own_a, own_b, count)

    strain, pay, resid1, z0, z1, q0, keep = call(
        functools.partial(second_strain, cases=cases, ncoarse=ncoarse, n_pay=len(pays)),
        [shape(cases, ROWS), shape(cases, 128)] + [shape(cases, OWN)] * 4 + [shape(cases, 128)],
        14 + len(pays),
    )(
        coarse_inverse, resid, side_a, side_b, ghost_a, ghost_b, own_a, own_b, got_a, got_b, *dense, *pays
    )
    for steps in rounds[:-1]:
        pay = sum(swap(pay, steps, count), pay)
    pays = [pay] + swap(pay, rounds[-1], count)
    own, back_a, back_b = call(
        second_image, [shape(cases, OWN), shape(cases, EDGE), shape(cases, EDGE)], 6
    )(z1, strain, *dense)
    got_a, got_b = across(back_a, back_b, count)
    return tuple(
        call(
            functools.partial(finish, n_pay=len(pays)),
            [shape(cases, OWN)] * 2,
            9 + len(pays),
            smem=(0,),
            raw_out=True,
            scratch=[
                pltpu.VMEM((cases, OWN), F32),
                pltpu.VMEM((cases, OWN), F32),
                pltpu.VMEM((2, NB, cases, B), F32),
                pltpu.SemaphoreType.DMA((2,)),
            ],
        )(interface_rows, resid1, z0, z1, q0, keep, own, got_a, got_b, *pays)
    )


def solution(mesh):
    placed = (
        P("rhs", "sub"),
        P("sub", None, None),
        P("sub", None),
        P("sub", None, None),
        P("sub", None),
        P("rhs", "sub"),
        P("sub"),
        P(),
    )
    return jax.shard_map(
        body,
        mesh=mesh,
        in_specs=placed,
        out_specs=(P("rhs", "sub"), P("rhs", "sub")),
        check_vma=False,
    )
```

time: 59.6 us -> 48.6 us (0.82)
  local copies, waits for them, and re-layouts: 10.4 us -> 2.9 us
  Pallas kernels: 13.1 us -> 9.68 us
  starting transfers between devices: 22.6 us -> 24.5 us
  waiting for transfers between devices: 12.2 us -> 10.4 us
    unnamed x15 -> x14, local copies, waits for them, and re-layouts: 9.6 us -> 2.9 us
    pallas_call x3 -> x4, Pallas kernels: 7.82 us -> 4.44 us  [the longest x1 2.58 us: body(): call(open_up, [shape(cases, OWN), shape(cases + 8, OWN), jax.ShapeDtypeSt...]
    ppermute x3, starting transfers between devices: 0.66 us -> 3.53 us  [across(): low = lax.ppermute(a, 'sub', [(i, i ^ 1) for i in range(count)])]
    ppermute x1, waiting for transfers between devices: 1.84 us -> 0.01 us  [body(): lax.ppermute(corner_basis, 'rhs', [((i + k) % parts, i) for i in range(pa...]
    ppermute x12, starting transfers between devices: 17 us -> 16 us  [swap(): lax.ppermute(x, 'sub', [(i, i ^ k) for i in range(count)])]
    pad x1 -> x0, local copies, waits for them, and re-layouts: 0.69 us -> none  [body(): jnp.pad(block_columns, ((0, 0), (0, KPAD - KNZ)), constant_values=-1)]
  transfers between devices with their start and end apart: 19 -> 19, of which waited for: 8 -> 8; matrix products, arithmetic and copies ran while one was open for 12% -> 0% of each run, Pallas kernels for 13% -> 9%
where the time goes in v2:
time: 48.6 us; the launch traced here: 48.4 us
  starting transfers between devices  24.5 us (50%)
  waiting for transfers between devices  10.4 us (21%)
  Pallas kernels  9.68 us (20%)
  local copies, waits for them, and re-layouts  2.9 us (6%)
  between operations  0.83 us (2%)
    ppermute x12, starting transfers between devices, swap(): lax.ppermute(x, 'sub', [(i, i ^ k) for i in range(count)])  16 us
    ppermute x12, waiting for transfers between devices, swap(): lax.ppermute(x, 'sub', [(i, i ^ k) for i in range(count)])  10.1 us
    ppermute x3, starting transfers between devices, across(): low = lax.ppermute(a, 'sub', [(i, i ^ 1) for i in range(count)])  3.53 us
    ppermute x1, starting transfers between devices, body(): lax.ppermute(corner_basis, 'rhs', [((i + k) % parts, i) for i in range(pa...  3 us
    unnamed x14, local copies, waits for them, and re-layouts  2.9 us
    pallas_call x1, Pallas kernels, body(): call(open_up, [shape(cases, OWN), shape(cases + 8, OWN), jax.ShapeDtypeSt...  2.58 us
    ppermute x3, starting transfers between devices, across(): return (low, lax.ppermute(b, 'sub', inner + [(j, i) for i, j in inner]))  1.99 us
    pallas_call x1, Pallas kernels, body(): call(functools.partial(finish, n_pay=len(pays)), [shape(cases, OWN)] * 2,...  1.81 us
  transfers between devices with their start and end apart: 19, of which 8 were waited for; matrix products, arithmetic and copies ran while one was open for 0% of the time, Pallas kernels for 9%

profile of v2, /device:TPU:0, one launch (start us, length us, event | category | flops | bytes accessed | tf_op | source)
XLA Modules:
  0.0 48.4 jit_solution(6194489427718194967)
XLA Ops:
  0.6 3.0 %collective-permute-start = (f32[4,512]{1,0:T(4,128)}, f32[4,512]{1,0:T(4,128)S(1)}, u32[]{:S(2)}, u32[]{:S(2)}) collective-permute-start(f32[4,512]{1,0:T(4,128)} %rest_0_.1), channel_id=1, source_target_pairs={{1,0},{0,1},{3,2},{2,3},{5,4},{4,5},{7,6},{6,7},{9,8},{8,9},{11,10... | collective-permute-start | bytes 24584 | tf_op jit(solution)/shard_map/ppermute | solution.py:418
  3.6 0.8 %copy-done = f32[32,512]{1,0:T(8,128)S(1)} copy-done((f32[32,512]{1,0:T(8,128)S(1)}, f32[32,512]{1,0:T(8,128)}, u32[]{:S(2)}) %copy-start) | copy-done | bytes 65560
  4.5 0.7 %copy-done.2 = s32[1,2,4]{2,1,0:T(2,128)S(1)} copy-done((s32[1,2,4]{2,1,0:T(2,128)S(1)}, s32[1,2,4]{2,1,0:T(2,128)}, u32[]{:S(2)}) %copy-start.2) | copy-done | bytes 56
  5.2 0.7 %copy-done.4 = s32[8,27]{1,0:T(8,128)S(1)} copy-done((s32[8,27]{1,0:T(8,128)S(1)}, s32[8,27]{1,0:T(8,128)}, u32[]{:S(2)}) %copy-start.4) | copy-done | bytes 888
  5.9 0.7 %copy-done.5 = f32[512]{0:T(512)S(1)} copy-done((f32[512]{0:T(512)S(1)}, f32[512]{0:T(512)}, u32[]{:S(2)}) %copy-start.5) | copy-done | bytes 2072
  6.5 2.6 %shard_map.95 = (f32[32,512]{1,0:T(8,128)S(1)}, f32[40,512]{1,0:T(8,128)S(1)}, bf16[128,256]{1,0:T(8,128)(2,1)S(1)}, f32[27,8,2048]{2,1,0:T(8,128)S(1)}, bf16[25...) custom-call(s32[1,2,4]{2,1,0:T(2,128)S(1)} %copy-done.2, f32[32,512]{1,0:T(8,128)S(1)} %copy-done, ...), custom_call_target="tpu_custom_call" | custom-call | tf_op jit(solution)/shard_map/pallas_call | solution.py:423
  9.1 0.0 copy-start.1
  9.1 0.0 collective-permute-done.rest_1_
  9.2 0.8 %shard_map.96 = (f32[72,256]{1,0:T(8,128)S(1)}, f32[72,256]{1,0:T(8,128)S(1)}) custom-call(s32[1,2,4]{2,1,0:T(2,128)S(1)} %copy-done.2, s32[1,8]{1,0:T(1,128)S(1)} %copy-done.6, f32[40,512]{1,0:T(8,128)S(1)} %get-tuple-element.27.fine_ref, f32[4,512]{1,0:T(4,128)S(1)} %copy-done.3, f32[4,512]{1,0:T(4,128)S(1)} %collective-permute-done.rest_1_), custom_call_target="tpu_custom_call" | custom-call | tf_op jit(solution)/shard_map/pallas_call | solution.py:451
  9.9 0.7 %collective-permute-start.2 = (f32[72,256]{1,0:T(8,128)S(1)}, f32[72,256]{1,0:T(8,128)S(1)}, u32[]{:S(2)}, u32[]{:S(2)}) collective-permute-start(f32[72,256]{1,0:T(8,128)S(1)} %get-tuple-element.29.b_ref), channel_id=1, source_target_pairs={{2,4},{6,8},{10,12},{14,16},{18,20},{22,24},{26,28},{4,2},{8,6},{1... | collective-permute-start | bytes 221192 | tf_op jit(solution)/shard_map/ppermute | solution.py:397
  10.6 2.9 %collective-permute-start.1 = (f32[72,256]{1,0:T(8,128)S(1)}, f32[72,256]{1,0:T(8,128)S(1)}, u32[]{:S(2)}, u32[]{:S(2)}) collective-permute-start(f32[72,256]{1,0:T(8,128)S(1)} %get-tuple-element.28.after_ref.a_ref), channel_id=1, source_target_pairs={{0,2},{2,0},{4,6},{6,4},{8,10},{10,8},{12,14},{14,12},{16,18},{18,... | collective-permute-start | bytes 221192 | tf_op jit(solution)/shard_map/ppermute | solution.py:395
  13.6 0.6 %shard_map.97 = (bf16[256,1024]{1,0:T(8,128)(2,1)S(1)}, bf16[256,1024]{1,0:T(8,128)(2,1)S(1)}) custom-call(bf16[128,256]{1,0:T(8,128)(2,1)S(1)} %get-tuple-element.32.onehot_ref, f32[27,8,2048]{2,1,0:T(8,128)S(1)} %get-tuple-element.33.raw_ref, f32[72,256]{1,0:T(8,128)S(1)} %get-tuple-element.28.after_ref.a_ref), custom_call_target="tpu_custom_call" | custom-call | tf_op jit(solution)/shard_map/pallas_call | solution.py:458
  14.2 0.0 collective-permute-done.2.gb_ref
  14.2 0.3 collective-permute-done.1.ga_ref
  14.5 1.2 %shard_map.98 = (f32[64,512]{1,0:T(8,128)S(1)}, f32[32,128]{1,0:T(8,128)S(1)}) custom-call(f32[32,512]{1,0:T(8,128)S(1)} %get-tuple-element.26.resid_ref, f32[72,256]{1,0:T(8,128)S(1)} %get-tuple-element.28.after_ref.a_ref, f32[72,256]{1,0:T(8,128)S(1)} %get-tuple-element.29.b_ref, f32[72,256]{1,0:T(8,128)S(1)} %collective-permute-done.1.ga_ref, ...), custom_call_target="tpu_custom_call" | custom-call | tf_op jit(solution)/shard_map/pallas_call | solution.py:463
  15.7 2.9 %collective-permute-start.7 = (f32[32,128]{1,0:T(8,128)S(1)}, f32[32,128]{1,0:T(8,128)S(1)}, u32[]{:S(2)}, u32[]{:S(2)}) collective-permute-start(f32[32,128]{1,0:T(8,128)S(1)} %get-tuple-element.39), channel_id=1, source_target_pairs={{0,6},{2,4},{4,2},{6,0},{8,14},{10,12},{12,10},{14,8},{16,22},{18,... | collective-permute-start | bytes 49160 | tf_op jit(solution)/shard_map/ppermute | solution.py:378
  18.6 0.7 %collective-permute-start.6 = (f32[32,128]{1,0:T(8,128)S(1)}, f32[32,128]{1,0:T(8,128)S(1)}, u32[]{:S(2)}, u32[]{:S(2)}) collective-permute-start(f32[32,128]{1,0:T(8,128)S(1)} %get-tuple-element.39), channel_id=1, source_target_pairs={{0,4},{2,6},{4,0},{6,2},{8,12},{10,14},{12,8},{14,10},{16,20},{18,... | collective-permute-start | bytes 49160 | tf_op jit(solution)/shard_map/ppermute | solution.py:378
  19.3 0.0 collective-permute-start.5
  19.3 0.5 shard_map.99
  19.8 0.5 %collective-permute-start.3 = (f32[128,256]{1,0:T(8,128)S(1)}, f32[128,256]{1,0:T(8,128)S(1)}, u32[]{:S(2)}, u32[]{:S(2)}) collective-permute-start(f32[128,256]{1,0:T(8,128)S(1)} %get-tuple-element.37.own_a_ref), channel_id=1, source_target_pairs={{0,2},{2,0},{4,6},{6,4},{8,10},{10,8},{12,14},{14,12},{16,18},{18,... | collective-permute-start | bytes 393224 | tf_op jit(solution)/shard_map/ppermute | solution.py:395
  20.3 0.7 %collective-permute-start.4 = (f32[128,256]{1,0:T(8,128)S(1)}, f32[128,256]{1,0:T(8,128)S(1)}, u32[]{:S(2)}, u32[]{:S(2)}) collective-permute-start(f32[128,256]{1,0:T(8,128)S(1)} %get-tuple-element.38.own_b_ref), channel_id=1, source_target_pairs={{2,4},{6,8},{10,12},{14,16},{18,20},{22,24},{26,28},{4,2},{8,6},{1... | collective-permute-start | bytes 393224 | tf_op jit(solution)/shard_map/ppermute | solution.py:397
  21.0 1.3 %collective-permute-done.6 = f32[32,128]{1,0:T(8,128)S(1)} collective-permute-done((f32[32,128]{1,0:T(8,128)S(1)}, f32[32,128]{1,0:T(8,128)S(1)}, u32[]{:S(2)}, u32[]{:S(2)}) %collective-permute-start.6) | collective-permute-done | bytes 16416 | tf_op jit(solution)/shard_map/ppermute | solution.py:378
  22.3 4.9 %collective-permute-start.10 = (f32[32,128]{1,0:T(8,128)S(1)}, f32[32,128]{1,0:T(8,128)S(1)}, u32[]{:S(2)}, u32[]{:S(2)}) collective-permute-start(f32[32,128]{1,0:T(8,128)S(1)} %add_add_fusion.1.rest_0_), channel_id=1, source_target_pairs={{0,24},{2,26},{4,28},{6,30},{8,16},{10,18},{12,20},{14,22},{16,8},... | collective-permute-start | bytes 49160 | tf_op jit(solution)/shard_map/ppermute | solution.py:378
  27.2 0.0 collective-permute-start.9
  27.2 0.6 %collective-permute-start.8 = (f32[32,128]{1,0:T(8,128)S(1)}, f32[32,128]{1,0:T(8,128)S(1)}, u32[]{:S(2)}, u32[]{:S(2)}) collective-permute-start(f32[32,128]{1,0:T(8,128)S(1)} %add_add_fusion.1.rest_0_), channel_id=1, source_target_pairs={{0,8},{2,10},{4,12},{6,14},{8,0},{10,2},{12,4},{14,6},{16,24},{18,... | collective-permute-start | bytes 49160 | tf_op jit(solution)/shard_map/ppermute | solution.py:378
  27.9 2.5 %collective-permute-done.10.rest_3_ = f32[32,128]{1,0:T(8,128)S(1)} collective-permute-done((f32[32,128]{1,0:T(8,128)S(1)}, f32[32,128]{1,0:T(8,128)S(1)}, u32[]{:S(2)}, u32[]{:S(2)}) %collective-permute-start.10) | collective-permute-done | bytes 16416 | tf_op jit(solution)/shard_map/ppermute | solution.py:378
  30.4 1.5 %collective-permute-done.9.rest_2_ = f32[32,128]{1,0:T(8,128)S(1)} collective-permute-done((f32[32,128]{1,0:T(8,128)S(1)}, f32[32,128]{1,0:T(8,128)S(1)}, u32[]{:S(2)}, u32[]{:S(2)}) %collective-permute-start.9) | collective-permute-done | bytes 16416 | tf_op jit(solution)/shard_map/ppermute | solution.py:378
  31.9 0.0 collective-permute-done.8.rest_1_
  31.9 0.0 collective-permute-done.3.got_a_ref
  31.9 0.0 collective-permute-done.4.got_b_ref
  31.9 1.8 %shard_map.100 = (f32[32,512]{1,0:T(8,128)S(1)}, f32[32,128]{1,0:T(8,128)S(1)}, f32[32,512]{1,0:T(8,128)S(1)}, f32[32,512]{1,0:T(8,128)S(1)}, f32[32,512]{1,0:T(...) custom-call(f32[32,32]{1,0:T(8,128)S(1)} %copy-done.1, f32[32,512]{1,0:T(8,128)S(1)} %get-tuple-element.26.resid_ref, ...), custom_call_target="tpu_custom_call" | custom-call | tf_op jit(solution)/shard_map/pallas_call | solution.py:474
  33.7 0.1 collective-permute-start.15
  33.8 0.8 %collective-permute-start.14 = (f32[32,128]{1,0:T(8,128)S(1)}, f32[32,128]{1,0:T(8,128)S(1)}, u32[]{:S(2)}, u32[]{:S(2)}) collective-permute-start(f32[32,128]{1,0:T(8,128)S(1)} %get-tuple-element.49), channel_id=1, source_target_pairs={{0,4},{2,6},{4,0},{6,2},{8,12},{10,14},{12,8},{14,10},{16,20},{18,... | collective-permute-start | bytes 49160 | tf_op jit(solution)/shard_map/ppermute | solution.py:378
  34.6 1.1 %collective-permute-start.13 = (f32[32,128]{1,0:T(8,128)S(1)}, f32[32,128]{1,0:T(8,128)S(1)}, u32[]{:S(2)}, u32[]{:S(2)}) collective-permute-start(f32[32,128]{1,0:T(8,128)S(1)} %get-tuple-element.49), channel_id=1, source_target_pairs={{0,2},{2,0},{4,6},{6,4},{8,10},{10,8},{12,14},{14,12},{16,18},{18,... | collective-permute-start | bytes 49160 | tf_op jit(solution)/shard_map/ppermute | solution.py:378
  35.6 0.5 shard_map.101
  36.1 0.1 collective-permute-start.11
  36.1 0.7 %collective-permute-start.12 = (f32[32,256]{1,0:T(8,128)S(1)}, f32[32,256]{1,0:T(8,128)S(1)}, u32[]{:S(2)}, u32[]{:S(2)}) collective-permute-start(f32[32,256]{1,0:T(8,128)S(1)} %get-tuple-element.48), channel_id=1, source_target_pairs={{2,4},{6,8},{10,12},{14,16},{18,20},{22,24},{26,28},{4,2},{8,6},{1... | collective-permute-start | bytes 98312 | tf_op jit(solution)/shard_map/ppermute | solution.py:397
  36.8 0.1 collective-permute-done.15
  36.9 0.7 %collective-permute-done.14 = f32[32,128]{1,0:T(8,128)S(1)} collective-permute-done((f32[32,128]{1,0:T(8,128)S(1)}, f32[32,128]{1,0:T(8,128)S(1)}, u32[]{:S(2)}, u32[]{:S(2)}) %collective-permute-start.14) | collective-permute-done | bytes 16416 | tf_op jit(solution)/shard_map/ppermute | solution.py:378
  37.6 0.0 collective-permute-done.13
  37.6 4.3 %collective-permute-start.18 = (f32[32,128]{1,0:T(8,128)S(1)}, f32[32,128]{1,0:T(8,128)S(1)}, u32[]{:S(2)}, u32[]{:S(2)}) collective-permute-start(f32[32,128]{1,0:T(8,128)S(1)} %add_add_fusion.rest_0_), channel_id=1, source_target_pairs={{0,24},{2,26},{4,28},{6,30},{8,16},{10,18},{12,20},{14,22},{16,8},... | collective-permute-start | bytes 49160 | tf_op jit(solution)/shard_map/ppermute | solution.py:378
  41.9 0.0 collective-permute-start.17
  41.9 0.6 %collective-permute-start.16 = (f32[32,128]{1,0:T(8,128)S(1)}, f32[32,128]{1,0:T(8,128)S(1)}, u32[]{:S(2)}, u32[]{:S(2)}) collective-permute-start(f32[32,128]{1,0:T(8,128)S(1)} %add_add_fusion.rest_0_), channel_id=1, source_target_pairs={{0,8},{2,10},{4,12},{6,14},{8,0},{10,2},{12,4},{14,6},{16,24},{18,... | collective-permute-start | bytes 49160 | tf_op jit(solution)/shard_map/ppermute | solution.py:378
  42.5 0.0 collective-permute-done.11.got_a_ref
  42.5 0.0 collective-permute-done.12.got_b_ref
  42.5 1.6 %collective-permute-done.18.rest_3_ = f32[32,128]{1,0:T(8,128)S(1)} collective-permute-done((f32[32,128]{1,0:T(8,128)S(1)}, f32[32,128]{1,0:T(8,128)S(1)}, u32[]{:S(2)}, u32[]{:S(2)}) %collective-permute-start.18) | collective-permute-done | bytes 16416 | tf_op jit(solution)/shard_map/ppermute | solution.py:378
  44.2 2.4 %collective-permute-done.17.rest_2_ = f32[32,128]{1,0:T(8,128)S(1)} collective-permute-done((f32[32,128]{1,0:T(8,128)S(1)}, f32[32,128]{1,0:T(8,128)S(1)}, u32[]{:S(2)}, u32[]{:S(2)}) %collective-permute-start.17) | collective-permute-done | bytes 16416 | tf_op jit(solution)/shard_map/ppermute | solution.py:378
  46.5 1.8 %shard_map.102 = (f32[32,512]{1,0:T(8,128)}, f32[32,512]{1,0:T(8,128)}) custom-call(s32[1,2,4]{2,1,0:T(2,128)S(1)} %copy-done.2, f32[32,512]{1,0:T(8,128)S(1)} %get-tuple-element.40.resid1_ref, f32[32,512]{1,0:T(8,128)S(1)} %get-tuple-element.41.z0_ref, f32[32,512]{1,0:T(8,128)S(1)} %get-tuple-element.42.z1_ref, f32[32,512]{1,0:T(8,128)S(1)} %get-tuple-element.43.q0_ref, ...), custom_call_target="tpu_custom_call" | custom-call | tf_op jit(solution)/shard_map/pallas_call | solution.py:489
  (14 shorter events, 0.0 us)
Async XLA Ops:
  0.6 8.5 %copy-start.6 = (s32[1,8]{1,0:T(1,128)S(1)}, s32[1,8]{1,0:T(1,128)}, u32[]{:S(2)}) copy-start(s32[1,8]{1,0:T(1,128)} %owner_ref.1) | copy-start | bytes 100
  0.6 8.5 %collective-permute-start = (f32[4,512]{1,0:T(4,128)}, f32[4,512]{1,0:T(4,128)S(1)}, u32[]{:S(2)}, u32[]{:S(2)}) collective-permute-start(f32[4,512]{1,0:T(4,128)} %rest_0_.1), channel_id=1, source_target_pairs={{1,0},{0,1},{3,2},{2,3},{5,4},{4,5},{7,6},{6,7},{9,8},{8,9},{11,10... | collective-permute-start | bytes 24584 | tf_op jit(solution)/shard_map/ppermute | solution.py:418
  3.6 0.8 %copy-start = (f32[32,512]{1,0:T(8,128)S(1)}, f32[32,512]{1,0:T(8,128)}, u32[]{:S(2)}) copy-start(f32[32,512]{1,0:T(8,128)} %right_hbm.1) | copy-start | bytes 196612
  4.5 0.7 %copy-start.2 = (s32[1,2,4]{2,1,0:T(2,128)S(1)}, s32[1,2,4]{2,1,0:T(2,128)}, u32[]{:S(2)}) copy-start(s32[1,2,4]{2,1,0:T(2,128)} %rows_ref.3) | copy-start | bytes 100
  5.2 0.7 %copy-start.4 = (s32[8,27]{1,0:T(8,128)S(1)}, s32[8,27]{1,0:T(8,128)}, u32[]{:S(2)}) copy-start(s32[8,27]{1,0:T(8,128)} %columns_hbm.1) | copy-start | bytes 2596
  5.9 0.7 %copy-start.5 = (f32[512]{0:T(512)S(1)}, f32[512]{0:T(512)}, u32[]{:S(2)}) copy-start(f32[512]{0:T(512)} %param.14) | copy-start | bytes 6148
  6.5 2.6 %copy-start.3 = (f32[4,512]{1,0:T(4,128)S(1)}, f32[4,512]{1,0:T(4,128)}, u32[]{:S(2)}) copy-start(f32[4,512]{1,0:T(4,128)} %rest_0_.1) | copy-start | bytes 24580
  9.1 22.7 %copy-start.1 = (f32[32,32]{1,0:T(8,128)S(1)}, f32[32,32]{1,0:T(8,128)}, u32[]{:S(2)}) copy-start(f32[32,32]{1,0:T(8,128)} %inverse_ref.1) | copy-start | bytes 12292
  9.9 4.2 %collective-permute-start.2 = (f32[72,256]{1,0:T(8,128)S(1)}, f32[72,256]{1,0:T(8,128)S(1)}, u32[]{:S(2)}, u32[]{:S(2)}) collective-permute-start(f32[72,256]{1,0:T(8,128)S(1)} %get-tuple-element.29.b_ref), channel_id=1, source_target_pairs={{2,4},{6,8},{10,12},{14,16},{18,20},{22,24},{26,28},{4,2},{8,6},{1... | collective-permute-start | bytes 221192 | tf_op jit(solution)/shard_map/ppermute | solution.py:397
  10.6 3.9 %collective-permute-start.1 = (f32[72,256]{1,0:T(8,128)S(1)}, f32[72,256]{1,0:T(8,128)S(1)}, u32[]{:S(2)}, u32[]{:S(2)}) collective-permute-start(f32[72,256]{1,0:T(8,128)S(1)} %get-tuple-element.28.after_ref.a_ref), channel_id=1, source_target_pairs={{0,2},{2,0},{4,6},{6,4},{8,10},{10,8},{12,14},{14,12},{16,18},{18,... | collective-permute-start | bytes 221192 | tf_op jit(solution)/shard_map/ppermute | solution.py:395
  15.7 5.3 %collective-permute-start.7 = (f32[32,128]{1,0:T(8,128)S(1)}, f32[32,128]{1,0:T(8,128)S(1)}, u32[]{:S(2)}, u32[]{:S(2)}) collective-permute-start(f32[32,128]{1,0:T(8,128)S(1)} %get-tuple-element.39), channel_id=1, source_target_pairs={{0,6},{2,4},{4,2},{6,0},{8,14},{10,12},{12,10},{14,8},{16,22},{18,... | collective-permute-start | bytes 49160 | tf_op jit(solution)/shard_map/ppermute | solution.py:378
  18.6 3.7 %collective-permute-start.6 = (f32[32,128]{1,0:T(8,128)S(1)}, f32[32,128]{1,0:T(8,128)S(1)}, u32[]{:S(2)}, u32[]{:S(2)}) collective-permute-start(f32[32,128]{1,0:T(8,128)S(1)} %get-tuple-element.39), channel_id=1, source_target_pairs={{0,4},{2,6},{4,0},{6,2},{8,12},{10,14},{12,8},{14,10},{16,20},{18,... | collective-permute-start | bytes 49160 | tf_op jit(solution)/shard_map/ppermute | solution.py:378
  19.3 3.0 %collective-permute-start.5 = (f32[32,128]{1,0:T(8,128)S(1)}, f32[32,128]{1,0:T(8,128)S(1)}, u32[]{:S(2)}, u32[]{:S(2)}) collective-permute-start(f32[32,128]{1,0:T(8,128)S(1)} %get-tuple-element.39), channel_id=1, source_target_pairs={{0,2},{2,0},{4,6},{6,4},{8,10},{10,8},{12,14},{14,12},{16,18},{18,... | collective-permute-start | bytes 49160 | tf_op jit(solution)/shard_map/ppermute | solution.py:378
  19.8 12.1 %collective-permute-start.3 = (f32[128,256]{1,0:T(8,128)S(1)}, f32[128,256]{1,0:T(8,128)S(1)}, u32[]{:S(2)}, u32[]{:S(2)}) collective-permute-start(f32[128,256]{1,0:T(8,128)S(1)} %get-tuple-element.37.own_a_ref), channel_id=1, source_target_pairs={{0,2},{2,0},{4,6},{6,4},{8,10},{10,8},{12,14},{14,12},{16,18},{18,... | collective-permute-start | bytes 393224 | tf_op jit(solution)/shard_map/ppermute | solution.py:395
  20.3 11.6 %collective-permute-start.4 = (f32[128,256]{1,0:T(8,128)S(1)}, f32[128,256]{1,0:T(8,128)S(1)}, u32[]{:S(2)}, u32[]{:S(2)}) collective-permute-start(f32[128,256]{1,0:T(8,128)S(1)} %get-tuple-element.38.own_b_ref), channel_id=1, source_target_pairs={{2,4},{6,8},{10,12},{14,16},{18,20},{22,24},{26,28},{4,2},{8,6},{1... | collective-permute-start | bytes 393224 | tf_op jit(solution)/shard_map/ppermute | solution.py:397
  22.3 8.1 %collective-permute-start.10 = (f32[32,128]{1,0:T(8,128)S(1)}, f32[32,128]{1,0:T(8,128)S(1)}, u32[]{:S(2)}, u32[]{:S(2)}) collective-permute-start(f32[32,128]{1,0:T(8,128)S(1)} %add_add_fusion.1.rest_0_), channel_id=1, source_target_pairs={{0,24},{2,26},{4,28},{6,30},{8,16},{10,18},{12,20},{14,22},{16,8},... | collective-permute-start | bytes 49160 | tf_op jit(solution)/shard_map/ppermute | solution.py:378
  27.2 4.6 %collective-permute-start.9 = (f32[32,128]{1,0:T(8,128)S(1)}, f32[32,128]{1,0:T(8,128)S(1)}, u32[]{:S(2)}, u32[]{:S(2)}) collective-permute-start(f32[32,128]{1,0:T(8,128)S(1)} %add_add_fusion.1.rest_0_), channel_id=1, source_target_pairs={{0,16},{2,18},{4,20},{6,22},{8,24},{10,26},{12,28},{14,30},{16,0},... | collective-permute-start | bytes 49160 | tf_op jit(solution)/shard_map/ppermute | solution.py:378
  27.2 4.6 %collective-permute-start.8 = (f32[32,128]{1,0:T(8,128)S(1)}, f32[32,128]{1,0:T(8,128)S(1)}, u32[]{:S(2)}, u32[]{:S(2)}) collective-permute-start(f32[32,128]{1,0:T(8,128)S(1)} %add_add_fusion.1.rest_0_), channel_id=1, source_target_pairs={{0,8},{2,10},{4,12},{6,14},{8,0},{10,2},{12,4},{14,6},{16,24},{18,... | collective-permute-start | bytes 49160 | tf_op jit(solution)/shard_map/ppermute | solution.py:378
  33.7 3.2 %collective-permute-start.15 = (f32[32,128]{1,0:T(8,128)S(1)}, f32[32,128]{1,0:T(8,128)S(1)}, u32[]{:S(2)}, u32[]{:S(2)}) collective-permute-start(f32[32,128]{1,0:T(8,128)S(1)} %get-tuple-element.49), channel_id=1, source_target_pairs={{0,6},{2,4},{4,2},{6,0},{8,14},{10,12},{12,10},{14,8},{16,22},{18,... | collective-permute-start | bytes 49160 | tf_op jit(solution)/shard_map/ppermute | solution.py:378
  33.8 3.8 %collective-permute-start.14 = (f32[32,128]{1,0:T(8,128)S(1)}, f32[32,128]{1,0:T(8,128)S(1)}, u32[]{:S(2)}, u32[]{:S(2)}) collective-permute-start(f32[32,128]{1,0:T(8,128)S(1)} %get-tuple-element.49), channel_id=1, source_target_pairs={{0,4},{2,6},{4,0},{6,2},{8,12},{10,14},{12,8},{14,10},{16,20},{18,... | collective-permute-start | bytes 49160 | tf_op jit(solution)/shard_map/ppermute | solution.py:378
  34.6 3.0 %collective-permute-start.13 = (f32[32,128]{1,0:T(8,128)S(1)}, f32[32,128]{1,0:T(8,128)S(1)}, u32[]{:S(2)}, u32[]{:S(2)}) collective-permute-start(f32[32,128]{1,0:T(8,128)S(1)} %get-tuple-element.49), channel_id=1, source_target_pairs={{0,2},{2,0},{4,6},{6,4},{8,10},{10,8},{12,14},{14,12},{16,18},{18,... | collective-permute-start | bytes 49160 | tf_op jit(solution)/shard_map/ppermute | solution.py:378
  36.1 6.5 %collective-permute-start.11 = (f32[32,256]{1,0:T(8,128)S(1)}, f32[32,256]{1,0:T(8,128)S(1)}, u32[]{:S(2)}, u32[]{:S(2)}) collective-permute-start(f32[32,256]{1,0:T(8,128)S(1)} %get-tuple-element.47), channel_id=1, source_target_pairs={{0,2},{2,0},{4,6},{6,4},{8,10},{10,8},{12,14},{14,12},{16,18},{18,... | collective-permute-start | bytes 98312 | tf_op jit(solution)/shard_map/ppermute | solution.py:395
  36.1 6.4 %collective-permute-start.12 = (f32[32,256]{1,0:T(8,128)S(1)}, f32[32,256]{1,0:T(8,128)S(1)}, u32[]{:S(2)}, u32[]{:S(2)}) collective-permute-start(f32[32,256]{1,0:T(8,128)S(1)} %get-tuple-element.48), channel_id=1, source_target_pairs={{2,4},{6,8},{10,12},{14,16},{18,20},{22,24},{26,28},{4,2},{8,6},{1... | collective-permute-start | bytes 98312 | tf_op jit(solution)/shard_map/ppermute | solution.py:397
  37.6 6.6 %collective-permute-start.18 = (f32[32,128]{1,0:T(8,128)S(1)}, f32[32,128]{1,0:T(8,128)S(1)}, u32[]{:S(2)}, u32[]{:S(2)}) collective-permute-start(f32[32,128]{1,0:T(8,128)S(1)} %add_add_fusion.rest_0_), channel_id=1, source_target_pairs={{0,24},{2,26},{4,28},{6,30},{8,16},{10,18},{12,20},{14,22},{16,8},... | collective-permute-start | bytes 49160 | tf_op jit(solution)/shard_map/ppermute | solution.py:378
  41.9 4.6 %collective-permute-start.17 = (f32[32,128]{1,0:T(8,128)S(1)}, f32[32,128]{1,0:T(8,128)S(1)}, u32[]{:S(2)}, u32[]{:S(2)}) collective-permute-start(f32[32,128]{1,0:T(8,128)S(1)} %add_add_fusion.rest_0_), channel_id=1, source_target_pairs={{0,16},{2,18},{4,20},{6,22},{8,24},{10,26},{12,28},{14,30},{16,0},... | collective-permute-start | bytes 49160 | tf_op jit(solution)/shard_map/ppermute | solution.py:378
  41.9 4.6 %collective-permute-start.16 = (f32[32,128]{1,0:T(8,128)S(1)}, f32[32,128]{1,0:T(8,128)S(1)}, u32[]{:S(2)}, u32[]{:S(2)}) collective-permute-start(f32[32,128]{1,0:T(8,128)S(1)} %add_add_fusion.rest_0_), channel_id=1, source_target_pairs={{0,8},{2,10},{4,12},{6,14},{8,0},{10,2},{12,4},{14,6},{16,24},{18,... | collective-permute-start | bytes 49160 | tf_op jit(solution)/shard_map/ppermute | solution.py:378

commit v3 on v0

v3 whole, which is shorter than its diff:
```python
import functools

import jax
import jax.numpy as jnp
from jax import lax
from jax.experimental import pallas as pl
from jax.experimental.pallas import tpu as pltpu
from jax.sharding import PartitionSpec as P

B = 64
KNZ = 27
IFB = 4
NCL = 8
NB = 2 * IFB
NE = NB + 2 * IFB
EDGE = IFB * B
OWN = NB * B
EXT = NE * B
ROWS = NB * B
KPAD = 32
F32 = jnp.float32
BF16 = jnp.bfloat16
HIGHEST = lax.Precision.HIGHEST
NT = (((1,), (1,)), ((), ()))
NN = (((1,), (0,)), ((), ()))
VMEM_SMALL = 16 * 1024 * 1024
VMEM_LARGE = 48 * 1024 * 1024
CHUNK = 512


def split(x):
    high = x.astype(BF16)
    return high, (x - high.astype(F32)).astype(BF16)


def times(x, high, low, dims):
    count = x.shape[0]
    xh, xl = split(x)
    both = lax.dot_general(
        jnp.concatenate([xh, xl], axis=0), high, dims, preferred_element_type=F32
    )
    return both[:count] + both[count:] + lax.dot_general(xh, low, dims, preferred_element_type=F32)


def exact(x, y, dims=NN):
    return lax.dot_general(x, y, dims, precision=HIGHEST, preferred_element_type=F32)


def call(kernel, outs, n_in, smem=(), raw=(), raw_out=False, scratch=(), bytes_moved=None, large=False):
    def spec(i):
        if i in raw:
            return pl.BlockSpec(memory_space=pltpu.HBM)
        return pl.BlockSpec(memory_space=pltpu.SMEM if i in smem else pltpu.VMEM)

    return pl.pallas_call(
        kernel,
        out_shape=outs,
        in_specs=[spec(i) for i in range(n_in)],
        out_specs=[
            pl.BlockSpec(memory_space=pltpu.HBM if raw_out else pltpu.VMEM) for _ in outs
        ],
        scratch_shapes=list(scratch),
        cost_estimate=bytes_moved
        and pl.CostEstimate(flops=0, transcendentals=0, bytes_accessed=bytes_moved),
        compiler_params=pltpu.CompilerParams(vmem_limit_bytes=VMEM_LARGE if large else VMEM_SMALL),
    )


def shape(*dims):
    return jax.ShapeDtypeStruct(dims, F32)


def place_of(rows_ref, odd, j):
    side = jnp.where(odd == 1, j // IFB, 1 - j // IFB)
    return rows_ref[0, side, j % IFB]


def load_blocks(blocks_hbm, high_ref, low_ref, chunk_ref, sems):
    chunks = [
        pltpu.make_async_copy(
            blocks_hbm.at[:, :, pl.ds(CHUNK * t, CHUNK)], chunk_ref.at[t], sems.at[t]
        )
        for t in range(B * B // CHUNK)
    ]
    for copy in chunks:
        copy.start()
    filler = jnp.zeros((NB * KPAD - NB * (KNZ + 1), B * B), BF16)
    high_ref[NB * (KNZ + 1) :, :] = filler
    low_ref[NB * (KNZ + 1) :, :] = filler
    for t, copy in enumerate(chunks):
        copy.wait()
        padded = jnp.concatenate([chunk_ref[t], jnp.zeros((1, NB, CHUNK), F32)], axis=0)
        wh, wl = split(padded.reshape(NB * (KNZ + 1), CHUNK))
        cut = slice(CHUNK * t, CHUNK * (t + 1))
        high_ref[: NB * (KNZ + 1), cut] = wh
        low_ref[: NB * (KNZ + 1), cut] = wl


def assemble(rows_ref, columns_ref, wh_ref, wl_ref, after_ref, high_ref, low_ref):
    odd = lax.axis_index("sub") % 2
    column = columns_ref[...]
    place = jnp.where(
        (column < NB + IFB) == (odd == 1), column % IFB + NB, column % IFB + NB + IFB
    )
    for j in range(NB):
        place = jnp.where(column == place_of(rows_ref, odd, j), j, place)
    slot = lax.broadcasted_iota(jnp.int32, (KNZ, NB * KPAD), 0)
    entry = lax.broadcasted_iota(jnp.int32, (KNZ, NB * KPAD), 1)
    widen = jnp.where(entry // NB == slot, 1.0, 0.0).astype(BF16)
    wide = lax.dot_general(place.astype(F32).astype(BF16), widen, NN, preferred_element_type=F32)
    r = lax.broadcasted_iota(jnp.int32, (NE * NB, NB * KPAD), 0)
    q = lax.broadcasted_iota(jnp.int32, (NE * NB, NB * KPAD), 1)
    hit = (jnp.concatenate([wide] * NE, axis=0) == (r // NB).astype(F32)) & (r % NB == q % NB)
    onehot = jnp.where(hit, 1.0, 0.0).astype(BF16)
    first = lax.broadcasted_iota(jnp.int32, (NB, 128), 1) < B
    for t in range(B * B // CHUNK):
        cut = slice(CHUNK * t, CHUNK * (t + 1))
        dense = lax.dot_general(
            onehot, wh_ref[:, cut], NN, preferred_element_type=F32
        ) + lax.dot_general(onehot, wl_ref[:, cut], NN, preferred_element_type=F32)
        for m in range(NE // 2):
            for h in range(CHUNK // 128):
                lane = slice(128 * h, 128 * (h + 1))
                left = dense[16 * m : 16 * m + 8, lane]
                right = dense[16 * m + 8 : 16 * m + 16, lane]
                tile = jnp.concatenate(
                    [
                        jnp.where(first, left, pltpu.roll(right, B, 1)),
                        jnp.where(first, pltpu.roll(left, B, 1), right),
                    ],
                    axis=0,
                )
                th, tl = split(tile)
                at = NB * CHUNK // B * t + 16 * h
                high_ref[at : at + 16, 128 * m : 128 * (m + 1)] = th
                low_ref[at : at + 16, 128 * m : 128 * (m + 1)] = tl


def sides(rows_ref, owner_ref, right_ref, scale_ref, after_ref, *rest, parts, ncoarse):
    basis_refs = rest[:parts]
    resid_ref, side_a_ref, side_b_ref, blk_ref = rest[parts:]
    odd = lax.axis_index("sub") % 2
    mine = lax.axis_index("rhs")
    cases = right_ref.shape[0]
    per = NCL // parts
    scale = jnp.broadcast_to(scale_ref[...], (8, OWN))
    unknown = lax.broadcasted_iota(jnp.int32, (ncoarse, OWN), 0)
    coarse = jnp.zeros((ncoarse, OWN), F32)
    for k in range(parts):
        for t in range(per):
            owner = owner_ref[0, ((mine + k) % parts) * per + t]
            coarse = coarse + jnp.where(unknown == owner, basis_refs[k][t : t + 1, :], 0.0)
    right = right_ref[...]
    fine = right * scale[0:1]
    live = cases + ncoarse
    for n in range(NB):
        cut = slice(B * n, B * (n + 1))
        blk_ref[n, 0:cases, :] = fine[:, cut]
        blk_ref[n, cases:live, :] = coarse[:, cut]
        blk_ref[n, live : live + 8, :] = scale[:, cut]
        blk_ref[n, live + 8 :, :] = right[:, cut]
    for j in range(0, NB, 2):
        pair = jnp.concatenate(
            [blk_ref[place_of(rows_ref, odd, j)], blk_ref[place_of(rows_ref, odd, j + 1)]], axis=1
        )
        target = side_a_ref if j < IFB else side_b_ref
        at = B * (j % IFB)
        target[:, at : at + 2 * B] = pair[: live + 8]
        resid_ref[:, B * j : B * (j + 2)] = pair[live + 8 :]


def first_apply(a_ref, b_ref, ga_ref, gb_ref, high_ref, low_ref, strain_ref, send_a_ref, send_b_ref):
    live = strain_ref.shape[0]
    field = jnp.concatenate([ref[:live, :] for ref in (a_ref, b_ref, ga_ref, gb_ref)], axis=1)
    strain = times(field, high_ref[...], low_ref[...], NT)
    strain_ref[...] = strain
    back = times(strain, high_ref[...], low_ref[...], NN)
    send_a_ref[:live, :] = field[:, :EDGE] + back[:, :EDGE]
    send_a_ref[live:, :] = back[:, OWN : OWN + EDGE]
    send_b_ref[:live, :] = field[:, EDGE:OWN] + back[:, EDGE:OWN]
    send_b_ref[live:, :] = back[:, OWN + EDGE :]


def first_sums(resid_ref, a_ref, b_ref, strain_ref, fixed_ref, *, cases, ncoarse):
    live = cases + ncoarse
    own = jnp.concatenate([a_ref[:live, :], b_ref[:live, :]], axis=1)
    paired = jnp.concatenate([own, strain_ref[...]], axis=1)
    gram = exact(paired, paired[cases:], NT)
    resid = resid_ref[...]
    lead = paired[:cases]
    fixed_ref[...] = jnp.zeros_like(fixed_ref)
    fixed_ref[:cases, 0:ncoarse] = exact(resid, own[cases:], NT)
    fixed_ref[:cases, ncoarse : 2 * ncoarse] = gram[:cases]
    fixed_ref[:ncoarse, 2 * ncoarse : 3 * ncoarse] = gram[cases:]
    at = 3 * ncoarse
    fixed_ref[:cases, at : at + 1] = jnp.sum(resid * own[:cases], axis=1, keepdims=True)
    fixed_ref[:cases, at + 1 : at + 2] = jnp.sum(lead * lead, axis=1, keepdims=True)


def second_apply(
    a_ref,
    b_ref,
    ga_ref,
    gb_ref,
    own_a_ref,
    own_b_ref,
    got_a_ref,
    got_b_ref,
    high_ref,
    low_ref,
    fixed_ref,
    strain_ref,
    image_ref,
    scaled_ref,
    pay_ref,
    *,
    cases,
    ncoarse,
):
    live = cases + ncoarse
    image = jnp.concatenate(
        [
            own_a_ref[:live, :] + got_a_ref[live:, :],
            own_b_ref[:live, :] + got_b_ref[live:, :],
            own_a_ref[live:, :] + got_a_ref[:live, :],
            own_b_ref[live:, :] + got_b_ref[:live, :],
        ],
        axis=1,
    )
    scale = jnp.concatenate(
        [ref[live : live + 1, :] for ref in (a_ref, b_ref, ga_ref, gb_ref)], axis=1
    )
    field = scale * image
    strain = times(field, high_ref[...], low_ref[...], NT)
    own = field[:, :OWN]
    first = image[:, :OWN]
    strain_ref[...] = strain
    image_ref[...] = first
    scaled_ref[...] = own
    paired = jnp.concatenate([own, strain], axis=1)
    gram = exact(paired, paired[cases:], NT)
    cross = exact(own, first[cases:], NT)
    lead = paired[:cases]
    pay_ref[...] = jnp.zeros_like(pay_ref)
    n = ncoarse
    pay_ref[:, 0 : 3 * n] = fixed_ref[:, 0 : 3 * n]
    pay_ref[:cases, 3 * n : 4 * n] = cross[:cases]
    pay_ref[:n, 4 * n : 5 * n] = cross[cases:]
    pay_ref[:cases, 5 * n : 6 * n] = gram[:cases]
    pay_ref[:n, 6 * n : 7 * n] = gram[cases:]
    at = 7 * n
    pay_ref[:, at : at + 2] = fixed_ref[:, 3 * n : 3 * n + 2]
    pay_ref[:cases, at + 2 : at + 3] = jnp.sum(own[:cases] * first[:cases], axis=1, keepdims=True)
    pay_ref[:cases, at + 3 : at + 4] = jnp.sum(lead * lead, axis=1, keepdims=True)


def second_image(scaled_ref, strain_ref, high_ref, low_ref, own_ref, send_a_ref, send_b_ref):
    back = times(strain_ref[...], high_ref[...], low_ref[...], NN)
    own_ref[...] = scaled_ref[...] + back[:, :OWN]
    send_a_ref[...] = back[:, OWN : OWN + EDGE]
    send_b_ref[...] = back[:, OWN + EDGE :]


def finish(
    rows_ref,
    inverse_ref,
    resid_ref,
    a_ref,
    b_ref,
    image_ref,
    scaled_ref,
    own_ref,
    got_a_ref,
    got_b_ref,
    *rest,
    cases,
    ncoarse,
    n_pay,
):
    pays = rest[:n_pay]
    field_hbm, resid2_hbm, field_ref, resid2_ref, blk_ref, sems = rest[n_pay:]
    odd = lax.axis_index("sub") % 2
    n = ncoarse
    live = cases + n
    pay = pays[0][...]
    for other in pays[1:]:
        pay = pay + other[...]

    def total(value):
        return jnp.sum(value, axis=1, keepdims=True)

    u0 = pay[:cases, 0:n]
    g12 = pay[:cases, n : 2 * n]
    g22 = pay[:n, 2 * n : 3 * n]
    g14 = pay[:cases, 3 * n : 4 * n]
    g34 = pay[:cases, 5 * n : 6 * n]
    at = 7 * n
    r0d, g11, g13, g33 = (pay[:cases, at + k : at + k + 1] for k in range(4))
    inverse = inverse_ref[...]
    y0 = exact(u0, inverse)
    y22 = exact(y0, g22)
    y24 = exact(y0, pay[:n, 4 * n : 5 * n])
    y44 = exact(y0, pay[:n, 6 * n : 7 * n])
    rz0 = r0d + total(u0 * y0)
    pq0 = g11 + total(y0 * (2.0 * g12 + y22))
    alpha = rz0 / pq0
    u1 = u0 - alpha * (g12 + y22)
    y1 = exact(u1, inverse)
    cross = g13 + total(y0 * g14)
    rz1 = (
        r0d
        - 2.0 * alpha * (g11 + total(y0 * g12))
        + alpha * alpha * (cross + total(y0 * (g14 + y24)))
        + total(u1 * y1)
    )
    beta = rz1 / rz0
    lead = 1.0 + beta
    coarse = y1 + beta * y0
    c22 = exact(y1, g22) + beta * y22
    pq1 = (
        lead * (lead * g11 + 2.0 * total(coarse * g12) - 2.0 * alpha * cross)
        + total(coarse * (c22 - 2.0 * alpha * (g14 + y24)))
        + alpha * alpha * (g33 + total(y0 * (2.0 * g34 + y44)))
    )
    alpha1 = rz1 / pq1
    lower = alpha1 * alpha
    upper = alpha + alpha1 * lead
    weights = jnp.concatenate([alpha * y0 + alpha1 * coarse, -lower * y0], axis=1)
    start = jnp.concatenate([a_ref[:live, :], b_ref[:live, :]], axis=1)
    scaled = scaled_ref[...]
    image = image_ref[...]
    image2 = own_ref[...] + jnp.concatenate([got_a_ref[...], got_b_ref[...]], axis=1)
    field = (
        upper * start[:cases]
        - lower * scaled[:cases]
        + exact(weights, jnp.concatenate([start[cases:], scaled[cases:]], axis=0))
    )
    resid2 = (
        resid_ref[...]
        - upper * image[:cases]
        + lower * image2[:cases]
        - exact(weights, jnp.concatenate([image[cases:], image2[cases:]], axis=0))
    )
    copies = []
    for k, (value, out, buf) in enumerate(
        ((field, field_hbm, field_ref), (resid2, resid2_hbm, resid2_ref))
    ):
        for j in range(NB):
            blk_ref[k, place_of(rows_ref, odd, j)] = value[:, B * j : B * (j + 1)]
        for m in range(0, NB, 2):
            buf[:, B * m : B * (m + 2)] = jnp.concatenate([blk_ref[k, m], blk_ref[k, m + 1]], axis=1)
        copies.append(pltpu.make_async_copy(buf, out, sems.at[k]))
        copies[-1].start()
    for copy in copies:
        copy.wait()


def lanes_for(width):
    return -(-width // 128) * 128


def swap(x, steps, count):
    return [lax.ppermute(x, "sub", [(i, i ^ k) for i in range(count)]) for k in steps]


def rounds_of(count):
    rounds = []
    base = 1
    while base < count:
        if base * 4 <= count:
            rounds.append((base, 2 * base, 3 * base))
            base *= 4
        else:
            rounds.append((base,))
            base *= 2
    return rounds


def across(a, b, count):
    low = lax.ppermute(a, "sub", [(i, i ^ 1) for i in range(count)])
    inner = [(i, i + 1) for i in range(1, count - 1, 2)]
    return low, lax.ppermute(b, "sub", inner + [(j, i) for i, j in inner])


def body(
    right_side,
    stiffness_blocks,
    block_columns,
    interface_rows,
    corner_owner,
    corner_basis,
    jacobi_scale,
    coarse_inverse,
):
    cases = right_side.shape[0]
    ncoarse = coarse_inverse.shape[0]
    count = lax.axis_size("sub")
    parts = lax.axis_size("rhs")
    live = cases + ncoarse
    rounds = rounds_of(count)
    run = functools.partial(call, large=live > 128)

    bases = [corner_basis] + [
        lax.ppermute(corner_basis, "rhs", [((i + k) % parts, i) for i in range(parts)])
        for k in range(1, parts)
    ]
    packed = jax.ShapeDtypeStruct((NB * KPAD, B * B), BF16)
    wh, wl = call(
        load_blocks,
        [packed, packed],
        1,
        raw=(0,),
        scratch=[
            pltpu.VMEM((B * B // CHUNK, KNZ, NB, CHUNK), F32),
            pltpu.SemaphoreType.DMA((B * B // CHUNK,)),
        ],
        bytes_moved=16 * 1024 * 1024,
        large=True,
    )(jnp.transpose(stiffness_blocks, (1, 0, 2)))
    resid, side_a, side_b = run(
        functools.partial(sides, parts=parts, ncoarse=ncoarse),
        [shape(cases, OWN), shape(live + 8, EDGE), shape(live + 8, EDGE)],
        5 + parts,
        smem=(0, 1),
        scratch=[pltpu.VMEM((NB, live + 8 + cases, B), F32)],
    )(interface_rows, corner_owner, right_side, jacobi_scale.reshape(1, OWN), wh, *bases)
    dense = jax.ShapeDtypeStruct((ROWS, EXT), BF16)
    high, low = run(assemble, [dense, dense], 5, smem=(0,))(
        interface_rows, block_columns, wh, wl, side_a
    )
    ghost_a, ghost_b = across(side_a, side_b, count)
    ends = (side_a, side_b, ghost_a, ghost_b)

    rows = max(cases, ncoarse)
    strain, own_a, own_b = run(
        first_apply, [shape(live, ROWS), shape(2 * live, EDGE), shape(2 * live, EDGE)], 6
    )(*ends, high, low)
    got_a, got_b = across(own_a, own_b, count)
    (fixed,) = run(
        functools.partial(first_sums, cases=cases, ncoarse=ncoarse),
        [shape(rows, lanes_for(3 * ncoarse + 2))],
        4,
    )(resid, side_a, side_b, strain)
    strain, image, scaled, pay = run(
        functools.partial(second_apply, cases=cases, ncoarse=ncoarse),
        [shape(live, ROWS), shape(live, OWN), shape(live, OWN), shape(rows, lanes_for(7 * ncoarse + 4))],
        11,
    )(*ends, own_a, own_b, got_a, got_b, high, low, fixed)
    for steps in rounds[:-1]:
        pay = sum(swap(pay, steps, count), pay)
    pays = [pay] + swap(pay, rounds[-1], count)
    own, back_a, back_b = run(
        second_image, [shape(live, OWN), shape(live, EDGE), shape(live, EDGE)], 4
    )(scaled, strain, high, low)
    got_a, got_b = across(back_a, back_b, count)
    return tuple(
        run(
            functools.partial(finish, cases=cases, ncoarse=ncoarse, n_pay=len(pays)),
            [shape(cases, OWN)] * 2,
            10 + len(pays),
            smem=(0,),
            raw_out=True,
            scratch=[
                pltpu.VMEM((cases, OWN), F32),
                pltpu.VMEM((cases, OWN), F32),
                pltpu.VMEM((2, NB, cases, B), F32),
                pltpu.SemaphoreType.DMA((2,)),
            ],
        )(
            interface_rows,
            coarse_inverse,
            resid,
            side_a,
            side_b,
            image,
            scaled,
            own,
            got_a,
            got_b,
            *pays,
        )
    )


def solution(mesh):
    placed = (
        P("rhs", "sub"),
        P("sub", None, None),
        P("sub", None),
        P("sub", None, None),
        P("sub", None),
        P("rhs", "sub"),
        P("sub"),
        P(),
    )
    return jax.shard_map(
        body,
        mesh=mesh,
        in_specs=placed,
        out_specs=(P("rhs", "sub"), P("rhs", "sub")),
        check_vma=False,
    )
```

time: 299 us -> 41 us (0.14)
  blocking collectives: 217 us -> 0 us
  matrix products: 39.2 us -> 0 us
  local copies, waits for them, and re-layouts: 15.8 us -> 0.03 us
  Pallas kernels: 0 us -> 11 us
  starting transfers between devices: 16.5 us -> 22.5 us
    psum x5 -> x0, blocking collectives: 212 us -> none  [the longest x2 118 us: precondition(): coarse = lax.psum(local_coarse, 'sub')]
    dot_general x20 -> x0, matrix products: 39.2 us -> none  [the longest x2 18.4 us: body(): strain = jnp.einsum('ikab,cikb->cia', blocks, picked, precision=highest)]
    pallas_call x0 -> x8, Pallas kernels: none -> 11 us  [the longest x1 3.09 us: body(): run(functools.partial(finish, cases=cases, ncoarse=ncoarse, n_pay=len(pay...]
    reshape x11 -> x0, local copies, waits for them, and re-layouts: 7.53 us -> none  [the longest x1 6.69 us: body(): blocks = stiffness_blocks.reshape(nblock, KNZ, B, B)]
    ppermute x8 -> x13, starting transfers between devices: 16.5 us -> 22.5 us  [the longest x6 13.6 us: swap(): lax.ppermute(x, 'sub', [(i, i ^ k) for i in range(count)])]
    gather x2 -> x0, local copies, waits for them, and re-layouts: 5.58 us -> none  [body(): picked = extended[:, block_columns]]
    all_gather x1 -> x0, blocking collectives: 5.52 us -> none  [body(): basis = lax.all_gather(corner_basis, 'rhs', axis=0, tiled=True)]
    ppermute x8 -> x13, waiting for transfers between devices: 5.74 us -> 6.4 us  [the longest x6 6.39 us: swap(): lax.ppermute(x, 'sub', [(i, i ^ k) for i in range(count)])]
  transfers between devices with their start and end apart: 8 -> 13, of which waited for: 3 -> 3; matrix products, arithmetic and copies ran while one was open for 3% -> 0% of each run, Pallas kernels for 0% -> 12%
where the time goes in v3:
time: 41 us; the launch traced here: 40.8 us
  starting transfers between devices  22.5 us (55%)
  Pallas kernels  11 us (27%)
  waiting for transfers between devices  6.4 us (16%)
  between operations  0.86 us (2%)
    ppermute x6, starting transfers between devices, swap(): lax.ppermute(x, 'sub', [(i, i ^ k) for i in range(count)])  13.6 us
    ppermute x6, waiting for transfers between devices, swap(): lax.ppermute(x, 'sub', [(i, i ^ k) for i in range(count)])  6.39 us
    ppermute x3, starting transfers between devices, across(): low = lax.ppermute(a, 'sub', [(i, i ^ 1) for i in range(count)])  3.89 us
    pallas_call x1, Pallas kernels, body(): run(functools.partial(finish, cases=cases, ncoarse=ncoarse, n_pay=len(pay...  3.09 us
    ppermute x1, starting transfers between devices, body(): lax.ppermute(corner_basis, 'rhs', [((i + k) % parts, i) for i in range(pa...  3 us
    pallas_call x1, Pallas kernels, body(): call(load_blocks, [packed, packed], 1, raw=(0,), scratch=[pltpu.VMEM((B *...  2.14 us
    ppermute x3, starting transfers between devices, across(): return (low, lax.ppermute(b, 'sub', inner + [(j, i) for i, j in inner]))  1.97 us
    pallas_call x1, Pallas kernels, body(): run(assemble, [dense, dense], 5, smem=(0,))  1.66 us
  transfers between devices with their start and end apart: 13, of which 3 were waited for; matrix products, arithmetic and copies ran while one was open for 0% of the time, Pallas kernels for 12%

profile of v3, /device:TPU:0, one launch (start us, length us, event | category | flops | bytes accessed | tf_op | source)
XLA Modules:
  0.0 40.8 jit_solution(13543419936297896893)
XLA Ops:
  0.6 0.0 copy-start.3
  0.6 0.0 copy-start.2
  0.7 0.0 copy-start.5
  0.7 0.0 copy-start.6
  0.7 0.0 copy-start
  0.7 3.0 %collective-permute-start = (f32[4,512]{1,0:T(4,128)}, f32[4,512]{1,0:T(4,128)S(1)}, u32[]{:S(2)}, u32[]{:S(2)}) collective-permute-start(f32[4,512]{1,0:T(4,128)} %rest_0_.1), channel_id=1, source_target_pairs={{1,0},{0,1},{3,2},{2,3},{5,4},{4,5},{7,6},{6,7},{9,8},{8,9},{11,10... | collective-permute-start | bytes 24584 | tf_op jit(solution)/shard_map/ppermute | solution.py:404
  3.7 0.0 copy-start.4
  3.7 2.1 %shard_map.95 = (bf16[256,4096]{1,0:T(8,128)(2,1)S(1)}, bf16[256,4096]{1,0:T(8,128)(2,1)S(1)}) custom-call(f32[27,8,4096]{2,1,0:T(8,128)} %bitcast.3), custom_call_target="tpu_custom_call" | custom-call | bytes 16777216 | tf_op jit(solution)/shard_map/pallas_call | solution.py:408
  5.8 0.0 collective-permute-done.rest_1_
  5.8 0.0 copy-done.3
  5.9 0.0 copy-done.2
  5.9 0.0 copy-done.5
  5.9 0.0 copy-done.6
  5.9 0.0 copy-done
  5.9 0.8 %shard_map.96 = (f32[32,512]{1,0:T(8,128)S(1)}, f32[72,256]{1,0:T(8,128)S(1)}, f32[72,256]{1,0:T(8,128)S(1)}) custom-call(s32[1,2,4]{2,1,0:T(2,128)S(1)} %copy-done.2, s32[1,8]{1,0:T(1,128)S(1)} %copy-done.6, f32[32,512]{1,0:T(8,128)S(1)} %copy-done, f32[1,512]{1,0:T(1,128)S(1)} %bitcast.2, bf16[256,4096]{1,0:T(8,128)(2,1)S(1)} %get-tuple-element.19.after_ref.wh_ref, ...), custom_call_target="tpu_custom_call" | custom-call | tf_op jit(solution)/shard_map/pallas_call | solution.py:420
  6.7 0.7 %collective-permute-start.2 = (f32[72,256]{1,0:T(8,128)S(1)}, f32[72,256]{1,0:T(8,128)S(1)}, u32[]{:S(2)}, u32[]{:S(2)}) collective-permute-start(f32[72,256]{1,0:T(8,128)S(1)} %get-tuple-element.22.b_ref), channel_id=1, source_target_pairs={{2,4},{6,8},{10,12},{14,16},{18,20},{22,24},{26,28},{4,2},{8,6},{1... | collective-permute-start | bytes 221192 | tf_op jit(solution)/shard_map/ppermute | solution.py:382
  7.4 3.1 %collective-permute-start.1 = (f32[72,256]{1,0:T(8,128)S(1)}, f32[72,256]{1,0:T(8,128)S(1)}, u32[]{:S(2)}, u32[]{:S(2)}) collective-permute-start(f32[72,256]{1,0:T(8,128)S(1)} %get-tuple-element.21.after_ref.a_ref), channel_id=1, source_target_pairs={{0,2},{2,0},{4,6},{6,4},{8,10},{10,8},{12,14},{14,12},{16,18},{18,... | collective-permute-start | bytes 221192 | tf_op jit(solution)/shard_map/ppermute | solution.py:380
  10.5 0.0 copy-done.4
  10.5 1.7 %shard_map.97 = (bf16[512,1024]{1,0:T(8,128)(2,1)S(1)}, bf16[512,1024]{1,0:T(8,128)(2,1)S(1)}) custom-call(s32[1,2,4]{2,1,0:T(2,128)S(1)} %copy-done.2, s32[8,27]{1,0:T(8,128)S(1)} %copy-done.4, bf16[256,4096]{1,0:T(8,128)(2,1)S(1)} %get-tuple-element.19.after_ref.wh_ref, bf16[256,4096]{1,0:T(8,128)(2,1)S(1)} %get-tuple-element.23.wl_ref, ...), custom_call_target="tpu_custom_call" | custom-call | tf_op jit(solution)/shard_map/pallas_call | solution.py:428
  12.2 0.0 collective-permute-done.2.gb_ref
  12.2 0.0 collective-permute-done.1.ga_ref
  12.2 1.2 %shard_map.98 = (f32[64,512]{1,0:T(8,128)S(1)}, f32[128,256]{1,0:T(8,128)S(1)}, f32[128,256]{1,0:T(8,128)S(1)}) custom-call(f32[72,256]{1,0:T(8,128)S(1)} %get-tuple-element.21.after_ref.a_ref, f32[72,256]{1,0:T(8,128)S(1)} %get-tuple-element.22.b_ref, f32[72,256]{1,0:T(8,128)S(1)} %collective-permute-done.1.ga_ref, ...), custom_call_target="tpu_custom_call" | custom-call | tf_op jit(solution)/shard_map/pallas_call | solution.py:435
  13.4 0.4 collective-permute-start.3
  13.8 0.7 %collective-permute-start.4 = (f32[128,256]{1,0:T(8,128)S(1)}, f32[128,256]{1,0:T(8,128)S(1)}, u32[]{:S(2)}, u32[]{:S(2)}) collective-permute-start(f32[128,256]{1,0:T(8,128)S(1)} %get-tuple-element.27.own_b_ref), channel_id=1, source_target_pairs={{2,4},{6,8},{10,12},{14,16},{18,20},{22,24},{26,28},{4,2},{8,6},{1... | collective-permute-start | bytes 393224 | tf_op jit(solution)/shard_map/ppermute | solution.py:382
  14.5 0.5 %shard_map.99.fixed_ref = f32[32,128]{1,0:T(8,128)S(1)} custom-call(f32[32,512]{1,0:T(8,128)S(1)} %get-tuple-element.20.resid_ref, f32[72,256]{1,0:T(8,128)S(1)} %get-tuple-element.21.after_ref.a_ref, f32[72,256]{1,0:T(8,128)S(1)} %get-tuple-element.22.b_ref, f32[64,512]{1,0:T(8,128)S(1)} %get-tuple-element.28.strain_ref), custom_call_target="tpu_custom_call" | custom-call | tf_op jit(solution)/shard_map/pallas_call | solution.py:439
  14.9 0.0 copy-start.1
  15.0 0.0 collective-permute-done.3.got_a_ref
  15.0 0.0 collective-permute-done.4.got_b_ref
  15.0 1.2 %shard_map.100 = (f32[64,512]{1,0:T(8,128)S(1)}, f32[64,512]{1,0:T(8,128)S(1)}, f32[64,512]{1,0:T(8,128)S(1)}, f32[32,256]{1,0:T(8,128)S(1)}) custom-call(f32[72,256]{1,0:T(8,128)S(1)} %get-tuple-element.21.after_ref.a_ref, f32[72,256]{1,0:T(8,128)S(1)} %get-tuple-element.22.b_ref, f32[72,256]{1,0:T(8,128)S(1)} %collective-permute-done.1.ga_ref, ...), custom_call_target="tpu_custom_call" | custom-call | tf_op jit(solution)/shard_map/pallas_call | solution.py:444
  16.1 8.5 %collective-permute-start.9 = (f32[32,256]{1,0:T(8,128)S(1)}, f32[32,256]{1,0:T(8,128)S(1)}, u32[]{:S(2)}, u32[]{:S(2)}) collective-permute-start(f32[32,256]{1,0:T(8,128)S(1)} %get-tuple-element.35), channel_id=1, source_target_pairs={{0,6},{2,4},{4,2},{6,0},{8,14},{10,12},{12,10},{14,8},{16,22},{18,... | collective-permute-start | bytes 98312 | tf_op jit(solution)/shard_map/ppermute | solution.py:363
  24.7 0.0 collective-permute-start.8
  24.7 0.2 collective-permute-start.7
  24.9 0.5 %shard_map.101 = (f32[64,512]{1,0:T(8,128)S(1)}, f32[64,256]{1,0:T(8,128)S(1)}, f32[64,256]{1,0:T(8,128)S(1)}) custom-call(f32[64,512]{1,0:T(8,128)S(1)} %get-tuple-element.30.scaled_ref, f32[64,512]{1,0:T(8,128)S(1)} %get-tuple-element.31.strain_ref, bf16[512,1024]{1,0:T(8,128)(2,1)S(1)} %get-tuple-element.24.high_ref, ...), custom_call_target="tpu_custom_call" | custom-call | tf_op jit(solution)/shard_map/pallas_call | solution.py:452
  25.3 0.4 collective-permute-start.5
  25.7 0.7 %collective-permute-start.6 = (f32[64,256]{1,0:T(8,128)S(1)}, f32[64,256]{1,0:T(8,128)S(1)}, u32[]{:S(2)}, u32[]{:S(2)}) collective-permute-start(f32[64,256]{1,0:T(8,128)S(1)} %get-tuple-element.34), channel_id=1, source_target_pairs={{2,4},{6,8},{10,12},{14,16},{18,20},{22,24},{26,28},{4,2},{8,6},{1... | collective-permute-start | bytes 196616 | tf_op jit(solution)/shard_map/ppermute | solution.py:382
  26.4 0.0 collective-permute-done.9
  26.4 2.2 %collective-permute-done.8 = f32[32,256]{1,0:T(8,128)S(1)} collective-permute-done((f32[32,256]{1,0:T(8,128)S(1)}, f32[32,256]{1,0:T(8,128)S(1)}, u32[]{:S(2)}, u32[]{:S(2)}) %collective-permute-start.8) | collective-permute-done | bytes 32800 | tf_op jit(solution)/shard_map/ppermute | solution.py:363
  28.6 0.0 collective-permute-done.7
  28.6 4.3 %collective-permute-start.12 = (f32[32,256]{1,0:T(8,128)S(1)}, f32[32,256]{1,0:T(8,128)S(1)}, u32[]{:S(2)}, u32[]{:S(2)}) collective-permute-start(f32[32,256]{1,0:T(8,128)S(1)} %add_add_fusion.rest_0_), channel_id=1, source_target_pairs={{0,24},{2,26},{4,28},{6,30},{8,16},{10,18},{12,20},{14,22},{16,8},... | collective-permute-start | bytes 98312 | tf_op jit(solution)/shard_map/ppermute | solution.py:363
  32.9 0.0 collective-permute-start.11
  32.9 0.6 %collective-permute-start.10 = (f32[32,256]{1,0:T(8,128)S(1)}, f32[32,256]{1,0:T(8,128)S(1)}, u32[]{:S(2)}, u32[]{:S(2)}) collective-permute-start(f32[32,256]{1,0:T(8,128)S(1)} %add_add_fusion.rest_0_), channel_id=1, source_target_pairs={{0,8},{2,10},{4,12},{6,14},{8,0},{10,2},{12,4},{14,6},{16,24},{18,... | collective-permute-start | bytes 98312 | tf_op jit(solution)/shard_map/ppermute | solution.py:363
  33.5 2.1 %collective-permute-done.12.rest_3_ = f32[32,256]{1,0:T(8,128)S(1)} collective-permute-done((f32[32,256]{1,0:T(8,128)S(1)}, f32[32,256]{1,0:T(8,128)S(1)}, u32[]{:S(2)}, u32[]{:S(2)}) %collective-permute-start.12) | collective-permute-done | bytes 32800 | tf_op jit(solution)/shard_map/ppermute | solution.py:363
  35.7 2.0 %collective-permute-done.11.rest_2_ = f32[32,256]{1,0:T(8,128)S(1)} collective-permute-done((f32[32,256]{1,0:T(8,128)S(1)}, f32[32,256]{1,0:T(8,128)S(1)}, u32[]{:S(2)}, u32[]{:S(2)}) %collective-permute-start.11) | collective-permute-done | bytes 32800 | tf_op jit(solution)/shard_map/ppermute | solution.py:363
  37.7 0.0 collective-permute-done.10.rest_1_
  37.7 0.0 collective-permute-done.5.got_a_ref
  37.7 0.0 collective-permute-done.6.got_b_ref
  37.7 0.0 copy-done.1
  37.7 3.1 %shard_map.102 = (f32[32,512]{1,0:T(8,128)}, f32[32,512]{1,0:T(8,128)}) custom-call(s32[1,2,4]{2,1,0:T(2,128)S(1)} %copy-done.2, f32[32,32]{1,0:T(8,128)S(1)} %copy-done.1, f32[32,512]{1,0:T(8,128)S(1)} %get-tuple-element.20.resid_ref, f32[72,256]{1,0:T(8,128)S(1)} %get-tuple-element.21.after_ref.a_ref, f32[72,256]{1,0:T(8,128)S(1)} %get-tuple-element.22.b_ref, ...), custom_call_target="tpu_custom_call" | custom-call | tf_op jit(solution)/shard_map/pallas_call | solution.py:457
  (1 shorter events, 0.0 us)
Async XLA Ops:
  0.6 5.2 %copy-start.3 = (f32[4,512]{1,0:T(4,128)S(1)}, f32[4,512]{1,0:T(4,128)}, u32[]{:S(2)}) copy-start(f32[4,512]{1,0:T(4,128)} %rest_0_.1) | copy-start | bytes 24580
  0.6 5.2 %copy-start.2 = (s32[1,2,4]{2,1,0:T(2,128)S(1)}, s32[1,2,4]{2,1,0:T(2,128)}, u32[]{:S(2)}) copy-start(s32[1,2,4]{2,1,0:T(2,128)} %rows_ref.5) | copy-start | bytes 100
  0.7 5.2 %copy-start.5 = (f32[512]{0:T(512)S(1)}, f32[512]{0:T(512)}, u32[]{:S(2)}) copy-start(f32[512]{0:T(512)} %param.14) | copy-start | bytes 6148
  0.7 5.2 %copy-start.6 = (s32[1,8]{1,0:T(1,128)S(1)}, s32[1,8]{1,0:T(1,128)}, u32[]{:S(2)}) copy-start(s32[1,8]{1,0:T(1,128)} %owner_ref.1) | copy-start | bytes 100
  0.7 5.2 %copy-start = (f32[32,512]{1,0:T(8,128)S(1)}, f32[32,512]{1,0:T(8,128)}, u32[]{:S(2)}) copy-start(f32[32,512]{1,0:T(8,128)} %right_ref.1) | copy-start | bytes 196612
  0.7 5.2 %collective-permute-start = (f32[4,512]{1,0:T(4,128)}, f32[4,512]{1,0:T(4,128)S(1)}, u32[]{:S(2)}, u32[]{:S(2)}) collective-permute-start(f32[4,512]{1,0:T(4,128)} %rest_0_.1), channel_id=1, source_target_pairs={{1,0},{0,1},{3,2},{2,3},{5,4},{4,5},{7,6},{6,7},{9,8},{8,9},{11,10... | collective-permute-start | bytes 24584 | tf_op jit(solution)/shard_map/ppermute | solution.py:404
  3.7 6.8 %copy-start.4 = (s32[8,27]{1,0:T(8,128)S(1)}, s32[8,27]{1,0:T(8,128)}, u32[]{:S(2)}) copy-start(s32[8,27]{1,0:T(8,128)} %columns_ref.1) | copy-start | bytes 2596
  6.7 5.5 %collective-permute-start.2 = (f32[72,256]{1,0:T(8,128)S(1)}, f32[72,256]{1,0:T(8,128)S(1)}, u32[]{:S(2)}, u32[]{:S(2)}) collective-permute-start(f32[72,256]{1,0:T(8,128)S(1)} %get-tuple-element.22.b_ref), channel_id=1, source_target_pairs={{2,4},{6,8},{10,12},{14,16},{18,20},{22,24},{26,28},{4,2},{8,6},{1... | collective-permute-start | bytes 221192 | tf_op jit(solution)/shard_map/ppermute | solution.py:382
  7.4 4.8 %collective-permute-start.1 = (f32[72,256]{1,0:T(8,128)S(1)}, f32[72,256]{1,0:T(8,128)S(1)}, u32[]{:S(2)}, u32[]{:S(2)}) collective-permute-start(f32[72,256]{1,0:T(8,128)S(1)} %get-tuple-element.21.after_ref.a_ref), channel_id=1, source_target_pairs={{0,2},{2,0},{4,6},{6,4},{8,10},{10,8},{12,14},{14,12},{16,18},{18,... | collective-permute-start | bytes 221192 | tf_op jit(solution)/shard_map/ppermute | solution.py:380
  13.4 1.5 %collective-permute-start.3 = (f32[128,256]{1,0:T(8,128)S(1)}, f32[128,256]{1,0:T(8,128)S(1)}, u32[]{:S(2)}, u32[]{:S(2)}) collective-permute-start(f32[128,256]{1,0:T(8,128)S(1)} %get-tuple-element.26.own_a_ref), channel_id=1, source_target_pairs={{0,2},{2,0},{4,6},{6,4},{8,10},{10,8},{12,14},{14,12},{16,18},{18,... | collective-permute-start | bytes 393224 | tf_op jit(solution)/shard_map/ppermute | solution.py:380
  13.8 1.2 %collective-permute-start.4 = (f32[128,256]{1,0:T(8,128)S(1)}, f32[128,256]{1,0:T(8,128)S(1)}, u32[]{:S(2)}, u32[]{:S(2)}) collective-permute-start(f32[128,256]{1,0:T(8,128)S(1)} %get-tuple-element.27.own_b_ref), channel_id=1, source_target_pairs={{2,4},{6,8},{10,12},{14,16},{18,20},{22,24},{26,28},{4,2},{8,6},{1... | collective-permute-start | bytes 393224 | tf_op jit(solution)/shard_map/ppermute | solution.py:382
  14.9 22.8 %copy-start.1 = (f32[32,32]{1,0:T(8,128)S(1)}, f32[32,32]{1,0:T(8,128)}, u32[]{:S(2)}) copy-start(f32[32,32]{1,0:T(8,128)} %inverse_ref.1) | copy-start | bytes 12292
  16.1 10.2 %collective-permute-start.9 = (f32[32,256]{1,0:T(8,128)S(1)}, f32[32,256]{1,0:T(8,128)S(1)}, u32[]{:S(2)}, u32[]{:S(2)}) collective-permute-start(f32[32,256]{1,0:T(8,128)S(1)} %get-tuple-element.35), channel_id=1, source_target_pairs={{0,6},{2,4},{4,2},{6,0},{8,14},{10,12},{12,10},{14,8},{16,22},{18,... | collective-permute-start | bytes 98312 | tf_op jit(solution)/shard_map/ppermute | solution.py:363
  24.7 3.9 %collective-permute-start.8 = (f32[32,256]{1,0:T(8,128)S(1)}, f32[32,256]{1,0:T(8,128)S(1)}, u32[]{:S(2)}, u32[]{:S(2)}) collective-permute-start(f32[32,256]{1,0:T(8,128)S(1)} %get-tuple-element.35), channel_id=1, source_target_pairs={{0,4},{2,6},{4,0},{6,2},{8,12},{10,14},{12,8},{14,10},{16,20},{18,... | collective-permute-start | bytes 98312 | tf_op jit(solution)/shard_map/ppermute | solution.py:363
  24.7 3.9 %collective-permute-start.7 = (f32[32,256]{1,0:T(8,128)S(1)}, f32[32,256]{1,0:T(8,128)S(1)}, u32[]{:S(2)}, u32[]{:S(2)}) collective-permute-start(f32[32,256]{1,0:T(8,128)S(1)} %get-tuple-element.35), channel_id=1, source_target_pairs={{0,2},{2,0},{4,6},{6,4},{8,10},{10,8},{12,14},{14,12},{16,18},{18,... | collective-permute-start | bytes 98312 | tf_op jit(solution)/shard_map/ppermute | solution.py:363
  25.3 12.4 %collective-permute-start.5 = (f32[64,256]{1,0:T(8,128)S(1)}, f32[64,256]{1,0:T(8,128)S(1)}, u32[]{:S(2)}, u32[]{:S(2)}) collective-permute-start(f32[64,256]{1,0:T(8,128)S(1)} %get-tuple-element.33), channel_id=1, source_target_pairs={{0,2},{2,0},{4,6},{6,4},{8,10},{10,8},{12,14},{14,12},{16,18},{18,... | collective-permute-start | bytes 196616 | tf_op jit(solution)/shard_map/ppermute | solution.py:380
  25.7 12.0 %collective-permute-start.6 = (f32[64,256]{1,0:T(8,128)S(1)}, f32[64,256]{1,0:T(8,128)S(1)}, u32[]{:S(2)}, u32[]{:S(2)}) collective-permute-start(f32[64,256]{1,0:T(8,128)S(1)} %get-tuple-element.34), channel_id=1, source_target_pairs={{2,4},{6,8},{10,12},{14,16},{18,20},{22,24},{26,28},{4,2},{8,6},{1... | collective-permute-start | bytes 196616 | tf_op jit(solution)/shard_map/ppermute | solution.py:382
  28.6 7.1 %collective-permute-start.12 = (f32[32,256]{1,0:T(8,128)S(1)}, f32[32,256]{1,0:T(8,128)S(1)}, u32[]{:S(2)}, u32[]{:S(2)}) collective-permute-start(f32[32,256]{1,0:T(8,128)S(1)} %add_add_fusion.rest_0_), channel_id=1, source_target_pairs={{0,24},{2,26},{4,28},{6,30},{8,16},{10,18},{12,20},{14,22},{16,8},... | collective-permute-start | bytes 98312 | tf_op jit(solution)/shard_map/ppermute | solution.py:363
  32.9 4.8 %collective-permute-start.11 = (f32[32,256]{1,0:T(8,128)S(1)}, f32[32,256]{1,0:T(8,128)S(1)}, u32[]{:S(2)}, u32[]{:S(2)}) collective-permute-start(f32[32,256]{1,0:T(8,128)S(1)} %add_add_fusion.rest_0_), channel_id=1, source_target_pairs={{0,16},{2,18},{4,20},{6,22},{8,24},{10,26},{12,28},{14,30},{16,0},... | collective-permute-start | bytes 98312 | tf_op jit(solution)/shard_map/ppermute | solution.py:363
  32.9 4.8 %collective-permute-start.10 = (f32[32,256]{1,0:T(8,128)S(1)}, f32[32,256]{1,0:T(8,128)S(1)}, u32[]{:S(2)}, u32[]{:S(2)}) collective-permute-start(f32[32,256]{1,0:T(8,128)S(1)} %add_add_fusion.rest_0_), channel_id=1, source_target_pairs={{0,8},{2,10},{4,12},{6,14},{8,0},{10,2},{12,4},{14,6},{16,24},{18,... | collective-permute-start | bytes 98312 | tf_op jit(solution)/shard_map/ppermute | solution.py:363

commit v4 on v3

--- a/solution.py
+++ b/solution.py
@@ -171,7 +171,9 @@
 
 def first_apply(a_ref, b_ref, ga_ref, gb_ref, high_ref, low_ref, strain_ref, send_a_ref, send_b_ref):
     live = strain_ref.shape[0]
-    field = jnp.concatenate([ref[:live, :] for ref in (a_ref, b_ref, ga_ref, gb_ref)], axis=1)
+    field = jnp.concatenate(
+        [a_ref[:live, :], b_ref[:live, :], ga_ref[:live, :], inside() * gb_ref[:live, :]], axis=1
+    )
     strain = times(field, high_ref[...], low_ref[...], NT)
     strain_ref[...] = strain
     back = times(strain, high_ref[...], low_ref[...], NN)
@@ -218,17 +220,19 @@
     ncoarse,
 ):
     live = cases + ncoarse
+    inner = inside()
     image = jnp.concatenate(
         [
             own_a_ref[:live, :] + got_a_ref[live:, :],
-            own_b_ref[:live, :] + got_b_ref[live:, :],
+            own_b_ref[:live, :] + inner * got_b_ref[live:, :],
             own_a_ref[live:, :] + got_a_ref[:live, :],
             own_b_ref[live:, :] + got_b_ref[:live, :],
         ],
         axis=1,
     )
+    end = slice(live, live + 1)
     scale = jnp.concatenate(
-        [ref[live : live + 1, :] for ref in (a_ref, b_ref, ga_ref, gb_ref)], axis=1
+        [a_ref[end, :], b_ref[end, :], ga_ref[end, :], inner * gb_ref[end, :]], axis=1
     )
     field = scale * image
     strain = times(field, high_ref[...], low_ref[...], NT)
@@ -329,7 +333,7 @@
     start = jnp.concatenate([a_ref[:live, :], b_ref[:live, :]], axis=1)
     scaled = scaled_ref[...]
     image = image_ref[...]
-    image2 = own_ref[...] + jnp.concatenate([got_a_ref[...], got_b_ref[...]], axis=1)
+    image2 = own_ref[...] + jnp.concatenate([got_a_ref[...], inside() * got_b_ref[...]], axis=1)
     field = (
         upper * start[:cases]
         - lower * scaled[:cases]
@@ -367,8 +371,9 @@
     rounds = []
     base = 1
     while base < count:
+        turn = 1 if base > 1 else 0
         if base * 4 <= count:
-            rounds.append((base, 2 * base, 3 * base))
+            rounds.append((base, 2 * base + turn, 3 * base + turn))
             base *= 4
         else:
             rounds.append((base,))
@@ -376,10 +381,18 @@
     return rounds
 
 
-def across(a, b, count):
+def across(a, b, count, parts):
     low = lax.ppermute(a, "sub", [(i, i ^ 1) for i in range(count)])
     inner = [(i, i + 1) for i in range(1, count - 1, 2)]
-    return low, lax.ppermute(b, "sub", inner + [(j, i) for i, j in inner])
+    pairs = [(i * parts + x, j * parts + x) for i, j in inner for x in range(parts)]
+    ends = [(i * parts + x, i * parts + x + 1) for i in (0, count - 1) for x in range(0, parts - 1, 2)]
+    pairs += ends
+    return low, lax.ppermute(b, ("sub", "rhs"), pairs + [(j, i) for i, j in pairs])
+
+
+def inside():
+    place = lax.axis_index("sub")
+    return jnp.where((place == 0) | (place == lax.axis_size("sub") - 1), 0.0, 1.0)
 
 
 def body(
@@ -428,14 +441,14 @@
     high, low = run(assemble, [dense, dense], 5, smem=(0,))(
         interface_rows, block_columns, wh, wl, side_a
     )
-    ghost_a, ghost_b = across(side_a, side_b, count)
+    ghost_a, ghost_b = across(side_a, side_b, count, parts)
     ends = (side_a, side_b, ghost_a, ghost_b)
 
     rows = max(cases, ncoarse)
     strain, own_a, own_b = run(
         first_apply, [shape(live, ROWS), shape(2 * live, EDGE), shape(2 * live, EDGE)], 6
     )(*ends, high, low)
-    got_a, got_b = across(own_a, own_b, count)
+    got_a, got_b = across(own_a, own_b, count, parts)
     (fixed,) = run(
         functools.partial(first_sums, cases=cases, ncoarse=ncoarse),
         [shape(rows, lanes_for(3 * ncoarse + 2))],
@@ -452,7 +465,7 @@
     own, back_a, back_b = run(
         second_image, [shape(live, OWN), shape(live, EDGE), shape(live, EDGE)], 4
     )(scaled, strain, high, low)
-    got_a, got_b = across(back_a, back_b, count)
+    got_a, got_b = across(back_a, back_b, count, parts)
     return tuple(
         run(
             functools.partial(finish, cases=cases, ncoarse=ncoarse, n_pay=len(pays)),

time: 41 us -> 35.2 us (0.86)
  starting transfers between devices: 22.5 us -> 15.3 us
  waiting for transfers between devices: 6.4 us -> 7.74 us
    ppermute x6, starting transfers between devices: 13.6 us -> 6.72 us  [swap(): lax.ppermute(x, 'sub', [(i, i ^ k) for i in range(count)])]
    ppermute x3, waiting for transfers between devices: 0.01 us -> 3.62 us  [across(): lax.ppermute(b, ('sub', 'rhs'), pairs + [(j, i) for i, j in pairs])]
    ppermute x3, starting transfers between devices: 3.89 us -> 0.6 us  [across(): low = lax.ppermute(a, 'sub', [(i, i ^ 1) for i in range(count)])]
    ppermute x3, starting transfers between devices: 1.97 us -> 5.02 us  [across(): lax.ppermute(b, ('sub', 'rhs'), pairs + [(j, i) for i, j in pairs])]
    ppermute x6, waiting for transfers between devices: 6.39 us -> 4.11 us  [swap(): lax.ppermute(x, 'sub', [(i, i ^ k) for i in range(count)])]
  transfers between devices with their start and end apart: 13 -> 13, of which waited for: 3 -> 6; matrix products, arithmetic and copies ran while one was open for 0% -> 0% of each run, Pallas kernels for 12% -> 14%
where the time goes in v4:
time: 35.2 us; the launch traced here: 34.9 us
  starting transfers between devices  15.3 us (43%)
  Pallas kernels  11 us (31%)
  waiting for transfers between devices  7.74 us (22%)
  between operations  0.8 us (2%)
    ppermute x6, starting transfers between devices, swap(): lax.ppermute(x, 'sub', [(i, i ^ k) for i in range(count)])  6.72 us
    ppermute x3, starting transfers between devices, across(): lax.ppermute(b, ('sub', 'rhs'), pairs + [(j, i) for i, j in pairs])  5.02 us
    ppermute x6, waiting for transfers between devices, swap(): lax.ppermute(x, 'sub', [(i, i ^ k) for i in range(count)])  4.11 us
    ppermute x3, waiting for transfers between devices, across(): lax.ppermute(b, ('sub', 'rhs'), pairs + [(j, i) for i, j in pairs])  3.62 us
    pallas_call x1, Pallas kernels, body(): run(functools.partial(finish, cases=cases, ncoarse=ncoarse, n_pay=len(pay...  3.09 us
    ppermute x1, starting transfers between devices, body(): lax.ppermute(corner_basis, 'rhs', [((i + k) % parts, i) for i in range(pa...  3 us
    pallas_call x1, Pallas kernels, body(): call(load_blocks, [packed, packed], 1, raw=(0,), scratch=[pltpu.VMEM((B *...  2.14 us
    pallas_call x1, Pallas kernels, body(): run(assemble, [dense, dense], 5, smem=(0,))  1.66 us
  transfers between devices with their start and end apart: 13, of which 6 were waited for; matrix products, arithmetic and copies ran while one was open for 0% of the time, Pallas kernels for 14%

profile of v4, /device:TPU:0, one launch (start us, length us, event | category | flops | bytes accessed | tf_op | source)
XLA Modules:
  0.0 34.9 jit_solution(6705972729859121090)
XLA Ops:
  0.6 0.0 copy-start.3
  0.6 0.0 copy-start.2
  0.7 0.0 copy-start.5
  0.7 0.0 copy-start.6
  0.7 0.0 copy-start
  0.7 3.0 %collective-permute-start = (f32[4,512]{1,0:T(4,128)}, f32[4,512]{1,0:T(4,128)S(1)}, u32[]{:S(2)}, u32[]{:S(2)}) collective-permute-start(f32[4,512]{1,0:T(4,128)} %rest_0_.1), channel_id=1, source_target_pairs={{1,0},{0,1},{3,2},{2,3},{5,4},{4,5},{7,6},{6,7},{9,8},{8,9},{11,10... | collective-permute-start | bytes 24584 | tf_op jit(solution)/shard_map/ppermute | solution.py:417
  3.7 0.0 copy-start.4
  3.7 2.1 %shard_map.95 = (bf16[256,4096]{1,0:T(8,128)(2,1)S(1)}, bf16[256,4096]{1,0:T(8,128)(2,1)S(1)}) custom-call(f32[27,8,4096]{2,1,0:T(8,128)} %bitcast.3), custom_call_target="tpu_custom_call" | custom-call | bytes 16777216 | tf_op jit(solution)/shard_map/pallas_call | solution.py:421
  5.8 0.0 collective-permute-done.rest_1_
  5.8 0.0 copy-done.3
  5.9 0.0 copy-done.2
  5.9 0.0 copy-done.5
  5.9 0.0 copy-done.6
  5.9 0.0 copy-done
  5.9 0.8 %shard_map.96 = (f32[32,512]{1,0:T(8,128)S(1)}, f32[72,256]{1,0:T(8,128)S(1)}, f32[72,256]{1,0:T(8,128)S(1)}) custom-call(s32[1,2,4]{2,1,0:T(2,128)S(1)} %copy-done.2, s32[1,8]{1,0:T(1,128)S(1)} %copy-done.6, f32[32,512]{1,0:T(8,128)S(1)} %copy-done, f32[1,512]{1,0:T(1,128)S(1)} %bitcast.2, bf16[256,4096]{1,0:T(8,128)(2,1)S(1)} %get-tuple-element.19.after_ref.wh_ref, ...), custom_call_target="tpu_custom_call" | custom-call | tf_op jit(solution)/shard_map/pallas_call | solution.py:433
  6.7 1.8 %collective-permute-start.2 = (f32[72,256]{1,0:T(8,128)S(1)}, f32[72,256]{1,0:T(8,128)S(1)}, u32[]{:S(2)}, u32[]{:S(2)}) collective-permute-start(f32[72,256]{1,0:T(8,128)S(1)} %get-tuple-element.22.b_ref), channel_id=1, source_target_pairs={{2,4},{3,5},{6,8},{7,9},{10,12},{11,13},{14,16},{15,17},{18,20},{1... | collective-permute-start | bytes 221192 | tf_op jit(solution)/shard_map/ppermute | solution.py:390
  8.5 0.1 collective-permute-start.1
  8.6 0.0 copy-done.4
  8.6 1.7 %shard_map.97 = (bf16[512,1024]{1,0:T(8,128)(2,1)S(1)}, bf16[512,1024]{1,0:T(8,128)(2,1)S(1)}) custom-call(s32[1,2,4]{2,1,0:T(2,128)S(1)} %copy-done.2, s32[8,27]{1,0:T(8,128)S(1)} %copy-done.4, bf16[256,4096]{1,0:T(8,128)(2,1)S(1)} %get-tuple-element.19.after_ref.wh_ref, bf16[256,4096]{1,0:T(8,128)(2,1)S(1)} %get-tuple-element.23.wl_ref, ...), custom_call_target="tpu_custom_call" | custom-call | tf_op jit(solution)/shard_map/pallas_call | solution.py:441
  10.3 0.9 %collective-permute-done.2.gb_ref = f32[72,256]{1,0:T(8,128)S(1)} collective-permute-done((f32[72,256]{1,0:T(8,128)S(1)}, f32[72,256]{1,0:T(8,128)S(1)}, u32[]{:S(2)}, u32[]{:S(2)}) %collective-permute-start.2) | collective-permute-done | bytes 73760 | tf_op jit(solution)/shard_map/ppermute | solution.py:390
  11.1 0.0 collective-permute-done.1.ga_ref
  11.1 1.2 %shard_map.98 = (f32[64,512]{1,0:T(8,128)S(1)}, f32[128,256]{1,0:T(8,128)S(1)}, f32[128,256]{1,0:T(8,128)S(1)}) custom-call(f32[72,256]{1,0:T(8,128)S(1)} %get-tuple-element.21.after_ref.a_ref, f32[72,256]{1,0:T(8,128)S(1)} %get-tuple-element.22.b_ref, f32[72,256]{1,0:T(8,128)S(1)} %collective-permute-done.1.ga_ref, ...), custom_call_target="tpu_custom_call" | custom-call | tf_op jit(solution)/shard_map/pallas_call | solution.py:448
  12.3 0.1 collective-permute-start.3
  12.4 1.8 %collective-permute-start.4 = (f32[128,256]{1,0:T(8,128)S(1)}, f32[128,256]{1,0:T(8,128)S(1)}, u32[]{:S(2)}, u32[]{:S(2)}) collective-permute-start(f32[128,256]{1,0:T(8,128)S(1)} %get-tuple-element.27.own_b_ref), channel_id=1, source_target_pairs={{2,4},{3,5},{6,8},{7,9},{10,12},{11,13},{14,16},{15,17},{18,20},{1... | collective-permute-start | bytes 393224 | tf_op jit(solution)/shard_map/ppermute | solution.py:390
  14.2 0.5 %shard_map.99.fixed_ref = f32[32,128]{1,0:T(8,128)S(1)} custom-call(f32[32,512]{1,0:T(8,128)S(1)} %get-tuple-element.20.resid_ref, f32[72,256]{1,0:T(8,128)S(1)} %get-tuple-element.21.after_ref.a_ref, f32[72,256]{1,0:T(8,128)S(1)} %get-tuple-element.22.b_ref, f32[64,512]{1,0:T(8,128)S(1)} %get-tuple-element.28.strain_ref), custom_call_target="tpu_custom_call" | custom-call | tf_op jit(solution)/shard_map/pallas_call | solution.py:452
  14.7 0.0 copy-start.1
  14.7 0.0 collective-permute-done.3.got_a_ref
  14.7 2.8 %collective-permute-done.4.got_b_ref = f32[128,256]{1,0:T(8,128)S(1)} collective-permute-done((f32[128,256]{1,0:T(8,128)S(1)}, f32[128,256]{1,0:T(8,128)S(1)}, u32[]{:S(2)}, u32[]{:S(2)}) %collective-permute-start.4) | collective-permute-done | bytes 131104 | tf_op jit(solution)/shard_map/ppermute | solution.py:390
  17.5 1.1 %shard_map.100 = (f32[64,512]{1,0:T(8,128)S(1)}, f32[64,512]{1,0:T(8,128)S(1)}, f32[64,512]{1,0:T(8,128)S(1)}, f32[32,256]{1,0:T(8,128)S(1)}) custom-call(f32[72,256]{1,0:T(8,128)S(1)} %get-tuple-element.21.after_ref.a_ref, f32[72,256]{1,0:T(8,128)S(1)} %get-tuple-element.22.b_ref, f32[72,256]{1,0:T(8,128)S(1)} %collective-permute-done.1.ga_ref, ...), custom_call_target="tpu_custom_call" | custom-call | tf_op jit(solution)/shard_map/pallas_call | solution.py:457
  18.6 2.4 %collective-permute-start.9 = (f32[32,256]{1,0:T(8,128)S(1)}, f32[32,256]{1,0:T(8,128)S(1)}, u32[]{:S(2)}, u32[]{:S(2)}) collective-permute-start(f32[32,256]{1,0:T(8,128)S(1)} %get-tuple-element.35), channel_id=1, source_target_pairs={{0,6},{2,4},{4,2},{6,0},{8,14},{10,12},{12,10},{14,8},{16,22},{18,... | collective-permute-start | bytes 98312 | tf_op jit(solution)/shard_map/ppermute | solution.py:367
  21.0 0.0 collective-permute-start.8
  21.0 0.2 collective-permute-start.7
  21.2 0.5 %shard_map.101 = (f32[64,512]{1,0:T(8,128)S(1)}, f32[64,256]{1,0:T(8,128)S(1)}, f32[64,256]{1,0:T(8,128)S(1)}) custom-call(f32[64,512]{1,0:T(8,128)S(1)} %get-tuple-element.30.scaled_ref, f32[64,512]{1,0:T(8,128)S(1)} %get-tuple-element.31.strain_ref, bf16[512,1024]{1,0:T(8,128)(2,1)S(1)} %get-tuple-element.24.high_ref, ...), custom_call_target="tpu_custom_call" | custom-call | tf_op jit(solution)/shard_map/pallas_call | solution.py:465
  21.6 0.4 %collective-permute-start.5 = (f32[64,256]{1,0:T(8,128)S(1)}, f32[64,256]{1,0:T(8,128)S(1)}, u32[]{:S(2)}, u32[]{:S(2)}) collective-permute-start(f32[64,256]{1,0:T(8,128)S(1)} %get-tuple-element.33), channel_id=1, source_target_pairs={{0,2},{2,0},{4,6},{6,4},{8,10},{10,8},{12,14},{14,12},{16,18},{18,... | collective-permute-start | bytes 196616 | tf_op jit(solution)/shard_map/ppermute | solution.py:385
  22.0 1.5 %collective-permute-start.6 = (f32[64,256]{1,0:T(8,128)S(1)}, f32[64,256]{1,0:T(8,128)S(1)}, u32[]{:S(2)}, u32[]{:S(2)}) collective-permute-start(f32[64,256]{1,0:T(8,128)S(1)} %get-tuple-element.34), channel_id=1, source_target_pairs={{2,4},{3,5},{6,8},{7,9},{10,12},{11,13},{14,16},{15,17},{18,20},{1... | collective-permute-start | bytes 196616 | tf_op jit(solution)/shard_map/ppermute | solution.py:390
  23.5 0.0 collective-permute-done.9
  23.5 1.4 %collective-permute-done.8 = f32[32,256]{1,0:T(8,128)S(1)} collective-permute-done((f32[32,256]{1,0:T(8,128)S(1)}, f32[32,256]{1,0:T(8,128)S(1)}, u32[]{:S(2)}, u32[]{:S(2)}) %collective-permute-start.8) | collective-permute-done | bytes 32800 | tf_op jit(solution)/shard_map/ppermute | solution.py:367
  24.9 0.0 collective-permute-done.7
  24.9 2.2 %collective-permute-start.12 = (f32[32,256]{1,0:T(8,128)S(1)}, f32[32,256]{1,0:T(8,128)S(1)}, u32[]{:S(2)}, u32[]{:S(2)}) collective-permute-start(f32[32,256]{1,0:T(8,128)S(1)} %add_add_fusion.rest_0_), channel_id=1, source_target_pairs={{0,26},{2,24},{4,30},{6,28},{8,18},{10,16},{12,22},{14,20},{16,10}... | collective-permute-start | bytes 98312 | tf_op jit(solution)/shard_map/ppermute | solution.py:367
  27.1 0.6 %collective-permute-start.11 = (f32[32,256]{1,0:T(8,128)S(1)}, f32[32,256]{1,0:T(8,128)S(1)}, u32[]{:S(2)}, u32[]{:S(2)}) collective-permute-start(f32[32,256]{1,0:T(8,128)S(1)} %add_add_fusion.rest_0_), channel_id=1, source_target_pairs={{0,18},{2,16},{4,22},{6,20},{8,26},{10,24},{12,30},{14,28},{16,2},... | collective-permute-start | bytes 98312 | tf_op jit(solution)/shard_map/ppermute | solution.py:367
  27.7 1.3 %collective-permute-start.10 = (f32[32,256]{1,0:T(8,128)S(1)}, f32[32,256]{1,0:T(8,128)S(1)}, u32[]{:S(2)}, u32[]{:S(2)}) collective-permute-start(f32[32,256]{1,0:T(8,128)S(1)} %add_add_fusion.rest_0_), channel_id=1, source_target_pairs={{0,8},{2,10},{4,12},{6,14},{8,0},{10,2},{12,4},{14,6},{16,24},{18,... | collective-permute-start | bytes 98312 | tf_op jit(solution)/shard_map/ppermute | solution.py:367
  29.1 1.3 %collective-permute-done.12.rest_3_ = f32[32,256]{1,0:T(8,128)S(1)} collective-permute-done((f32[32,256]{1,0:T(8,128)S(1)}, f32[32,256]{1,0:T(8,128)S(1)}, u32[]{:S(2)}, u32[]{:S(2)}) %collective-permute-start.12) | collective-permute-done | bytes 32800 | tf_op jit(solution)/shard_map/ppermute | solution.py:367
  30.4 1.1 %collective-permute-done.11.rest_2_ = f32[32,256]{1,0:T(8,128)S(1)} collective-permute-done((f32[32,256]{1,0:T(8,128)S(1)}, f32[32,256]{1,0:T(8,128)S(1)}, u32[]{:S(2)}, u32[]{:S(2)}) %collective-permute-start.11) | collective-permute-done | bytes 32800 | tf_op jit(solution)/shard_map/ppermute | solution.py:367
  31.4 0.4 %collective-permute-done.10.rest_1_ = f32[32,256]{1,0:T(8,128)S(1)} collective-permute-done((f32[32,256]{1,0:T(8,128)S(1)}, f32[32,256]{1,0:T(8,128)S(1)}, u32[]{:S(2)}, u32[]{:S(2)}) %collective-permute-start.10) | collective-permute-done | bytes 32800 | tf_op jit(solution)/shard_map/ppermute | solution.py:367
  31.8 0.0 collective-permute-done.5.got_a_ref
  31.8 0.0 collective-permute-done.6.got_b_ref
  31.8 0.0 copy-done.1
  31.8 3.1 %shard_map.102 = (f32[32,512]{1,0:T(8,128)}, f32[32,512]{1,0:T(8,128)}) custom-call(s32[1,2,4]{2,1,0:T(2,128)S(1)} %copy-done.2, f32[32,32]{1,0:T(8,128)S(1)} %copy-done.1, f32[32,512]{1,0:T(8,128)S(1)} %get-tuple-element.20.resid_ref, f32[72,256]{1,0:T(8,128)S(1)} %get-tuple-element.21.after_ref.a_ref, f32[72,256]{1,0:T(8,128)S(1)} %get-tuple-element.22.b_ref, ...), custom_call_target="tpu_custom_call" | custom-call | tf_op jit(solution)/shard_map/pallas_call | solution.py:470
  (1 shorter events, 0.0 us)
Async XLA Ops:
  0.6 5.2 %copy-start.3 = (f32[4,512]{1,0:T(4,128)S(1)}, f32[4,512]{1,0:T(4,128)}, u32[]{:S(2)}) copy-start(f32[4,512]{1,0:T(4,128)} %rest_0_.1) | copy-start | bytes 24580
  0.6 5.2 %copy-start.2 = (s32[1,2,4]{2,1,0:T(2,128)S(1)}, s32[1,2,4]{2,1,0:T(2,128)}, u32[]{:S(2)}) copy-start(s32[1,2,4]{2,1,0:T(2,128)} %rows_ref.5) | copy-start | bytes 100
  0.7 5.2 %copy-start.5 = (f32[512]{0:T(512)S(1)}, f32[512]{0:T(512)}, u32[]{:S(2)}) copy-start(f32[512]{0:T(512)} %param.14) | copy-start | bytes 6148
  0.7 5.2 %copy-start.6 = (s32[1,8]{1,0:T(1,128)S(1)}, s32[1,8]{1,0:T(1,128)}, u32[]{:S(2)}) copy-start(s32[1,8]{1,0:T(1,128)} %owner_ref.1) | copy-start | bytes 100
  0.7 5.2 %copy-start = (f32[32,512]{1,0:T(8,128)S(1)}, f32[32,512]{1,0:T(8,128)}, u32[]{:S(2)}) copy-start(f32[32,512]{1,0:T(8,128)} %right_ref.1) | copy-start | bytes 196612
  0.7 5.2 %collective-permute-start = (f32[4,512]{1,0:T(4,128)}, f32[4,512]{1,0:T(4,128)S(1)}, u32[]{:S(2)}, u32[]{:S(2)}) collective-permute-start(f32[4,512]{1,0:T(4,128)} %rest_0_.1), channel_id=1, source_target_pairs={{1,0},{0,1},{3,2},{2,3},{5,4},{4,5},{7,6},{6,7},{9,8},{8,9},{11,10... | collective-permute-start | bytes 24584 | tf_op jit(solution)/shard_map/ppermute | solution.py:417
  3.7 4.9 %copy-start.4 = (s32[8,27]{1,0:T(8,128)S(1)}, s32[8,27]{1,0:T(8,128)}, u32[]{:S(2)}) copy-start(s32[8,27]{1,0:T(8,128)} %columns_ref.1) | copy-start | bytes 2596
  6.7 4.4 %collective-permute-start.2 = (f32[72,256]{1,0:T(8,128)S(1)}, f32[72,256]{1,0:T(8,128)S(1)}, u32[]{:S(2)}, u32[]{:S(2)}) collective-permute-start(f32[72,256]{1,0:T(8,128)S(1)} %get-tuple-element.22.b_ref), channel_id=1, source_target_pairs={{2,4},{3,5},{6,8},{7,9},{10,12},{11,13},{14,16},{15,17},{18,20},{1... | collective-permute-start | bytes 221192 | tf_op jit(solution)/shard_map/ppermute | solution.py:390
  8.5 2.7 %collective-permute-start.1 = (f32[72,256]{1,0:T(8,128)S(1)}, f32[72,256]{1,0:T(8,128)S(1)}, u32[]{:S(2)}, u32[]{:S(2)}) collective-permute-start(f32[72,256]{1,0:T(8,128)S(1)} %get-tuple-element.21.after_ref.a_ref), channel_id=1, source_target_pairs={{0,2},{2,0},{4,6},{6,4},{8,10},{10,8},{12,14},{14,12},{16,18},{18,... | collective-permute-start | bytes 221192 | tf_op jit(solution)/shard_map/ppermute | solution.py:385
  12.3 2.3 %collective-permute-start.3 = (f32[128,256]{1,0:T(8,128)S(1)}, f32[128,256]{1,0:T(8,128)S(1)}, u32[]{:S(2)}, u32[]{:S(2)}) collective-permute-start(f32[128,256]{1,0:T(8,128)S(1)} %get-tuple-element.26.own_a_ref), channel_id=1, source_target_pairs={{0,2},{2,0},{4,6},{6,4},{8,10},{10,8},{12,14},{14,12},{16,18},{18,... | collective-permute-start | bytes 393224 | tf_op jit(solution)/shard_map/ppermute | solution.py:385
  12.4 5.0 %collective-permute-start.4 = (f32[128,256]{1,0:T(8,128)S(1)}, f32[128,256]{1,0:T(8,128)S(1)}, u32[]{:S(2)}, u32[]{:S(2)}) collective-permute-start(f32[128,256]{1,0:T(8,128)S(1)} %get-tuple-element.27.own_b_ref), channel_id=1, source_target_pairs={{2,4},{3,5},{6,8},{7,9},{10,12},{11,13},{14,16},{15,17},{18,20},{1... | collective-permute-start | bytes 393224 | tf_op jit(solution)/shard_map/ppermute | solution.py:390
  14.7 17.1 %copy-start.1 = (f32[32,32]{1,0:T(8,128)S(1)}, f32[32,32]{1,0:T(8,128)}, u32[]{:S(2)}) copy-start(f32[32,32]{1,0:T(8,128)} %inverse_ref.1) | copy-start | bytes 12292
  18.6 4.9 %collective-permute-start.9 = (f32[32,256]{1,0:T(8,128)S(1)}, f32[32,256]{1,0:T(8,128)S(1)}, u32[]{:S(2)}, u32[]{:S(2)}) collective-permute-start(f32[32,256]{1,0:T(8,128)S(1)} %get-tuple-element.35), channel_id=1, source_target_pairs={{0,6},{2,4},{4,2},{6,0},{8,14},{10,12},{12,10},{14,8},{16,22},{18,... | collective-permute-start | bytes 98312 | tf_op jit(solution)/shard_map/ppermute | solution.py:367
  21.0 3.9 %collective-permute-start.8 = (f32[32,256]{1,0:T(8,128)S(1)}, f32[32,256]{1,0:T(8,128)S(1)}, u32[]{:S(2)}, u32[]{:S(2)}) collective-permute-start(f32[32,256]{1,0:T(8,128)S(1)} %get-tuple-element.35), channel_id=1, source_target_pairs={{0,4},{2,6},{4,0},{6,2},{8,12},{10,14},{12,8},{14,10},{16,20},{18,... | collective-permute-start | bytes 98312 | tf_op jit(solution)/shard_map/ppermute | solution.py:367
  21.0 3.9 %collective-permute-start.7 = (f32[32,256]{1,0:T(8,128)S(1)}, f32[32,256]{1,0:T(8,128)S(1)}, u32[]{:S(2)}, u32[]{:S(2)}) collective-permute-start(f32[32,256]{1,0:T(8,128)S(1)} %get-tuple-element.35), channel_id=1, source_target_pairs={{0,2},{2,0},{4,6},{6,4},{8,10},{10,8},{12,14},{14,12},{16,18},{18,... | collective-permute-start | bytes 98312 | tf_op jit(solution)/shard_map/ppermute | solution.py:367
  21.6 10.2 %collective-permute-start.5 = (f32[64,256]{1,0:T(8,128)S(1)}, f32[64,256]{1,0:T(8,128)S(1)}, u32[]{:S(2)}, u32[]{:S(2)}) collective-permute-start(f32[64,256]{1,0:T(8,128)S(1)} %get-tuple-element.33), channel_id=1, source_target_pairs={{0,2},{2,0},{4,6},{6,4},{8,10},{10,8},{12,14},{14,12},{16,18},{18,... | collective-permute-start | bytes 196616 | tf_op jit(solution)/shard_map/ppermute | solution.py:385
  22.0 9.8 %collective-permute-start.6 = (f32[64,256]{1,0:T(8,128)S(1)}, f32[64,256]{1,0:T(8,128)S(1)}, u32[]{:S(2)}, u32[]{:S(2)}) collective-permute-start(f32[64,256]{1,0:T(8,128)S(1)} %get-tuple-element.34), channel_id=1, source_target_pairs={{2,4},{3,5},{6,8},{7,9},{10,12},{11,13},{14,16},{15,17},{18,20},{1... | collective-permute-start | bytes 196616 | tf_op jit(solution)/shard_map/ppermute | solution.py:390
  24.9 5.5 %collective-permute-start.12 = (f32[32,256]{1,0:T(8,128)S(1)}, f32[32,256]{1,0:T(8,128)S(1)}, u32[]{:S(2)}, u32[]{:S(2)}) collective-permute-start(f32[32,256]{1,0:T(8,128)S(1)} %add_add_fusion.rest_0_), channel_id=1, source_target_pairs={{0,26},{2,24},{4,30},{6,28},{8,18},{10,16},{12,22},{14,20},{16,10}... | collective-permute-start | bytes 98312 | tf_op jit(solution)/shard_map/ppermute | solution.py:367
  27.1 4.3 %collective-permute-start.11 = (f32[32,256]{1,0:T(8,128)S(1)}, f32[32,256]{1,0:T(8,128)S(1)}, u32[]{:S(2)}, u32[]{:S(2)}) collective-permute-start(f32[32,256]{1,0:T(8,128)S(1)} %add_add_fusion.rest_0_), channel_id=1, source_target_pairs={{0,18},{2,16},{4,22},{6,20},{8,26},{10,24},{12,30},{14,28},{16,2},... | collective-permute-start | bytes 98312 | tf_op jit(solution)/shard_map/ppermute | solution.py:367
  27.7 4.1 %collective-permute-start.10 = (f32[32,256]{1,0:T(8,128)S(1)}, f32[32,256]{1,0:T(8,128)S(1)}, u32[]{:S(2)}, u32[]{:S(2)}) collective-permute-start(f32[32,256]{1,0:T(8,128)S(1)} %add_add_fusion.rest_0_), channel_id=1, source_target_pairs={{0,8},{2,10},{4,12},{6,14},{8,0},{10,2},{12,4},{14,6},{16,24},{18,... | collective-permute-start | bytes 98312 | tf_op jit(solution)/shard_map/ppermute | solution.py:367

commit v5 on v4

--- a/solution.py
+++ b/solution.py
@@ -26,6 +26,10 @@
 VMEM_SMALL = 16 * 1024 * 1024
 VMEM_LARGE = 48 * 1024 * 1024
 CHUNK = 512
+STEP = 2
+FRAME = 16
+WIDE = 24
+TN = (((0,), (0,)), ((), ()))
 
 
 def split(x):
@@ -136,7 +140,7 @@
                 low_ref[at : at + 16, 128 * m : 128 * (m + 1)] = tl
 
 
-def sides(rows_ref, owner_ref, right_ref, scale_ref, after_ref, *rest, parts, ncoarse):
+def sides(rows_ref, owner_ref, right_ref, scale_ref, after_ref, *rest, parts):
     basis_refs = rest[:parts]
     resid_ref, side_a_ref, side_b_ref, blk_ref = rest[parts:]
     odd = lax.axis_index("sub") % 2
@@ -144,15 +148,15 @@
     cases = right_ref.shape[0]
     per = NCL // parts
     scale = jnp.broadcast_to(scale_ref[...], (8, OWN))
-    unknown = lax.broadcasted_iota(jnp.int32, (ncoarse, OWN), 0)
-    coarse = jnp.zeros((ncoarse, OWN), F32)
+    unknown = lax.broadcasted_iota(jnp.int32, (FRAME, OWN), 0) + frame_start()
+    coarse = jnp.zeros((FRAME, OWN), F32)
     for k in range(parts):
         for t in range(per):
             owner = owner_ref[0, ((mine + k) % parts) * per + t]
             coarse = coarse + jnp.where(unknown == owner, basis_refs[k][t : t + 1, :], 0.0)
     right = right_ref[...]
     fine = right * scale[0:1]
-    live = cases + ncoarse
+    live = cases + FRAME
     for n in range(NB):
         cut = slice(B * n, B * (n + 1))
         blk_ref[n, 0:cases, :] = fine[:, cut]
@@ -169,10 +173,32 @@
         resid_ref[:, B * j : B * (j + 2)] = pair[live + 8 :]
 
 
+def frame_start():
+    return STEP * lax.axis_index("sub") - 6
+
+
+def turned(rows, upper):
+    up = pltpu.roll(rows, STEP, 0)
+    down = pltpu.roll(rows, rows.shape[0] - STEP, 0)
+    return jnp.where(upper, up, down)
+
+
+def arrived(rows, upper):
+    cases = rows.shape[0] - FRAME
+    return jnp.concatenate([rows[:cases], turned(rows[cases:], upper)], axis=0)
+
+
 def first_apply(a_ref, b_ref, ga_ref, gb_ref, high_ref, low_ref, strain_ref, send_a_ref, send_b_ref):
     live = strain_ref.shape[0]
+    odd = lax.axis_index("sub") % 2 == 1
     field = jnp.concatenate(
-        [a_ref[:live, :], b_ref[:live, :], ga_ref[:live, :], inside() * gb_ref[:live, :]], axis=1
+        [
+            a_ref[:live, :],
+            b_ref[:live, :],
+            arrived(ga_ref[:live, :], jnp.logical_not(odd)),
+            arrived(inside() * gb_ref[:live, :], odd),
+        ],
+        axis=1,
     )
     strain = times(field, high_ref[...], low_ref[...], NT)
     strain_ref[...] = strain
@@ -183,20 +209,33 @@
     send_b_ref[live:, :] = back[:, OWN + EDGE :]
 
 
-def first_sums(resid_ref, a_ref, b_ref, strain_ref, fixed_ref, *, cases, ncoarse):
-    live = cases + ncoarse
+def to_lanes(block, wide_ref):
+    width = wide_ref.shape[1]
+    wide_ref[...] = jnp.zeros_like(wide_ref)
+    wide_ref[:, :FRAME] = block
+    return pltpu.roll(wide_ref[...], (frame_start() + width) % width, 1)
+
+
+def row_sums(value):
+    return exact(jnp.ones((8, value.shape[1]), F32), value, NT)[0:1]
+
+
+def first_sums(resid_ref, a_ref, b_ref, strain_ref, frame_ref, scalar_ref, wide_ref, *, ncoarse):
+    live = strain_ref.shape[0]
+    cases = live - FRAME
     own = jnp.concatenate([a_ref[:live, :], b_ref[:live, :]], axis=1)
     paired = jnp.concatenate([own, strain_ref[...]], axis=1)
-    gram = exact(paired, paired[cases:], NT)
+    gram = exact(paired[cases:], paired, NT)
     resid = resid_ref[...]
     lead = paired[:cases]
-    fixed_ref[...] = jnp.zeros_like(fixed_ref)
-    fixed_ref[:cases, 0:ncoarse] = exact(resid, own[cases:], NT)
-    fixed_ref[:cases, ncoarse : 2 * ncoarse] = gram[:cases]
-    fixed_ref[:ncoarse, 2 * ncoarse : 3 * ncoarse] = gram[cases:]
-    at = 3 * ncoarse
-    fixed_ref[:cases, at : at + 1] = jnp.sum(resid * own[:cases], axis=1, keepdims=True)
-    fixed_ref[:cases, at + 1 : at + 2] = jnp.sum(lead * lead, axis=1, keepdims=True)
+    width = cases + ncoarse
+    frame_ref[...] = jnp.zeros_like(frame_ref)
+    frame_ref[:, 0:cases] = gram[:, :cases]
+    frame_ref[:, cases:width] = to_lanes(gram[:, cases:], wide_ref)[:, :ncoarse]
+    frame_ref[:, 3 * width : 3 * width + cases] = exact(own[cases:], resid, NT)
+    scalar_ref[...] = jnp.zeros_like(scalar_ref)
+    scalar_ref[0:1, :] = row_sums(resid * own[:cases])
+    scalar_ref[1:2, :] = row_sums(lead * lead)
 
 
 def second_apply(
@@ -210,23 +249,28 @@
     got_b_ref,
     high_ref,
     low_ref,
-    fixed_ref,
+    frame_ref,
+    scalar_ref,
     strain_ref,
     image_ref,
     scaled_ref,
     pay_ref,
+    wide_ref,
+    tall_ref,
     *,
-    cases,
     ncoarse,
 ):
-    live = cases + ncoarse
+    live = strain_ref.shape[0]
+    cases = live - FRAME
+    odd = lax.axis_index("sub") % 2 == 1
+    even = jnp.logical_not(odd)
     inner = inside()
     image = jnp.concatenate(
         [
-            own_a_ref[:live, :] + got_a_ref[live:, :],
-            own_b_ref[:live, :] + inner * got_b_ref[live:, :],
-            own_a_ref[live:, :] + got_a_ref[:live, :],
-            own_b_ref[live:, :] + got_b_ref[:live, :],
+            own_a_ref[:live, :] + arrived(got_a_ref[live:, :], even),
+            own_b_ref[:live, :] + inner * arrived(got_b_ref[live:, :], odd),
+            own_a_ref[live:, :] + arrived(got_a_ref[:live, :], even),
+            own_b_ref[live:, :] + arrived(got_b_ref[:live, :], odd),
         ],
         axis=1,
     )
@@ -242,20 +286,20 @@
     image_ref[...] = first
     scaled_ref[...] = own
     paired = jnp.concatenate([own, strain], axis=1)
-    gram = exact(paired, paired[cases:], NT)
-    cross = exact(own, first[cases:], NT)
+    gram = exact(paired[cases:], paired, NT)
+    cross = exact(first[cases:], own, NT)
     lead = paired[:cases]
-    pay_ref[...] = jnp.zeros_like(pay_ref)
-    n = ncoarse
-    pay_ref[:, 0 : 3 * n] = fixed_ref[:, 0 : 3 * n]
-    pay_ref[:cases, 3 * n : 4 * n] = cross[:cases]
-    pay_ref[:n, 4 * n : 5 * n] = cross[cases:]
-    pay_ref[:cases, 5 * n : 6 * n] = gram[:cases]
-    pay_ref[:n, 6 * n : 7 * n] = gram[cases:]
-    at = 7 * n
-    pay_ref[:, at : at + 2] = fixed_ref[:, 3 * n : 3 * n + 2]
-    pay_ref[:cases, at + 2 : at + 3] = jnp.sum(own[:cases] * first[:cases], axis=1, keepdims=True)
-    pay_ref[:cases, at + 3 : at + 4] = jnp.sum(lead * lead, axis=1, keepdims=True)
+    width = cases + ncoarse
+    tall_ref[...] = jnp.zeros_like(tall_ref)
+    tall_ref[:FRAME, :] = frame_ref[...]
+    for at, block in ((width, cross), (2 * width, gram)):
+        tall_ref[:FRAME, at : at + cases] = block[:, :cases]
+        tall_ref[:FRAME, at + cases : at + width] = to_lanes(block[:, cases:], wide_ref)[:, :ncoarse]
+    pay_ref[...] = pltpu.roll(tall_ref[...], (frame_start() + ncoarse) % ncoarse, 0)
+    at = 3 * width + cases
+    pay_ref[0:8, at : at + cases] = scalar_ref[...]
+    pay_ref[2:3, at : at + cases] = row_sums(own[:cases] * first[:cases])
+    pay_ref[3:4, at : at + cases] = row_sums(lead * lead)
 
 
 def second_image(scaled_ref, strain_ref, high_ref, low_ref, own_ref, send_a_ref, send_b_ref):
@@ -263,6 +307,27 @@
     own_ref[...] = scaled_ref[...] + back[:, :OWN]
     send_a_ref[...] = back[:, OWN : OWN + EDGE]
     send_b_ref[...] = back[:, OWN + EDGE :]
+
+
+def window(value, start, count):
+    rows = value.shape[0] + 32
+    longer = jnp.concatenate([value, jnp.zeros((32, value.shape[1]), F32)], axis=0)
+    return pltpu.roll(longer, (rows - start) % rows, 0)[:count]
+
+
+def widened(own, got_a, got_b, even):
+    gap = WIDE - FRAME
+
+    def placed(rows, upper):
+        none = jnp.zeros((gap, rows.shape[1]), F32)
+        low = jnp.concatenate([rows, none], axis=0)
+        return jnp.where(upper, pltpu.roll(low, 2 * STEP, 0), low)
+
+    none = jnp.zeros((gap, own.shape[1]), F32)
+    middle = pltpu.roll(jnp.concatenate([own, none], axis=0), STEP, 0)
+    return middle + jnp.concatenate(
+        [placed(got_a, even), placed(got_b, jnp.logical_not(even))], axis=1
+    )
 
 
 def finish(
@@ -277,39 +342,37 @@
     got_a_ref,
     got_b_ref,
     *rest,
-    cases,
     ncoarse,
     n_pay,
 ):
     pays = rest[:n_pay]
     field_hbm, resid2_hbm, field_ref, resid2_ref, blk_ref, sems = rest[n_pay:]
     odd = lax.axis_index("sub") % 2
-    n = ncoarse
-    live = cases + n
+    live = own_ref.shape[0]
+    cases = live - FRAME
+    width = cases + ncoarse
     pay = pays[0][...]
     for other in pays[1:]:
         pay = pay + other[...]
 
     def total(value):
-        return jnp.sum(value, axis=1, keepdims=True)
-
-    u0 = pay[:cases, 0:n]
-    g12 = pay[:cases, n : 2 * n]
-    g22 = pay[:n, 2 * n : 3 * n]
-    g14 = pay[:cases, 3 * n : 4 * n]
-    g34 = pay[:cases, 5 * n : 6 * n]
-    at = 7 * n
-    r0d, g11, g13, g33 = (pay[:cases, at + k : at + k + 1] for k in range(4))
+        return jnp.sum(value, axis=0, keepdims=True)
+
+    def piece(k):
+        at = (k // 2) * width + (k % 2) * cases
+        return pay[:, at : at + (ncoarse if k % 2 and k < 6 else cases)]
+
+    g12, g22, g14, g24, g34, g44, u0, scalars = (piece(k) for k in range(8))
+    r0d, g11, g13, g33 = (scalars[k : k + 1] for k in range(4))
     inverse = inverse_ref[...]
-    y0 = exact(u0, inverse)
-    y22 = exact(y0, g22)
-    y24 = exact(y0, pay[:n, 4 * n : 5 * n])
-    y44 = exact(y0, pay[:n, 6 * n : 7 * n])
+    y0 = exact(inverse, u0)
+    stacked = exact(jnp.concatenate([g22, g24, g44], axis=0), y0)
+    y22, y24, y44 = (stacked[k * ncoarse : (k + 1) * ncoarse] for k in range(3))
     rz0 = r0d + total(u0 * y0)
     pq0 = g11 + total(y0 * (2.0 * g12 + y22))
     alpha = rz0 / pq0
     u1 = u0 - alpha * (g12 + y22)
-    y1 = exact(u1, inverse)
+    y1 = exact(inverse, u1)
     cross = g13 + total(y0 * g14)
     rz1 = (
         r0d
@@ -320,7 +383,7 @@
     beta = rz1 / rz0
     lead = 1.0 + beta
     coarse = y1 + beta * y0
-    c22 = exact(y1, g22) + beta * y22
+    c22 = exact(g22, y1) + beta * y22
     pq1 = (
         lead * (lead * g11 + 2.0 * total(coarse * g12) - 2.0 * alpha * cross)
         + total(coarse * (c22 - 2.0 * alpha * (g14 + y24)))
@@ -329,21 +392,36 @@
     alpha1 = rz1 / pq1
     lower = alpha1 * alpha
     upper = alpha + alpha1 * lead
-    weights = jnp.concatenate([alpha * y0 + alpha1 * coarse, -lower * y0], axis=1)
+    first = alpha * y0 + alpha1 * coarse
+    second = -lower * y0
+    begin = frame_start()
+    first16 = window(first, begin, FRAME)
+    weights = jnp.concatenate([first16, window(second, begin, FRAME)], axis=0)
+    weights2 = jnp.concatenate([first16, window(second, begin - STEP, WIDE)], axis=0)
+    row = lax.broadcasted_iota(jnp.int32, (8, 256), 0)
+    half = lax.broadcasted_iota(jnp.int32, (8, 256), 1) // 128
+    pair = jnp.concatenate([upper, lower, jnp.zeros((6, cases), F32)], axis=0)
+    columns = exact(pair, jnp.where(row == half, 1.0, 0.0), TN)
+    upper = jnp.concatenate([columns[:, :128]] * (OWN // 128), axis=1)
+    lower = jnp.concatenate([columns[:, 128:]] * (OWN // 128), axis=1)
     start = jnp.concatenate([a_ref[:live, :], b_ref[:live, :]], axis=1)
     scaled = scaled_ref[...]
     image = image_ref[...]
-    image2 = own_ref[...] + jnp.concatenate([got_a_ref[...], inside() * got_b_ref[...]], axis=1)
+    own = own_ref[...]
+    got_a = got_a_ref[...]
+    got_b = inside() * got_b_ref[...]
+    image2 = own[:cases] + jnp.concatenate([got_a[:cases], got_b[:cases]], axis=1)
+    coarse2 = widened(own[cases:], got_a[cases:], got_b[cases:], odd == 0)
     field = (
         upper * start[:cases]
         - lower * scaled[:cases]
-        + exact(weights, jnp.concatenate([start[cases:], scaled[cases:]], axis=0))
+        + exact(weights, jnp.concatenate([start[cases:], scaled[cases:]], axis=0), TN)
     )
     resid2 = (
         resid_ref[...]
         - upper * image[:cases]
-        + lower * image2[:cases]
-        - exact(weights, jnp.concatenate([image[cases:], image2[cases:]], axis=0))
+        + lower * image2
+        - exact(weights2, jnp.concatenate([image[cases:], coarse2], axis=0), TN)
     )
     copies = []
     for k, (value, out, buf) in enumerate(
@@ -409,9 +487,9 @@
     ncoarse = coarse_inverse.shape[0]
     count = lax.axis_size("sub")
     parts = lax.axis_size("rhs")
-    live = cases + ncoarse
+    live = cases + FRAME
     rounds = rounds_of(count)
-    run = functools.partial(call, large=live > 128)
+    run = functools.partial(call, large=ncoarse > 128)
 
     bases = [corner_basis] + [
         lax.ppermute(corner_basis, "rhs", [((i + k) % parts, i) for i in range(parts)])
@@ -431,7 +509,7 @@
         large=True,
     )(jnp.transpose(stiffness_blocks, (1, 0, 2)))
     resid, side_a, side_b = run(
-        functools.partial(sides, parts=parts, ncoarse=ncoarse),
+        functools.partial(sides, parts=parts),
         [shape(cases, OWN), shape(live + 8, EDGE), shape(live + 8, EDGE)],
         5 + parts,
         smem=(0, 1),
@@ -444,21 +522,24 @@
     ghost_a, ghost_b = across(side_a, side_b, count, parts)
     ends = (side_a, side_b, ghost_a, ghost_b)
 
-    rows = max(cases, ncoarse)
+    lanes = lanes_for(3 * (cases + ncoarse) + 2 * cases)
+    wide = pltpu.VMEM((FRAME, lanes_for(ncoarse)), F32)
     strain, own_a, own_b = run(
         first_apply, [shape(live, ROWS), shape(2 * live, EDGE), shape(2 * live, EDGE)], 6
     )(*ends, high, low)
     got_a, got_b = across(own_a, own_b, count, parts)
-    (fixed,) = run(
-        functools.partial(first_sums, cases=cases, ncoarse=ncoarse),
-        [shape(rows, lanes_for(3 * ncoarse + 2))],
+    frame, scalars = run(
+        functools.partial(first_sums, ncoarse=ncoarse),
+        [shape(FRAME, lanes), shape(8, cases)],
         4,
+        scratch=[wide],
     )(resid, side_a, side_b, strain)
     strain, image, scaled, pay = run(
-        functools.partial(second_apply, cases=cases, ncoarse=ncoarse),
-        [shape(live, ROWS), shape(live, OWN), shape(live, OWN), shape(rows, lanes_for(7 * ncoarse + 4))],
-        11,
-    )(*ends, own_a, own_b, got_a, got_b, high, low, fixed)
+        functools.partial(second_apply, ncoarse=ncoarse),
+        [shape(live, ROWS), shape(live, OWN), shape(live, OWN), shape(ncoarse, lanes)],
+        12,
+        scratch=[wide, pltpu.VMEM((ncoarse, lanes), F32)],
+    )(*ends, own_a, own_b, got_a, got_b, high, low, frame, scalars)
     for steps in rounds[:-1]:
         pay = sum(swap(pay, steps, count), pay)
     pays = [pay] + swap(pay, rounds[-1], count)
@@ -468,7 +549,7 @@
     got_a, got_b = across(back_a, back_b, count, parts)
     return tuple(
         run(
-            functools.partial(finish, cases=cases, ncoarse=ncoarse, n_pay=len(pays)),
+            functools.partial(finish, ncoarse=ncoarse, n_pay=len(pays)),
             [shape(cases, OWN)] * 2,
             10 + len(pays),
             smem=(0,),

time: 35.2 us -> 34.3 us (0.974)
  waiting for transfers between devices: 7.74 us -> 7 us
    ppermute x3, waiting for transfers between devices: 3.62 us -> 2.99 us  [across(): lax.ppermute(b, ('sub', 'rhs'), pairs + [(j, i) for i, j in pairs])]
where the time goes in v5:
time: 34.3 us; the launch traced here: 34 us
  starting transfers between devices  15.1 us (44%)
  Pallas kernels  11.1 us (32%)
  waiting for transfers between devices  7 us (20%)
  between operations  0.78 us (2%)
    ppermute x6, starting transfers between devices, swap(): lax.ppermute(x, 'sub', [(i, i ^ k) for i in range(count)])  6.54 us
    ppermute x3, starting transfers between devices, across(): lax.ppermute(b, ('sub', 'rhs'), pairs + [(j, i) for i, j in pairs])  4.99 us
    ppermute x6, waiting for transfers between devices, swap(): lax.ppermute(x, 'sub', [(i, i ^ k) for i in range(count)])  4 us
    ppermute x1, starting transfers between devices, body(): lax.ppermute(corner_basis, 'rhs', [((i + k) % parts, i) for i in range(pa...  3 us
    ppermute x3, waiting for transfers between devices, across(): lax.ppermute(b, ('sub', 'rhs'), pairs + [(j, i) for i, j in pairs])  2.99 us
    pallas_call x1, Pallas kernels, body(): run(functools.partial(finish, ncoarse=ncoarse, n_pay=len(pays)), [shape(c...  2.91 us
    pallas_call x1, Pallas kernels, body(): call(load_blocks, [packed, packed], 1, raw=(0,), scratch=[pltpu.VMEM((B *...  2.14 us
    pallas_call x1, Pallas kernels, body(): run(assemble, [dense, dense], 5, smem=(0,))  1.66 us
  transfers between devices with their start and end apart: 13, of which 6 were waited for; matrix products, arithmetic and copies ran while one was open for 0% of the time, Pallas kernels for 14%

profile of v5, /device:TPU:0, one launch (start us, length us, event | category | flops | bytes accessed | tf_op | source)
XLA Modules:
  0.0 34.0 jit_solution(309485719643038649)
XLA Ops:
  0.6 0.0 copy-start.3
  0.6 0.0 copy-start.2
  0.7 0.0 copy-start.5
  0.7 0.0 copy-start.6
  0.7 0.0 copy-start
  0.7 3.0 %collective-permute-start = (f32[4,512]{1,0:T(4,128)}, f32[4,512]{1,0:T(4,128)S(1)}, u32[]{:S(2)}, u32[]{:S(2)}) collective-permute-start(f32[4,512]{1,0:T(4,128)} %rest_0_.1), channel_id=1, source_target_pairs={{1,0},{0,1},{3,2},{2,3},{5,4},{4,5},{7,6},{6,7},{9,8},{8,9},{11,10... | collective-permute-start | bytes 24584 | tf_op jit(solution)/shard_map/ppermute | solution.py:495
  3.7 0.0 copy-start.4
  3.7 2.1 %shard_map.95 = (bf16[256,4096]{1,0:T(8,128)(2,1)S(1)}, bf16[256,4096]{1,0:T(8,128)(2,1)S(1)}) custom-call(f32[27,8,4096]{2,1,0:T(8,128)} %bitcast.3), custom_call_target="tpu_custom_call" | custom-call | bytes 16777216 | tf_op jit(solution)/shard_map/pallas_call | solution.py:499
  5.8 0.0 collective-permute-done.rest_1_
  5.8 0.0 copy-done.3
  5.9 0.0 copy-done.2
  5.9 0.0 copy-done.5
  5.9 0.0 copy-done.6
  5.9 0.0 copy-done
  5.9 0.8 %shard_map.96 = (f32[32,512]{1,0:T(8,128)S(1)}, f32[56,256]{1,0:T(8,128)S(1)}, f32[56,256]{1,0:T(8,128)S(1)}) custom-call(s32[1,2,4]{2,1,0:T(2,128)S(1)} %copy-done.2, s32[1,8]{1,0:T(1,128)S(1)} %copy-done.6, f32[32,512]{1,0:T(8,128)S(1)} %copy-done, f32[1,512]{1,0:T(1,128)S(1)} %bitcast.2, bf16[256,4096]{1,0:T(8,128)(2,1)S(1)} %get-tuple-element.21.after_ref.wh_ref, ...), custom_call_target="tpu_custom_call" | custom-call | tf_op jit(solution)/shard_map/pallas_call | solution.py:511
  6.7 1.8 %collective-permute-start.2 = (f32[56,256]{1,0:T(8,128)S(1)}, f32[56,256]{1,0:T(8,128)S(1)}, u32[]{:S(2)}, u32[]{:S(2)}) collective-permute-start(f32[56,256]{1,0:T(8,128)S(1)} %get-tuple-element.24.b_ref), channel_id=1, source_target_pairs={{2,4},{3,5},{6,8},{7,9},{10,12},{11,13},{14,16},{15,17},{18,20},{1... | collective-permute-start | bytes 172040 | tf_op jit(solution)/shard_map/ppermute | solution.py:468
  8.4 0.1 collective-permute-start.1
  8.6 0.0 copy-done.4
  8.6 1.7 %shard_map.97 = (bf16[512,1024]{1,0:T(8,128)(2,1)S(1)}, bf16[512,1024]{1,0:T(8,128)(2,1)S(1)}) custom-call(s32[1,2,4]{2,1,0:T(2,128)S(1)} %copy-done.2, s32[8,27]{1,0:T(8,128)S(1)} %copy-done.4, bf16[256,4096]{1,0:T(8,128)(2,1)S(1)} %get-tuple-element.21.after_ref.wh_ref, bf16[256,4096]{1,0:T(8,128)(2,1)S(1)} %get-tuple-element.25.wl_ref, ...), custom_call_target="tpu_custom_call" | custom-call | tf_op jit(solution)/shard_map/pallas_call | solution.py:519
  10.2 0.7 %collective-permute-done.2.gb_ref = f32[56,256]{1,0:T(8,128)S(1)} collective-permute-done((f32[56,256]{1,0:T(8,128)S(1)}, f32[56,256]{1,0:T(8,128)S(1)}, u32[]{:S(2)}, u32[]{:S(2)}) %collective-permute-start.2) | collective-permute-done | bytes 57376 | tf_op jit(solution)/shard_map/ppermute | solution.py:468
  10.9 0.0 collective-permute-done.1.ga_ref
  10.9 1.2 %shard_map.98 = (f32[48,512]{1,0:T(8,128)S(1)}, f32[96,256]{1,0:T(8,128)S(1)}, f32[96,256]{1,0:T(8,128)S(1)}) custom-call(f32[56,256]{1,0:T(8,128)S(1)} %get-tuple-element.23.after_ref.a_ref, f32[56,256]{1,0:T(8,128)S(1)} %get-tuple-element.24.b_ref, f32[56,256]{1,0:T(8,128)S(1)} %collective-permute-done.1.ga_ref, ...), custom_call_target="tpu_custom_call" | custom-call | tf_op jit(solution)/shard_map/pallas_call | solution.py:527
  12.1 0.1 collective-permute-start.3
  12.2 1.8 %collective-permute-start.4 = (f32[96,256]{1,0:T(8,128)S(1)}, f32[96,256]{1,0:T(8,128)S(1)}, u32[]{:S(2)}, u32[]{:S(2)}) collective-permute-start(f32[96,256]{1,0:T(8,128)S(1)} %get-tuple-element.29.own_b_ref), channel_id=1, source_target_pairs={{2,4},{3,5},{6,8},{7,9},{10,12},{11,13},{14,16},{15,17},{18,20},{1... | collective-permute-start | bytes 294920 | tf_op jit(solution)/shard_map/ppermute | solution.py:468
  13.9 0.6 %shard_map.99 = (f32[16,256]{1,0:T(8,128)S(1)}, f32[8,32]{1,0:T(8,128)S(1)}) custom-call(f32[32,512]{1,0:T(8,128)S(1)} %get-tuple-element.22.resid_ref, f32[56,256]{1,0:T(8,128)S(1)} %get-tuple-element.23.after_ref.a_ref, f32[56,256]{1,0:T(8,128)S(1)} %get-tuple-element.24.b_ref, f32[48,512]{1,0:T(8,128)S(1)} %get-tuple-element.30.strain_ref), custom_call_target="tpu_custom_call" | custom-call | tf_op jit(solution)/shard_map/pallas_call | solution.py:531
  14.6 0.0 collective-permute-done.3.got_a_ref
  14.6 2.3 %collective-permute-done.4.got_b_ref = f32[96,256]{1,0:T(8,128)S(1)} collective-permute-done((f32[96,256]{1,0:T(8,128)S(1)}, f32[96,256]{1,0:T(8,128)S(1)}, u32[]{:S(2)}, u32[]{:S(2)}) %collective-permute-start.4) | collective-permute-done | bytes 98336 | tf_op jit(solution)/shard_map/ppermute | solution.py:468
  16.9 0.0 copy-start.1
  16.9 1.3 %shard_map.100 = (f32[48,512]{1,0:T(8,128)S(1)}, f32[48,512]{1,0:T(8,128)S(1)}, f32[48,512]{1,0:T(8,128)S(1)}, f32[32,256]{1,0:T(8,128)S(1)}) custom-call(f32[56,256]{1,0:T(8,128)S(1)} %get-tuple-element.23.after_ref.a_ref, f32[56,256]{1,0:T(8,128)S(1)} %get-tuple-element.24.b_ref, f32[56,256]{1,0:T(8,128)S(1)} %collective-permute-done.1.ga_ref, ...), custom_call_target="tpu_custom_call" | custom-call | tf_op jit(solution)/shard_map/pallas_call | solution.py:537
  18.2 2.2 %collective-permute-start.9 = (f32[32,256]{1,0:T(8,128)S(1)}, f32[32,256]{1,0:T(8,128)S(1)}, u32[]{:S(2)}, u32[]{:S(2)}) collective-permute-start(f32[32,256]{1,0:T(8,128)S(1)} %get-tuple-element.39), channel_id=1, source_target_pairs={{0,6},{2,4},{4,2},{6,0},{8,14},{10,12},{12,10},{14,8},{16,22},{18,... | collective-permute-start | bytes 98312 | tf_op jit(solution)/shard_map/ppermute | solution.py:445
  20.4 0.0 collective-permute-start.8
  20.4 0.2 collective-permute-start.7
  20.6 0.5 %shard_map.101 = (f32[48,512]{1,0:T(8,128)S(1)}, f32[48,256]{1,0:T(8,128)S(1)}, f32[48,256]{1,0:T(8,128)S(1)}) custom-call(f32[48,512]{1,0:T(8,128)S(1)} %get-tuple-element.34.scaled_ref, f32[48,512]{1,0:T(8,128)S(1)} %get-tuple-element.35.strain_ref, bf16[512,1024]{1,0:T(8,128)(2,1)S(1)} %get-tuple-element.26.high_ref, ...), custom_call_target="tpu_custom_call" | custom-call | tf_op jit(solution)/shard_map/pallas_call | solution.py:546
  21.1 0.3 collective-permute-start.5
  21.4 1.5 %collective-permute-start.6 = (f32[48,256]{1,0:T(8,128)S(1)}, f32[48,256]{1,0:T(8,128)S(1)}, u32[]{:S(2)}, u32[]{:S(2)}) collective-permute-start(f32[48,256]{1,0:T(8,128)S(1)} %get-tuple-element.38), channel_id=1, source_target_pairs={{2,4},{3,5},{6,8},{7,9},{10,12},{11,13},{14,16},{15,17},{18,20},{1... | collective-permute-start | bytes 147464 | tf_op jit(solution)/shard_map/ppermute | solution.py:468
  22.9 0.0 collective-permute-done.9
  22.9 1.4 %collective-permute-done.8 = f32[32,256]{1,0:T(8,128)S(1)} collective-permute-done((f32[32,256]{1,0:T(8,128)S(1)}, f32[32,256]{1,0:T(8,128)S(1)}, u32[]{:S(2)}, u32[]{:S(2)}) %collective-permute-start.8) | collective-permute-done | bytes 32800 | tf_op jit(solution)/shard_map/ppermute | solution.py:445
  24.3 0.0 collective-permute-done.7
  24.3 2.1 %collective-permute-start.12 = (f32[32,256]{1,0:T(8,128)S(1)}, f32[32,256]{1,0:T(8,128)S(1)}, u32[]{:S(2)}, u32[]{:S(2)}) collective-permute-start(f32[32,256]{1,0:T(8,128)S(1)} %add_add_fusion.rest_0_), channel_id=1, source_target_pairs={{0,26},{2,24},{4,30},{6,28},{8,18},{10,16},{12,22},{14,20},{16,10}... | collective-permute-start | bytes 98312 | tf_op jit(solution)/shard_map/ppermute | solution.py:445
  26.4 0.8 %collective-permute-start.11 = (f32[32,256]{1,0:T(8,128)S(1)}, f32[32,256]{1,0:T(8,128)S(1)}, u32[]{:S(2)}, u32[]{:S(2)}) collective-permute-start(f32[32,256]{1,0:T(8,128)S(1)} %add_add_fusion.rest_0_), channel_id=1, source_target_pairs={{0,18},{2,16},{4,22},{6,20},{8,26},{10,24},{12,30},{14,28},{16,2},... | collective-permute-start | bytes 98312 | tf_op jit(solution)/shard_map/ppermute | solution.py:445
  27.1 1.3 %collective-permute-start.10 = (f32[32,256]{1,0:T(8,128)S(1)}, f32[32,256]{1,0:T(8,128)S(1)}, u32[]{:S(2)}, u32[]{:S(2)}) collective-permute-start(f32[32,256]{1,0:T(8,128)S(1)} %add_add_fusion.rest_0_), channel_id=1, source_target_pairs={{0,8},{2,10},{4,12},{6,14},{8,0},{10,2},{12,4},{14,6},{16,24},{18,... | collective-permute-start | bytes 98312 | tf_op jit(solution)/shard_map/ppermute | solution.py:445
  28.5 0.0 collective-permute-done.5.got_a_ref
  28.5 0.0 collective-permute-done.6.got_b_ref
  28.5 1.1 %collective-permute-done.12.rest_3_ = f32[32,256]{1,0:T(8,128)S(1)} collective-permute-done((f32[32,256]{1,0:T(8,128)S(1)}, f32[32,256]{1,0:T(8,128)S(1)}, u32[]{:S(2)}, u32[]{:S(2)}) %collective-permute-start.12) | collective-permute-done | bytes 32800 | tf_op jit(solution)/shard_map/ppermute | solution.py:445
  29.7 1.1 %collective-permute-done.11.rest_2_ = f32[32,256]{1,0:T(8,128)S(1)} collective-permute-done((f32[32,256]{1,0:T(8,128)S(1)}, f32[32,256]{1,0:T(8,128)S(1)}, u32[]{:S(2)}, u32[]{:S(2)}) %collective-permute-start.11) | collective-permute-done | bytes 32800 | tf_op jit(solution)/shard_map/ppermute | solution.py:445
  30.7 0.4 %collective-permute-done.10.rest_1_ = f32[32,256]{1,0:T(8,128)S(1)} collective-permute-done((f32[32,256]{1,0:T(8,128)S(1)}, f32[32,256]{1,0:T(8,128)S(1)}, u32[]{:S(2)}, u32[]{:S(2)}) %collective-permute-start.10) | collective-permute-done | bytes 32800 | tf_op jit(solution)/shard_map/ppermute | solution.py:445
  31.1 0.0 copy-done.1
  31.1 2.9 %shard_map.102 = (f32[32,512]{1,0:T(8,128)}, f32[32,512]{1,0:T(8,128)}) custom-call(s32[1,2,4]{2,1,0:T(2,128)S(1)} %copy-done.2, f32[32,32]{1,0:T(8,128)S(1)} %copy-done.1, f32[32,512]{1,0:T(8,128)S(1)} %get-tuple-element.22.resid_ref, f32[56,256]{1,0:T(8,128)S(1)} %get-tuple-element.23.after_ref.a_ref, f32[56,256]{1,0:T(8,128)S(1)} %get-tuple-element.24.b_ref, ...), custom_call_target="tpu_custom_call" | custom-call | tf_op jit(solution)/shard_map/pallas_call | solution.py:551
  (1 shorter events, 0.0 us)
Async XLA Ops:
  0.6 5.2 %copy-start.3 = (f32[4,512]{1,0:T(4,128)S(1)}, f32[4,512]{1,0:T(4,128)}, u32[]{:S(2)}) copy-start(f32[4,512]{1,0:T(4,128)} %rest_0_.1) | copy-start | bytes 24580
  0.6 5.2 %copy-start.2 = (s32[1,2,4]{2,1,0:T(2,128)S(1)}, s32[1,2,4]{2,1,0:T(2,128)}, u32[]{:S(2)}) copy-start(s32[1,2,4]{2,1,0:T(2,128)} %rows_ref.5) | copy-start | bytes 100
  0.7 5.2 %copy-start.5 = (f32[512]{0:T(512)S(1)}, f32[512]{0:T(512)}, u32[]{:S(2)}) copy-start(f32[512]{0:T(512)} %param.14) | copy-start | bytes 6148
  0.7 5.2 %copy-start.6 = (s32[1,8]{1,0:T(1,128)S(1)}, s32[1,8]{1,0:T(1,128)}, u32[]{:S(2)}) copy-start(s32[1,8]{1,0:T(1,128)} %owner_ref.1) | copy-start | bytes 100
  0.7 5.2 %copy-start = (f32[32,512]{1,0:T(8,128)S(1)}, f32[32,512]{1,0:T(8,128)}, u32[]{:S(2)}) copy-start(f32[32,512]{1,0:T(8,128)} %right_ref.1) | copy-start | bytes 196612
  0.7 5.2 %collective-permute-start = (f32[4,512]{1,0:T(4,128)}, f32[4,512]{1,0:T(4,128)S(1)}, u32[]{:S(2)}, u32[]{:S(2)}) collective-permute-start(f32[4,512]{1,0:T(4,128)} %rest_0_.1), channel_id=1, source_target_pairs={{1,0},{0,1},{3,2},{2,3},{5,4},{4,5},{7,6},{6,7},{9,8},{8,9},{11,10... | collective-permute-start | bytes 24584 | tf_op jit(solution)/shard_map/ppermute | solution.py:495
  3.7 4.9 %copy-start.4 = (s32[8,27]{1,0:T(8,128)S(1)}, s32[8,27]{1,0:T(8,128)}, u32[]{:S(2)}) copy-start(s32[8,27]{1,0:T(8,128)} %columns_ref.1) | copy-start | bytes 2596
  6.7 4.2 %collective-permute-start.2 = (f32[56,256]{1,0:T(8,128)S(1)}, f32[56,256]{1,0:T(8,128)S(1)}, u32[]{:S(2)}, u32[]{:S(2)}) collective-permute-start(f32[56,256]{1,0:T(8,128)S(1)} %get-tuple-element.24.b_ref), channel_id=1, source_target_pairs={{2,4},{3,5},{6,8},{7,9},{10,12},{11,13},{14,16},{15,17},{18,20},{1... | collective-permute-start | bytes 172040 | tf_op jit(solution)/shard_map/ppermute | solution.py:468
  8.4 2.5 %collective-permute-start.1 = (f32[56,256]{1,0:T(8,128)S(1)}, f32[56,256]{1,0:T(8,128)S(1)}, u32[]{:S(2)}, u32[]{:S(2)}) collective-permute-start(f32[56,256]{1,0:T(8,128)S(1)} %get-tuple-element.23.after_ref.a_ref), channel_id=1, source_target_pairs={{0,2},{2,0},{4,6},{6,4},{8,10},{10,8},{12,14},{14,12},{16,18},{18,... | collective-permute-start | bytes 172040 | tf_op jit(solution)/shard_map/ppermute | solution.py:463
  12.1 2.5 %collective-permute-start.3 = (f32[96,256]{1,0:T(8,128)S(1)}, f32[96,256]{1,0:T(8,128)S(1)}, u32[]{:S(2)}, u32[]{:S(2)}) collective-permute-start(f32[96,256]{1,0:T(8,128)S(1)} %get-tuple-element.28.own_a_ref), channel_id=1, source_target_pairs={{0,2},{2,0},{4,6},{6,4},{8,10},{10,8},{12,14},{14,12},{16,18},{18,... | collective-permute-start | bytes 294920 | tf_op jit(solution)/shard_map/ppermute | solution.py:463
  12.2 4.7 %collective-permute-start.4 = (f32[96,256]{1,0:T(8,128)S(1)}, f32[96,256]{1,0:T(8,128)S(1)}, u32[]{:S(2)}, u32[]{:S(2)}) collective-permute-start(f32[96,256]{1,0:T(8,128)S(1)} %get-tuple-element.29.own_b_ref), channel_id=1, source_target_pairs={{2,4},{3,5},{6,8},{7,9},{10,12},{11,13},{14,16},{15,17},{18,20},{1... | collective-permute-start | bytes 294920 | tf_op jit(solution)/shard_map/ppermute | solution.py:468
  16.9 14.2 %copy-start.1 = (f32[32,32]{1,0:T(8,128)S(1)}, f32[32,32]{1,0:T(8,128)}, u32[]{:S(2)}) copy-start(f32[32,32]{1,0:T(8,128)} %inverse_ref.1) | copy-start | bytes 12292
  18.2 4.7 %collective-permute-start.9 = (f32[32,256]{1,0:T(8,128)S(1)}, f32[32,256]{1,0:T(8,128)S(1)}, u32[]{:S(2)}, u32[]{:S(2)}) collective-permute-start(f32[32,256]{1,0:T(8,128)S(1)} %get-tuple-element.39), channel_id=1, source_target_pairs={{0,6},{2,4},{4,2},{6,0},{8,14},{10,12},{12,10},{14,8},{16,22},{18,... | collective-permute-start | bytes 98312 | tf_op jit(solution)/shard_map/ppermute | solution.py:445
  20.4 3.9 %collective-permute-start.8 = (f32[32,256]{1,0:T(8,128)S(1)}, f32[32,256]{1,0:T(8,128)S(1)}, u32[]{:S(2)}, u32[]{:S(2)}) collective-permute-start(f32[32,256]{1,0:T(8,128)S(1)} %get-tuple-element.39), channel_id=1, source_target_pairs={{0,4},{2,6},{4,0},{6,2},{8,12},{10,14},{12,8},{14,10},{16,20},{18,... | collective-permute-start | bytes 98312 | tf_op jit(solution)/shard_map/ppermute | solution.py:445
  20.4 3.9 %collective-permute-start.7 = (f32[32,256]{1,0:T(8,128)S(1)}, f32[32,256]{1,0:T(8,128)S(1)}, u32[]{:S(2)}, u32[]{:S(2)}) collective-permute-start(f32[32,256]{1,0:T(8,128)S(1)} %get-tuple-element.39), channel_id=1, source_target_pairs={{0,2},{2,0},{4,6},{6,4},{8,10},{10,8},{12,14},{14,12},{16,18},{18,... | collective-permute-start | bytes 98312 | tf_op jit(solution)/shard_map/ppermute | solution.py:445
  21.1 7.5 %collective-permute-start.5 = (f32[48,256]{1,0:T(8,128)S(1)}, f32[48,256]{1,0:T(8,128)S(1)}, u32[]{:S(2)}, u32[]{:S(2)}) collective-permute-start(f32[48,256]{1,0:T(8,128)S(1)} %get-tuple-element.37), channel_id=1, source_target_pairs={{0,2},{2,0},{4,6},{6,4},{8,10},{10,8},{12,14},{14,12},{16,18},{18,... | collective-permute-start | bytes 147464 | tf_op jit(solution)/shard_map/ppermute | solution.py:463
  21.4 7.1 %collective-permute-start.6 = (f32[48,256]{1,0:T(8,128)S(1)}, f32[48,256]{1,0:T(8,128)S(1)}, u32[]{:S(2)}, u32[]{:S(2)}) collective-permute-start(f32[48,256]{1,0:T(8,128)S(1)} %get-tuple-element.38), channel_id=1, source_target_pairs={{2,4},{3,5},{6,8},{7,9},{10,12},{11,13},{14,16},{15,17},{18,20},{1... | collective-permute-start | bytes 147464 | tf_op jit(solution)/shard_map/ppermute | solution.py:468
  24.3 5.3 %collective-permute-start.12 = (f32[32,256]{1,0:T(8,128)S(1)}, f32[32,256]{1,0:T(8,128)S(1)}, u32[]{:S(2)}, u32[]{:S(2)}) collective-permute-start(f32[32,256]{1,0:T(8,128)S(1)} %add_add_fusion.rest_0_), channel_id=1, source_target_pairs={{0,26},{2,24},{4,30},{6,28},{8,18},{10,16},{12,22},{14,20},{16,10}... | collective-permute-start | bytes 98312 | tf_op jit(solution)/shard_map/ppermute | solution.py:445
  26.4 4.3 %collective-permute-start.11 = (f32[32,256]{1,0:T(8,128)S(1)}, f32[32,256]{1,0:T(8,128)S(1)}, u32[]{:S(2)}, u32[]{:S(2)}) collective-permute-start(f32[32,256]{1,0:T(8,128)S(1)} %add_add_fusion.rest_0_), channel_id=1, source_target_pairs={{0,18},{2,16},{4,22},{6,20},{8,26},{10,24},{12,30},{14,28},{16,2},... | collective-permute-start | bytes 98312 | tf_op jit(solution)/shard_map/ppermute | solution.py:445
  27.1 3.9 %collective-permute-start.10 = (f32[32,256]{1,0:T(8,128)S(1)}, f32[32,256]{1,0:T(8,128)S(1)}, u32[]{:S(2)}, u32[]{:S(2)}) collective-permute-start(f32[32,256]{1,0:T(8,128)S(1)} %add_add_fusion.rest_0_), channel_id=1, source_target_pairs={{0,8},{2,10},{4,12},{6,14},{8,0},{10,2},{12,4},{14,6},{16,24},{18,... | collective-permute-start | bytes 98312 | tf_op jit(solution)/shard_map/ppermute | solution.py:445

commit v6 on v5

--- a/solution.py
+++ b/solution.py
@@ -48,6 +48,18 @@
 
 def exact(x, y, dims=NN):
     return lax.dot_general(x, y, dims, precision=HIGHEST, preferred_element_type=F32)
+
+
+def near(x, y, dims=NN):
+    xh, xl = split(x)
+    yh, yl = split(y)
+    (left,), (right,) = dims[0]
+    return lax.dot_general(
+        jnp.concatenate([xh, xh, xl], axis=left),
+        jnp.concatenate([yh, yl, yh], axis=right),
+        dims,
+        preferred_element_type=F32,
+    )
 
 
 def call(kernel, outs, n_in, smem=(), raw=(), raw_out=False, scratch=(), bytes_moved=None, large=False):
@@ -228,11 +240,11 @@
     gram = exact(paired[cases:], paired, NT)
     resid = resid_ref[...]
     lead = paired[:cases]
-    width = cases + ncoarse
+    second = places(cases, ncoarse)[0]
     frame_ref[...] = jnp.zeros_like(frame_ref)
-    frame_ref[:, 0:cases] = gram[:, :cases]
-    frame_ref[:, cases:width] = to_lanes(gram[:, cases:], wide_ref)[:, :ncoarse]
-    frame_ref[:, 3 * width : 3 * width + cases] = exact(own[cases:], resid, NT)
+    frame_ref[:, 0:cases] = exact(own[cases:], resid, NT)
+    frame_ref[:, cases : cases + ncoarse] = to_lanes(gram[:, cases:], wide_ref)[:, :ncoarse]
+    frame_ref[:, second : second + cases] = gram[:, :cases]
     scalar_ref[...] = jnp.zeros_like(scalar_ref)
     scalar_ref[0:1, :] = row_sums(resid * own[:cases])
     scalar_ref[1:2, :] = row_sums(lead * lead)
@@ -292,11 +304,15 @@
     width = cases + ncoarse
     tall_ref[...] = jnp.zeros_like(tall_ref)
     tall_ref[:FRAME, :] = frame_ref[...]
-    for at, block in ((width, cross), (2 * width, gram)):
+    second = places(cases, ncoarse)[0]
+    for block, at, far in (
+        (cross, width, width + cases),
+        (gram, second + width, second + cases),
+    ):
         tall_ref[:FRAME, at : at + cases] = block[:, :cases]
-        tall_ref[:FRAME, at + cases : at + width] = to_lanes(block[:, cases:], wide_ref)[:, :ncoarse]
+        tall_ref[:FRAME, far : far + ncoarse] = to_lanes(block[:, cases:], wide_ref)[:, :ncoarse]
     pay_ref[...] = pltpu.roll(tall_ref[...], (frame_start() + ncoarse) % ncoarse, 0)
-    at = 3 * width + cases
+    at = second + width + cases
     pay_ref[0:8, at : at + cases] = scalar_ref[...]
     pay_ref[2:3, at : at + cases] = row_sums(own[:cases] * first[:cases])
     pay_ref[3:4, at : at + cases] = row_sums(lead * lead)
@@ -358,21 +374,32 @@
     def total(value):
         return jnp.sum(value, axis=0, keepdims=True)
 
-    def piece(k):
-        at = (k // 2) * width + (k % 2) * cases
-        return pay[:, at : at + (ncoarse if k % 2 and k < 6 else cases)]
-
-    g12, g22, g14, g24, g34, g44, u0, scalars = (piece(k) for k in range(8))
+    lead, full = places(cases, ncoarse)
+    one, two = pay[:, :lead], pay[:, lead:]
+    tile = slice(0, 128)
+    u0, g12 = one[:, tile], two[:, tile]
+    g14 = pltpu.roll(one, lead - width, 1)[:, tile]
+    g34 = pltpu.roll(two, full - lead - width, 1)[:, tile]
+    scalars = pltpu.roll(two[0:8], full - lead - width - cases, 1)[:, tile]
     r0d, g11, g13, g33 = (scalars[k : k + 1] for k in range(4))
     inverse = inverse_ref[...]
-    y0 = exact(inverse, u0)
-    stacked = exact(jnp.concatenate([g22, g24, g44], axis=0), y0)
-    y22, y24, y44 = (stacked[k * ncoarse : (k + 1) * ncoarse] for k in range(3))
+    y0 = near(inverse, u0)
+
+    def picked(left, at, y):
+        def none(rows):
+            return [jnp.zeros((rows, 128), F32)] if rows else []
+
+        rest = left.shape[1] - at - ncoarse
+        return near(left, jnp.concatenate(none(at) + [y] + none(rest), axis=0))
+
+    y22 = picked(one, cases, y0)
+    y24 = picked(one, width + cases, y0)
+    y44 = picked(two, cases, y0)
     rz0 = r0d + total(u0 * y0)
     pq0 = g11 + total(y0 * (2.0 * g12 + y22))
     alpha = rz0 / pq0
     u1 = u0 - alpha * (g12 + y22)
-    y1 = exact(inverse, u1)
+    y1 = near(inverse, u1)
     cross = g13 + total(y0 * g14)
     rz1 = (
         r0d
@@ -381,26 +408,26 @@
         + total(u1 * y1)
     )
     beta = rz1 / rz0
-    lead = 1.0 + beta
+    ahead = 1.0 + beta
     coarse = y1 + beta * y0
-    c22 = exact(g22, y1) + beta * y22
+    c22 = picked(one, cases, y1) + beta * y22
     pq1 = (
-        lead * (lead * g11 + 2.0 * total(coarse * g12) - 2.0 * alpha * cross)
+        ahead * (ahead * g11 + 2.0 * total(coarse * g12) - 2.0 * alpha * cross)
         + total(coarse * (c22 - 2.0 * alpha * (g14 + y24)))
         + alpha * alpha * (g33 + total(y0 * (2.0 * g34 + y44)))
     )
     alpha1 = rz1 / pq1
     lower = alpha1 * alpha
-    upper = alpha + alpha1 * lead
+    upper = alpha + alpha1 * ahead
     first = alpha * y0 + alpha1 * coarse
     second = -lower * y0
     begin = frame_start()
     first16 = window(first, begin, FRAME)
-    weights = jnp.concatenate([first16, window(second, begin, FRAME)], axis=0)
-    weights2 = jnp.concatenate([first16, window(second, begin - STEP, WIDE)], axis=0)
+    weights = jnp.concatenate([first16, window(second, begin, FRAME)], axis=0)[:, :cases]
+    weights2 = jnp.concatenate([first16, window(second, begin - STEP, WIDE)], axis=0)[:, :cases]
     row = lax.broadcasted_iota(jnp.int32, (8, 256), 0)
     half = lax.broadcasted_iota(jnp.int32, (8, 256), 1) // 128
-    pair = jnp.concatenate([upper, lower, jnp.zeros((6, cases), F32)], axis=0)
+    pair = jnp.concatenate([upper, lower, jnp.zeros((6, 128), F32)], axis=0)[:, :cases]
     columns = exact(pair, jnp.where(row == half, 1.0, 0.0), TN)
     upper = jnp.concatenate([columns[:, :128]] * (OWN // 128), axis=1)
     lower = jnp.concatenate([columns[:, 128:]] * (OWN // 128), axis=1)
@@ -415,13 +442,13 @@
     field = (
         upper * start[:cases]
         - lower * scaled[:cases]
-        + exact(weights, jnp.concatenate([start[cases:], scaled[cases:]], axis=0), TN)
+        + near(weights, jnp.concatenate([start[cases:], scaled[cases:]], axis=0), TN)
     )
     resid2 = (
         resid_ref[...]
         - upper * image[:cases]
         + lower * image2
-        - exact(weights2, jnp.concatenate([image[cases:], coarse2], axis=0), TN)
+        - near(weights2, jnp.concatenate([image[cases:], coarse2], axis=0), TN)
     )
     copies = []
     for k, (value, out, buf) in enumerate(
@@ -435,6 +462,12 @@
         copies[-1].start()
     for copy in copies:
         copy.wait()
+
+
+def places(cases, ncoarse):
+    both = cases + ncoarse
+    lead = lanes_for(2 * both)
+    return lead, lead + lanes_for(2 * cases + both)
 
 
 def lanes_for(width):
@@ -522,7 +555,7 @@
     ghost_a, ghost_b = across(side_a, side_b, count, parts)
     ends = (side_a, side_b, ghost_a, ghost_b)
 
-    lanes = lanes_for(3 * (cases + ncoarse) + 2 * cases)
+    lanes = places(cases, ncoarse)[1]
     wide = pltpu.VMEM((FRAME, lanes_for(ncoarse)), F32)
     strain, own_a, own_b = run(
         first_apply, [shape(live, ROWS), shape(2 * live, EDGE), shape(2 * live, EDGE)], 6

time: 34.3 us -> 33.7 us (0.983)
  Pallas kernels: 11.1 us -> 10.4 us
    pallas_call x1, Pallas kernels: 2.91 us -> 2.28 us  [body(): run(functools.partial(finish, ncoarse=ncoarse, n_pay=len(pays)), [shape(c...]
  transfers between devices with their start and end apart: 13 -> 13, of which waited for: 6 -> 6; matrix products, arithmetic and copies ran while one was open for 0% -> 0% of each run, Pallas kernels for 14% -> 15%
where the time goes in v6:
time: 33.7 us; the launch traced here: 33.4 us
  starting transfers between devices  15.1 us (45%)
  Pallas kernels  10.4 us (31%)
  waiting for transfers between devices  7 us (21%)
  between operations  0.78 us (2%)
    ppermute x6, starting transfers between devices, swap(): lax.ppermute(x, 'sub', [(i, i ^ k) for i in range(count)])  6.54 us
    ppermute x3, starting transfers between devices, across(): lax.ppermute(b, ('sub', 'rhs'), pairs + [(j, i) for i, j in pairs])  4.99 us
    ppermute x6, waiting for transfers between devices, swap(): lax.ppermute(x, 'sub', [(i, i ^ k) for i in range(count)])  4 us
    ppermute x1, starting transfers between devices, body(): lax.ppermute(corner_basis, 'rhs', [((i + k) % parts, i) for i in range(pa...  3 us
    ppermute x3, waiting for transfers between devices, across(): lax.ppermute(b, ('sub', 'rhs'), pairs + [(j, i) for i, j in pairs])  2.99 us
    pallas_call x1, Pallas kernels, body(): run(functools.partial(finish, ncoarse=ncoarse, n_pay=len(pays)), [shape(c...  2.28 us
    pallas_call x1, Pallas kernels, body(): call(load_blocks, [packed, packed], 1, raw=(0,), scratch=[pltpu.VMEM((B *...  2.14 us
    pallas_call x1, Pallas kernels, body(): run(assemble, [dense, dense], 5, smem=(0,))  1.66 us
  transfers between devices with their start and end apart: 13, of which 6 were waited for; matrix products, arithmetic and copies ran while one was open for 0% of the time, Pallas kernels for 15%

profile of v6, /device:TPU:0, one launch (start us, length us, event | category | flops | bytes accessed | tf_op | source)
XLA Modules:
  0.0 33.4 jit_solution(4697223530439727888)
XLA Ops:
  0.6 0.0 copy-start.3
  0.6 0.0 copy-start.2
  0.7 0.0 copy-start.5
  0.7 0.0 copy-start.6
  0.7 0.0 copy-start
  0.7 3.0 %collective-permute-start = (f32[4,512]{1,0:T(4,128)}, f32[4,512]{1,0:T(4,128)S(1)}, u32[]{:S(2)}, u32[]{:S(2)}) collective-permute-start(f32[4,512]{1,0:T(4,128)} %rest_0_.1), channel_id=1, source_target_pairs={{1,0},{0,1},{3,2},{2,3},{5,4},{4,5},{7,6},{6,7},{9,8},{8,9},{11,10... | collective-permute-start | bytes 24584 | tf_op jit(solution)/shard_map/ppermute | solution.py:528
  3.7 0.0 copy-start.4
  3.7 2.1 %shard_map.95 = (bf16[256,4096]{1,0:T(8,128)(2,1)S(1)}, bf16[256,4096]{1,0:T(8,128)(2,1)S(1)}) custom-call(f32[27,8,4096]{2,1,0:T(8,128)} %bitcast.3), custom_call_target="tpu_custom_call" | custom-call | bytes 16777216 | tf_op jit(solution)/shard_map/pallas_call | solution.py:532
  5.8 0.0 collective-permute-done.rest_1_
  5.8 0.0 copy-done.3
  5.9 0.0 copy-done.2
  5.9 0.0 copy-done.5
  5.9 0.0 copy-done.6
  5.9 0.0 copy-done
  5.9 0.8 %shard_map.96 = (f32[32,512]{1,0:T(8,128)S(1)}, f32[56,256]{1,0:T(8,128)S(1)}, f32[56,256]{1,0:T(8,128)S(1)}) custom-call(s32[1,2,4]{2,1,0:T(2,128)S(1)} %copy-done.2, s32[1,8]{1,0:T(1,128)S(1)} %copy-done.6, f32[32,512]{1,0:T(8,128)S(1)} %copy-done, f32[1,512]{1,0:T(1,128)S(1)} %bitcast.2, bf16[256,4096]{1,0:T(8,128)(2,1)S(1)} %get-tuple-element.21.after_ref.wh_ref, ...), custom_call_target="tpu_custom_call" | custom-call | tf_op jit(solution)/shard_map/pallas_call | solution.py:544
  6.7 1.8 %collective-permute-start.2 = (f32[56,256]{1,0:T(8,128)S(1)}, f32[56,256]{1,0:T(8,128)S(1)}, u32[]{:S(2)}, u32[]{:S(2)}) collective-permute-start(f32[56,256]{1,0:T(8,128)S(1)} %get-tuple-element.24.b_ref), channel_id=1, source_target_pairs={{2,4},{3,5},{6,8},{7,9},{10,12},{11,13},{14,16},{15,17},{18,20},{1... | collective-permute-start | bytes 172040 | tf_op jit(solution)/shard_map/ppermute | solution.py:501
  8.4 0.1 collective-permute-start.1
  8.6 0.0 copy-done.4
  8.6 1.7 %shard_map.97 = (bf16[512,1024]{1,0:T(8,128)(2,1)S(1)}, bf16[512,1024]{1,0:T(8,128)(2,1)S(1)}) custom-call(s32[1,2,4]{2,1,0:T(2,128)S(1)} %copy-done.2, s32[8,27]{1,0:T(8,128)S(1)} %copy-done.4, bf16[256,4096]{1,0:T(8,128)(2,1)S(1)} %get-tuple-element.21.after_ref.wh_ref, bf16[256,4096]{1,0:T(8,128)(2,1)S(1)} %get-tuple-element.25.wl_ref, ...), custom_call_target="tpu_custom_call" | custom-call | tf_op jit(solution)/shard_map/pallas_call | solution.py:552
  10.2 0.7 %collective-permute-done.2.gb_ref = f32[56,256]{1,0:T(8,128)S(1)} collective-permute-done((f32[56,256]{1,0:T(8,128)S(1)}, f32[56,256]{1,0:T(8,128)S(1)}, u32[]{:S(2)}, u32[]{:S(2)}) %collective-permute-start.2) | collective-permute-done | bytes 57376 | tf_op jit(solution)/shard_map/ppermute | solution.py:501
  10.9 0.0 collective-permute-done.1.ga_ref
  10.9 1.2 %shard_map.98 = (f32[48,512]{1,0:T(8,128)S(1)}, f32[96,256]{1,0:T(8,128)S(1)}, f32[96,256]{1,0:T(8,128)S(1)}) custom-call(f32[56,256]{1,0:T(8,128)S(1)} %get-tuple-element.23.after_ref.a_ref, f32[56,256]{1,0:T(8,128)S(1)} %get-tuple-element.24.b_ref, f32[56,256]{1,0:T(8,128)S(1)} %collective-permute-done.1.ga_ref, ...), custom_call_target="tpu_custom_call" | custom-call | tf_op jit(solution)/shard_map/pallas_call | solution.py:560
  12.1 0.1 collective-permute-start.3
  12.2 1.8 %collective-permute-start.4 = (f32[96,256]{1,0:T(8,128)S(1)}, f32[96,256]{1,0:T(8,128)S(1)}, u32[]{:S(2)}, u32[]{:S(2)}) collective-permute-start(f32[96,256]{1,0:T(8,128)S(1)} %get-tuple-element.29.own_b_ref), channel_id=1, source_target_pairs={{2,4},{3,5},{6,8},{7,9},{10,12},{11,13},{14,16},{15,17},{18,20},{1... | collective-permute-start | bytes 294920 | tf_op jit(solution)/shard_map/ppermute | solution.py:501
  13.9 0.6 %shard_map.99 = (f32[16,256]{1,0:T(8,128)S(1)}, f32[8,32]{1,0:T(8,128)S(1)}) custom-call(f32[32,512]{1,0:T(8,128)S(1)} %get-tuple-element.22.resid_ref, f32[56,256]{1,0:T(8,128)S(1)} %get-tuple-element.23.after_ref.a_ref, f32[56,256]{1,0:T(8,128)S(1)} %get-tuple-element.24.b_ref, f32[48,512]{1,0:T(8,128)S(1)} %get-tuple-element.30.strain_ref), custom_call_target="tpu_custom_call" | custom-call | tf_op jit(solution)/shard_map/pallas_call | solution.py:564
  14.6 0.0 collective-permute-done.3.got_a_ref
  14.6 2.3 %collective-permute-done.4.got_b_ref = f32[96,256]{1,0:T(8,128)S(1)} collective-permute-done((f32[96,256]{1,0:T(8,128)S(1)}, f32[96,256]{1,0:T(8,128)S(1)}, u32[]{:S(2)}, u32[]{:S(2)}) %collective-permute-start.4) | collective-permute-done | bytes 98336 | tf_op jit(solution)/shard_map/ppermute | solution.py:501
  16.9 0.0 copy-start.1
  16.9 1.3 %shard_map.100 = (f32[48,512]{1,0:T(8,128)S(1)}, f32[48,512]{1,0:T(8,128)S(1)}, f32[48,512]{1,0:T(8,128)S(1)}, f32[32,256]{1,0:T(8,128)S(1)}) custom-call(f32[56,256]{1,0:T(8,128)S(1)} %get-tuple-element.23.after_ref.a_ref, f32[56,256]{1,0:T(8,128)S(1)} %get-tuple-element.24.b_ref, f32[56,256]{1,0:T(8,128)S(1)} %collective-permute-done.1.ga_ref, ...), custom_call_target="tpu_custom_call" | custom-call | tf_op jit(solution)/shard_map/pallas_call | solution.py:570
  18.2 2.2 %collective-permute-start.9 = (f32[32,256]{1,0:T(8,128)S(1)}, f32[32,256]{1,0:T(8,128)S(1)}, u32[]{:S(2)}, u32[]{:S(2)}) collective-permute-start(f32[32,256]{1,0:T(8,128)S(1)} %get-tuple-element.39), channel_id=1, source_target_pairs={{0,6},{2,4},{4,2},{6,0},{8,14},{10,12},{12,10},{14,8},{16,22},{18,... | collective-permute-start | bytes 98312 | tf_op jit(solution)/shard_map/ppermute | solution.py:478
  20.4 0.0 collective-permute-start.8
  20.4 0.2 collective-permute-start.7
  20.6 0.5 %shard_map.101 = (f32[48,512]{1,0:T(8,128)S(1)}, f32[48,256]{1,0:T(8,128)S(1)}, f32[48,256]{1,0:T(8,128)S(1)}) custom-call(f32[48,512]{1,0:T(8,128)S(1)} %get-tuple-element.34.scaled_ref, f32[48,512]{1,0:T(8,128)S(1)} %get-tuple-element.35.strain_ref, bf16[512,1024]{1,0:T(8,128)(2,1)S(1)} %get-tuple-element.26.high_ref, ...), custom_call_target="tpu_custom_call" | custom-call | tf_op jit(solution)/shard_map/pallas_call | solution.py:579
  21.1 0.3 collective-permute-start.5
  21.4 1.5 %collective-permute-start.6 = (f32[48,256]{1,0:T(8,128)S(1)}, f32[48,256]{1,0:T(8,128)S(1)}, u32[]{:S(2)}, u32[]{:S(2)}) collective-permute-start(f32[48,256]{1,0:T(8,128)S(1)} %get-tuple-element.38), channel_id=1, source_target_pairs={{2,4},{3,5},{6,8},{7,9},{10,12},{11,13},{14,16},{15,17},{18,20},{1... | collective-permute-start | bytes 147464 | tf_op jit(solution)/shard_map/ppermute | solution.py:501
  22.9 0.0 collective-permute-done.9
  22.9 1.4 %collective-permute-done.8 = f32[32,256]{1,0:T(8,128)S(1)} collective-permute-done((f32[32,256]{1,0:T(8,128)S(1)}, f32[32,256]{1,0:T(8,128)S(1)}, u32[]{:S(2)}, u32[]{:S(2)}) %collective-permute-start.8) | collective-permute-done | bytes 32800 | tf_op jit(solution)/shard_map/ppermute | solution.py:478
  24.3 0.0 collective-permute-done.7
  24.3 2.1 %collective-permute-start.12 = (f32[32,256]{1,0:T(8,128)S(1)}, f32[32,256]{1,0:T(8,128)S(1)}, u32[]{:S(2)}, u32[]{:S(2)}) collective-permute-start(f32[32,256]{1,0:T(8,128)S(1)} %add_add_fusion.rest_0_), channel_id=1, source_target_pairs={{0,26},{2,24},{4,30},{6,28},{8,18},{10,16},{12,22},{14,20},{16,10}... | collective-permute-start | bytes 98312 | tf_op jit(solution)/shard_map/ppermute | solution.py:478
  26.4 0.8 %collective-permute-start.11 = (f32[32,256]{1,0:T(8,128)S(1)}, f32[32,256]{1,0:T(8,128)S(1)}, u32[]{:S(2)}, u32[]{:S(2)}) collective-permute-start(f32[32,256]{1,0:T(8,128)S(1)} %add_add_fusion.rest_0_), channel_id=1, source_target_pairs={{0,18},{2,16},{4,22},{6,20},{8,26},{10,24},{12,30},{14,28},{16,2},... | collective-permute-start | bytes 98312 | tf_op jit(solution)/shard_map/ppermute | solution.py:478
  27.1 1.3 %collective-permute-start.10 = (f32[32,256]{1,0:T(8,128)S(1)}, f32[32,256]{1,0:T(8,128)S(1)}, u32[]{:S(2)}, u32[]{:S(2)}) collective-permute-start(f32[32,256]{1,0:T(8,128)S(1)} %add_add_fusion.rest_0_), channel_id=1, source_target_pairs={{0,8},{2,10},{4,12},{6,14},{8,0},{10,2},{12,4},{14,6},{16,24},{18,... | collective-permute-start | bytes 98312 | tf_op jit(solution)/shard_map/ppermute | solution.py:478
  28.5 0.0 collective-permute-done.5.got_a_ref
  28.5 0.0 collective-permute-done.6.got_b_ref
  28.5 1.1 %collective-permute-done.12.rest_3_ = f32[32,256]{1,0:T(8,128)S(1)} collective-permute-done((f32[32,256]{1,0:T(8,128)S(1)}, f32[32,256]{1,0:T(8,128)S(1)}, u32[]{:S(2)}, u32[]{:S(2)}) %collective-permute-start.12) | collective-permute-done | bytes 32800 | tf_op jit(solution)/shard_map/ppermute | solution.py:478
  29.7 1.1 %collective-permute-done.11.rest_2_ = f32[32,256]{1,0:T(8,128)S(1)} collective-permute-done((f32[32,256]{1,0:T(8,128)S(1)}, f32[32,256]{1,0:T(8,128)S(1)}, u32[]{:S(2)}, u32[]{:S(2)}) %collective-permute-start.11) | collective-permute-done | bytes 32800 | tf_op jit(solution)/shard_map/ppermute | solution.py:478
  30.7 0.4 %collective-permute-done.10.rest_1_ = f32[32,256]{1,0:T(8,128)S(1)} collective-permute-done((f32[32,256]{1,0:T(8,128)S(1)}, f32[32,256]{1,0:T(8,128)S(1)}, u32[]{:S(2)}, u32[]{:S(2)}) %collective-permute-start.10) | collective-permute-done | bytes 32800 | tf_op jit(solution)/shard_map/ppermute | solution.py:478
  31.1 0.0 copy-done.1
  31.1 2.3 %shard_map.102 = (f32[32,512]{1,0:T(8,128)}, f32[32,512]{1,0:T(8,128)}) custom-call(s32[1,2,4]{2,1,0:T(2,128)S(1)} %copy-done.2, f32[32,32]{1,0:T(8,128)S(1)} %copy-done.1, f32[32,512]{1,0:T(8,128)S(1)} %get-tuple-element.22.resid_ref, f32[56,256]{1,0:T(8,128)S(1)} %get-tuple-element.23.after_ref.a_ref, f32[56,256]{1,0:T(8,128)S(1)} %get-tuple-element.24.b_ref, ...), custom_call_target="tpu_custom_call" | custom-call | tf_op jit(solution)/shard_map/pallas_call | solution.py:584
  (1 shorter events, 0.0 us)
Async XLA Ops:
  0.6 5.2 %copy-start.3 = (f32[4,512]{1,0:T(4,128)S(1)}, f32[4,512]{1,0:T(4,128)}, u32[]{:S(2)}) copy-start(f32[4,512]{1,0:T(4,128)} %rest_0_.1) | copy-start | bytes 24580
  0.6 5.2 %copy-start.2 = (s32[1,2,4]{2,1,0:T(2,128)S(1)}, s32[1,2,4]{2,1,0:T(2,128)}, u32[]{:S(2)}) copy-start(s32[1,2,4]{2,1,0:T(2,128)} %rows_ref.5) | copy-start | bytes 100
  0.7 5.2 %copy-start.5 = (f32[512]{0:T(512)S(1)}, f32[512]{0:T(512)}, u32[]{:S(2)}) copy-start(f32[512]{0:T(512)} %param.14) | copy-start | bytes 6148
  0.7 5.2 %copy-start.6 = (s32[1,8]{1,0:T(1,128)S(1)}, s32[1,8]{1,0:T(1,128)}, u32[]{:S(2)}) copy-start(s32[1,8]{1,0:T(1,128)} %owner_ref.1) | copy-start | bytes 100
  0.7 5.2 %copy-start = (f32[32,512]{1,0:T(8,128)S(1)}, f32[32,512]{1,0:T(8,128)}, u32[]{:S(2)}) copy-start(f32[32,512]{1,0:T(8,128)} %right_ref.1) | copy-start | bytes 196612
  0.7 5.2 %collective-permute-start = (f32[4,512]{1,0:T(4,128)}, f32[4,512]{1,0:T(4,128)S(1)}, u32[]{:S(2)}, u32[]{:S(2)}) collective-permute-start(f32[4,512]{1,0:T(4,128)} %rest_0_.1), channel_id=1, source_target_pairs={{1,0},{0,1},{3,2},{2,3},{5,4},{4,5},{7,6},{6,7},{9,8},{8,9},{11,10... | collective-permute-start | bytes 24584 | tf_op jit(solution)/shard_map/ppermute | solution.py:528
  3.7 4.9 %copy-start.4 = (s32[8,27]{1,0:T(8,128)S(1)}, s32[8,27]{1,0:T(8,128)}, u32[]{:S(2)}) copy-start(s32[8,27]{1,0:T(8,128)} %columns_ref.1) | copy-start | bytes 2596
  6.7 4.2 %collective-permute-start.2 = (f32[56,256]{1,0:T(8,128)S(1)}, f32[56,256]{1,0:T(8,128)S(1)}, u32[]{:S(2)}, u32[]{:S(2)}) collective-permute-start(f32[56,256]{1,0:T(8,128)S(1)} %get-tuple-element.24.b_ref), channel_id=1, source_target_pairs={{2,4},{3,5},{6,8},{7,9},{10,12},{11,13},{14,16},{15,17},{18,20},{1... | collective-permute-start | bytes 172040 | tf_op jit(solution)/shard_map/ppermute | solution.py:501
  8.4 2.5 %collective-permute-start.1 = (f32[56,256]{1,0:T(8,128)S(1)}, f32[56,256]{1,0:T(8,128)S(1)}, u32[]{:S(2)}, u32[]{:S(2)}) collective-permute-start(f32[56,256]{1,0:T(8,128)S(1)} %get-tuple-element.23.after_ref.a_ref), channel_id=1, source_target_pairs={{0,2},{2,0},{4,6},{6,4},{8,10},{10,8},{12,14},{14,12},{16,18},{18,... | collective-permute-start | bytes 172040 | tf_op jit(solution)/shard_map/ppermute | solution.py:496
  12.1 2.5 %collective-permute-start.3 = (f32[96,256]{1,0:T(8,128)S(1)}, f32[96,256]{1,0:T(8,128)S(1)}, u32[]{:S(2)}, u32[]{:S(2)}) collective-permute-start(f32[96,256]{1,0:T(8,128)S(1)} %get-tuple-element.28.own_a_ref), channel_id=1, source_target_pairs={{0,2},{2,0},{4,6},{6,4},{8,10},{10,8},{12,14},{14,12},{16,18},{18,... | collective-permute-start | bytes 294920 | tf_op jit(solution)/shard_map/ppermute | solution.py:496
  12.2 4.7 %collective-permute-start.4 = (f32[96,256]{1,0:T(8,128)S(1)}, f32[96,256]{1,0:T(8,128)S(1)}, u32[]{:S(2)}, u32[]{:S(2)}) collective-permute-start(f32[96,256]{1,0:T(8,128)S(1)} %get-tuple-element.29.own_b_ref), channel_id=1, source_target_pairs={{2,4},{3,5},{6,8},{7,9},{10,12},{11,13},{14,16},{15,17},{18,20},{1... | collective-permute-start | bytes 294920 | tf_op jit(solution)/shard_map/ppermute | solution.py:501
  16.9 14.2 %copy-start.1 = (f32[32,32]{1,0:T(8,128)S(1)}, f32[32,32]{1,0:T(8,128)}, u32[]{:S(2)}) copy-start(f32[32,32]{1,0:T(8,128)} %inverse_ref.1) | copy-start | bytes 12292
  18.2 4.7 %collective-permute-start.9 = (f32[32,256]{1,0:T(8,128)S(1)}, f32[32,256]{1,0:T(8,128)S(1)}, u32[]{:S(2)}, u32[]{:S(2)}) collective-permute-start(f32[32,256]{1,0:T(8,128)S(1)} %get-tuple-element.39), channel_id=1, source_target_pairs={{0,6},{2,4},{4,2},{6,0},{8,14},{10,12},{12,10},{14,8},{16,22},{18,... | collective-permute-start | bytes 98312 | tf_op jit(solution)/shard_map/ppermute | solution.py:478
  20.4 3.9 %collective-permute-start.8 = (f32[32,256]{1,0:T(8,128)S(1)}, f32[32,256]{1,0:T(8,128)S(1)}, u32[]{:S(2)}, u32[]{:S(2)}) collective-permute-start(f32[32,256]{1,0:T(8,128)S(1)} %get-tuple-element.39), channel_id=1, source_target_pairs={{0,4},{2,6},{4,0},{6,2},{8,12},{10,14},{12,8},{14,10},{16,20},{18,... | collective-permute-start | bytes 98312 | tf_op jit(solution)/shard_map/ppermute | solution.py:478
  20.4 3.9 %collective-permute-start.7 = (f32[32,256]{1,0:T(8,128)S(1)}, f32[32,256]{1,0:T(8,128)S(1)}, u32[]{:S(2)}, u32[]{:S(2)}) collective-permute-start(f32[32,256]{1,0:T(8,128)S(1)} %get-tuple-element.39), channel_id=1, source_target_pairs={{0,2},{2,0},{4,6},{6,4},{8,10},{10,8},{12,14},{14,12},{16,18},{18,... | collective-permute-start | bytes 98312 | tf_op jit(solution)/shard_map/ppermute | solution.py:478
  21.1 7.5 %collective-permute-start.5 = (f32[48,256]{1,0:T(8,128)S(1)}, f32[48,256]{1,0:T(8,128)S(1)}, u32[]{:S(2)}, u32[]{:S(2)}) collective-permute-start(f32[48,256]{1,0:T(8,128)S(1)} %get-tuple-element.37), channel_id=1, source_target_pairs={{0,2},{2,0},{4,6},{6,4},{8,10},{10,8},{12,14},{14,12},{16,18},{18,... | collective-permute-start | bytes 147464 | tf_op jit(solution)/shard_map/ppermute | solution.py:496
  21.4 7.1 %collective-permute-start.6 = (f32[48,256]{1,0:T(8,128)S(1)}, f32[48,256]{1,0:T(8,128)S(1)}, u32[]{:S(2)}, u32[]{:S(2)}) collective-permute-start(f32[48,256]{1,0:T(8,128)S(1)} %get-tuple-element.38), channel_id=1, source_target_pairs={{2,4},{3,5},{6,8},{7,9},{10,12},{11,13},{14,16},{15,17},{18,20},{1... | collective-permute-start | bytes 147464 | tf_op jit(solution)/shard_map/ppermute | solution.py:501
  24.3 5.3 %collective-permute-start.12 = (f32[32,256]{1,0:T(8,128)S(1)}, f32[32,256]{1,0:T(8,128)S(1)}, u32[]{:S(2)}, u32[]{:S(2)}) collective-permute-start(f32[32,256]{1,0:T(8,128)S(1)} %add_add_fusion.rest_0_), channel_id=1, source_target_pairs={{0,26},{2,24},{4,30},{6,28},{8,18},{10,16},{12,22},{14,20},{16,10}... | collective-permute-start | bytes 98312 | tf_op jit(solution)/shard_map/ppermute | solution.py:478
  26.4 4.3 %collective-permute-start.11 = (f32[32,256]{1,0:T(8,128)S(1)}, f32[32,256]{1,0:T(8,128)S(1)}, u32[]{:S(2)}, u32[]{:S(2)}) collective-permute-start(f32[32,256]{1,0:T(8,128)S(1)} %add_add_fusion.rest_0_), channel_id=1, source_target_pairs={{0,18},{2,16},{4,22},{6,20},{8,26},{10,24},{12,30},{14,28},{16,2},... | collective-permute-start | bytes 98312 | tf_op jit(solution)/shard_map/ppermute | solution.py:478
  27.1 3.9 %collective-permute-start.10 = (f32[32,256]{1,0:T(8,128)S(1)}, f32[32,256]{1,0:T(8,128)S(1)}, u32[]{:S(2)}, u32[]{:S(2)}) collective-permute-start(f32[32,256]{1,0:T(8,128)S(1)} %add_add_fusion.rest_0_), channel_id=1, source_target_pairs={{0,8},{2,10},{4,12},{6,14},{8,0},{10,2},{12,4},{14,6},{16,24},{18,... | collective-permute-start | bytes 98312 | tf_op jit(solution)/shard_map/ppermute | solution.py:478

commit v7 on v6

--- a/solution.py
+++ b/solution.py
@@ -152,6 +152,11 @@
                 low_ref[at : at + 16, 128 * m : 128 * (m + 1)] = tl
 
 
+def turn(high_ref, low_ref, high_t_ref, low_t_ref):
+    high_t_ref[...] = high_ref[...].T
+    low_t_ref[...] = low_ref[...].T
+
+
 def sides(rows_ref, owner_ref, right_ref, scale_ref, after_ref, *rest, parts):
     basis_refs = rest[:parts]
     resid_ref, side_a_ref, side_b_ref, blk_ref = rest[parts:]
@@ -200,7 +205,9 @@
     return jnp.concatenate([rows[:cases], turned(rows[cases:], upper)], axis=0)
 
 
-def first_apply(a_ref, b_ref, ga_ref, gb_ref, high_ref, low_ref, strain_ref, send_a_ref, send_b_ref):
+def first_apply(
+    a_ref, b_ref, ga_ref, gb_ref, high_ref, low_ref, high_t, low_t, strain_ref, send_a_ref, send_b_ref
+):
     live = strain_ref.shape[0]
     odd = lax.axis_index("sub") % 2 == 1
     field = jnp.concatenate(
@@ -212,7 +219,7 @@
         ],
         axis=1,
     )
-    strain = times(field, high_ref[...], low_ref[...], NT)
+    strain = times(field, high_t[...], low_t[...], NN)
     strain_ref[...] = strain
     back = times(strain, high_ref[...], low_ref[...], NN)
     send_a_ref[:live, :] = field[:, :EDGE] + back[:, :EDGE]
@@ -259,8 +266,8 @@
     own_b_ref,
     got_a_ref,
     got_b_ref,
-    high_ref,
-    low_ref,
+    high_t,
+    low_t,
     frame_ref,
     scalar_ref,
     strain_ref,
@@ -291,7 +298,7 @@
         [a_ref[end, :], b_ref[end, :], ga_ref[end, :], inner * gb_ref[end, :]], axis=1
     )
     field = scale * image
-    strain = times(field, high_ref[...], low_ref[...], NT)
+    strain = times(field, high_t[...], low_t[...], NN)
     own = field[:, :OWN]
     first = image[:, :OWN]
     strain_ref[...] = strain
@@ -552,14 +559,16 @@
     high, low = run(assemble, [dense, dense], 5, smem=(0,))(
         interface_rows, block_columns, wh, wl, side_a
     )
+    turned_g = jax.ShapeDtypeStruct((EXT, ROWS), BF16)
+    high_t, low_t = run(turn, [turned_g, turned_g], 2)(high, low)
     ghost_a, ghost_b = across(side_a, side_b, count, parts)
     ends = (side_a, side_b, ghost_a, ghost_b)
 
     lanes = places(cases, ncoarse)[1]
     wide = pltpu.VMEM((FRAME, lanes_for(ncoarse)), F32)
     strain, own_a, own_b = run(
-        first_apply, [shape(live, ROWS), shape(2 * live, EDGE), shape(2 * live, EDGE)], 6
-    )(*ends, high, low)
+        first_apply, [shape(live, ROWS), shape(2 * live, EDGE), shape(2 * live, EDGE)], 8
+    )(*ends, high, low, high_t, low_t)
     got_a, got_b = across(own_a, own_b, count, parts)
     frame, scalars = run(
         functools.partial(first_sums, ncoarse=ncoarse),
@@ -572,7 +581,7 @@
         [shape(live, ROWS), shape(live, OWN), shape(live, OWN), shape(ncoarse, lanes)],
         12,
         scratch=[wide, pltpu.VMEM((ncoarse, lanes), F32)],
-    )(*ends, own_a, own_b, got_a, got_b, high, low, frame, scalars)
+    )(*ends, own_a, own_b, got_a, got_b, high_t, low_t, frame, scalars)
     for steps in rounds[:-1]:
         pay = sum(swap(pay, steps, count), pay)
     pays = [pay] + swap(pay, rounds[-1], count)

time: 33.7 us -> 33.1 us (0.982)
  waiting for transfers between devices: 7 us -> 6.64 us
    pallas_call x0 -> x1, Pallas kernels: none -> 0.59 us  [body(): high_t, low_t = run(turn, [turned_g, turned_g], 2)(high, low)]
    ppermute x3, waiting for transfers between devices: 2.99 us -> 2.62 us  [across(): lax.ppermute(b, ('sub', 'rhs'), pairs + [(j, i) for i, j in pairs])]
  transfers between devices with their start and end apart: 13 -> 13, of which waited for: 6 -> 6; matrix products, arithmetic and copies ran while one was open for 0% -> 0% of each run, Pallas kernels for 15% -> 17%
where the time goes in v7:
time: 33.1 us; the launch traced here: 32.8 us
  starting transfers between devices  14.9 us (45%)
  Pallas kernels  10.5 us (32%)
  waiting for transfers between devices  6.64 us (20%)
  between operations  0.77 us (2%)
    ppermute x6, starting transfers between devices, swap(): lax.ppermute(x, 'sub', [(i, i ^ k) for i in range(count)])  6.31 us
    ppermute x3, starting transfers between devices, across(): lax.ppermute(b, ('sub', 'rhs'), pairs + [(j, i) for i, j in pairs])  4.69 us
    ppermute x6, waiting for transfers between devices, swap(): lax.ppermute(x, 'sub', [(i, i ^ k) for i in range(count)])  4 us
    ppermute x1, starting transfers between devices, body(): lax.ppermute(corner_basis, 'rhs', [((i + k) % parts, i) for i in range(pa...  3 us
    ppermute x3, waiting for transfers between devices, across(): lax.ppermute(b, ('sub', 'rhs'), pairs + [(j, i) for i, j in pairs])  2.62 us
    pallas_call x1, Pallas kernels, body(): run(functools.partial(finish, ncoarse=ncoarse, n_pay=len(pays)), [shape(c...  2.28 us
    pallas_call x1, Pallas kernels, body(): call(load_blocks, [packed, packed], 1, raw=(0,), scratch=[pltpu.VMEM((B *...  2.14 us
    pallas_call x1, Pallas kernels, body(): run(assemble, [dense, dense], 5, smem=(0,))  1.66 us
  transfers between devices with their start and end apart: 13, of which 6 were waited for; matrix products, arithmetic and copies ran while one was open for 0% of the time, Pallas kernels for 17%

profile of v7, /device:TPU:0, one launch (start us, length us, event | category | flops | bytes accessed | tf_op | source)
XLA Modules:
  0.0 32.8 jit_solution(5375942705774742980)
XLA Ops:
  0.6 0.0 copy-start.3
  0.6 0.0 copy-start.2
  0.7 0.0 copy-start.5
  0.7 0.0 copy-start.6
  0.7 0.0 copy-start
  0.7 3.0 %collective-permute-start = (f32[4,512]{1,0:T(4,128)}, f32[4,512]{1,0:T(4,128)S(1)}, u32[]{:S(2)}, u32[]{:S(2)}) collective-permute-start(f32[4,512]{1,0:T(4,128)} %rest_0_.1), channel_id=1, source_target_pairs={{1,0},{0,1},{3,2},{2,3},{5,4},{4,5},{7,6},{6,7},{9,8},{8,9},{11,10... | collective-permute-start | bytes 24584 | tf_op jit(solution)/shard_map/ppermute | solution.py:535
  3.7 0.0 copy-start.4
  3.7 2.1 %shard_map.95 = (bf16[256,4096]{1,0:T(8,128)(2,1)S(1)}, bf16[256,4096]{1,0:T(8,128)(2,1)S(1)}) custom-call(f32[27,8,4096]{2,1,0:T(8,128)} %bitcast.3), custom_call_target="tpu_custom_call" | custom-call | bytes 16777216 | tf_op jit(solution)/shard_map/pallas_call | solution.py:539
  5.8 0.0 collective-permute-done.rest_1_
  5.8 0.0 copy-done.3
  5.9 0.0 copy-done.2
  5.9 0.0 copy-done.5
  5.9 0.0 copy-done.6
  5.9 0.0 copy-done
  5.9 0.8 %shard_map.96 = (f32[32,512]{1,0:T(8,128)S(1)}, f32[56,256]{1,0:T(8,128)S(1)}, f32[56,256]{1,0:T(8,128)S(1)}) custom-call(s32[1,2,4]{2,1,0:T(2,128)S(1)} %copy-done.2, s32[1,8]{1,0:T(1,128)S(1)} %copy-done.6, f32[32,512]{1,0:T(8,128)S(1)} %copy-done, f32[1,512]{1,0:T(1,128)S(1)} %bitcast.2, bf16[256,4096]{1,0:T(8,128)(2,1)S(1)} %get-tuple-element.23.after_ref.wh_ref, ...), custom_call_target="tpu_custom_call" | custom-call | tf_op jit(solution)/shard_map/pallas_call | solution.py:551
  6.7 1.8 %collective-permute-start.2 = (f32[56,256]{1,0:T(8,128)S(1)}, f32[56,256]{1,0:T(8,128)S(1)}, u32[]{:S(2)}, u32[]{:S(2)}) collective-permute-start(f32[56,256]{1,0:T(8,128)S(1)} %get-tuple-element.26.b_ref), channel_id=1, source_target_pairs={{2,4},{3,5},{6,8},{7,9},{10,12},{11,13},{14,16},{15,17},{18,20},{1... | collective-permute-start | bytes 172040 | tf_op jit(solution)/shard_map/ppermute | solution.py:508
  8.4 0.1 collective-permute-start.1
  8.6 0.0 copy-done.4
  8.6 1.7 %shard_map.97 = (bf16[512,1024]{1,0:T(8,128)(2,1)S(1)}, bf16[512,1024]{1,0:T(8,128)(2,1)S(1)}) custom-call(s32[1,2,4]{2,1,0:T(2,128)S(1)} %copy-done.2, s32[8,27]{1,0:T(8,128)S(1)} %copy-done.4, bf16[256,4096]{1,0:T(8,128)(2,1)S(1)} %get-tuple-element.23.after_ref.wh_ref, bf16[256,4096]{1,0:T(8,128)(2,1)S(1)} %get-tuple-element.27.wl_ref, ...), custom_call_target="tpu_custom_call" | custom-call | tf_op jit(solution)/shard_map/pallas_call | solution.py:559
  10.2 0.6 %shard_map.98 = (bf16[1024,512]{1,0:T(8,128)(2,1)S(1)}, bf16[1024,512]{1,0:T(8,128)(2,1)S(1)}) custom-call(bf16[512,1024]{1,0:T(8,128)(2,1)S(1)} %get-tuple-element.28.high_ref, bf16[512,1024]{1,0:T(8,128)(2,1)S(1)} %get-tuple-element.29.low_ref), custom_call_target="tpu_custom_call" | custom-call | tf_op jit(solution)/shard_map/pallas_call | solution.py:563
  10.8 0.1 collective-permute-done.2.gb_ref
  10.9 0.0 collective-permute-done.1.ga_ref
  10.9 0.9 %shard_map.99 = (f32[48,512]{1,0:T(8,128)S(1)}, f32[96,256]{1,0:T(8,128)S(1)}, f32[96,256]{1,0:T(8,128)S(1)}) custom-call(f32[56,256]{1,0:T(8,128)S(1)} %get-tuple-element.25.after_ref.a_ref, f32[56,256]{1,0:T(8,128)S(1)} %get-tuple-element.26.b_ref, f32[56,256]{1,0:T(8,128)S(1)} %collective-permute-done.1.ga_ref, ...), custom_call_target="tpu_custom_call" | custom-call | tf_op jit(solution)/shard_map/pallas_call | solution.py:569
  11.8 0.4 %collective-permute-start.3 = (f32[96,256]{1,0:T(8,128)S(1)}, f32[96,256]{1,0:T(8,128)S(1)}, u32[]{:S(2)}, u32[]{:S(2)}) collective-permute-start(f32[96,256]{1,0:T(8,128)S(1)} %get-tuple-element.32.own_a_ref), channel_id=1, source_target_pairs={{0,2},{2,0},{4,6},{6,4},{8,10},{10,8},{12,14},{14,12},{16,18},{18,... | collective-permute-start | bytes 294920 | tf_op jit(solution)/shard_map/ppermute | solution.py:503
  12.2 1.5 %collective-permute-start.4 = (f32[96,256]{1,0:T(8,128)S(1)}, f32[96,256]{1,0:T(8,128)S(1)}, u32[]{:S(2)}, u32[]{:S(2)}) collective-permute-start(f32[96,256]{1,0:T(8,128)S(1)} %get-tuple-element.33.own_b_ref), channel_id=1, source_target_pairs={{2,4},{3,5},{6,8},{7,9},{10,12},{11,13},{14,16},{15,17},{18,20},{1... | collective-permute-start | bytes 294920 | tf_op jit(solution)/shard_map/ppermute | solution.py:508
  13.6 0.6 %shard_map.100 = (f32[16,256]{1,0:T(8,128)S(1)}, f32[8,32]{1,0:T(8,128)S(1)}) custom-call(f32[32,512]{1,0:T(8,128)S(1)} %get-tuple-element.24.resid_ref, f32[56,256]{1,0:T(8,128)S(1)} %get-tuple-element.25.after_ref.a_ref, f32[56,256]{1,0:T(8,128)S(1)} %get-tuple-element.26.b_ref, f32[48,512]{1,0:T(8,128)S(1)} %get-tuple-element.34.strain_ref), custom_call_target="tpu_custom_call" | custom-call | tf_op jit(solution)/shard_map/pallas_call | solution.py:573
  14.3 0.0 collective-permute-done.3.got_a_ref
  14.3 2.5 %collective-permute-done.4.got_b_ref = f32[96,256]{1,0:T(8,128)S(1)} collective-permute-done((f32[96,256]{1,0:T(8,128)S(1)}, f32[96,256]{1,0:T(8,128)S(1)}, u32[]{:S(2)}, u32[]{:S(2)}) %collective-permute-start.4) | collective-permute-done | bytes 98336 | tf_op jit(solution)/shard_map/ppermute | solution.py:508
  16.8 1.0 %shard_map.101 = (f32[48,512]{1,0:T(8,128)S(1)}, f32[48,512]{1,0:T(8,128)S(1)}, f32[48,512]{1,0:T(8,128)S(1)}, f32[32,256]{1,0:T(8,128)S(1)}) custom-call(f32[56,256]{1,0:T(8,128)S(1)} %get-tuple-element.25.after_ref.a_ref, f32[56,256]{1,0:T(8,128)S(1)} %get-tuple-element.26.b_ref, f32[56,256]{1,0:T(8,128)S(1)} %collective-permute-done.1.ga_ref, ...), custom_call_target="tpu_custom_call" | custom-call | tf_op jit(solution)/shard_map/pallas_call | solution.py:579
  17.9 1.9 %collective-permute-start.9 = (f32[32,256]{1,0:T(8,128)S(1)}, f32[32,256]{1,0:T(8,128)S(1)}, u32[]{:S(2)}, u32[]{:S(2)}) collective-permute-start(f32[32,256]{1,0:T(8,128)S(1)} %get-tuple-element.43), channel_id=1, source_target_pairs={{0,6},{2,4},{4,2},{6,0},{8,14},{10,12},{12,10},{14,8},{16,22},{18,... | collective-permute-start | bytes 98312 | tf_op jit(solution)/shard_map/ppermute | solution.py:485
  19.8 0.0 collective-permute-start.8
  19.8 0.2 collective-permute-start.7
  20.0 0.5 %shard_map.102 = (f32[48,512]{1,0:T(8,128)S(1)}, f32[48,256]{1,0:T(8,128)S(1)}, f32[48,256]{1,0:T(8,128)S(1)}) custom-call(f32[48,512]{1,0:T(8,128)S(1)} %get-tuple-element.38.scaled_ref, f32[48,512]{1,0:T(8,128)S(1)} %get-tuple-element.39.strain_ref, bf16[512,1024]{1,0:T(8,128)(2,1)S(1)} %get-tuple-element.28.high_ref, ...), custom_call_target="tpu_custom_call" | custom-call | tf_op jit(solution)/shard_map/pallas_call | solution.py:588
  20.5 0.3 %collective-permute-start.5 = (f32[48,256]{1,0:T(8,128)S(1)}, f32[48,256]{1,0:T(8,128)S(1)}, u32[]{:S(2)}, u32[]{:S(2)}) collective-permute-start(f32[48,256]{1,0:T(8,128)S(1)} %get-tuple-element.41), channel_id=1, source_target_pairs={{0,2},{2,0},{4,6},{6,4},{8,10},{10,8},{12,14},{14,12},{16,18},{18,... | collective-permute-start | bytes 147464 | tf_op jit(solution)/shard_map/ppermute | solution.py:503
  20.8 1.5 %collective-permute-start.6 = (f32[48,256]{1,0:T(8,128)S(1)}, f32[48,256]{1,0:T(8,128)S(1)}, u32[]{:S(2)}, u32[]{:S(2)}) collective-permute-start(f32[48,256]{1,0:T(8,128)S(1)} %get-tuple-element.42), channel_id=1, source_target_pairs={{2,4},{3,5},{6,8},{7,9},{10,12},{11,13},{14,16},{15,17},{18,20},{1... | collective-permute-start | bytes 147464 | tf_op jit(solution)/shard_map/ppermute | solution.py:508
  22.3 0.0 collective-permute-done.9
  22.3 1.4 %collective-permute-done.8 = f32[32,256]{1,0:T(8,128)S(1)} collective-permute-done((f32[32,256]{1,0:T(8,128)S(1)}, f32[32,256]{1,0:T(8,128)S(1)}, u32[]{:S(2)}, u32[]{:S(2)}) %collective-permute-start.8) | collective-permute-done | bytes 32800 | tf_op jit(solution)/shard_map/ppermute | solution.py:485
  23.7 0.0 collective-permute-done.7
  23.7 2.1 %collective-permute-start.12 = (f32[32,256]{1,0:T(8,128)S(1)}, f32[32,256]{1,0:T(8,128)S(1)}, u32[]{:S(2)}, u32[]{:S(2)}) collective-permute-start(f32[32,256]{1,0:T(8,128)S(1)} %add_add_fusion.rest_0_), channel_id=1, source_target_pairs={{0,26},{2,24},{4,30},{6,28},{8,18},{10,16},{12,22},{14,20},{16,10}... | collective-permute-start | bytes 98312 | tf_op jit(solution)/shard_map/ppermute | solution.py:485
  25.8 0.8 %collective-permute-start.11 = (f32[32,256]{1,0:T(8,128)S(1)}, f32[32,256]{1,0:T(8,128)S(1)}, u32[]{:S(2)}, u32[]{:S(2)}) collective-permute-start(f32[32,256]{1,0:T(8,128)S(1)} %add_add_fusion.rest_0_), channel_id=1, source_target_pairs={{0,18},{2,16},{4,22},{6,20},{8,26},{10,24},{12,30},{14,28},{16,2},... | collective-permute-start | bytes 98312 | tf_op jit(solution)/shard_map/ppermute | solution.py:485
  26.6 1.3 %collective-permute-start.10 = (f32[32,256]{1,0:T(8,128)S(1)}, f32[32,256]{1,0:T(8,128)S(1)}, u32[]{:S(2)}, u32[]{:S(2)}) collective-permute-start(f32[32,256]{1,0:T(8,128)S(1)} %add_add_fusion.rest_0_), channel_id=1, source_target_pairs={{0,8},{2,10},{4,12},{6,14},{8,0},{10,2},{12,4},{14,6},{16,24},{18,... | collective-permute-start | bytes 98312 | tf_op jit(solution)/shard_map/ppermute | solution.py:485
  27.9 0.0 collective-permute-done.5.got_a_ref
  27.9 0.0 collective-permute-done.6.got_b_ref
  27.9 1.2 %collective-permute-done.12.rest_3_ = f32[32,256]{1,0:T(8,128)S(1)} collective-permute-done((f32[32,256]{1,0:T(8,128)S(1)}, f32[32,256]{1,0:T(8,128)S(1)}, u32[]{:S(2)}, u32[]{:S(2)}) %collective-permute-start.12) | collective-permute-done | bytes 32800 | tf_op jit(solution)/shard_map/ppermute | solution.py:485
  29.1 1.1 %collective-permute-done.11.rest_2_ = f32[32,256]{1,0:T(8,128)S(1)} collective-permute-done((f32[32,256]{1,0:T(8,128)S(1)}, f32[32,256]{1,0:T(8,128)S(1)}, u32[]{:S(2)}, u32[]{:S(2)}) %collective-permute-start.11) | collective-permute-done | bytes 32800 | tf_op jit(solution)/shard_map/ppermute | solution.py:485
  30.1 0.4 %collective-permute-done.10.rest_1_ = f32[32,256]{1,0:T(8,128)S(1)} collective-permute-done((f32[32,256]{1,0:T(8,128)S(1)}, f32[32,256]{1,0:T(8,128)S(1)}, u32[]{:S(2)}, u32[]{:S(2)}) %collective-permute-start.10) | collective-permute-done | bytes 32800 | tf_op jit(solution)/shard_map/ppermute | solution.py:485
  30.5 0.0 copy-done.1
  30.5 2.3 %shard_map.103 = (f32[32,512]{1,0:T(8,128)}, f32[32,512]{1,0:T(8,128)}) custom-call(s32[1,2,4]{2,1,0:T(2,128)S(1)} %copy-done.2, f32[32,32]{1,0:T(8,128)S(1)} %copy-done.1, f32[32,512]{1,0:T(8,128)S(1)} %get-tuple-element.24.resid_ref, f32[56,256]{1,0:T(8,128)S(1)} %get-tuple-element.25.after_ref.a_ref, f32[56,256]{1,0:T(8,128)S(1)} %get-tuple-element.26.b_ref, ...), custom_call_target="tpu_custom_call" | custom-call | tf_op jit(solution)/shard_map/pallas_call | solution.py:593
  (2 shorter events, 0.0 us)
Async XLA Ops:
  0.6 5.2 %copy-start.3 = (f32[4,512]{1,0:T(4,128)S(1)}, f32[4,512]{1,0:T(4,128)}, u32[]{:S(2)}) copy-start(f32[4,512]{1,0:T(4,128)} %rest_0_.1) | copy-start | bytes 24580
  0.6 5.2 %copy-start.2 = (s32[1,2,4]{2,1,0:T(2,128)S(1)}, s32[1,2,4]{2,1,0:T(2,128)}, u32[]{:S(2)}) copy-start(s32[1,2,4]{2,1,0:T(2,128)} %rows_ref.5) | copy-start | bytes 100
  0.7 5.2 %copy-start.5 = (f32[512]{0:T(512)S(1)}, f32[512]{0:T(512)}, u32[]{:S(2)}) copy-start(f32[512]{0:T(512)} %param.14) | copy-start | bytes 6148
  0.7 5.2 %copy-start.6 = (s32[1,8]{1,0:T(1,128)S(1)}, s32[1,8]{1,0:T(1,128)}, u32[]{:S(2)}) copy-start(s32[1,8]{1,0:T(1,128)} %owner_ref.1) | copy-start | bytes 100
  0.7 5.2 %copy-start = (f32[32,512]{1,0:T(8,128)S(1)}, f32[32,512]{1,0:T(8,128)}, u32[]{:S(2)}) copy-start(f32[32,512]{1,0:T(8,128)} %right_ref.1) | copy-start | bytes 196612
  0.7 5.2 %collective-permute-start = (f32[4,512]{1,0:T(4,128)}, f32[4,512]{1,0:T(4,128)S(1)}, u32[]{:S(2)}, u32[]{:S(2)}) collective-permute-start(f32[4,512]{1,0:T(4,128)} %rest_0_.1), channel_id=1, source_target_pairs={{1,0},{0,1},{3,2},{2,3},{5,4},{4,5},{7,6},{6,7},{9,8},{8,9},{11,10... | collective-permute-start | bytes 24584 | tf_op jit(solution)/shard_map/ppermute | solution.py:535
  3.7 4.9 %copy-start.4 = (s32[8,27]{1,0:T(8,128)S(1)}, s32[8,27]{1,0:T(8,128)}, u32[]{:S(2)}) copy-start(s32[8,27]{1,0:T(8,128)} %columns_ref.1) | copy-start | bytes 2596
  6.7 4.2 %collective-permute-start.2 = (f32[56,256]{1,0:T(8,128)S(1)}, f32[56,256]{1,0:T(8,128)S(1)}, u32[]{:S(2)}, u32[]{:S(2)}) collective-permute-start(f32[56,256]{1,0:T(8,128)S(1)} %get-tuple-element.26.b_ref), channel_id=1, source_target_pairs={{2,4},{3,5},{6,8},{7,9},{10,12},{11,13},{14,16},{15,17},{18,20},{1... | collective-permute-start | bytes 172040 | tf_op jit(solution)/shard_map/ppermute | solution.py:508
  8.4 2.5 %collective-permute-start.1 = (f32[56,256]{1,0:T(8,128)S(1)}, f32[56,256]{1,0:T(8,128)S(1)}, u32[]{:S(2)}, u32[]{:S(2)}) collective-permute-start(f32[56,256]{1,0:T(8,128)S(1)} %get-tuple-element.25.after_ref.a_ref), channel_id=1, source_target_pairs={{0,2},{2,0},{4,6},{6,4},{8,10},{10,8},{12,14},{14,12},{16,18},{18,... | collective-permute-start | bytes 172040 | tf_op jit(solution)/shard_map/ppermute | solution.py:503
  11.8 2.4 %collective-permute-start.3 = (f32[96,256]{1,0:T(8,128)S(1)}, f32[96,256]{1,0:T(8,128)S(1)}, u32[]{:S(2)}, u32[]{:S(2)}) collective-permute-start(f32[96,256]{1,0:T(8,128)S(1)} %get-tuple-element.32.own_a_ref), channel_id=1, source_target_pairs={{0,2},{2,0},{4,6},{6,4},{8,10},{10,8},{12,14},{14,12},{16,18},{18,... | collective-permute-start | bytes 294920 | tf_op jit(solution)/shard_map/ppermute | solution.py:503
  12.2 4.6 %collective-permute-start.4 = (f32[96,256]{1,0:T(8,128)S(1)}, f32[96,256]{1,0:T(8,128)S(1)}, u32[]{:S(2)}, u32[]{:S(2)}) collective-permute-start(f32[96,256]{1,0:T(8,128)S(1)} %get-tuple-element.33.own_b_ref), channel_id=1, source_target_pairs={{2,4},{3,5},{6,8},{7,9},{10,12},{11,13},{14,16},{15,17},{18,20},{1... | collective-permute-start | bytes 294920 | tf_op jit(solution)/shard_map/ppermute | solution.py:508
  16.8 13.7 %copy-start.1 = (f32[32,32]{1,0:T(8,128)S(1)}, f32[32,32]{1,0:T(8,128)}, u32[]{:S(2)}) copy-start(f32[32,32]{1,0:T(8,128)} %inverse_ref.1) | copy-start | bytes 12292
  17.9 4.4 %collective-permute-start.9 = (f32[32,256]{1,0:T(8,128)S(1)}, f32[32,256]{1,0:T(8,128)S(1)}, u32[]{:S(2)}, u32[]{:S(2)}) collective-permute-start(f32[32,256]{1,0:T(8,128)S(1)} %get-tuple-element.43), channel_id=1, source_target_pairs={{0,6},{2,4},{4,2},{6,0},{8,14},{10,12},{12,10},{14,8},{16,22},{18,... | collective-permute-start | bytes 98312 | tf_op jit(solution)/shard_map/ppermute | solution.py:485
  19.8 3.9 %collective-permute-start.8 = (f32[32,256]{1,0:T(8,128)S(1)}, f32[32,256]{1,0:T(8,128)S(1)}, u32[]{:S(2)}, u32[]{:S(2)}) collective-permute-start(f32[32,256]{1,0:T(8,128)S(1)} %get-tuple-element.43), channel_id=1, source_target_pairs={{0,4},{2,6},{4,0},{6,2},{8,12},{10,14},{12,8},{14,10},{16,20},{18,... | collective-permute-start | bytes 98312 | tf_op jit(solution)/shard_map/ppermute | solution.py:485
  19.8 3.9 %collective-permute-start.7 = (f32[32,256]{1,0:T(8,128)S(1)}, f32[32,256]{1,0:T(8,128)S(1)}, u32[]{:S(2)}, u32[]{:S(2)}) collective-permute-start(f32[32,256]{1,0:T(8,128)S(1)} %get-tuple-element.43), channel_id=1, source_target_pairs={{0,2},{2,0},{4,6},{6,4},{8,10},{10,8},{12,14},{14,12},{16,18},{18,... | collective-permute-start | bytes 98312 | tf_op jit(solution)/shard_map/ppermute | solution.py:485
  20.5 7.5 %collective-permute-start.5 = (f32[48,256]{1,0:T(8,128)S(1)}, f32[48,256]{1,0:T(8,128)S(1)}, u32[]{:S(2)}, u32[]{:S(2)}) collective-permute-start(f32[48,256]{1,0:T(8,128)S(1)} %get-tuple-element.41), channel_id=1, source_target_pairs={{0,2},{2,0},{4,6},{6,4},{8,10},{10,8},{12,14},{14,12},{16,18},{18,... | collective-permute-start | bytes 147464 | tf_op jit(solution)/shard_map/ppermute | solution.py:503
  20.8 7.1 %collective-permute-start.6 = (f32[48,256]{1,0:T(8,128)S(1)}, f32[48,256]{1,0:T(8,128)S(1)}, u32[]{:S(2)}, u32[]{:S(2)}) collective-permute-start(f32[48,256]{1,0:T(8,128)S(1)} %get-tuple-element.42), channel_id=1, source_target_pairs={{2,4},{3,5},{6,8},{7,9},{10,12},{11,13},{14,16},{15,17},{18,20},{1... | collective-permute-start | bytes 147464 | tf_op jit(solution)/shard_map/ppermute | solution.py:508
  23.7 5.3 %collective-permute-start.12 = (f32[32,256]{1,0:T(8,128)S(1)}, f32[32,256]{1,0:T(8,128)S(1)}, u32[]{:S(2)}, u32[]{:S(2)}) collective-permute-start(f32[32,256]{1,0:T(8,128)S(1)} %add_add_fusion.rest_0_), channel_id=1, source_target_pairs={{0,26},{2,24},{4,30},{6,28},{8,18},{10,16},{12,22},{14,20},{16,10}... | collective-permute-start | bytes 98312 | tf_op jit(solution)/shard_map/ppermute | solution.py:485
  25.8 4.3 %collective-permute-start.11 = (f32[32,256]{1,0:T(8,128)S(1)}, f32[32,256]{1,0:T(8,128)S(1)}, u32[]{:S(2)}, u32[]{:S(2)}) collective-permute-start(f32[32,256]{1,0:T(8,128)S(1)} %add_add_fusion.rest_0_), channel_id=1, source_target_pairs={{0,18},{2,16},{4,22},{6,20},{8,26},{10,24},{12,30},{14,28},{16,2},... | collective-permute-start | bytes 98312 | tf_op jit(solution)/shard_map/ppermute | solution.py:485
  26.6 3.9 %collective-permute-start.10 = (f32[32,256]{1,0:T(8,128)S(1)}, f32[32,256]{1,0:T(8,128)S(1)}, u32[]{:S(2)}, u32[]{:S(2)}) collective-permute-start(f32[32,256]{1,0:T(8,128)S(1)} %add_add_fusion.rest_0_), channel_id=1, source_target_pairs={{0,8},{2,10},{4,12},{6,14},{8,0},{10,2},{12,4},{14,6},{16,24},{18,... | collective-permute-start | bytes 98312 | tf_op jit(solution)/shard_map/ppermute | solution.py:485

commit v8 on v7

--- a/solution.py
+++ b/solution.py
@@ -353,9 +353,8 @@
     )
 
 
-def finish(
+def settle(
     rows_ref,
-    inverse_ref,
     resid_ref,
     a_ref,
     b_ref,
@@ -364,15 +363,44 @@
     own_ref,
     got_a_ref,
     got_b_ref,
-    *rest,
-    ncoarse,
-    n_pay,
+    all_ref,
+    blk_ref,
 ):
-    pays = rest[:n_pay]
-    field_hbm, resid2_hbm, field_ref, resid2_ref, blk_ref, sems = rest[n_pay:]
     odd = lax.axis_index("sub") % 2
     live = own_ref.shape[0]
     cases = live - FRAME
+    own = own_ref[...]
+    got_a = got_a_ref[...]
+    got_b = inside() * got_b_ref[...]
+    image2 = own[:cases] + jnp.concatenate([got_a[:cases], got_b[:cases]], axis=1)
+    coarse2 = widened(own[cases:], got_a[cases:], got_b[cases:], odd == 0)
+    start = jnp.concatenate([a_ref[:live, :], b_ref[:live, :]], axis=1)
+    scaled = scaled_ref[...]
+    image = image_ref[...]
+    at = 0
+    for value in (
+        resid_ref[...],
+        start[:cases],
+        scaled[:cases],
+        image[:cases],
+        image2,
+        start[cases:],
+        scaled[cases:],
+        image[cases:],
+        coarse2,
+    ):
+        end = at + value.shape[0]
+        for j in range(NB):
+            blk_ref[place_of(rows_ref, odd, j), at:end, :] = value[:, B * j : B * (j + 1)]
+        at = end
+    for m in range(0, NB, 2):
+        all_ref[:, B * m : B * (m + 2)] = jnp.concatenate([blk_ref[m], blk_ref[m + 1]], axis=1)
+
+
+def finish(inverse_ref, all_ref, *rest, ncoarse, n_pay):
+    pays = rest[:n_pay]
+    field_hbm, resid2_hbm, field_ref, resid2_ref, sems = rest[n_pay:]
+    cases = field_ref.shape[0]
     width = cases + ncoarse
     pay = pays[0][...]
     for other in pays[1:]:
@@ -438,35 +466,22 @@
     columns = exact(pair, jnp.where(row == half, 1.0, 0.0), TN)
     upper = jnp.concatenate([columns[:, :128]] * (OWN // 128), axis=1)
     lower = jnp.concatenate([columns[:, 128:]] * (OWN // 128), axis=1)
-    start = jnp.concatenate([a_ref[:live, :], b_ref[:live, :]], axis=1)
-    scaled = scaled_ref[...]
-    image = image_ref[...]
-    own = own_ref[...]
-    got_a = got_a_ref[...]
-    got_b = inside() * got_b_ref[...]
-    image2 = own[:cases] + jnp.concatenate([got_a[:cases], got_b[:cases]], axis=1)
-    coarse2 = widened(own[cases:], got_a[cases:], got_b[cases:], odd == 0)
-    field = (
-        upper * start[:cases]
-        - lower * scaled[:cases]
-        + near(weights, jnp.concatenate([start[cases:], scaled[cases:]], axis=0), TN)
-    )
-    resid2 = (
-        resid_ref[...]
-        - upper * image[:cases]
+    resid, fine, scaled, image, image2 = (
+        all_ref[k * cases : (k + 1) * cases, :] for k in range(5)
+    )
+    at = 5 * cases
+    field_ref[...] = upper * fine - lower * scaled + near(weights, all_ref[at : at + 2 * FRAME, :], TN)
+    copies = [pltpu.make_async_copy(field_ref, field_hbm, sems.at[0])]
+    copies[0].start()
+    at += 2 * FRAME
+    resid2_ref[...] = (
+        resid
+        - upper * image
         + lower * image2
-        - near(weights2, jnp.concatenate([image[cases:], coarse2], axis=0), TN)
-    )
-    copies = []
-    for k, (value, out, buf) in enumerate(
-        ((field, field_hbm, field_ref), (resid2, resid2_hbm, resid2_ref))
-    ):
-        for j in range(NB):
-            blk_ref[k, place_of(rows_ref, odd, j)] = value[:, B * j : B * (j + 1)]
-        for m in range(0, NB, 2):
-            buf[:, B * m : B * (m + 2)] = jnp.concatenate([blk_ref[k, m], blk_ref[k, m + 1]], axis=1)
-        copies.append(pltpu.make_async_copy(buf, out, sems.at[k]))
-        copies[-1].start()
+        - near(weights2, all_ref[at : at + FRAME + WIDE, :], TN)
+    )
+    copies.append(pltpu.make_async_copy(resid2_ref, resid2_hbm, sems.at[1]))
+    copies[1].start()
     for copy in copies:
         copy.wait()
 
@@ -589,32 +604,26 @@
         second_image, [shape(live, OWN), shape(live, EDGE), shape(live, EDGE)], 4
     )(scaled, strain, high, low)
     got_a, got_b = across(back_a, back_b, count, parts)
+    height = 5 * cases + 3 * FRAME + WIDE
+    (everything,) = run(
+        settle,
+        [shape(height, OWN)],
+        9,
+        smem=(0,),
+        scratch=[pltpu.VMEM((NB, height, B), F32)],
+    )(interface_rows, resid, side_a, side_b, image, scaled, own, got_a, got_b)
     return tuple(
         run(
             functools.partial(finish, ncoarse=ncoarse, n_pay=len(pays)),
             [shape(cases, OWN)] * 2,
-            10 + len(pays),
-            smem=(0,),
+            2 + len(pays),
             raw_out=True,
             scratch=[
                 pltpu.VMEM((cases, OWN), F32),
                 pltpu.VMEM((cases, OWN), F32),
-                pltpu.VMEM((2, NB, cases, B), F32),
                 pltpu.SemaphoreType.DMA((2,)),
             ],
-        )(
-            interface_rows,
-            coarse_inverse,
-            resid,
-            side_a,
-            side_b,
-            image,
-            scaled,
-            own,
-            got_a,
-            got_b,
-            *pays,
-        )
+        )(coarse_inverse, everything, *pays)
     )
 
 

time: 33.1 us -> 32.4 us (0.979)
  waiting for transfers between devices: 6.64 us -> 5.71 us
    ppermute x6, waiting for transfers between devices: 4 us -> 3.07 us  [swap(): lax.ppermute(x, 'sub', [(i, i ^ k) for i in range(count)])]
    pallas_call x0 -> x1, Pallas kernels: none -> 0.92 us  [body(): run(settle, [shape(height, OWN)], 9, smem=(0,), scratch=[pltpu.VMEM((NB,...]
    pallas_call x1, Pallas kernels: 2.28 us -> 1.56 us  [body(): run(functools.partial(finish, ncoarse=ncoarse, n_pay=len(pays)), [shape(c...]
  transfers between devices with their start and end apart: 13 -> 13, of which waited for: 6 -> 6; matrix products, arithmetic and copies ran while one was open for 0% -> 0% of each run, Pallas kernels for 17% -> 20%
where the time goes in v8:
time: 32.4 us; the launch traced here: 32 us
  starting transfers between devices  14.9 us (46%)
  Pallas kernels  10.7 us (33%)
  waiting for transfers between devices  5.71 us (18%)
  between operations  0.79 us (2%)
    ppermute x6, starting transfers between devices, swap(): lax.ppermute(x, 'sub', [(i, i ^ k) for i in range(count)])  6.32 us
    ppermute x3, starting transfers between devices, across(): lax.ppermute(b, ('sub', 'rhs'), pairs + [(j, i) for i, j in pairs])  4.69 us
    ppermute x6, waiting for transfers between devices, swap(): lax.ppermute(x, 'sub', [(i, i ^ k) for i in range(count)])  3.07 us
    ppermute x1, starting transfers between devices, body(): lax.ppermute(corner_basis, 'rhs', [((i + k) % parts, i) for i in range(pa...  3 us
    ppermute x3, waiting for transfers between devices, across(): lax.ppermute(b, ('sub', 'rhs'), pairs + [(j, i) for i, j in pairs])  2.62 us
    pallas_call x1, Pallas kernels, body(): call(load_blocks, [packed, packed], 1, raw=(0,), scratch=[pltpu.VMEM((B *...  2.14 us
    pallas_call x1, Pallas kernels, body(): run(assemble, [dense, dense], 5, smem=(0,))  1.66 us
    pallas_call x1, Pallas kernels, body(): run(functools.partial(finish, ncoarse=ncoarse, n_pay=len(pays)), [shape(c...  1.56 us
  transfers between devices with their start and end apart: 13, of which 6 were waited for; matrix products, arithmetic and copies ran while one was open for 0% of the time, Pallas kernels for 20%

profile of v8, /device:TPU:0, one launch (start us, length us, event | category | flops | bytes accessed | tf_op | source)
XLA Modules:
  0.0 32.0 jit_solution(17092180555176786191)
XLA Ops:
  0.6 0.0 copy-start.3
  0.6 0.0 copy-start.2
  0.7 0.0 copy-start.5
  0.7 0.0 copy-start.6
  0.7 0.0 copy-start
  0.7 3.0 %collective-permute-start = (f32[4,512]{1,0:T(4,128)}, f32[4,512]{1,0:T(4,128)S(1)}, u32[]{:S(2)}, u32[]{:S(2)}) collective-permute-start(f32[4,512]{1,0:T(4,128)} %rest_0_.1), channel_id=1, source_target_pairs={{1,0},{0,1},{3,2},{2,3},{5,4},{4,5},{7,6},{6,7},{9,8},{8,9},{11,10... | collective-permute-start | bytes 24584 | tf_op jit(solution)/shard_map/ppermute | solution.py:550
  3.7 2.1 %shard_map.95 = (bf16[256,4096]{1,0:T(8,128)(2,1)S(1)}, bf16[256,4096]{1,0:T(8,128)(2,1)S(1)}) custom-call(f32[27,8,4096]{2,1,0:T(8,128)} %bitcast.3), custom_call_target="tpu_custom_call" | custom-call | bytes 16777216 | tf_op jit(solution)/shard_map/pallas_call | solution.py:554
  5.8 0.0 collective-permute-done.rest_1_
  5.8 0.0 copy-done.3
  5.9 0.0 copy-done.2
  5.9 0.0 copy-done.5
  5.9 0.0 copy-done.6
  5.9 0.0 copy-done
  5.9 0.8 %shard_map.96 = (f32[32,512]{1,0:T(8,128)S(1)}, f32[56,256]{1,0:T(8,128)S(1)}, f32[56,256]{1,0:T(8,128)S(1)}) custom-call(s32[1,2,4]{2,1,0:T(2,128)S(1)} %copy-done.2, s32[1,8]{1,0:T(1,128)S(1)} %copy-done.6, f32[32,512]{1,0:T(8,128)S(1)} %copy-done, f32[1,512]{1,0:T(1,128)S(1)} %bitcast.2, bf16[256,4096]{1,0:T(8,128)(2,1)S(1)} %get-tuple-element.23.after_ref.wh_ref, ...), custom_call_target="tpu_custom_call" | custom-call | tf_op jit(solution)/shard_map/pallas_call | solution.py:566
  6.7 1.8 %collective-permute-start.2 = (f32[56,256]{1,0:T(8,128)S(1)}, f32[56,256]{1,0:T(8,128)S(1)}, u32[]{:S(2)}, u32[]{:S(2)}) collective-permute-start(f32[56,256]{1,0:T(8,128)S(1)} %get-tuple-element.26.b_ref), channel_id=1, source_target_pairs={{2,4},{3,5},{6,8},{7,9},{10,12},{11,13},{14,16},{15,17},{18,20},{1... | collective-permute-start | bytes 172040 | tf_op jit(solution)/shard_map/ppermute | solution.py:523
  8.4 0.1 collective-permute-start.1
  8.6 0.0 copy-done.4
  8.6 1.7 %shard_map.97 = (bf16[512,1024]{1,0:T(8,128)(2,1)S(1)}, bf16[512,1024]{1,0:T(8,128)(2,1)S(1)}) custom-call(s32[1,2,4]{2,1,0:T(2,128)S(1)} %copy-done.2, s32[8,27]{1,0:T(8,128)S(1)} %copy-done.4, bf16[256,4096]{1,0:T(8,128)(2,1)S(1)} %get-tuple-element.23.after_ref.wh_ref, bf16[256,4096]{1,0:T(8,128)(2,1)S(1)} %get-tuple-element.27.wl_ref, ...), custom_call_target="tpu_custom_call" | custom-call | tf_op jit(solution)/shard_map/pallas_call | solution.py:574
  10.2 0.6 %shard_map.98 = (bf16[1024,512]{1,0:T(8,128)(2,1)S(1)}, bf16[1024,512]{1,0:T(8,128)(2,1)S(1)}) custom-call(bf16[512,1024]{1,0:T(8,128)(2,1)S(1)} %get-tuple-element.28.high_ref, bf16[512,1024]{1,0:T(8,128)(2,1)S(1)} %get-tuple-element.29.low_ref), custom_call_target="tpu_custom_call" | custom-call | tf_op jit(solution)/shard_map/pallas_call | solution.py:578
  10.8 0.1 collective-permute-done.2.gb_ref
  10.9 0.0 collective-permute-done.1.ga_ref
  10.9 0.9 %shard_map.99 = (f32[48,512]{1,0:T(8,128)S(1)}, f32[96,256]{1,0:T(8,128)S(1)}, f32[96,256]{1,0:T(8,128)S(1)}) custom-call(f32[56,256]{1,0:T(8,128)S(1)} %get-tuple-element.25.after_ref.a_ref, f32[56,256]{1,0:T(8,128)S(1)} %get-tuple-element.26.b_ref, f32[56,256]{1,0:T(8,128)S(1)} %collective-permute-done.1.ga_ref, ...), custom_call_target="tpu_custom_call" | custom-call | tf_op jit(solution)/shard_map/pallas_call | solution.py:584
  11.8 0.4 %collective-permute-start.3 = (f32[96,256]{1,0:T(8,128)S(1)}, f32[96,256]{1,0:T(8,128)S(1)}, u32[]{:S(2)}, u32[]{:S(2)}) collective-permute-start(f32[96,256]{1,0:T(8,128)S(1)} %get-tuple-element.32.own_a_ref), channel_id=1, source_target_pairs={{0,2},{2,0},{4,6},{6,4},{8,10},{10,8},{12,14},{14,12},{16,18},{18,... | collective-permute-start | bytes 294920 | tf_op jit(solution)/shard_map/ppermute | solution.py:518
  12.2 1.5 %collective-permute-start.4 = (f32[96,256]{1,0:T(8,128)S(1)}, f32[96,256]{1,0:T(8,128)S(1)}, u32[]{:S(2)}, u32[]{:S(2)}) collective-permute-start(f32[96,256]{1,0:T(8,128)S(1)} %get-tuple-element.33.own_b_ref), channel_id=1, source_target_pairs={{2,4},{3,5},{6,8},{7,9},{10,12},{11,13},{14,16},{15,17},{18,20},{1... | collective-permute-start | bytes 294920 | tf_op jit(solution)/shard_map/ppermute | solution.py:523
  13.6 0.6 %shard_map.100 = (f32[16,256]{1,0:T(8,128)S(1)}, f32[8,32]{1,0:T(8,128)S(1)}) custom-call(f32[32,512]{1,0:T(8,128)S(1)} %get-tuple-element.24.resid_ref, f32[56,256]{1,0:T(8,128)S(1)} %get-tuple-element.25.after_ref.a_ref, f32[56,256]{1,0:T(8,128)S(1)} %get-tuple-element.26.b_ref, f32[48,512]{1,0:T(8,128)S(1)} %get-tuple-element.34.strain_ref), custom_call_target="tpu_custom_call" | custom-call | tf_op jit(solution)/shard_map/pallas_call | solution.py:588
  14.3 0.0 collective-permute-done.3.got_a_ref
  14.3 2.5 %collective-permute-done.4.got_b_ref = f32[96,256]{1,0:T(8,128)S(1)} collective-permute-done((f32[96,256]{1,0:T(8,128)S(1)}, f32[96,256]{1,0:T(8,128)S(1)}, u32[]{:S(2)}, u32[]{:S(2)}) %collective-permute-start.4) | collective-permute-done | bytes 98336 | tf_op jit(solution)/shard_map/ppermute | solution.py:523
  16.8 1.0 %shard_map.101 = (f32[48,512]{1,0:T(8,128)S(1)}, f32[48,512]{1,0:T(8,128)S(1)}, f32[48,512]{1,0:T(8,128)S(1)}, f32[32,256]{1,0:T(8,128)S(1)}) custom-call(f32[56,256]{1,0:T(8,128)S(1)} %get-tuple-element.25.after_ref.a_ref, f32[56,256]{1,0:T(8,128)S(1)} %get-tuple-element.26.b_ref, f32[56,256]{1,0:T(8,128)S(1)} %collective-permute-done.1.ga_ref, ...), custom_call_target="tpu_custom_call" | custom-call | tf_op jit(solution)/shard_map/pallas_call | solution.py:594
  17.8 0.0 copy-start.1
  17.9 1.9 %collective-permute-start.9 = (f32[32,256]{1,0:T(8,128)S(1)}, f32[32,256]{1,0:T(8,128)S(1)}, u32[]{:S(2)}, u32[]{:S(2)}) collective-permute-start(f32[32,256]{1,0:T(8,128)S(1)} %get-tuple-element.43), channel_id=1, source_target_pairs={{0,6},{2,4},{4,2},{6,0},{8,14},{10,12},{12,10},{14,8},{16,22},{18,... | collective-permute-start | bytes 98312 | tf_op jit(solution)/shard_map/ppermute | solution.py:500
  19.8 0.0 collective-permute-start.8
  19.8 0.2 collective-permute-start.7
  20.0 0.5 %shard_map.102 = (f32[48,512]{1,0:T(8,128)S(1)}, f32[48,256]{1,0:T(8,128)S(1)}, f32[48,256]{1,0:T(8,128)S(1)}) custom-call(f32[48,512]{1,0:T(8,128)S(1)} %get-tuple-element.38.scaled_ref, f32[48,512]{1,0:T(8,128)S(1)} %get-tuple-element.39.strain_ref, bf16[512,1024]{1,0:T(8,128)(2,1)S(1)} %get-tuple-element.28.high_ref, ...), custom_call_target="tpu_custom_call" | custom-call | tf_op jit(solution)/shard_map/pallas_call | solution.py:603
  20.5 0.3 %collective-permute-start.5 = (f32[48,256]{1,0:T(8,128)S(1)}, f32[48,256]{1,0:T(8,128)S(1)}, u32[]{:S(2)}, u32[]{:S(2)}) collective-permute-start(f32[48,256]{1,0:T(8,128)S(1)} %get-tuple-element.41), channel_id=1, source_target_pairs={{0,2},{2,0},{4,6},{6,4},{8,10},{10,8},{12,14},{14,12},{16,18},{18,... | collective-permute-start | bytes 147464 | tf_op jit(solution)/shard_map/ppermute | solution.py:518
  20.8 1.5 %collective-permute-start.6 = (f32[48,256]{1,0:T(8,128)S(1)}, f32[48,256]{1,0:T(8,128)S(1)}, u32[]{:S(2)}, u32[]{:S(2)}) collective-permute-start(f32[48,256]{1,0:T(8,128)S(1)} %get-tuple-element.42), channel_id=1, source_target_pairs={{2,4},{3,5},{6,8},{7,9},{10,12},{11,13},{14,16},{15,17},{18,20},{1... | collective-permute-start | bytes 147464 | tf_op jit(solution)/shard_map/ppermute | solution.py:523
  22.3 0.0 collective-permute-done.9
  22.3 1.4 %collective-permute-done.8 = f32[32,256]{1,0:T(8,128)S(1)} collective-permute-done((f32[32,256]{1,0:T(8,128)S(1)}, f32[32,256]{1,0:T(8,128)S(1)}, u32[]{:S(2)}, u32[]{:S(2)}) %collective-permute-start.8) | collective-permute-done | bytes 32800 | tf_op jit(solution)/shard_map/ppermute | solution.py:500
  23.7 0.0 collective-permute-done.7
  23.7 2.1 %collective-permute-start.12 = (f32[32,256]{1,0:T(8,128)S(1)}, f32[32,256]{1,0:T(8,128)S(1)}, u32[]{:S(2)}, u32[]{:S(2)}) collective-permute-start(f32[32,256]{1,0:T(8,128)S(1)} %add_add_fusion.rest_0_), channel_id=1, source_target_pairs={{0,26},{2,24},{4,30},{6,28},{8,18},{10,16},{12,22},{14,20},{16,10}... | collective-permute-start | bytes 98312 | tf_op jit(solution)/shard_map/ppermute | solution.py:500
  25.8 0.8 %collective-permute-start.11 = (f32[32,256]{1,0:T(8,128)S(1)}, f32[32,256]{1,0:T(8,128)S(1)}, u32[]{:S(2)}, u32[]{:S(2)}) collective-permute-start(f32[32,256]{1,0:T(8,128)S(1)} %add_add_fusion.rest_0_), channel_id=1, source_target_pairs={{0,18},{2,16},{4,22},{6,20},{8,26},{10,24},{12,30},{14,28},{16,2},... | collective-permute-start | bytes 98312 | tf_op jit(solution)/shard_map/ppermute | solution.py:500
  26.6 1.3 %collective-permute-start.10 = (f32[32,256]{1,0:T(8,128)S(1)}, f32[32,256]{1,0:T(8,128)S(1)}, u32[]{:S(2)}, u32[]{:S(2)}) collective-permute-start(f32[32,256]{1,0:T(8,128)S(1)} %add_add_fusion.rest_0_), channel_id=1, source_target_pairs={{0,8},{2,10},{4,12},{6,14},{8,0},{10,2},{12,4},{14,6},{16,24},{18,... | collective-permute-start | bytes 98312 | tf_op jit(solution)/shard_map/ppermute | solution.py:500
  27.9 0.0 collective-permute-done.5.got_a_ref
  27.9 0.0 collective-permute-done.6.got_b_ref
  27.9 0.9 %shard_map.103.all_ref = f32[232,512]{1,0:T(8,128)S(1)} custom-call(s32[1,2,4]{2,1,0:T(2,128)S(1)} %copy-done.2, f32[32,512]{1,0:T(8,128)S(1)} %get-tuple-element.24.resid_ref, f32[56,256]{1,0:T(8,128)S(1)} %get-tuple-element.25.after_ref.a_ref, f32[56,256]{1,0:T(8,128)S(1)} %get-tuple-element.26.b_ref, f32[48,512]{1,0:T(8,128)S(1)} %get-tuple-element.37.image_ref, ...), custom_call_target="tpu_custom_call" | custom-call | tf_op jit(solution)/shard_map/pallas_call | solution.py:608
  28.9 0.2 collective-permute-done.12.rest_3_
  29.1 1.1 %collective-permute-done.11.rest_2_ = f32[32,256]{1,0:T(8,128)S(1)} collective-permute-done((f32[32,256]{1,0:T(8,128)S(1)}, f32[32,256]{1,0:T(8,128)S(1)}, u32[]{:S(2)}, u32[]{:S(2)}) %collective-permute-start.11) | collective-permute-done | bytes 32800 | tf_op jit(solution)/shard_map/ppermute | solution.py:500
  30.1 0.4 %collective-permute-done.10.rest_1_ = f32[32,256]{1,0:T(8,128)S(1)} collective-permute-done((f32[32,256]{1,0:T(8,128)S(1)}, f32[32,256]{1,0:T(8,128)S(1)}, u32[]{:S(2)}, u32[]{:S(2)}) %collective-permute-start.10) | collective-permute-done | bytes 32800 | tf_op jit(solution)/shard_map/ppermute | solution.py:500
  30.5 1.6 %shard_map.104 = (f32[32,512]{1,0:T(8,128)}, f32[32,512]{1,0:T(8,128)}) custom-call(f32[32,32]{1,0:T(8,128)S(1)} %copy-done.1, f32[232,512]{1,0:T(8,128)S(1)} %shard_map.103.all_ref, f32[32,256]{1,0:T(8,128)S(1)} %add_add_fusion.rest_0_, f32[32,256]{1,0:T(8,128)S(1)} %collective-permute-done.10.rest_1_, f32[32,256]{1,0:T(8,128)S(1)} %collective-permute-done.11.rest_2_, ...), custom_call_target="tpu_custom_call" | custom-call | tf_op jit(solution)/shard_map/pallas_call | solution.py:616
  (3 shorter events, 0.0 us)
Async XLA Ops:
  0.6 5.2 %copy-start.3 = (f32[4,512]{1,0:T(4,128)S(1)}, f32[4,512]{1,0:T(4,128)}, u32[]{:S(2)}) copy-start(f32[4,512]{1,0:T(4,128)} %rest_0_.1) | copy-start | bytes 24580
  0.6 5.2 %copy-start.2 = (s32[1,2,4]{2,1,0:T(2,128)S(1)}, s32[1,2,4]{2,1,0:T(2,128)}, u32[]{:S(2)}) copy-start(s32[1,2,4]{2,1,0:T(2,128)} %rows_ref.5) | copy-start | bytes 100
  0.7 5.2 %copy-start.5 = (f32[512]{0:T(512)S(1)}, f32[512]{0:T(512)}, u32[]{:S(2)}) copy-start(f32[512]{0:T(512)} %param.14) | copy-start | bytes 6148
  0.7 5.2 %copy-start.6 = (s32[1,8]{1,0:T(1,128)S(1)}, s32[1,8]{1,0:T(1,128)}, u32[]{:S(2)}) copy-start(s32[1,8]{1,0:T(1,128)} %owner_ref.1) | copy-start | bytes 100
  0.7 5.2 %copy-start = (f32[32,512]{1,0:T(8,128)S(1)}, f32[32,512]{1,0:T(8,128)}, u32[]{:S(2)}) copy-start(f32[32,512]{1,0:T(8,128)} %right_ref.1) | copy-start | bytes 196612
  0.7 5.2 %collective-permute-start = (f32[4,512]{1,0:T(4,128)}, f32[4,512]{1,0:T(4,128)S(1)}, u32[]{:S(2)}, u32[]{:S(2)}) collective-permute-start(f32[4,512]{1,0:T(4,128)} %rest_0_.1), channel_id=1, source_target_pairs={{1,0},{0,1},{3,2},{2,3},{5,4},{4,5},{7,6},{6,7},{9,8},{8,9},{11,10... | collective-permute-start | bytes 24584 | tf_op jit(solution)/shard_map/ppermute | solution.py:550
  3.7 4.9 %copy-start.4 = (s32[8,27]{1,0:T(8,128)S(1)}, s32[8,27]{1,0:T(8,128)}, u32[]{:S(2)}) copy-start(s32[8,27]{1,0:T(8,128)} %columns_ref.1) | copy-start | bytes 2596
  6.7 4.2 %collective-permute-start.2 = (f32[56,256]{1,0:T(8,128)S(1)}, f32[56,256]{1,0:T(8,128)S(1)}, u32[]{:S(2)}, u32[]{:S(2)}) collective-permute-start(f32[56,256]{1,0:T(8,128)S(1)} %get-tuple-element.26.b_ref), channel_id=1, source_target_pairs={{2,4},{3,5},{6,8},{7,9},{10,12},{11,13},{14,16},{15,17},{18,20},{1... | collective-permute-start | bytes 172040 | tf_op jit(solution)/shard_map/ppermute | solution.py:523
  8.4 2.5 %collective-permute-start.1 = (f32[56,256]{1,0:T(8,128)S(1)}, f32[56,256]{1,0:T(8,128)S(1)}, u32[]{:S(2)}, u32[]{:S(2)}) collective-permute-start(f32[56,256]{1,0:T(8,128)S(1)} %get-tuple-element.25.after_ref.a_ref), channel_id=1, source_target_pairs={{0,2},{2,0},{4,6},{6,4},{8,10},{10,8},{12,14},{14,12},{16,18},{18,... | collective-permute-start | bytes 172040 | tf_op jit(solution)/shard_map/ppermute | solution.py:518
  11.8 2.4 %collective-permute-start.3 = (f32[96,256]{1,0:T(8,128)S(1)}, f32[96,256]{1,0:T(8,128)S(1)}, u32[]{:S(2)}, u32[]{:S(2)}) collective-permute-start(f32[96,256]{1,0:T(8,128)S(1)} %get-tuple-element.32.own_a_ref), channel_id=1, source_target_pairs={{0,2},{2,0},{4,6},{6,4},{8,10},{10,8},{12,14},{14,12},{16,18},{18,... | collective-permute-start | bytes 294920 | tf_op jit(solution)/shard_map/ppermute | solution.py:518
  12.2 4.6 %collective-permute-start.4 = (f32[96,256]{1,0:T(8,128)S(1)}, f32[96,256]{1,0:T(8,128)S(1)}, u32[]{:S(2)}, u32[]{:S(2)}) collective-permute-start(f32[96,256]{1,0:T(8,128)S(1)} %get-tuple-element.33.own_b_ref), channel_id=1, source_target_pairs={{2,4},{3,5},{6,8},{7,9},{10,12},{11,13},{14,16},{15,17},{18,20},{1... | collective-permute-start | bytes 294920 | tf_op jit(solution)/shard_map/ppermute | solution.py:523
  17.8 12.6 %copy-start.1 = (f32[32,32]{1,0:T(8,128)S(1)}, f32[32,32]{1,0:T(8,128)}, u32[]{:S(2)}) copy-start(f32[32,32]{1,0:T(8,128)} %inverse_ref.1) | copy-start | bytes 12292
  17.9 4.4 %collective-permute-start.9 = (f32[32,256]{1,0:T(8,128)S(1)}, f32[32,256]{1,0:T(8,128)S(1)}, u32[]{:S(2)}, u32[]{:S(2)}) collective-permute-start(f32[32,256]{1,0:T(8,128)S(1)} %get-tuple-element.43), channel_id=1, source_target_pairs={{0,6},{2,4},{4,2},{6,0},{8,14},{10,12},{12,10},{14,8},{16,22},{18,... | collective-permute-start | bytes 98312 | tf_op jit(solution)/shard_map/ppermute | solution.py:500
  19.8 3.9 %collective-permute-start.8 = (f32[32,256]{1,0:T(8,128)S(1)}, f32[32,256]{1,0:T(8,128)S(1)}, u32[]{:S(2)}, u32[]{:S(2)}) collective-permute-start(f32[32,256]{1,0:T(8,128)S(1)} %get-tuple-element.43), channel_id=1, source_target_pairs={{0,4},{2,6},{4,0},{6,2},{8,12},{10,14},{12,8},{14,10},{16,20},{18,... | collective-permute-start | bytes 98312 | tf_op jit(solution)/shard_map/ppermute | solution.py:500
  19.8 3.9 %collective-permute-start.7 = (f32[32,256]{1,0:T(8,128)S(1)}, f32[32,256]{1,0:T(8,128)S(1)}, u32[]{:S(2)}, u32[]{:S(2)}) collective-permute-start(f32[32,256]{1,0:T(8,128)S(1)} %get-tuple-element.43), channel_id=1, source_target_pairs={{0,2},{2,0},{4,6},{6,4},{8,10},{10,8},{12,14},{14,12},{16,18},{18,... | collective-permute-start | bytes 98312 | tf_op jit(solution)/shard_map/ppermute | solution.py:500
  20.5 7.4 %collective-permute-start.5 = (f32[48,256]{1,0:T(8,128)S(1)}, f32[48,256]{1,0:T(8,128)S(1)}, u32[]{:S(2)}, u32[]{:S(2)}) collective-permute-start(f32[48,256]{1,0:T(8,128)S(1)} %get-tuple-element.41), channel_id=1, source_target_pairs={{0,2},{2,0},{4,6},{6,4},{8,10},{10,8},{12,14},{14,12},{16,18},{18,... | collective-permute-start | bytes 147464 | tf_op jit(solution)/shard_map/ppermute | solution.py:518
  20.8 7.1 %collective-permute-start.6 = (f32[48,256]{1,0:T(8,128)S(1)}, f32[48,256]{1,0:T(8,128)S(1)}, u32[]{:S(2)}, u32[]{:S(2)}) collective-permute-start(f32[48,256]{1,0:T(8,128)S(1)} %get-tuple-element.42), channel_id=1, source_target_pairs={{2,4},{3,5},{6,8},{7,9},{10,12},{11,13},{14,16},{15,17},{18,20},{1... | collective-permute-start | bytes 147464 | tf_op jit(solution)/shard_map/ppermute | solution.py:523
  23.7 5.3 %collective-permute-start.12 = (f32[32,256]{1,0:T(8,128)S(1)}, f32[32,256]{1,0:T(8,128)S(1)}, u32[]{:S(2)}, u32[]{:S(2)}) collective-permute-start(f32[32,256]{1,0:T(8,128)S(1)} %add_add_fusion.rest_0_), channel_id=1, source_target_pairs={{0,26},{2,24},{4,30},{6,28},{8,18},{10,16},{12,22},{14,20},{16,10}... | collective-permute-start | bytes 98312 | tf_op jit(solution)/shard_map/ppermute | solution.py:500
  25.8 4.3 %collective-permute-start.11 = (f32[32,256]{1,0:T(8,128)S(1)}, f32[32,256]{1,0:T(8,128)S(1)}, u32[]{:S(2)}, u32[]{:S(2)}) collective-permute-start(f32[32,256]{1,0:T(8,128)S(1)} %add_add_fusion.rest_0_), channel_id=1, source_target_pairs={{0,18},{2,16},{4,22},{6,20},{8,26},{10,24},{12,30},{14,28},{16,2},... | collective-permute-start | bytes 98312 | tf_op jit(solution)/shard_map/ppermute | solution.py:500
  26.6 3.9 %collective-permute-start.10 = (f32[32,256]{1,0:T(8,128)S(1)}, f32[32,256]{1,0:T(8,128)S(1)}, u32[]{:S(2)}, u32[]{:S(2)}) collective-permute-start(f32[32,256]{1,0:T(8,128)S(1)} %add_add_fusion.rest_0_), channel_id=1, source_target_pairs={{0,8},{2,10},{4,12},{6,14},{8,0},{10,2},{12,4},{14,6},{16,24},{18,... | collective-permute-start | bytes 98312 | tf_op jit(solution)/shard_map/ppermute | solution.py:500

commit v9 on v8

--- a/solution.py
+++ b/solution.py
@@ -504,9 +504,8 @@
     rounds = []
     base = 1
     while base < count:
-        turn = 1 if base > 1 else 0
         if base * 4 <= count:
-            rounds.append((base, 2 * base + turn, 3 * base + turn))
+            rounds.append((base, 2 * base + 1, 3 * base + 1) if base > 1 else (1, 3, 2))
             base *= 4
         else:
             rounds.append((base,))

time: 32.4 us -> 32.2 us (level)
  waiting for transfers between devices: 5.71 us -> 5.33 us
    ppermute x6, waiting for transfers between devices: 3.07 us -> 2.7 us  [swap(): lax.ppermute(x, 'sub', [(i, i ^ k) for i in range(count)])]
    ppermute x6, starting transfers between devices: 6.32 us -> 6.69 us  [swap(): lax.ppermute(x, 'sub', [(i, i ^ k) for i in range(count)])]
  transfers between devices with their start and end apart: 13 -> 13, of which waited for: 6 -> 4; matrix products, arithmetic and copies ran while one was open for 0% -> 0% of each run, Pallas kernels for 20% -> 20%
where the time goes in v9:
time: 32.2 us; the launch traced here: 32.1 us
  starting transfers between devices  15.2 us (47%)
  Pallas kernels  10.7 us (33%)
  waiting for transfers between devices  5.33 us (17%)
  between operations  0.79 us (2%)
    ppermute x6, starting transfers between devices, swap(): lax.ppermute(x, 'sub', [(i, i ^ k) for i in range(count)])  6.69 us
    ppermute x3, starting transfers between devices, across(): lax.ppermute(b, ('sub', 'rhs'), pairs + [(j, i) for i, j in pairs])  4.7 us
    ppermute x1, starting transfers between devices, body(): lax.ppermute(corner_basis, 'rhs', [((i + k) % parts, i) for i in range(pa...  3 us
    ppermute x6, waiting for transfers between devices, swap(): lax.ppermute(x, 'sub', [(i, i ^ k) for i in range(count)])  2.7 us
    ppermute x3, waiting for transfers between devices, across(): lax.ppermute(b, ('sub', 'rhs'), pairs + [(j, i) for i, j in pairs])  2.62 us
    pallas_call x1, Pallas kernels, body(): call(load_blocks, [packed, packed], 1, raw=(0,), scratch=[pltpu.VMEM((B *...  2.14 us
    pallas_call x1, Pallas kernels, body(): run(assemble, [dense, dense], 5, smem=(0,))  1.66 us
    pallas_call x1, Pallas kernels, body(): run(functools.partial(finish, ncoarse=ncoarse, n_pay=len(pays)), [shape(c...  1.56 us
  transfers between devices with their start and end apart: 13, of which 4 were waited for; matrix products, arithmetic and copies ran while one was open for 0% of the time, Pallas kernels for 20%

profile of v9, /device:TPU:0, one launch (start us, length us, event | category | flops | bytes accessed | tf_op | source)
XLA Modules:
  0.0 32.1 jit_solution(853595493925183911)
XLA Ops:
  0.6 0.0 copy-start.3
  0.6 0.0 copy-start.2
  0.7 0.0 copy-start.5
  0.7 0.0 copy-start.6
  0.7 0.0 copy-start
  0.7 3.0 %collective-permute-start = (f32[4,512]{1,0:T(4,128)}, f32[4,512]{1,0:T(4,128)S(1)}, u32[]{:S(2)}, u32[]{:S(2)}) collective-permute-start(f32[4,512]{1,0:T(4,128)} %rest_0_.1), channel_id=1, source_target_pairs={{1,0},{0,1},{3,2},{2,3},{5,4},{4,5},{7,6},{6,7},{9,8},{8,9},{11,10... | collective-permute-start | bytes 24584 | tf_op jit(solution)/shard_map/ppermute | solution.py:549
  3.7 2.1 %shard_map.95 = (bf16[256,4096]{1,0:T(8,128)(2,1)S(1)}, bf16[256,4096]{1,0:T(8,128)(2,1)S(1)}) custom-call(f32[27,8,4096]{2,1,0:T(8,128)} %bitcast.3), custom_call_target="tpu_custom_call" | custom-call | bytes 16777216 | tf_op jit(solution)/shard_map/pallas_call | solution.py:553
  5.8 0.0 collective-permute-done.rest_1_
  5.8 0.0 copy-done.3
  5.9 0.0 copy-done.2
  5.9 0.0 copy-done.5
  5.9 0.0 copy-done.6
  5.9 0.0 copy-done
  5.9 0.8 %shard_map.96 = (f32[32,512]{1,0:T(8,128)S(1)}, f32[56,256]{1,0:T(8,128)S(1)}, f32[56,256]{1,0:T(8,128)S(1)}) custom-call(s32[1,2,4]{2,1,0:T(2,128)S(1)} %copy-done.2, s32[1,8]{1,0:T(1,128)S(1)} %copy-done.6, f32[32,512]{1,0:T(8,128)S(1)} %copy-done, f32[1,512]{1,0:T(1,128)S(1)} %bitcast.2, bf16[256,4096]{1,0:T(8,128)(2,1)S(1)} %get-tuple-element.23.after_ref.wh_ref, ...), custom_call_target="tpu_custom_call" | custom-call | tf_op jit(solution)/shard_map/pallas_call | solution.py:565
  6.7 1.8 %collective-permute-start.2 = (f32[56,256]{1,0:T(8,128)S(1)}, f32[56,256]{1,0:T(8,128)S(1)}, u32[]{:S(2)}, u32[]{:S(2)}) collective-permute-start(f32[56,256]{1,0:T(8,128)S(1)} %get-tuple-element.26.b_ref), channel_id=1, source_target_pairs={{2,4},{3,5},{6,8},{7,9},{10,12},{11,13},{14,16},{15,17},{18,20},{1... | collective-permute-start | bytes 172040 | tf_op jit(solution)/shard_map/ppermute | solution.py:522
  8.4 0.1 collective-permute-start.1
  8.6 0.0 copy-done.4
  8.6 1.7 %shard_map.97 = (bf16[512,1024]{1,0:T(8,128)(2,1)S(1)}, bf16[512,1024]{1,0:T(8,128)(2,1)S(1)}) custom-call(s32[1,2,4]{2,1,0:T(2,128)S(1)} %copy-done.2, s32[8,27]{1,0:T(8,128)S(1)} %copy-done.4, bf16[256,4096]{1,0:T(8,128)(2,1)S(1)} %get-tuple-element.23.after_ref.wh_ref, bf16[256,4096]{1,0:T(8,128)(2,1)S(1)} %get-tuple-element.27.wl_ref, ...), custom_call_target="tpu_custom_call" | custom-call | tf_op jit(solution)/shard_map/pallas_call | solution.py:573
  10.2 0.6 %shard_map.98 = (bf16[1024,512]{1,0:T(8,128)(2,1)S(1)}, bf16[1024,512]{1,0:T(8,128)(2,1)S(1)}) custom-call(bf16[512,1024]{1,0:T(8,128)(2,1)S(1)} %get-tuple-element.28.high_ref, bf16[512,1024]{1,0:T(8,128)(2,1)S(1)} %get-tuple-element.29.low_ref), custom_call_target="tpu_custom_call" | custom-call | tf_op jit(solution)/shard_map/pallas_call | solution.py:577
  10.8 0.1 collective-permute-done.2.gb_ref
  10.9 0.0 collective-permute-done.1.ga_ref
  10.9 0.9 %shard_map.99 = (f32[48,512]{1,0:T(8,128)S(1)}, f32[96,256]{1,0:T(8,128)S(1)}, f32[96,256]{1,0:T(8,128)S(1)}) custom-call(f32[56,256]{1,0:T(8,128)S(1)} %get-tuple-element.25.after_ref.a_ref, f32[56,256]{1,0:T(8,128)S(1)} %get-tuple-element.26.b_ref, f32[56,256]{1,0:T(8,128)S(1)} %collective-permute-done.1.ga_ref, ...), custom_call_target="tpu_custom_call" | custom-call | tf_op jit(solution)/shard_map/pallas_call | solution.py:583
  11.8 0.4 %collective-permute-start.3 = (f32[96,256]{1,0:T(8,128)S(1)}, f32[96,256]{1,0:T(8,128)S(1)}, u32[]{:S(2)}, u32[]{:S(2)}) collective-permute-start(f32[96,256]{1,0:T(8,128)S(1)} %get-tuple-element.32.own_a_ref), channel_id=1, source_target_pairs={{0,2},{2,0},{4,6},{6,4},{8,10},{10,8},{12,14},{14,12},{16,18},{18,... | collective-permute-start | bytes 294920 | tf_op jit(solution)/shard_map/ppermute | solution.py:517
  12.2 1.5 %collective-permute-start.4 = (f32[96,256]{1,0:T(8,128)S(1)}, f32[96,256]{1,0:T(8,128)S(1)}, u32[]{:S(2)}, u32[]{:S(2)}) collective-permute-start(f32[96,256]{1,0:T(8,128)S(1)} %get-tuple-element.33.own_b_ref), channel_id=1, source_target_pairs={{2,4},{3,5},{6,8},{7,9},{10,12},{11,13},{14,16},{15,17},{18,20},{1... | collective-permute-start | bytes 294920 | tf_op jit(solution)/shard_map/ppermute | solution.py:522
  13.6 0.6 %shard_map.100 = (f32[16,256]{1,0:T(8,128)S(1)}, f32[8,32]{1,0:T(8,128)S(1)}) custom-call(f32[32,512]{1,0:T(8,128)S(1)} %get-tuple-element.24.resid_ref, f32[56,256]{1,0:T(8,128)S(1)} %get-tuple-element.25.after_ref.a_ref, f32[56,256]{1,0:T(8,128)S(1)} %get-tuple-element.26.b_ref, f32[48,512]{1,0:T(8,128)S(1)} %get-tuple-element.34.strain_ref), custom_call_target="tpu_custom_call" | custom-call | tf_op jit(solution)/shard_map/pallas_call | solution.py:587
  14.3 0.0 collective-permute-done.3.got_a_ref
  14.3 2.5 %collective-permute-done.4.got_b_ref = f32[96,256]{1,0:T(8,128)S(1)} collective-permute-done((f32[96,256]{1,0:T(8,128)S(1)}, f32[96,256]{1,0:T(8,128)S(1)}, u32[]{:S(2)}, u32[]{:S(2)}) %collective-permute-start.4) | collective-permute-done | bytes 98336 | tf_op jit(solution)/shard_map/ppermute | solution.py:522
  16.8 1.0 %shard_map.101 = (f32[48,512]{1,0:T(8,128)S(1)}, f32[48,512]{1,0:T(8,128)S(1)}, f32[48,512]{1,0:T(8,128)S(1)}, f32[32,256]{1,0:T(8,128)S(1)}) custom-call(f32[56,256]{1,0:T(8,128)S(1)} %get-tuple-element.25.after_ref.a_ref, f32[56,256]{1,0:T(8,128)S(1)} %get-tuple-element.26.b_ref, f32[56,256]{1,0:T(8,128)S(1)} %collective-permute-done.1.ga_ref, ...), custom_call_target="tpu_custom_call" | custom-call | tf_op jit(solution)/shard_map/pallas_call | solution.py:593
  17.8 0.0 copy-start.1
  17.9 1.0 %collective-permute-start.9 = (f32[32,256]{1,0:T(8,128)S(1)}, f32[32,256]{1,0:T(8,128)S(1)}, u32[]{:S(2)}, u32[]{:S(2)}) collective-permute-start(f32[32,256]{1,0:T(8,128)S(1)} %get-tuple-element.43), channel_id=1, source_target_pairs={{0,4},{2,6},{4,0},{6,2},{8,12},{10,14},{12,8},{14,10},{16,20},{18,... | collective-permute-start | bytes 98312 | tf_op jit(solution)/shard_map/ppermute | solution.py:500
  18.9 1.0 %collective-permute-start.8 = (f32[32,256]{1,0:T(8,128)S(1)}, f32[32,256]{1,0:T(8,128)S(1)}, u32[]{:S(2)}, u32[]{:S(2)}) collective-permute-start(f32[32,256]{1,0:T(8,128)S(1)} %get-tuple-element.43), channel_id=1, source_target_pairs={{0,6},{2,4},{4,2},{6,0},{8,14},{10,12},{12,10},{14,8},{16,22},{18,... | collective-permute-start | bytes 98312 | tf_op jit(solution)/shard_map/ppermute | solution.py:500
  19.9 0.2 collective-permute-start.7
  20.1 0.5 %shard_map.102 = (f32[48,512]{1,0:T(8,128)S(1)}, f32[48,256]{1,0:T(8,128)S(1)}, f32[48,256]{1,0:T(8,128)S(1)}) custom-call(f32[48,512]{1,0:T(8,128)S(1)} %get-tuple-element.38.scaled_ref, f32[48,512]{1,0:T(8,128)S(1)} %get-tuple-element.39.strain_ref, bf16[512,1024]{1,0:T(8,128)(2,1)S(1)} %get-tuple-element.28.high_ref, ...), custom_call_target="tpu_custom_call" | custom-call | tf_op jit(solution)/shard_map/pallas_call | solution.py:602
  20.5 0.3 %collective-permute-start.5 = (f32[48,256]{1,0:T(8,128)S(1)}, f32[48,256]{1,0:T(8,128)S(1)}, u32[]{:S(2)}, u32[]{:S(2)}) collective-permute-start(f32[48,256]{1,0:T(8,128)S(1)} %get-tuple-element.41), channel_id=1, source_target_pairs={{0,2},{2,0},{4,6},{6,4},{8,10},{10,8},{12,14},{14,12},{16,18},{18,... | collective-permute-start | bytes 147464 | tf_op jit(solution)/shard_map/ppermute | solution.py:517
  20.9 1.5 %collective-permute-start.6 = (f32[48,256]{1,0:T(8,128)S(1)}, f32[48,256]{1,0:T(8,128)S(1)}, u32[]{:S(2)}, u32[]{:S(2)}) collective-permute-start(f32[48,256]{1,0:T(8,128)S(1)} %get-tuple-element.42), channel_id=1, source_target_pairs={{2,4},{3,5},{6,8},{7,9},{10,12},{11,13},{14,16},{15,17},{18,20},{1... | collective-permute-start | bytes 147464 | tf_op jit(solution)/shard_map/ppermute | solution.py:522
  22.4 0.0 collective-permute-done.9
  22.4 0.0 collective-permute-done.8
  22.4 0.0 collective-permute-done.7
  22.4 3.8 %collective-permute-start.12 = (f32[32,256]{1,0:T(8,128)S(1)}, f32[32,256]{1,0:T(8,128)S(1)}, u32[]{:S(2)}, u32[]{:S(2)}) collective-permute-start(f32[32,256]{1,0:T(8,128)S(1)} %add_add_fusion.rest_0_), channel_id=1, source_target_pairs={{0,26},{2,24},{4,30},{6,28},{8,18},{10,16},{12,22},{14,20},{16,10}... | collective-permute-start | bytes 98312 | tf_op jit(solution)/shard_map/ppermute | solution.py:500
  26.2 0.0 collective-permute-start.11
  26.2 0.6 %collective-permute-start.10 = (f32[32,256]{1,0:T(8,128)S(1)}, f32[32,256]{1,0:T(8,128)S(1)}, u32[]{:S(2)}, u32[]{:S(2)}) collective-permute-start(f32[32,256]{1,0:T(8,128)S(1)} %add_add_fusion.rest_0_), channel_id=1, source_target_pairs={{0,8},{2,10},{4,12},{6,14},{8,0},{10,2},{12,4},{14,6},{16,24},{18,... | collective-permute-start | bytes 98312 | tf_op jit(solution)/shard_map/ppermute | solution.py:500
  26.9 0.0 collective-permute-done.5.got_a_ref
  26.9 0.0 collective-permute-done.6.got_b_ref
  26.9 0.9 %shard_map.103.all_ref = f32[232,512]{1,0:T(8,128)S(1)} custom-call(s32[1,2,4]{2,1,0:T(2,128)S(1)} %copy-done.2, f32[32,512]{1,0:T(8,128)S(1)} %get-tuple-element.24.resid_ref, f32[56,256]{1,0:T(8,128)S(1)} %get-tuple-element.25.after_ref.a_ref, f32[56,256]{1,0:T(8,128)S(1)} %get-tuple-element.26.b_ref, f32[48,512]{1,0:T(8,128)S(1)} %get-tuple-element.37.image_ref, ...), custom_call_target="tpu_custom_call" | custom-call | tf_op jit(solution)/shard_map/pallas_call | solution.py:607
  27.8 0.4 %collective-permute-done.12.rest_3_ = f32[32,256]{1,0:T(8,128)S(1)} collective-permute-done((f32[32,256]{1,0:T(8,128)S(1)}, f32[32,256]{1,0:T(8,128)S(1)}, u32[]{:S(2)}, u32[]{:S(2)}) %collective-permute-start.12) | collective-permute-done | bytes 32800 | tf_op jit(solution)/shard_map/ppermute | solution.py:500
  28.2 2.3 %collective-permute-done.11.rest_2_ = f32[32,256]{1,0:T(8,128)S(1)} collective-permute-done((f32[32,256]{1,0:T(8,128)S(1)}, f32[32,256]{1,0:T(8,128)S(1)}, u32[]{:S(2)}, u32[]{:S(2)}) %collective-permute-start.11) | collective-permute-done | bytes 32800 | tf_op jit(solution)/shard_map/ppermute | solution.py:500
  30.5 0.0 collective-permute-done.10.rest_1_
  30.5 1.6 %shard_map.104 = (f32[32,512]{1,0:T(8,128)}, f32[32,512]{1,0:T(8,128)}) custom-call(f32[32,32]{1,0:T(8,128)S(1)} %copy-done.1, f32[232,512]{1,0:T(8,128)S(1)} %shard_map.103.all_ref, f32[32,256]{1,0:T(8,128)S(1)} %add_add_fusion.rest_0_, f32[32,256]{1,0:T(8,128)S(1)} %collective-permute-done.10.rest_1_, f32[32,256]{1,0:T(8,128)S(1)} %collective-permute-done.11.rest_2_, ...), custom_call_target="tpu_custom_call" | custom-call | tf_op jit(solution)/shard_map/pallas_call | solution.py:615
  (3 shorter events, 0.0 us)
Async XLA Ops:
  0.6 5.2 %copy-start.3 = (f32[4,512]{1,0:T(4,128)S(1)}, f32[4,512]{1,0:T(4,128)}, u32[]{:S(2)}) copy-start(f32[4,512]{1,0:T(4,128)} %rest_0_.1) | copy-start | bytes 24580
  0.6 5.2 %copy-start.2 = (s32[1,2,4]{2,1,0:T(2,128)S(1)}, s32[1,2,4]{2,1,0:T(2,128)}, u32[]{:S(2)}) copy-start(s32[1,2,4]{2,1,0:T(2,128)} %rows_ref.5) | copy-start | bytes 100
  0.7 5.2 %copy-start.5 = (f32[512]{0:T(512)S(1)}, f32[512]{0:T(512)}, u32[]{:S(2)}) copy-start(f32[512]{0:T(512)} %param.14) | copy-start | bytes 6148
  0.7 5.2 %copy-start.6 = (s32[1,8]{1,0:T(1,128)S(1)}, s32[1,8]{1,0:T(1,128)}, u32[]{:S(2)}) copy-start(s32[1,8]{1,0:T(1,128)} %owner_ref.1) | copy-start | bytes 100
  0.7 5.2 %copy-start = (f32[32,512]{1,0:T(8,128)S(1)}, f32[32,512]{1,0:T(8,128)}, u32[]{:S(2)}) copy-start(f32[32,512]{1,0:T(8,128)} %right_ref.1) | copy-start | bytes 196612
  0.7 5.2 %collective-permute-start = (f32[4,512]{1,0:T(4,128)}, f32[4,512]{1,0:T(4,128)S(1)}, u32[]{:S(2)}, u32[]{:S(2)}) collective-permute-start(f32[4,512]{1,0:T(4,128)} %rest_0_.1), channel_id=1, source_target_pairs={{1,0},{0,1},{3,2},{2,3},{5,4},{4,5},{7,6},{6,7},{9,8},{8,9},{11,10... | collective-permute-start | bytes 24584 | tf_op jit(solution)/shard_map/ppermute | solution.py:549
  3.7 4.9 %copy-start.4 = (s32[8,27]{1,0:T(8,128)S(1)}, s32[8,27]{1,0:T(8,128)}, u32[]{:S(2)}) copy-start(s32[8,27]{1,0:T(8,128)} %columns_ref.1) | copy-start | bytes 2596
  6.7 4.2 %collective-permute-start.2 = (f32[56,256]{1,0:T(8,128)S(1)}, f32[56,256]{1,0:T(8,128)S(1)}, u32[]{:S(2)}, u32[]{:S(2)}) collective-permute-start(f32[56,256]{1,0:T(8,128)S(1)} %get-tuple-element.26.b_ref), channel_id=1, source_target_pairs={{2,4},{3,5},{6,8},{7,9},{10,12},{11,13},{14,16},{15,17},{18,20},{1... | collective-permute-start | bytes 172040 | tf_op jit(solution)/shard_map/ppermute | solution.py:522
  8.4 2.5 %collective-permute-start.1 = (f32[56,256]{1,0:T(8,128)S(1)}, f32[56,256]{1,0:T(8,128)S(1)}, u32[]{:S(2)}, u32[]{:S(2)}) collective-permute-start(f32[56,256]{1,0:T(8,128)S(1)} %get-tuple-element.25.after_ref.a_ref), channel_id=1, source_target_pairs={{0,2},{2,0},{4,6},{6,4},{8,10},{10,8},{12,14},{14,12},{16,18},{18,... | collective-permute-start | bytes 172040 | tf_op jit(solution)/shard_map/ppermute | solution.py:517
  11.8 2.4 %collective-permute-start.3 = (f32[96,256]{1,0:T(8,128)S(1)}, f32[96,256]{1,0:T(8,128)S(1)}, u32[]{:S(2)}, u32[]{:S(2)}) collective-permute-start(f32[96,256]{1,0:T(8,128)S(1)} %get-tuple-element.32.own_a_ref), channel_id=1, source_target_pairs={{0,2},{2,0},{4,6},{6,4},{8,10},{10,8},{12,14},{14,12},{16,18},{18,... | collective-permute-start | bytes 294920 | tf_op jit(solution)/shard_map/ppermute | solution.py:517
  12.2 4.6 %collective-permute-start.4 = (f32[96,256]{1,0:T(8,128)S(1)}, f32[96,256]{1,0:T(8,128)S(1)}, u32[]{:S(2)}, u32[]{:S(2)}) collective-permute-start(f32[96,256]{1,0:T(8,128)S(1)} %get-tuple-element.33.own_b_ref), channel_id=1, source_target_pairs={{2,4},{3,5},{6,8},{7,9},{10,12},{11,13},{14,16},{15,17},{18,20},{1... | collective-permute-start | bytes 294920 | tf_op jit(solution)/shard_map/ppermute | solution.py:522
  17.8 12.7 %copy-start.1 = (f32[32,32]{1,0:T(8,128)S(1)}, f32[32,32]{1,0:T(8,128)}, u32[]{:S(2)}) copy-start(f32[32,32]{1,0:T(8,128)} %inverse_ref.1) | copy-start | bytes 12292
  17.9 4.5 %collective-permute-start.9 = (f32[32,256]{1,0:T(8,128)S(1)}, f32[32,256]{1,0:T(8,128)S(1)}, u32[]{:S(2)}, u32[]{:S(2)}) collective-permute-start(f32[32,256]{1,0:T(8,128)S(1)} %get-tuple-element.43), channel_id=1, source_target_pairs={{0,4},{2,6},{4,0},{6,2},{8,12},{10,14},{12,8},{14,10},{16,20},{18,... | collective-permute-start | bytes 98312 | tf_op jit(solution)/shard_map/ppermute | solution.py:500
  18.9 3.5 %collective-permute-start.8 = (f32[32,256]{1,0:T(8,128)S(1)}, f32[32,256]{1,0:T(8,128)S(1)}, u32[]{:S(2)}, u32[]{:S(2)}) collective-permute-start(f32[32,256]{1,0:T(8,128)S(1)} %get-tuple-element.43), channel_id=1, source_target_pairs={{0,6},{2,4},{4,2},{6,0},{8,14},{10,12},{12,10},{14,8},{16,22},{18,... | collective-permute-start | bytes 98312 | tf_op jit(solution)/shard_map/ppermute | solution.py:500
  19.9 2.5 %collective-permute-start.7 = (f32[32,256]{1,0:T(8,128)S(1)}, f32[32,256]{1,0:T(8,128)S(1)}, u32[]{:S(2)}, u32[]{:S(2)}) collective-permute-start(f32[32,256]{1,0:T(8,128)S(1)} %get-tuple-element.43), channel_id=1, source_target_pairs={{0,2},{2,0},{4,6},{6,4},{8,10},{10,8},{12,14},{14,12},{16,18},{18,... | collective-permute-start | bytes 98312 | tf_op jit(solution)/shard_map/ppermute | solution.py:500
  20.5 6.4 %collective-permute-start.5 = (f32[48,256]{1,0:T(8,128)S(1)}, f32[48,256]{1,0:T(8,128)S(1)}, u32[]{:S(2)}, u32[]{:S(2)}) collective-permute-start(f32[48,256]{1,0:T(8,128)S(1)} %get-tuple-element.41), channel_id=1, source_target_pairs={{0,2},{2,0},{4,6},{6,4},{8,10},{10,8},{12,14},{14,12},{16,18},{18,... | collective-permute-start | bytes 147464 | tf_op jit(solution)/shard_map/ppermute | solution.py:517
  20.9 6.0 %collective-permute-start.6 = (f32[48,256]{1,0:T(8,128)S(1)}, f32[48,256]{1,0:T(8,128)S(1)}, u32[]{:S(2)}, u32[]{:S(2)}) collective-permute-start(f32[48,256]{1,0:T(8,128)S(1)} %get-tuple-element.42), channel_id=1, source_target_pairs={{2,4},{3,5},{6,8},{7,9},{10,12},{11,13},{14,16},{15,17},{18,20},{1... | collective-permute-start | bytes 147464 | tf_op jit(solution)/shard_map/ppermute | solution.py:522
  22.4 5.8 %collective-permute-start.12 = (f32[32,256]{1,0:T(8,128)S(1)}, f32[32,256]{1,0:T(8,128)S(1)}, u32[]{:S(2)}, u32[]{:S(2)}) collective-permute-start(f32[32,256]{1,0:T(8,128)S(1)} %add_add_fusion.rest_0_), channel_id=1, source_target_pairs={{0,26},{2,24},{4,30},{6,28},{8,18},{10,16},{12,22},{14,20},{16,10}... | collective-permute-start | bytes 98312 | tf_op jit(solution)/shard_map/ppermute | solution.py:500
  26.2 4.3 %collective-permute-start.11 = (f32[32,256]{1,0:T(8,128)S(1)}, f32[32,256]{1,0:T(8,128)S(1)}, u32[]{:S(2)}, u32[]{:S(2)}) collective-permute-start(f32[32,256]{1,0:T(8,128)S(1)} %add_add_fusion.rest_0_), channel_id=1, source_target_pairs={{0,18},{2,16},{4,22},{6,20},{8,26},{10,24},{12,30},{14,28},{16,2},... | collective-permute-start | bytes 98312 | tf_op jit(solution)/shard_map/ppermute | solution.py:500
  26.2 4.3 %collective-permute-start.10 = (f32[32,256]{1,0:T(8,128)S(1)}, f32[32,256]{1,0:T(8,128)S(1)}, u32[]{:S(2)}, u32[]{:S(2)}) collective-permute-start(f32[32,256]{1,0:T(8,128)S(1)} %add_add_fusion.rest_0_), channel_id=1, source_target_pairs={{0,8},{2,10},{4,12},{6,14},{8,0},{10,2},{12,4},{14,6},{16,24},{18,... | collective-permute-start | bytes 98312 | tf_op jit(solution)/shard_map/ppermute | solution.py:500

commit v10 on v8

--- a/solution.py
+++ b/solution.py
@@ -172,22 +172,21 @@
             owner = owner_ref[0, ((mine + k) % parts) * per + t]
             coarse = coarse + jnp.where(unknown == owner, basis_refs[k][t : t + 1, :], 0.0)
     right = right_ref[...]
-    fine = right * scale[0:1]
     live = cases + FRAME
     for n in range(NB):
         cut = slice(B * n, B * (n + 1))
-        blk_ref[n, 0:cases, :] = fine[:, cut]
+        blk_ref[n, 0:cases, :] = right[:, cut]
         blk_ref[n, cases:live, :] = coarse[:, cut]
-        blk_ref[n, live : live + 8, :] = scale[:, cut]
-        blk_ref[n, live + 8 :, :] = right[:, cut]
+        blk_ref[n, live:, :] = scale[:, cut]
     for j in range(0, NB, 2):
         pair = jnp.concatenate(
             [blk_ref[place_of(rows_ref, odd, j)], blk_ref[place_of(rows_ref, odd, j + 1)]], axis=1
         )
         target = side_a_ref if j < IFB else side_b_ref
         at = B * (j % IFB)
-        target[:, at : at + 2 * B] = pair[: live + 8]
-        resid_ref[:, B * j : B * (j + 2)] = pair[live + 8 :]
+        target[:cases, at : at + 2 * B] = pair[:cases] * pair[live : live + 1]
+        target[cases:, at : at + 2 * B] = pair[cases:]
+        resid_ref[:, B * j : B * (j + 2)] = pair[:cases]
 
 
 def frame_start():
@@ -305,8 +304,12 @@
     image_ref[...] = first
     scaled_ref[...] = own
     paired = jnp.concatenate([own, strain], axis=1)
-    gram = exact(paired[cases:], paired, NT)
-    cross = exact(first[cases:], own, NT)
+    blank = jnp.zeros((FRAME, ROWS), F32)
+    left = jnp.concatenate(
+        [paired[cases:], jnp.concatenate([first[cases:], blank], axis=1)], axis=0
+    )
+    both = near(left, paired, NT)
+    gram, cross = both[:FRAME], both[FRAME:]
     lead = paired[:cases]
     width = cases + ncoarse
     tall_ref[...] = jnp.zeros_like(tall_ref)
@@ -568,7 +571,7 @@
         [shape(cases, OWN), shape(live + 8, EDGE), shape(live + 8, EDGE)],
         5 + parts,
         smem=(0, 1),
-        scratch=[pltpu.VMEM((NB, live + 8 + cases, B), F32)],
+        scratch=[pltpu.VMEM((NB, live + 8, B), F32)],
     )(interface_rows, corner_owner, right_side, jacobi_scale.reshape(1, OWN), wh, *bases)
     dense = jax.ShapeDtypeStruct((ROWS, EXT), BF16)
     high, low = run(assemble, [dense, dense], 5, smem=(0,))(

time: 32.4 us -> 32.3 us (level)
  no operation moved by 1% of the time
where the time goes in v10:
time: 32.3 us; the launch traced here: 32 us
  starting transfers between devices  14.9 us (46%)
  Pallas kernels  10.6 us (33%)
  waiting for transfers between devices  5.7 us (18%)
  between operations  0.79 us (2%)
    ppermute x6, starting transfers between devices, swap(): lax.ppermute(x, 'sub', [(i, i ^ k) for i in range(count)])  6.32 us
    ppermute x3, starting transfers between devices, across(): lax.ppermute(b, ('sub', 'rhs'), pairs + [(j, i) for i, j in pairs])  4.7 us
    ppermute x6, waiting for transfers between devices, swap(): lax.ppermute(x, 'sub', [(i, i ^ k) for i in range(count)])  3.07 us
    ppermute x1, starting transfers between devices, body(): lax.ppermute(corner_basis, 'rhs', [((i + k) % parts, i) for i in range(pa...  3 us
    ppermute x3, waiting for transfers between devices, across(): lax.ppermute(b, ('sub', 'rhs'), pairs + [(j, i) for i, j in pairs])  2.62 us
    pallas_call x1, Pallas kernels, body(): call(load_blocks, [packed, packed], 1, raw=(0,), scratch=[pltpu.VMEM((B *...  2.14 us
    pallas_call x1, Pallas kernels, body(): run(assemble, [dense, dense], 5, smem=(0,))  1.66 us
    pallas_call x1, Pallas kernels, body(): run(functools.partial(finish, ncoarse=ncoarse, n_pay=len(pays)), [shape(c...  1.56 us
  transfers between devices with their start and end apart: 13, of which 6 were waited for; matrix products, arithmetic and copies ran while one was open for 0% of the time, Pallas kernels for 20%

profile of v10, /device:TPU:0, one launch (start us, length us, event | category | flops | bytes accessed | tf_op | source)
XLA Modules:
  0.0 32.0 jit_solution(4315369517934539986)
XLA Ops:
  0.6 0.0 copy-start.3
  0.6 0.0 copy-start.2
  0.7 0.0 copy-start.5
  0.7 0.0 copy-start.6
  0.7 0.0 copy-start
  0.7 3.0 %collective-permute-start = (f32[4,512]{1,0:T(4,128)}, f32[4,512]{1,0:T(4,128)S(1)}, u32[]{:S(2)}, u32[]{:S(2)}) collective-permute-start(f32[4,512]{1,0:T(4,128)} %rest_0_.1), channel_id=1, source_target_pairs={{1,0},{0,1},{3,2},{2,3},{5,4},{4,5},{7,6},{6,7},{9,8},{8,9},{11,10... | collective-permute-start | bytes 24584 | tf_op jit(solution)/shard_map/ppermute | solution.py:553
  3.7 2.1 %shard_map.95 = (bf16[256,4096]{1,0:T(8,128)(2,1)S(1)}, bf16[256,4096]{1,0:T(8,128)(2,1)S(1)}) custom-call(f32[27,8,4096]{2,1,0:T(8,128)} %bitcast.3), custom_call_target="tpu_custom_call" | custom-call | bytes 16777216 | tf_op jit(solution)/shard_map/pallas_call | solution.py:557
  5.8 0.0 collective-permute-done.rest_1_
  5.8 0.0 copy-done.3
  5.9 0.0 copy-done.2
  5.9 0.0 copy-done.5
  5.9 0.0 copy-done.6
  5.9 0.0 copy-done
  5.9 0.8 %shard_map.96 = (f32[32,512]{1,0:T(8,128)S(1)}, f32[56,256]{1,0:T(8,128)S(1)}, f32[56,256]{1,0:T(8,128)S(1)}) custom-call(s32[1,2,4]{2,1,0:T(2,128)S(1)} %copy-done.2, s32[1,8]{1,0:T(1,128)S(1)} %copy-done.6, f32[32,512]{1,0:T(8,128)S(1)} %copy-done, f32[1,512]{1,0:T(1,128)S(1)} %bitcast.2, bf16[256,4096]{1,0:T(8,128)(2,1)S(1)} %get-tuple-element.23.after_ref.wh_ref, ...), custom_call_target="tpu_custom_call" | custom-call | tf_op jit(solution)/shard_map/pallas_call | solution.py:569
  6.7 1.8 %collective-permute-start.2 = (f32[56,256]{1,0:T(8,128)S(1)}, f32[56,256]{1,0:T(8,128)S(1)}, u32[]{:S(2)}, u32[]{:S(2)}) collective-permute-start(f32[56,256]{1,0:T(8,128)S(1)} %get-tuple-element.26.b_ref), channel_id=1, source_target_pairs={{2,4},{3,5},{6,8},{7,9},{10,12},{11,13},{14,16},{15,17},{18,20},{1... | collective-permute-start | bytes 172040 | tf_op jit(solution)/shard_map/ppermute | solution.py:526
  8.4 0.1 collective-permute-start.1
  8.6 0.0 copy-done.4
  8.6 1.7 %shard_map.97 = (bf16[512,1024]{1,0:T(8,128)(2,1)S(1)}, bf16[512,1024]{1,0:T(8,128)(2,1)S(1)}) custom-call(s32[1,2,4]{2,1,0:T(2,128)S(1)} %copy-done.2, s32[8,27]{1,0:T(8,128)S(1)} %copy-done.4, bf16[256,4096]{1,0:T(8,128)(2,1)S(1)} %get-tuple-element.23.after_ref.wh_ref, bf16[256,4096]{1,0:T(8,128)(2,1)S(1)} %get-tuple-element.27.wl_ref, ...), custom_call_target="tpu_custom_call" | custom-call | tf_op jit(solution)/shard_map/pallas_call | solution.py:577
  10.2 0.6 %shard_map.98 = (bf16[1024,512]{1,0:T(8,128)(2,1)S(1)}, bf16[1024,512]{1,0:T(8,128)(2,1)S(1)}) custom-call(bf16[512,1024]{1,0:T(8,128)(2,1)S(1)} %get-tuple-element.28.high_ref, bf16[512,1024]{1,0:T(8,128)(2,1)S(1)} %get-tuple-element.29.low_ref), custom_call_target="tpu_custom_call" | custom-call | tf_op jit(solution)/shard_map/pallas_call | solution.py:581
  10.8 0.1 collective-permute-done.2.gb_ref
  10.9 0.0 collective-permute-done.1.ga_ref
  10.9 0.9 %shard_map.99 = (f32[48,512]{1,0:T(8,128)S(1)}, f32[96,256]{1,0:T(8,128)S(1)}, f32[96,256]{1,0:T(8,128)S(1)}) custom-call(f32[56,256]{1,0:T(8,128)S(1)} %get-tuple-element.25.after_ref.a_ref, f32[56,256]{1,0:T(8,128)S(1)} %get-tuple-element.26.b_ref, f32[56,256]{1,0:T(8,128)S(1)} %collective-permute-done.1.ga_ref, ...), custom_call_target="tpu_custom_call" | custom-call | tf_op jit(solution)/shard_map/pallas_call | solution.py:587
  11.8 0.4 %collective-permute-start.3 = (f32[96,256]{1,0:T(8,128)S(1)}, f32[96,256]{1,0:T(8,128)S(1)}, u32[]{:S(2)}, u32[]{:S(2)}) collective-permute-start(f32[96,256]{1,0:T(8,128)S(1)} %get-tuple-element.32.own_a_ref), channel_id=1, source_target_pairs={{0,2},{2,0},{4,6},{6,4},{8,10},{10,8},{12,14},{14,12},{16,18},{18,... | collective-permute-start | bytes 294920 | tf_op jit(solution)/shard_map/ppermute | solution.py:521
  12.2 1.5 %collective-permute-start.4 = (f32[96,256]{1,0:T(8,128)S(1)}, f32[96,256]{1,0:T(8,128)S(1)}, u32[]{:S(2)}, u32[]{:S(2)}) collective-permute-start(f32[96,256]{1,0:T(8,128)S(1)} %get-tuple-element.33.own_b_ref), channel_id=1, source_target_pairs={{2,4},{3,5},{6,8},{7,9},{10,12},{11,13},{14,16},{15,17},{18,20},{1... | collective-permute-start | bytes 294920 | tf_op jit(solution)/shard_map/ppermute | solution.py:526
  13.6 0.6 %shard_map.100 = (f32[16,256]{1,0:T(8,128)S(1)}, f32[8,32]{1,0:T(8,128)S(1)}) custom-call(f32[32,512]{1,0:T(8,128)S(1)} %get-tuple-element.24.resid_ref, f32[56,256]{1,0:T(8,128)S(1)} %get-tuple-element.25.after_ref.a_ref, f32[56,256]{1,0:T(8,128)S(1)} %get-tuple-element.26.b_ref, f32[48,512]{1,0:T(8,128)S(1)} %get-tuple-element.34.strain_ref), custom_call_target="tpu_custom_call" | custom-call | tf_op jit(solution)/shard_map/pallas_call | solution.py:591
  14.2 0.0 collective-permute-done.3.got_a_ref
  14.2 2.5 %collective-permute-done.4.got_b_ref = f32[96,256]{1,0:T(8,128)S(1)} collective-permute-done((f32[96,256]{1,0:T(8,128)S(1)}, f32[96,256]{1,0:T(8,128)S(1)}, u32[]{:S(2)}, u32[]{:S(2)}) %collective-permute-start.4) | collective-permute-done | bytes 98336 | tf_op jit(solution)/shard_map/ppermute | solution.py:526
  16.8 1.0 %shard_map.101 = (f32[48,512]{1,0:T(8,128)S(1)}, f32[48,512]{1,0:T(8,128)S(1)}, f32[48,512]{1,0:T(8,128)S(1)}, f32[32,256]{1,0:T(8,128)S(1)}) custom-call(f32[56,256]{1,0:T(8,128)S(1)} %get-tuple-element.25.after_ref.a_ref, f32[56,256]{1,0:T(8,128)S(1)} %get-tuple-element.26.b_ref, f32[56,256]{1,0:T(8,128)S(1)} %collective-permute-done.1.ga_ref, ...), custom_call_target="tpu_custom_call" | custom-call | tf_op jit(solution)/shard_map/pallas_call | solution.py:597
  17.8 0.0 copy-start.1
  17.8 2.0 %collective-permute-start.9 = (f32[32,256]{1,0:T(8,128)S(1)}, f32[32,256]{1,0:T(8,128)S(1)}, u32[]{:S(2)}, u32[]{:S(2)}) collective-permute-start(f32[32,256]{1,0:T(8,128)S(1)} %get-tuple-element.43), channel_id=1, source_target_pairs={{0,6},{2,4},{4,2},{6,0},{8,14},{10,12},{12,10},{14,8},{16,22},{18,... | collective-permute-start | bytes 98312 | tf_op jit(solution)/shard_map/ppermute | solution.py:503
  19.7 0.0 collective-permute-start.8
  19.7 0.2 collective-permute-start.7
  19.9 0.5 %shard_map.102 = (f32[48,512]{1,0:T(8,128)S(1)}, f32[48,256]{1,0:T(8,128)S(1)}, f32[48,256]{1,0:T(8,128)S(1)}) custom-call(f32[48,512]{1,0:T(8,128)S(1)} %get-tuple-element.38.scaled_ref, f32[48,512]{1,0:T(8,128)S(1)} %get-tuple-element.39.strain_ref, bf16[512,1024]{1,0:T(8,128)(2,1)S(1)} %get-tuple-element.28.high_ref, ...), custom_call_target="tpu_custom_call" | custom-call | tf_op jit(solution)/shard_map/pallas_call | solution.py:606
  20.4 0.3 %collective-permute-start.5 = (f32[48,256]{1,0:T(8,128)S(1)}, f32[48,256]{1,0:T(8,128)S(1)}, u32[]{:S(2)}, u32[]{:S(2)}) collective-permute-start(f32[48,256]{1,0:T(8,128)S(1)} %get-tuple-element.41), channel_id=1, source_target_pairs={{0,2},{2,0},{4,6},{6,4},{8,10},{10,8},{12,14},{14,12},{16,18},{18,... | collective-permute-start | bytes 147464 | tf_op jit(solution)/shard_map/ppermute | solution.py:521
  20.7 1.5 %collective-permute-start.6 = (f32[48,256]{1,0:T(8,128)S(1)}, f32[48,256]{1,0:T(8,128)S(1)}, u32[]{:S(2)}, u32[]{:S(2)}) collective-permute-start(f32[48,256]{1,0:T(8,128)S(1)} %get-tuple-element.42), channel_id=1, source_target_pairs={{2,4},{3,5},{6,8},{7,9},{10,12},{11,13},{14,16},{15,17},{18,20},{1... | collective-permute-start | bytes 147464 | tf_op jit(solution)/shard_map/ppermute | solution.py:526
  22.2 0.0 collective-permute-done.9
  22.2 1.4 %collective-permute-done.8 = f32[32,256]{1,0:T(8,128)S(1)} collective-permute-done((f32[32,256]{1,0:T(8,128)S(1)}, f32[32,256]{1,0:T(8,128)S(1)}, u32[]{:S(2)}, u32[]{:S(2)}) %collective-permute-start.8) | collective-permute-done | bytes 32800 | tf_op jit(solution)/shard_map/ppermute | solution.py:503
  23.6 0.0 collective-permute-done.7
  23.7 2.1 %collective-permute-start.12 = (f32[32,256]{1,0:T(8,128)S(1)}, f32[32,256]{1,0:T(8,128)S(1)}, u32[]{:S(2)}, u32[]{:S(2)}) collective-permute-start(f32[32,256]{1,0:T(8,128)S(1)} %add_add_fusion.rest_0_), channel_id=1, source_target_pairs={{0,26},{2,24},{4,30},{6,28},{8,18},{10,16},{12,22},{14,20},{16,10}... | collective-permute-start | bytes 98312 | tf_op jit(solution)/shard_map/ppermute | solution.py:503
  25.7 0.8 %collective-permute-start.11 = (f32[32,256]{1,0:T(8,128)S(1)}, f32[32,256]{1,0:T(8,128)S(1)}, u32[]{:S(2)}, u32[]{:S(2)}) collective-permute-start(f32[32,256]{1,0:T(8,128)S(1)} %add_add_fusion.rest_0_), channel_id=1, source_target_pairs={{0,18},{2,16},{4,22},{6,20},{8,26},{10,24},{12,30},{14,28},{16,2},... | collective-permute-start | bytes 98312 | tf_op jit(solution)/shard_map/ppermute | solution.py:503
  26.5 1.3 %collective-permute-start.10 = (f32[32,256]{1,0:T(8,128)S(1)}, f32[32,256]{1,0:T(8,128)S(1)}, u32[]{:S(2)}, u32[]{:S(2)}) collective-permute-start(f32[32,256]{1,0:T(8,128)S(1)} %add_add_fusion.rest_0_), channel_id=1, source_target_pairs={{0,8},{2,10},{4,12},{6,14},{8,0},{10,2},{12,4},{14,6},{16,24},{18,... | collective-permute-start | bytes 98312 | tf_op jit(solution)/shard_map/ppermute | solution.py:503
  27.8 0.0 collective-permute-done.5.got_a_ref
  27.8 0.0 collective-permute-done.6.got_b_ref
  27.8 0.9 %shard_map.103.all_ref = f32[232,512]{1,0:T(8,128)S(1)} custom-call(s32[1,2,4]{2,1,0:T(2,128)S(1)} %copy-done.2, f32[32,512]{1,0:T(8,128)S(1)} %get-tuple-element.24.resid_ref, f32[56,256]{1,0:T(8,128)S(1)} %get-tuple-element.25.after_ref.a_ref, f32[56,256]{1,0:T(8,128)S(1)} %get-tuple-element.26.b_ref, f32[48,512]{1,0:T(8,128)S(1)} %get-tuple-element.37.image_ref, ...), custom_call_target="tpu_custom_call" | custom-call | tf_op jit(solution)/shard_map/pallas_call | solution.py:611
  28.8 0.2 collective-permute-done.12.rest_3_
  29.0 1.1 %collective-permute-done.11.rest_2_ = f32[32,256]{1,0:T(8,128)S(1)} collective-permute-done((f32[32,256]{1,0:T(8,128)S(1)}, f32[32,256]{1,0:T(8,128)S(1)}, u32[]{:S(2)}, u32[]{:S(2)}) %collective-permute-start.11) | collective-permute-done | bytes 32800 | tf_op jit(solution)/shard_map/ppermute | solution.py:503
  30.1 0.4 %collective-permute-done.10.rest_1_ = f32[32,256]{1,0:T(8,128)S(1)} collective-permute-done((f32[32,256]{1,0:T(8,128)S(1)}, f32[32,256]{1,0:T(8,128)S(1)}, u32[]{:S(2)}, u32[]{:S(2)}) %collective-permute-start.10) | collective-permute-done | bytes 32800 | tf_op jit(solution)/shard_map/ppermute | solution.py:503
  30.4 1.6 %shard_map.104 = (f32[32,512]{1,0:T(8,128)}, f32[32,512]{1,0:T(8,128)}) custom-call(f32[32,32]{1,0:T(8,128)S(1)} %copy-done.1, f32[232,512]{1,0:T(8,128)S(1)} %shard_map.103.all_ref, f32[32,256]{1,0:T(8,128)S(1)} %add_add_fusion.rest_0_, f32[32,256]{1,0:T(8,128)S(1)} %collective-permute-done.10.rest_1_, f32[32,256]{1,0:T(8,128)S(1)} %collective-permute-done.11.rest_2_, ...), custom_call_target="tpu_custom_call" | custom-call | tf_op jit(solution)/shard_map/pallas_call | solution.py:619
  (3 shorter events, 0.0 us)
Async XLA Ops:
  0.6 5.2 %copy-start.3 = (f32[4,512]{1,0:T(4,128)S(1)}, f32[4,512]{1,0:T(4,128)}, u32[]{:S(2)}) copy-start(f32[4,512]{1,0:T(4,128)} %rest_0_.1) | copy-start | bytes 24580
  0.6 5.2 %copy-start.2 = (s32[1,2,4]{2,1,0:T(2,128)S(1)}, s32[1,2,4]{2,1,0:T(2,128)}, u32[]{:S(2)}) copy-start(s32[1,2,4]{2,1,0:T(2,128)} %rows_ref.5) | copy-start | bytes 100
  0.7 5.2 %copy-start.5 = (f32[512]{0:T(512)S(1)}, f32[512]{0:T(512)}, u32[]{:S(2)}) copy-start(f32[512]{0:T(512)} %param.14) | copy-start | bytes 6148
  0.7 5.2 %copy-start.6 = (s32[1,8]{1,0:T(1,128)S(1)}, s32[1,8]{1,0:T(1,128)}, u32[]{:S(2)}) copy-start(s32[1,8]{1,0:T(1,128)} %owner_ref.1) | copy-start | bytes 100
  0.7 5.2 %copy-start = (f32[32,512]{1,0:T(8,128)S(1)}, f32[32,512]{1,0:T(8,128)}, u32[]{:S(2)}) copy-start(f32[32,512]{1,0:T(8,128)} %right_ref.1) | copy-start | bytes 196612
  0.7 5.2 %collective-permute-start = (f32[4,512]{1,0:T(4,128)}, f32[4,512]{1,0:T(4,128)S(1)}, u32[]{:S(2)}, u32[]{:S(2)}) collective-permute-start(f32[4,512]{1,0:T(4,128)} %rest_0_.1), channel_id=1, source_target_pairs={{1,0},{0,1},{3,2},{2,3},{5,4},{4,5},{7,6},{6,7},{9,8},{8,9},{11,10... | collective-permute-start | bytes 24584 | tf_op jit(solution)/shard_map/ppermute | solution.py:553
  3.7 4.9 %copy-start.4 = (s32[8,27]{1,0:T(8,128)S(1)}, s32[8,27]{1,0:T(8,128)}, u32[]{:S(2)}) copy-start(s32[8,27]{1,0:T(8,128)} %columns_ref.1) | copy-start | bytes 2596
  6.7 4.2 %collective-permute-start.2 = (f32[56,256]{1,0:T(8,128)S(1)}, f32[56,256]{1,0:T(8,128)S(1)}, u32[]{:S(2)}, u32[]{:S(2)}) collective-permute-start(f32[56,256]{1,0:T(8,128)S(1)} %get-tuple-element.26.b_ref), channel_id=1, source_target_pairs={{2,4},{3,5},{6,8},{7,9},{10,12},{11,13},{14,16},{15,17},{18,20},{1... | collective-permute-start | bytes 172040 | tf_op jit(solution)/shard_map/ppermute | solution.py:526
  8.4 2.5 %collective-permute-start.1 = (f32[56,256]{1,0:T(8,128)S(1)}, f32[56,256]{1,0:T(8,128)S(1)}, u32[]{:S(2)}, u32[]{:S(2)}) collective-permute-start(f32[56,256]{1,0:T(8,128)S(1)} %get-tuple-element.25.after_ref.a_ref), channel_id=1, source_target_pairs={{0,2},{2,0},{4,6},{6,4},{8,10},{10,8},{12,14},{14,12},{16,18},{18,... | collective-permute-start | bytes 172040 | tf_op jit(solution)/shard_map/ppermute | solution.py:521
  11.8 2.4 %collective-permute-start.3 = (f32[96,256]{1,0:T(8,128)S(1)}, f32[96,256]{1,0:T(8,128)S(1)}, u32[]{:S(2)}, u32[]{:S(2)}) collective-permute-start(f32[96,256]{1,0:T(8,128)S(1)} %get-tuple-element.32.own_a_ref), channel_id=1, source_target_pairs={{0,2},{2,0},{4,6},{6,4},{8,10},{10,8},{12,14},{14,12},{16,18},{18,... | collective-permute-start | bytes 294920 | tf_op jit(solution)/shard_map/ppermute | solution.py:521
  12.2 4.6 %collective-permute-start.4 = (f32[96,256]{1,0:T(8,128)S(1)}, f32[96,256]{1,0:T(8,128)S(1)}, u32[]{:S(2)}, u32[]{:S(2)}) collective-permute-start(f32[96,256]{1,0:T(8,128)S(1)} %get-tuple-element.33.own_b_ref), channel_id=1, source_target_pairs={{2,4},{3,5},{6,8},{7,9},{10,12},{11,13},{14,16},{15,17},{18,20},{1... | collective-permute-start | bytes 294920 | tf_op jit(solution)/shard_map/ppermute | solution.py:526
  17.8 12.7 %copy-start.1 = (f32[32,32]{1,0:T(8,128)S(1)}, f32[32,32]{1,0:T(8,128)}, u32[]{:S(2)}) copy-start(f32[32,32]{1,0:T(8,128)} %inverse_ref.1) | copy-start | bytes 12292
  17.8 4.4 %collective-permute-start.9 = (f32[32,256]{1,0:T(8,128)S(1)}, f32[32,256]{1,0:T(8,128)S(1)}, u32[]{:S(2)}, u32[]{:S(2)}) collective-permute-start(f32[32,256]{1,0:T(8,128)S(1)} %get-tuple-element.43), channel_id=1, source_target_pairs={{0,6},{2,4},{4,2},{6,0},{8,14},{10,12},{12,10},{14,8},{16,22},{18,... | collective-permute-start | bytes 98312 | tf_op jit(solution)/shard_map/ppermute | solution.py:503
  19.7 3.9 %collective-permute-start.8 = (f32[32,256]{1,0:T(8,128)S(1)}, f32[32,256]{1,0:T(8,128)S(1)}, u32[]{:S(2)}, u32[]{:S(2)}) collective-permute-start(f32[32,256]{1,0:T(8,128)S(1)} %get-tuple-element.43), channel_id=1, source_target_pairs={{0,4},{2,6},{4,0},{6,2},{8,12},{10,14},{12,8},{14,10},{16,20},{18,... | collective-permute-start | bytes 98312 | tf_op jit(solution)/shard_map/ppermute | solution.py:503
  19.7 3.9 %collective-permute-start.7 = (f32[32,256]{1,0:T(8,128)S(1)}, f32[32,256]{1,0:T(8,128)S(1)}, u32[]{:S(2)}, u32[]{:S(2)}) collective-permute-start(f32[32,256]{1,0:T(8,128)S(1)} %get-tuple-element.43), channel_id=1, source_target_pairs={{0,2},{2,0},{4,6},{6,4},{8,10},{10,8},{12,14},{14,12},{16,18},{18,... | collective-permute-start | bytes 98312 | tf_op jit(solution)/shard_map/ppermute | solution.py:503
  20.4 7.5 %collective-permute-start.5 = (f32[48,256]{1,0:T(8,128)S(1)}, f32[48,256]{1,0:T(8,128)S(1)}, u32[]{:S(2)}, u32[]{:S(2)}) collective-permute-start(f32[48,256]{1,0:T(8,128)S(1)} %get-tuple-element.41), channel_id=1, source_target_pairs={{0,2},{2,0},{4,6},{6,4},{8,10},{10,8},{12,14},{14,12},{16,18},{18,... | collective-permute-start | bytes 147464 | tf_op jit(solution)/shard_map/ppermute | solution.py:521
  20.7 7.1 %collective-permute-start.6 = (f32[48,256]{1,0:T(8,128)S(1)}, f32[48,256]{1,0:T(8,128)S(1)}, u32[]{:S(2)}, u32[]{:S(2)}) collective-permute-start(f32[48,256]{1,0:T(8,128)S(1)} %get-tuple-element.42), channel_id=1, source_target_pairs={{2,4},{3,5},{6,8},{7,9},{10,12},{11,13},{14,16},{15,17},{18,20},{1... | collective-permute-start | bytes 147464 | tf_op jit(solution)/shard_map/ppermute | solution.py:526
  23.7 5.3 %collective-permute-start.12 = (f32[32,256]{1,0:T(8,128)S(1)}, f32[32,256]{1,0:T(8,128)S(1)}, u32[]{:S(2)}, u32[]{:S(2)}) collective-permute-start(f32[32,256]{1,0:T(8,128)S(1)} %add_add_fusion.rest_0_), channel_id=1, source_target_pairs={{0,26},{2,24},{4,30},{6,28},{8,18},{10,16},{12,22},{14,20},{16,10}... | collective-permute-start | bytes 98312 | tf_op jit(solution)/shard_map/ppermute | solution.py:503
  25.7 4.3 %collective-permute-start.11 = (f32[32,256]{1,0:T(8,128)S(1)}, f32[32,256]{1,0:T(8,128)S(1)}, u32[]{:S(2)}, u32[]{:S(2)}) collective-permute-start(f32[32,256]{1,0:T(8,128)S(1)} %add_add_fusion.rest_0_), channel_id=1, source_target_pairs={{0,18},{2,16},{4,22},{6,20},{8,26},{10,24},{12,30},{14,28},{16,2},... | collective-permute-start | bytes 98312 | tf_op jit(solution)/shard_map/ppermute | solution.py:503
  26.5 3.9 %collective-permute-start.10 = (f32[32,256]{1,0:T(8,128)S(1)}, f32[32,256]{1,0:T(8,128)S(1)}, u32[]{:S(2)}, u32[]{:S(2)}) collective-permute-start(f32[32,256]{1,0:T(8,128)S(1)} %add_add_fusion.rest_0_), channel_id=1, source_target_pairs={{0,8},{2,10},{4,12},{6,14},{8,0},{10,2},{12,4},{14,6},{16,24},{18,... | collective-permute-start | bytes 98312 | tf_op jit(solution)/shard_map/ppermute | solution.py:503

commit v11 on v10

--- a/solution.py
+++ b/solution.py
@@ -507,9 +507,8 @@
     rounds = []
     base = 1
     while base < count:
-        turn = 1 if base > 1 else 0
         if base * 4 <= count:
-            rounds.append((base, 2 * base + turn, 3 * base + turn))
+            rounds.append((base + 1, 2 * base + 1, 3 * base + 1) if base > 1 else (1, 3, 2))
             base *= 4
         else:
             rounds.append((base,))

time: 32.3 us -> 32.1 us (level)
  waiting for transfers between devices: 5.7 us -> 5.12 us
  starting transfers between devices: 14.9 us -> 15.4 us
    ppermute x6, waiting for transfers between devices: 3.07 us -> 2.49 us  [swap(): lax.ppermute(x, 'sub', [(i, i ^ k) for i in range(count)])]
    ppermute x6, starting transfers between devices: 6.32 us -> 6.87 us  [swap(): lax.ppermute(x, 'sub', [(i, i ^ k) for i in range(count)])]
  transfers between devices with their start and end apart: 13 -> 13, of which waited for: 6 -> 4; matrix products, arithmetic and copies ran while one was open for 0% -> 0% of each run, Pallas kernels for 20% -> 20%
where the time goes in v11:
time: 32.1 us; the launch traced here: 32 us
  starting transfers between devices  15.4 us (48%)
  Pallas kernels  10.6 us (33%)
  waiting for transfers between devices  5.12 us (16%)
  between operations  0.8 us (2%)
    ppermute x6, starting transfers between devices, swap(): lax.ppermute(x, 'sub', [(i, i ^ k) for i in range(count)])  6.87 us
    ppermute x3, starting transfers between devices, across(): lax.ppermute(b, ('sub', 'rhs'), pairs + [(j, i) for i, j in pairs])  4.7 us
    ppermute x1, starting transfers between devices, body(): lax.ppermute(corner_basis, 'rhs', [((i + k) % parts, i) for i in range(pa...  3 us
    ppermute x3, waiting for transfers between devices, across(): lax.ppermute(b, ('sub', 'rhs'), pairs + [(j, i) for i, j in pairs])  2.62 us
    ppermute x6, waiting for transfers between devices, swap(): lax.ppermute(x, 'sub', [(i, i ^ k) for i in range(count)])  2.49 us
    pallas_call x1, Pallas kernels, body(): call(load_blocks, [packed, packed], 1, raw=(0,), scratch=[pltpu.VMEM((B *...  2.14 us
    pallas_call x1, Pallas kernels, body(): run(assemble, [dense, dense], 5, smem=(0,))  1.66 us
    pallas_call x1, Pallas kernels, body(): run(functools.partial(finish, ncoarse=ncoarse, n_pay=len(pays)), [shape(c...  1.56 us
  transfers between devices with their start and end apart: 13, of which 4 were waited for; matrix products, arithmetic and copies ran while one was open for 0% of the time, Pallas kernels for 20%

profile of v11, /device:TPU:0, one launch (start us, length us, event | category | flops | bytes accessed | tf_op | source)
XLA Modules:
  0.0 32.0 jit_solution(15354729453721063073)
XLA Ops:
  0.6 0.0 copy-start.3
  0.6 0.0 copy-start.2
  0.7 0.0 copy-start.5
  0.7 0.0 copy-start.6
  0.7 0.0 copy-start
  0.7 3.0 %collective-permute-start = (f32[4,512]{1,0:T(4,128)}, f32[4,512]{1,0:T(4,128)S(1)}, u32[]{:S(2)}, u32[]{:S(2)}) collective-permute-start(f32[4,512]{1,0:T(4,128)} %rest_0_.1), channel_id=1, source_target_pairs={{1,0},{0,1},{3,2},{2,3},{5,4},{4,5},{7,6},{6,7},{9,8},{8,9},{11,10... | collective-permute-start | bytes 24584 | tf_op jit(solution)/shard_map/ppermute | solution.py:552
  3.7 2.1 %shard_map.95 = (bf16[256,4096]{1,0:T(8,128)(2,1)S(1)}, bf16[256,4096]{1,0:T(8,128)(2,1)S(1)}) custom-call(f32[27,8,4096]{2,1,0:T(8,128)} %bitcast.3), custom_call_target="tpu_custom_call" | custom-call | bytes 16777216 | tf_op jit(solution)/shard_map/pallas_call | solution.py:556
  5.8 0.0 collective-permute-done.rest_1_
  5.8 0.0 copy-done.3
  5.9 0.0 copy-done.2
  5.9 0.0 copy-done.5
  5.9 0.0 copy-done.6
  5.9 0.0 copy-done
  5.9 0.8 %shard_map.96 = (f32[32,512]{1,0:T(8,128)S(1)}, f32[56,256]{1,0:T(8,128)S(1)}, f32[56,256]{1,0:T(8,128)S(1)}) custom-call(s32[1,2,4]{2,1,0:T(2,128)S(1)} %copy-done.2, s32[1,8]{1,0:T(1,128)S(1)} %copy-done.6, f32[32,512]{1,0:T(8,128)S(1)} %copy-done, f32[1,512]{1,0:T(1,128)S(1)} %bitcast.2, bf16[256,4096]{1,0:T(8,128)(2,1)S(1)} %get-tuple-element.23.after_ref.wh_ref, ...), custom_call_target="tpu_custom_call" | custom-call | tf_op jit(solution)/shard_map/pallas_call | solution.py:568
  6.7 1.8 %collective-permute-start.2 = (f32[56,256]{1,0:T(8,128)S(1)}, f32[56,256]{1,0:T(8,128)S(1)}, u32[]{:S(2)}, u32[]{:S(2)}) collective-permute-start(f32[56,256]{1,0:T(8,128)S(1)} %get-tuple-element.26.b_ref), channel_id=1, source_target_pairs={{2,4},{3,5},{6,8},{7,9},{10,12},{11,13},{14,16},{15,17},{18,20},{1... | collective-permute-start | bytes 172040 | tf_op jit(solution)/shard_map/ppermute | solution.py:525
  8.4 0.1 collective-permute-start.1
  8.6 0.0 copy-done.4
  8.6 1.7 %shard_map.97 = (bf16[512,1024]{1,0:T(8,128)(2,1)S(1)}, bf16[512,1024]{1,0:T(8,128)(2,1)S(1)}) custom-call(s32[1,2,4]{2,1,0:T(2,128)S(1)} %copy-done.2, s32[8,27]{1,0:T(8,128)S(1)} %copy-done.4, bf16[256,4096]{1,0:T(8,128)(2,1)S(1)} %get-tuple-element.23.after_ref.wh_ref, bf16[256,4096]{1,0:T(8,128)(2,1)S(1)} %get-tuple-element.27.wl_ref, ...), custom_call_target="tpu_custom_call" | custom-call | tf_op jit(solution)/shard_map/pallas_call | solution.py:576
  10.2 0.6 %shard_map.98 = (bf16[1024,512]{1,0:T(8,128)(2,1)S(1)}, bf16[1024,512]{1,0:T(8,128)(2,1)S(1)}) custom-call(bf16[512,1024]{1,0:T(8,128)(2,1)S(1)} %get-tuple-element.28.high_ref, bf16[512,1024]{1,0:T(8,128)(2,1)S(1)} %get-tuple-element.29.low_ref), custom_call_target="tpu_custom_call" | custom-call | tf_op jit(solution)/shard_map/pallas_call | solution.py:580
  10.8 0.1 collective-permute-done.2.gb_ref
  10.9 0.0 collective-permute-done.1.ga_ref
  10.9 0.9 %shard_map.99 = (f32[48,512]{1,0:T(8,128)S(1)}, f32[96,256]{1,0:T(8,128)S(1)}, f32[96,256]{1,0:T(8,128)S(1)}) custom-call(f32[56,256]{1,0:T(8,128)S(1)} %get-tuple-element.25.after_ref.a_ref, f32[56,256]{1,0:T(8,128)S(1)} %get-tuple-element.26.b_ref, f32[56,256]{1,0:T(8,128)S(1)} %collective-permute-done.1.ga_ref, ...), custom_call_target="tpu_custom_call" | custom-call | tf_op jit(solution)/shard_map/pallas_call | solution.py:586
  11.8 0.4 %collective-permute-start.3 = (f32[96,256]{1,0:T(8,128)S(1)}, f32[96,256]{1,0:T(8,128)S(1)}, u32[]{:S(2)}, u32[]{:S(2)}) collective-permute-start(f32[96,256]{1,0:T(8,128)S(1)} %get-tuple-element.32.own_a_ref), channel_id=1, source_target_pairs={{0,2},{2,0},{4,6},{6,4},{8,10},{10,8},{12,14},{14,12},{16,18},{18,... | collective-permute-start | bytes 294920 | tf_op jit(solution)/shard_map/ppermute | solution.py:520
  12.2 1.5 %collective-permute-start.4 = (f32[96,256]{1,0:T(8,128)S(1)}, f32[96,256]{1,0:T(8,128)S(1)}, u32[]{:S(2)}, u32[]{:S(2)}) collective-permute-start(f32[96,256]{1,0:T(8,128)S(1)} %get-tuple-element.33.own_b_ref), channel_id=1, source_target_pairs={{2,4},{3,5},{6,8},{7,9},{10,12},{11,13},{14,16},{15,17},{18,20},{1... | collective-permute-start | bytes 294920 | tf_op jit(solution)/shard_map/ppermute | solution.py:525
  13.6 0.6 %shard_map.100 = (f32[16,256]{1,0:T(8,128)S(1)}, f32[8,32]{1,0:T(8,128)S(1)}) custom-call(f32[32,512]{1,0:T(8,128)S(1)} %get-tuple-element.24.resid_ref, f32[56,256]{1,0:T(8,128)S(1)} %get-tuple-element.25.after_ref.a_ref, f32[56,256]{1,0:T(8,128)S(1)} %get-tuple-element.26.b_ref, f32[48,512]{1,0:T(8,128)S(1)} %get-tuple-element.34.strain_ref), custom_call_target="tpu_custom_call" | custom-call | tf_op jit(solution)/shard_map/pallas_call | solution.py:590
  14.2 0.0 collective-permute-done.3.got_a_ref
  14.2 2.5 %collective-permute-done.4.got_b_ref = f32[96,256]{1,0:T(8,128)S(1)} collective-permute-done((f32[96,256]{1,0:T(8,128)S(1)}, f32[96,256]{1,0:T(8,128)S(1)}, u32[]{:S(2)}, u32[]{:S(2)}) %collective-permute-start.4) | collective-permute-done | bytes 98336 | tf_op jit(solution)/shard_map/ppermute | solution.py:525
  16.8 1.0 %shard_map.101 = (f32[48,512]{1,0:T(8,128)S(1)}, f32[48,512]{1,0:T(8,128)S(1)}, f32[48,512]{1,0:T(8,128)S(1)}, f32[32,256]{1,0:T(8,128)S(1)}) custom-call(f32[56,256]{1,0:T(8,128)S(1)} %get-tuple-element.25.after_ref.a_ref, f32[56,256]{1,0:T(8,128)S(1)} %get-tuple-element.26.b_ref, f32[56,256]{1,0:T(8,128)S(1)} %collective-permute-done.1.ga_ref, ...), custom_call_target="tpu_custom_call" | custom-call | tf_op jit(solution)/shard_map/pallas_call | solution.py:596
  17.8 0.0 copy-start.1
  17.8 1.0 %collective-permute-start.9 = (f32[32,256]{1,0:T(8,128)S(1)}, f32[32,256]{1,0:T(8,128)S(1)}, u32[]{:S(2)}, u32[]{:S(2)}) collective-permute-start(f32[32,256]{1,0:T(8,128)S(1)} %get-tuple-element.43), channel_id=1, source_target_pairs={{0,4},{2,6},{4,0},{6,2},{8,12},{10,14},{12,8},{14,10},{16,20},{18,... | collective-permute-start | bytes 98312 | tf_op jit(solution)/shard_map/ppermute | solution.py:503
  18.8 1.0 %collective-permute-start.8 = (f32[32,256]{1,0:T(8,128)S(1)}, f32[32,256]{1,0:T(8,128)S(1)}, u32[]{:S(2)}, u32[]{:S(2)}) collective-permute-start(f32[32,256]{1,0:T(8,128)S(1)} %get-tuple-element.43), channel_id=1, source_target_pairs={{0,6},{2,4},{4,2},{6,0},{8,14},{10,12},{12,10},{14,8},{16,22},{18,... | collective-permute-start | bytes 98312 | tf_op jit(solution)/shard_map/ppermute | solution.py:503
  19.8 0.2 collective-permute-start.7
  20.0 0.5 %shard_map.102 = (f32[48,512]{1,0:T(8,128)S(1)}, f32[48,256]{1,0:T(8,128)S(1)}, f32[48,256]{1,0:T(8,128)S(1)}) custom-call(f32[48,512]{1,0:T(8,128)S(1)} %get-tuple-element.38.scaled_ref, f32[48,512]{1,0:T(8,128)S(1)} %get-tuple-element.39.strain_ref, bf16[512,1024]{1,0:T(8,128)(2,1)S(1)} %get-tuple-element.28.high_ref, ...), custom_call_target="tpu_custom_call" | custom-call | tf_op jit(solution)/shard_map/pallas_call | solution.py:605
  20.4 0.3 %collective-permute-start.5 = (f32[48,256]{1,0:T(8,128)S(1)}, f32[48,256]{1,0:T(8,128)S(1)}, u32[]{:S(2)}, u32[]{:S(2)}) collective-permute-start(f32[48,256]{1,0:T(8,128)S(1)} %get-tuple-element.41), channel_id=1, source_target_pairs={{0,2},{2,0},{4,6},{6,4},{8,10},{10,8},{12,14},{14,12},{16,18},{18,... | collective-permute-start | bytes 147464 | tf_op jit(solution)/shard_map/ppermute | solution.py:520
  20.8 1.5 %collective-permute-start.6 = (f32[48,256]{1,0:T(8,128)S(1)}, f32[48,256]{1,0:T(8,128)S(1)}, u32[]{:S(2)}, u32[]{:S(2)}) collective-permute-start(f32[48,256]{1,0:T(8,128)S(1)} %get-tuple-element.42), channel_id=1, source_target_pairs={{2,4},{3,5},{6,8},{7,9},{10,12},{11,13},{14,16},{15,17},{18,20},{1... | collective-permute-start | bytes 147464 | tf_op jit(solution)/shard_map/ppermute | solution.py:525
  22.3 0.0 collective-permute-done.9
  22.3 0.0 collective-permute-done.8
  22.3 0.0 collective-permute-done.7
  22.3 3.8 %collective-permute-start.12 = (f32[32,256]{1,0:T(8,128)S(1)}, f32[32,256]{1,0:T(8,128)S(1)}, u32[]{:S(2)}, u32[]{:S(2)}) collective-permute-start(f32[32,256]{1,0:T(8,128)S(1)} %add_add_fusion.rest_0_), channel_id=1, source_target_pairs={{0,26},{2,24},{4,30},{6,28},{8,18},{10,16},{12,22},{14,20},{16,10}... | collective-permute-start | bytes 98312 | tf_op jit(solution)/shard_map/ppermute | solution.py:503
  26.2 0.0 collective-permute-start.11
  26.2 0.8 %collective-permute-start.10 = (f32[32,256]{1,0:T(8,128)S(1)}, f32[32,256]{1,0:T(8,128)S(1)}, u32[]{:S(2)}, u32[]{:S(2)}) collective-permute-start(f32[32,256]{1,0:T(8,128)S(1)} %add_add_fusion.rest_0_), channel_id=1, source_target_pairs={{0,10},{2,8},{4,14},{6,12},{8,2},{10,0},{12,6},{14,4},{16,26},{18,... | collective-permute-start | bytes 98312 | tf_op jit(solution)/shard_map/ppermute | solution.py:503
  27.0 0.0 collective-permute-done.5.got_a_ref
  27.0 0.0 collective-permute-done.6.got_b_ref
  27.0 0.9 %shard_map.103.all_ref = f32[232,512]{1,0:T(8,128)S(1)} custom-call(s32[1,2,4]{2,1,0:T(2,128)S(1)} %copy-done.2, f32[32,512]{1,0:T(8,128)S(1)} %get-tuple-element.24.resid_ref, f32[56,256]{1,0:T(8,128)S(1)} %get-tuple-element.25.after_ref.a_ref, f32[56,256]{1,0:T(8,128)S(1)} %get-tuple-element.26.b_ref, f32[48,512]{1,0:T(8,128)S(1)} %get-tuple-element.37.image_ref, ...), custom_call_target="tpu_custom_call" | custom-call | tf_op jit(solution)/shard_map/pallas_call | solution.py:610
  27.9 0.2 collective-permute-done.12.rest_3_
  28.1 2.3 %collective-permute-done.11.rest_2_ = f32[32,256]{1,0:T(8,128)S(1)} collective-permute-done((f32[32,256]{1,0:T(8,128)S(1)}, f32[32,256]{1,0:T(8,128)S(1)}, u32[]{:S(2)}, u32[]{:S(2)}) %collective-permute-start.11) | collective-permute-done | bytes 32800 | tf_op jit(solution)/shard_map/ppermute | solution.py:503
  30.4 0.0 collective-permute-done.10.rest_1_
  30.4 1.6 %shard_map.104 = (f32[32,512]{1,0:T(8,128)}, f32[32,512]{1,0:T(8,128)}) custom-call(f32[32,32]{1,0:T(8,128)S(1)} %copy-done.1, f32[232,512]{1,0:T(8,128)S(1)} %shard_map.103.all_ref, f32[32,256]{1,0:T(8,128)S(1)} %add_add_fusion.rest_0_, f32[32,256]{1,0:T(8,128)S(1)} %collective-permute-done.10.rest_1_, f32[32,256]{1,0:T(8,128)S(1)} %collective-permute-done.11.rest_2_, ...), custom_call_target="tpu_custom_call" | custom-call | tf_op jit(solution)/shard_map/pallas_call | solution.py:618
  (3 shorter events, 0.0 us)
Async XLA Ops:
  0.6 5.2 %copy-start.3 = (f32[4,512]{1,0:T(4,128)S(1)}, f32[4,512]{1,0:T(4,128)}, u32[]{:S(2)}) copy-start(f32[4,512]{1,0:T(4,128)} %rest_0_.1) | copy-start | bytes 24580
  0.6 5.2 %copy-start.2 = (s32[1,2,4]{2,1,0:T(2,128)S(1)}, s32[1,2,4]{2,1,0:T(2,128)}, u32[]{:S(2)}) copy-start(s32[1,2,4]{2,1,0:T(2,128)} %rows_ref.5) | copy-start | bytes 100
  0.7 5.2 %copy-start.5 = (f32[512]{0:T(512)S(1)}, f32[512]{0:T(512)}, u32[]{:S(2)}) copy-start(f32[512]{0:T(512)} %param.14) | copy-start | bytes 6148
  0.7 5.2 %copy-start.6 = (s32[1,8]{1,0:T(1,128)S(1)}, s32[1,8]{1,0:T(1,128)}, u32[]{:S(2)}) copy-start(s32[1,8]{1,0:T(1,128)} %owner_ref.1) | copy-start | bytes 100
  0.7 5.2 %copy-start = (f32[32,512]{1,0:T(8,128)S(1)}, f32[32,512]{1,0:T(8,128)}, u32[]{:S(2)}) copy-start(f32[32,512]{1,0:T(8,128)} %right_ref.1) | copy-start | bytes 196612
  0.7 5.2 %collective-permute-start = (f32[4,512]{1,0:T(4,128)}, f32[4,512]{1,0:T(4,128)S(1)}, u32[]{:S(2)}, u32[]{:S(2)}) collective-permute-start(f32[4,512]{1,0:T(4,128)} %rest_0_.1), channel_id=1, source_target_pairs={{1,0},{0,1},{3,2},{2,3},{5,4},{4,5},{7,6},{6,7},{9,8},{8,9},{11,10... | collective-permute-start | bytes 24584 | tf_op jit(solution)/shard_map/ppermute | solution.py:552
  3.7 4.9 %copy-start.4 = (s32[8,27]{1,0:T(8,128)S(1)}, s32[8,27]{1,0:T(8,128)}, u32[]{:S(2)}) copy-start(s32[8,27]{1,0:T(8,128)} %columns_ref.1) | copy-start | bytes 2596
  6.7 4.2 %collective-permute-start.2 = (f32[56,256]{1,0:T(8,128)S(1)}, f32[56,256]{1,0:T(8,128)S(1)}, u32[]{:S(2)}, u32[]{:S(2)}) collective-permute-start(f32[56,256]{1,0:T(8,128)S(1)} %get-tuple-element.26.b_ref), channel_id=1, source_target_pairs={{2,4},{3,5},{6,8},{7,9},{10,12},{11,13},{14,16},{15,17},{18,20},{1... | collective-permute-start | bytes 172040 | tf_op jit(solution)/shard_map/ppermute | solution.py:525
  8.4 2.5 %collective-permute-start.1 = (f32[56,256]{1,0:T(8,128)S(1)}, f32[56,256]{1,0:T(8,128)S(1)}, u32[]{:S(2)}, u32[]{:S(2)}) collective-permute-start(f32[56,256]{1,0:T(8,128)S(1)} %get-tuple-element.25.after_ref.a_ref), channel_id=1, source_target_pairs={{0,2},{2,0},{4,6},{6,4},{8,10},{10,8},{12,14},{14,12},{16,18},{18,... | collective-permute-start | bytes 172040 | tf_op jit(solution)/shard_map/ppermute | solution.py:520
  11.8 2.4 %collective-permute-start.3 = (f32[96,256]{1,0:T(8,128)S(1)}, f32[96,256]{1,0:T(8,128)S(1)}, u32[]{:S(2)}, u32[]{:S(2)}) collective-permute-start(f32[96,256]{1,0:T(8,128)S(1)} %get-tuple-element.32.own_a_ref), channel_id=1, source_target_pairs={{0,2},{2,0},{4,6},{6,4},{8,10},{10,8},{12,14},{14,12},{16,18},{18,... | collective-permute-start | bytes 294920 | tf_op jit(solution)/shard_map/ppermute | solution.py:520
  12.2 4.6 %collective-permute-start.4 = (f32[96,256]{1,0:T(8,128)S(1)}, f32[96,256]{1,0:T(8,128)S(1)}, u32[]{:S(2)}, u32[]{:S(2)}) collective-permute-start(f32[96,256]{1,0:T(8,128)S(1)} %get-tuple-element.33.own_b_ref), channel_id=1, source_target_pairs={{2,4},{3,5},{6,8},{7,9},{10,12},{11,13},{14,16},{15,17},{18,20},{1... | collective-permute-start | bytes 294920 | tf_op jit(solution)/shard_map/ppermute | solution.py:525
  17.8 12.6 %copy-start.1 = (f32[32,32]{1,0:T(8,128)S(1)}, f32[32,32]{1,0:T(8,128)}, u32[]{:S(2)}) copy-start(f32[32,32]{1,0:T(8,128)} %inverse_ref.1) | copy-start | bytes 12292
  17.8 4.5 %collective-permute-start.9 = (f32[32,256]{1,0:T(8,128)S(1)}, f32[32,256]{1,0:T(8,128)S(1)}, u32[]{:S(2)}, u32[]{:S(2)}) collective-permute-start(f32[32,256]{1,0:T(8,128)S(1)} %get-tuple-element.43), channel_id=1, source_target_pairs={{0,4},{2,6},{4,0},{6,2},{8,12},{10,14},{12,8},{14,10},{16,20},{18,... | collective-permute-start | bytes 98312 | tf_op jit(solution)/shard_map/ppermute | solution.py:503
  18.8 3.5 %collective-permute-start.8 = (f32[32,256]{1,0:T(8,128)S(1)}, f32[32,256]{1,0:T(8,128)S(1)}, u32[]{:S(2)}, u32[]{:S(2)}) collective-permute-start(f32[32,256]{1,0:T(8,128)S(1)} %get-tuple-element.43), channel_id=1, source_target_pairs={{0,6},{2,4},{4,2},{6,0},{8,14},{10,12},{12,10},{14,8},{16,22},{18,... | collective-permute-start | bytes 98312 | tf_op jit(solution)/shard_map/ppermute | solution.py:503
  19.8 2.5 %collective-permute-start.7 = (f32[32,256]{1,0:T(8,128)S(1)}, f32[32,256]{1,0:T(8,128)S(1)}, u32[]{:S(2)}, u32[]{:S(2)}) collective-permute-start(f32[32,256]{1,0:T(8,128)S(1)} %get-tuple-element.43), channel_id=1, source_target_pairs={{0,2},{2,0},{4,6},{6,4},{8,10},{10,8},{12,14},{14,12},{16,18},{18,... | collective-permute-start | bytes 98312 | tf_op jit(solution)/shard_map/ppermute | solution.py:503
  20.4 6.5 %collective-permute-start.5 = (f32[48,256]{1,0:T(8,128)S(1)}, f32[48,256]{1,0:T(8,128)S(1)}, u32[]{:S(2)}, u32[]{:S(2)}) collective-permute-start(f32[48,256]{1,0:T(8,128)S(1)} %get-tuple-element.41), channel_id=1, source_target_pairs={{0,2},{2,0},{4,6},{6,4},{8,10},{10,8},{12,14},{14,12},{16,18},{18,... | collective-permute-start | bytes 147464 | tf_op jit(solution)/shard_map/ppermute | solution.py:520
  20.8 6.2 %collective-permute-start.6 = (f32[48,256]{1,0:T(8,128)S(1)}, f32[48,256]{1,0:T(8,128)S(1)}, u32[]{:S(2)}, u32[]{:S(2)}) collective-permute-start(f32[48,256]{1,0:T(8,128)S(1)} %get-tuple-element.42), channel_id=1, source_target_pairs={{2,4},{3,5},{6,8},{7,9},{10,12},{11,13},{14,16},{15,17},{18,20},{1... | collective-permute-start | bytes 147464 | tf_op jit(solution)/shard_map/ppermute | solution.py:525
  22.3 5.8 %collective-permute-start.12 = (f32[32,256]{1,0:T(8,128)S(1)}, f32[32,256]{1,0:T(8,128)S(1)}, u32[]{:S(2)}, u32[]{:S(2)}) collective-permute-start(f32[32,256]{1,0:T(8,128)S(1)} %add_add_fusion.rest_0_), channel_id=1, source_target_pairs={{0,26},{2,24},{4,30},{6,28},{8,18},{10,16},{12,22},{14,20},{16,10}... | collective-permute-start | bytes 98312 | tf_op jit(solution)/shard_map/ppermute | solution.py:503
  26.2 4.2 %collective-permute-start.11 = (f32[32,256]{1,0:T(8,128)S(1)}, f32[32,256]{1,0:T(8,128)S(1)}, u32[]{:S(2)}, u32[]{:S(2)}) collective-permute-start(f32[32,256]{1,0:T(8,128)S(1)} %add_add_fusion.rest_0_), channel_id=1, source_target_pairs={{0,18},{2,16},{4,22},{6,20},{8,26},{10,24},{12,30},{14,28},{16,2},... | collective-permute-start | bytes 98312 | tf_op jit(solution)/shard_map/ppermute | solution.py:503
  26.2 4.2 %collective-permute-start.10 = (f32[32,256]{1,0:T(8,128)S(1)}, f32[32,256]{1,0:T(8,128)S(1)}, u32[]{:S(2)}, u32[]{:S(2)}) collective-permute-start(f32[32,256]{1,0:T(8,128)S(1)} %add_add_fusion.rest_0_), channel_id=1, source_target_pairs={{0,10},{2,8},{4,14},{6,12},{8,2},{10,0},{12,6},{14,4},{16,26},{18,... | collective-permute-start | bytes 98312 | tf_op jit(solution)/shard_map/ppermute | solution.py:503
